TPU v7x, 128 devices: a whole 4x4x4 slice. The times are simulated.
128 devices in a mesh: tm: 32 (over y, z, core), series: 4 (over x).
Axes of the slice: x: 4, y: 4, z: 4, core: 2. Of those that a mesh axis runs over, the one named last changes fastest.
Arguments:
- signal: float32 [64, 1048576], P('series', 'tm')
- valid_start: int32 [64], replicated, may hold values from 0 to 262143
- valid_end: int32 [64], replicated, may hold values from 786433 to 1048576
Outputs:
- smooth: float32 [64, 1048576], P('series', 'tm')
- slope: float32 [64, 1048576], P('series', 'tm')
- covariance: float32 [64, 64], P('series')
Inputs may be any that keep to these rules, and one draw needn't show every extreme that they name: `valid_end`: end of the valid samples of each series.
All inputs are finite; a program needn't handle non-finite values.
Results may differ from a plain program's by a relative error of at most 0.00015.
Values sent between devices are 32-bit elements; how exact they have to be, the bound alone decides.
No kernel may reach another device: no remote copies, remote signals or barrier semaphores. Data moves between devices by JAX's collectives and lax.ppermute only.
A program may use at most 64 MiB of HBM per device.

v0:
```python
import jax
import jax.numpy as jnp
from jax import lax
from jax.sharding import PartitionSpec as P

HALF = 16


def padded(cells, sides, width):
    for axis, dim in sides:
        count = lax.axis_size(axis)
        ends = count - 1
        head = lax.slice_in_dim(cells, 0, width, axis=dim)
        tail = lax.slice_in_dim(cells, cells.shape[dim] - width, cells.shape[dim], axis=dim)
        cells = jnp.concatenate(
            [
                lax.ppermute(tail, axis, [(i, (i + 1) % count) for i in range(ends)]),
                cells,
                lax.ppermute(head, axis, [((i + 1) % count, i) for i in range(ends)]),
            ],
            axis=dim,
        )
    return cells


def split_up(shard, dim, count):
    before, after = (shard.shape[:dim], shard.shape[dim + 1 :])
    return jnp.moveaxis(shard.reshape(*before, count, -1, *after), dim, 0)


def summed_on_arrival(shard, axis, dim):
    count = lax.axis_size(axis)
    tiles = lax.all_to_all(split_up(shard, dim, count), axis, 0, 0, tiled=True)
    return jnp.sum(tiles, axis=0)


def from_everyone(shard, axis):
    copies = jnp.broadcast_to(shard, (lax.axis_size(axis), *shard.shape))
    return lax.all_to_all(copies, axis, split_axis=0, concat_axis=0, tiled=True)


def over_copies(shard, axis):
    return from_everyone(shard, axis).sum(axis=0)


def cross_rows(left, right):
    return lax.dot_general(
        left,
        right,
        (((1,), (1,)), ((), ())),
        precision=lax.Precision.HIGHEST,
        preferred_element_type=jnp.float32,
    )


def held_value(field, spot):
    return jnp.take_along_axis(field, spot, axis=1)


def shards(signal, valid_start, valid_end):
    rows, width = signal.shape
    taps = 2 * HALF + 1
    offsets = jnp.arange(-HALF, HALF + 1).astype(jnp.float32)
    second = jnp.sum(offsets * offsets)
    centre_sq = second / taps
    curved = offsets * offsets - centre_sq
    fourth = jnp.sum(curved * curved)
    extended = padded(signal, (("tm", 1),), 2 * HALF)
    span = width + 2 * HALF
    level = jnp.zeros((rows, span), jnp.float32)
    tilt = jnp.zeros((rows, span), jnp.float32)
    bend = jnp.zeros((rows, span), jnp.float32)
    for m in range(taps):
        window = extended[:, m : m + span]
        level = level + window * (1.0 / taps)
        tilt = tilt + window * (offsets[m] / second)
        bend = bend + window * (curved[m] / fourth)
    begin = lax.axis_index("tm") * width
    group = lax.axis_index("series") * rows
    first = lax.dynamic_slice_in_dim(valid_start, group, rows)[:, None]
    last = lax.dynamic_slice_in_dim(valid_end, group, rows)[:, None]
    moment = begin + jnp.arange(width, dtype=jnp.int32)[None, :]
    low_centre = first + HALF
    high_centre = last - HALF - 1
    centre = jnp.clip(moment, low_centre, high_centre)
    low_spot = jnp.clip(low_centre - begin + HALF, 0, span - 1)
    high_spot = jnp.clip(high_centre - begin + HALF, 0, span - 1)
    below = moment < low_centre
    above = moment > high_centre
    along = (moment - centre).astype(jnp.float32)
    lv = jnp.where(
        below,
        held_value(level, low_spot),
        jnp.where(above, held_value(level, high_spot), level[:, HALF : HALF + width]),
    )
    tl = jnp.where(
        below,
        held_value(tilt, low_spot),
        jnp.where(above, held_value(tilt, high_spot), tilt[:, HALF : HALF + width]),
    )
    bd = jnp.where(
        below,
        held_value(bend, low_spot),
        jnp.where(above, held_value(bend, high_spot), bend[:, HALF : HALF + width]),
    )
    inside = (moment >= first) & (moment < last)
    smooth = jnp.where(inside, lv + tl * along + bd * (along * along - centre_sq), 0.0)
    slope = jnp.where(inside, HALF * (tl + 2.0 * along * bd), 0.0)
    resid = jnp.where(inside, signal - smooth, 0.0)
    mixed = lax.all_to_all(resid, "series", split_axis=1, concat_axis=0, tiled=True)
    gram = summed_on_arrival(cross_rows(mixed, mixed), "series", 0)
    gram = over_copies(gram, "tm")
    correlation = (
        jnp.minimum(last, valid_end[None, :]) - jnp.maximum(first, valid_start[None, :])
    ).astype(jnp.float32)
    return (smooth, slope, gram / correlation)


def solution(mesh):
    in_specs = (P("series", "tm"), P(), P())
    out_specs = (P("series", "tm"), P("series", "tm"), P("series", None))
    return jax.shard_map(shards, mesh=mesh, in_specs=in_specs, out_specs=out_specs, check_vma=False)
```

profile of v0, /device:TPU:1, one launch (start us, length us, event | category | flops | bytes accessed | tf_op | source)
XLA Modules:
  0.0 243.7 jit_solution(17497777037096725441)
XLA Ops:
  0.6 0.8 fusion.16
  1.4 4.9 %collective-permute-start = (f32[16,32]{1,0:T(8,128)S(1)}, f32[16,32]{1,0:T(8,128)S(1)}, u32[]{:S(2)}, u32[]{:S(2)}) collective-permute-start(f32[16,32]{1,0:T(8,128)S(1)} %get-tuple-element.11), channel_id=1, source_target_pairs={{0,4},{4,8},{8,12},{12,16},{16,20},{20,24},{24,28},{28,32},{32,36}... | collective-permute-start | bytes 6152 | tf_op jit(solution)/shard_map/ppermute | solution.py:17
  6.3 1.9 collective-permute-start.1
  8.3 0.6 multiply_reduce_fusion.1
  8.9 0.7 fusion.17
  9.6 0.7 fusion.18
  10.3 3.1 %constant_dynamic-update-slice_fusion.1 = f32[16,32800]{1,0:T(8,128)} fusion(f32[16,32768]{1,0:T(8,128)} %param.5), kind=kLoop, calls=%fused_computation.29 | loop fusion | bytes 4194304
  14.1 0.6 multiply_reduce_fusion
  14.7 0.7 fusion.19
  15.4 0.7 fusion.20
  101.5 0.3 dynamic-update-slice.2
  101.8 6.4 %dynamic-update-slice.3 = f32[16,32832]{1,0:T(8,128)S(1)} dynamic-update-slice(f32[16,32832]{1,0:T(8,128)S(1)} %dynamic-update-slice.2, f32[16,32768]{1,0:T(8,128)} %param.5, s32[]{} %constant.163, s32[]{} %constant.165) | dynamic-update-slice | bytes 4194308
  108.2 0.6 constant_dynamic-update-slice_fusion
  108.9 19.9 %multiply_add_fusion.1 = f32[16,32800]{1,0:T(8,128)} fusion(f32[16,32800]{1,0:T(8,128)} %constant_dynamic-update-slice_fusion, f32[16,32832]{1,0:T(8,128)S(1)} %dynamic-update-slice.4, f32[16,32768]{1,0:T(8,128)} %param.5, f32[16,32]{1,0:T(8,128)S(1)} %collective-permute-done, f32[]{:T(128)S(6)} %div.236, f32[]{:T(128)S(6)} %div.235, f32[]{:T(128)S(6)} %div.234, ...), kind=kLoop, calls=%fused_computation.15 | loop fusion | flops 34636800 | bytes 71372928 | tf_op jit(solution)/shard_map/add | solution.py:76
  128.8 1.5 gather_fusion.2
  130.3 1.6 gather_fusion.3
  132.0 19.9 %multiply_add_fusion = f32[16,32800]{1,0:T(8,128)} fusion(f32[16,32800]{1,0:T(8,128)} %constant_dynamic-update-slice_fusion, f32[16,32832]{1,0:T(8,128)S(1)} %dynamic-update-slice.4, f32[16,32768]{1,0:T(8,128)} %param.5, f32[16,32]{1,0:T(8,128)S(1)} %collective-permute-done, f32[]{:T(128)S(6)} %div.270, f32[]{:T(128)S(6)} %div.269, f32[]{:T(128)S(6)} %div.268, ...), kind=kLoop, calls=%fused_computation.14 | loop fusion | flops 34636800 | bytes 71372928 | tf_op jit(solution)/shard_map/add | solution.py:77
  151.8 1.5 gather_fusion.4
  153.3 1.6 gather_fusion.5
  155.0 19.9 %add_multiply_fusion = f32[16,32800]{1,0:T(8,128)} fusion(f32[16,32800]{1,0:T(8,128)} %constant_dynamic-update-slice_fusion, f32[16,32832]{1,0:T(8,128)S(1)} %dynamic-update-slice.4, f32[16,32768]{1,0:T(8,128)} %param.5, f32[16,32]{1,0:T(8,128)S(1)} %collective-permute-done), kind=kLoop, calls=%fused_computation.13 | loop fusion | flops 17843200 | bytes 71372800 | tf_op jit(solution)/shard_map/add | solution.py:75
  174.9 1.5 gather_fusion
  176.4 1.7 gather_fusion.1
  178.0 6.0 %subtract_select_fusion = (f32[16,32768]{1,0:T(8,128)S(1)}, f32[16,32768]{1,0:T(8,128)}, f32[16,32768]{1,0:T(8,128)}) fusion(f32[16,32768]{1,0:T(8,128)} %param.5, s32[32768]{0:T(1024)S(1)} %iota_add_fusion, s32[16]{0:T(128)S(1)} %get-tuple-element.9, s32[16]{0:T(128)S(1)} %get-tuple-element.7, f32[]{:T(128)S(6)} %div.237, f32[16,32800]{1,0:T(8,128)} %multiply_add_fusion, ...), kind=kLoop, calls=%fused_computation.22 | loop fusion | flops 15204352 | bytes 14811780 | tf_op jit(solution)/shard_map/jit(_where)/select_n | solution.py:109
  184.1 29.2 %all_to_all.29 = f32[16,4,8192]{2,0,1:T(8,128)S(1)} all-to-all(f32[16,4,8192]{2,0,1:T(8,128)S(1)} %bitcast.164), channel_id=1, replica_groups=mesh['tm'=32,'series'=4] {'series'}, dimensions={1} | all-to-all | bytes 4194304 | tf_op jit(solution)/shard_map/all_to_all | solution.py:110
  213.4 1.8 fusion.3
  215.3 6.6 %all_to_all.30 = f32[4,1,1024]{2,1,0:T(1,128)S(1)} all-to-all(f32[4,1,1024]{2,1,0:T(1,128)S(1)} %reshape.138), channel_id=1, replica_groups=mesh['tm'=32,'series'=4] {'series'}, dimensions={0} | all-to-all | bytes 32768 | tf_op jit(solution)/shard_map/all_to_all | solution.py:33
  221.8 0.5 broadcast.317
  222.4 0.7 reduce
  223.2 0.2 reshape.140
  223.4 18.5 %all_to_all.31 = f32[32,1,1024]{2,1,0:T(1,128)S(1)} all-to-all(f32[32,1,1024]{2,1,0:T(1,128)S(1)} %reshape.140), channel_id=1, replica_groups=mesh['tm'=32,'series'=4] {'tm'}, dimensions={0} | all-to-all | bytes 262144 | tf_op jit(solution)/shard_map/all_to_all | solution.py:39
  241.9 1.0 reduce.1
  243.0 0.7 convert_divide_fusion
  (27 shorter events, 0.9 us)
Async XLA Ops:
  1.4 100.1 %collective-permute-start = (f32[16,32]{1,0:T(8,128)S(1)}, f32[16,32]{1,0:T(8,128)S(1)}, u32[]{:S(2)}, u32[]{:S(2)}) collective-permute-start(f32[16,32]{1,0:T(8,128)S(1)} %get-tuple-element.11), channel_id=1, source_target_pairs={{0,4},{4,8},{8,12},{12,16},{16,20},{20,24},{24,28},{28,32},{32,36}... | collective-permute-start | bytes 6152 | tf_op jit(solution)/shard_map/ppermute | solution.py:17
  6.3 101.8 %collective-permute-start.1 = (f32[16,32]{1,0:T(8,128)S(1)}, f32[16,32]{1,0:T(8,128)S(1)}, u32[]{:S(2)}, u32[]{:S(2)}) collective-permute-start(f32[16,32]{1,0:T(8,128)S(1)} %get-tuple-element.12), channel_id=1, source_target_pairs={{4,0},{8,4},{12,8},{16,12},{20,16},{24,20},{28,24},{32,28},{36,32}... | collective-permute-start | bytes 6152 | tf_op jit(solution)/shard_map/ppermute | solution.py:19
  10.3 49.0 %copy-start.1 = (s32[64]{0:T(128)S(1)}, s32[64]{0:T(128)}, u32[]{:S(2)}) copy-start(s32[64]{0:T(128)} %param.6) | copy-start | bytes 772
  10.3 49.1 %copy-start = (s32[64]{0:T(128)S(1)}, s32[64]{0:T(128)}, u32[]{:S(2)}) copy-start(s32[64]{0:T(128)} %param.7) | copy-start | bytes 772
where the time goes:
time: 246 us; the launch traced here: 244 us
  between operations  86.5 us (35%)
  other arithmetic  69.5 us (28%)
  blocking collectives  54.3 us (22%)
  local copies, waits for them, and re-layouts  24.7 us (10%)
  starting transfers between devices  6.83 us (3%)
    all_to_all x1, blocking collectives, shards(): lax.all_to_all(resid, 'series', split_axis=1, concat_axis=0, tiled=True)  29.2 us
    add x1, other arithmetic, shards(): bend = bend + window * (curved[m] / fourth)  19.9 us
    add x1, other arithmetic, shards(): tilt = tilt + window * (offsets[m] / second)  19.9 us
    add x1, other arithmetic, shards(): level = level + window * (1.0 / taps)  19.9 us
    all_to_all x1, blocking collectives, from_everyone(): return lax.all_to_all(copies, axis, split_axis=0, concat_axis=0, tiled=True)  18.5 us
    unnamed x11, local copies, waits for them, and re-layouts  10.2 us
    gather x6, local copies, waits for them, and re-layouts, held_value(): return jnp.take_along_axis(field, spot, axis=1)  9.45 us
    all_to_all x1, blocking collectives, summed_on_arrival(): tiles = lax.all_to_all(split_up(shard, dim, count), axis, 0, 0, tiled=True)  6.56 us
  transfers between devices with their start and end apart: 2, of which 0 were waited for; matrix products, arithmetic and copies ran while one was open for 6% of the time, Pallas kernels for 0%

commit v1 on v0

v1 whole, which is shorter than its diff:
```python
import functools

import jax
import jax.numpy as jnp
import numpy as np
from jax import lax
from jax.experimental import pallas as pl
from jax.experimental.pallas import tpu as pltpu
from jax.sharding import Mesh
from jax.sharding import PartitionSpec as P


HALF = 16
TAPS = 2 * HALF + 1
ROWS = 16
GROUPS = 4
LANES = 128
SPAN = 2048
BLOCKS = SPAN // LANES
TIME = ("y", "z", "core")
MIB = 1 << 20

SECOND = float(sum(j * j for j in range(-HALF, HALF + 1)))
CENTRE_SQ = SECOND / TAPS
FOURTH = float(sum((j * j - CENTRE_SQ) ** 2 for j in range(-HALF, HALF + 1)))
SMOOTH_SCALE = 2048.0 / 2387.0
SLOPE_SCALE = HALF * 16.0 / SECOND


def filter_matrix():
    place = np.concatenate([np.arange(128), np.arange(128, 192), np.arange(-64, 0)])
    j = place[:, None] - np.arange(LANES)[None, :]
    near = np.abs(j) <= HALF
    smooth = np.where(near, (163 - j * j) / 2048.0, 0.0)
    slope = np.where(near, j / 16.0, 0.0)
    return np.concatenate([smooth, slope], axis=1).astype(np.float32)


def thirds(x):
    a = x.astype(jnp.bfloat16)
    rest = x - a.astype(jnp.float32)
    b = rest.astype(jnp.bfloat16)
    c = (rest - b.astype(jnp.float32)).astype(jnp.bfloat16)
    return a, b, c


def aligned(start, size):
    return pl.ds(pl.multiple_of(start, LANES), size)


def fit_kernel(base, count, ends, chain, *refs):
    refs = list(refs)
    first_ref, last_ref, signal_ref, taps_hbm = refs[:4]
    refs = refs[4:]
    if ends:
        halo_refs, refs = refs[:2], refs[2:]
    if chain:
        refs = refs[2:]
    smooth_hbm, slope_hbm = refs[:2]
    outs, refs = refs[2:6], refs[6:]
    if not ends:
        edge_refs, refs = refs[:2], refs[2:]
    x_ref, fit_ref, resid_ref, taps_ref, in_sems, out_sems, piece_sems, side_sems = refs

    width = signal_ref.shape[1]
    total = width // SPAN
    per = count // GROUPS
    half = count // 2
    mine = lax.axis_index("series")
    begin = lax.axis_index(TIME) * width

    def place(n):
        return LANES + n * SPAN + (2 * LANES * (n // half) if ends else 0)

    def fetch(n):
        return pltpu.make_async_copy(
            signal_ref.at[:, aligned((base + n) % total * SPAN, SPAN)],
            x_ref.at[:, aligned(place(n), SPAN)],
            in_sems.at[n],
        )

    middle = place(half)
    tail = place(count - 1) + SPAN
    sides = [
        (signal_ref.at[:, pl.ds(base * SPAN - LANES, LANES)], x_ref.at[:, pl.ds(0, LANES)]),
        (
            signal_ref.at[:, pl.ds((base + count) % total * SPAN, LANES)],
            x_ref.at[:, pl.ds(tail, LANES)],
        ),
        (taps_hbm, taps_ref),
    ]
    if ends:
        sides += [
            (halo_refs[0], x_ref.at[:, pl.ds(middle - LANES, LANES)]),
            (halo_refs[1], x_ref.at[:, pl.ds(middle - 2 * LANES, LANES)]),
        ]
    else:
        sides += [
            (signal_ref.at[:, pl.ds(0, LANES)], edge_refs[0]),
            (signal_ref.at[:, pl.ds(width - LANES, LANES)], edge_refs[1]),
        ]
    sides = [pltpu.make_async_copy(a, b, side_sems.at[n]) for n, (a, b) in enumerate(sides)]
    for copy in sides[:3]:
        copy.start()
    for n in range(count):
        fetch(n).start()
    for copy in sides[3:]:
        copy.start()

    def give(n, kind):
        return pltpu.make_async_copy(
            fit_ref.at[kind, :, aligned(n * SPAN, SPAN)],
            (smooth_hbm, slope_hbm)[kind].at[:, aligned((base + n) % total * SPAN, SPAN)],
            out_sems.at[kind, n],
        )

    def piece(k):
        return pltpu.make_async_copy(resid_ref.at[k], outs[k], piece_sems.at[k])

    lane = lax.broadcasted_iota(jnp.int32, (ROWS, LANES), 1)
    low = lane < 64
    height = ROWS * BLOCKS

    for copy in sides:
        copy.wait()
    fetch(0).wait()

    def body(n, carry):
        at = place(n)
        k = (n // per + GROUPS - mine) % GROUPS
        mark = begin + (base + n) % total * SPAN
        out_at = n * SPAN
        piece_at = n % per * SPAN

        @pl.when(n + 1 < count)
        def _():
            fetch(n + 1).wait()

        x = x_ref[:, aligned(at - LANES, SPAN + 2 * LANES)]
        parts = thirds(x)

        def cut(m, b):
            return parts[m][:, b * LANES : (b + 1) * LANES]

        rows = [
            jnp.concatenate(
                [cut(m, b + 1), jnp.where(low, cut(m, b + 2), cut(m, b))], axis=1
            )
            for m in range(3)
            for b in range(BLOCKS)
        ]
        fit = jnp.dot(
            jnp.concatenate(rows, axis=0), taps_ref[...], preferred_element_type=jnp.float32
        )
        fit = fit[:height] + (fit[height : 2 * height] + fit[2 * height :])
        for b in range(BLOCKS):
            part = fit[b * ROWS : (b + 1) * ROWS]
            smooth = part[:, :LANES] * SMOOTH_SCALE
            fit_ref[0, :, aligned(out_at + b * LANES, LANES)] = smooth
            fit_ref[1, :, aligned(out_at + b * LANES, LANES)] = part[:, LANES:] * SLOPE_SCALE
            resid_ref[k, :, aligned(piece_at + b * LANES, LANES)] = (
                x[:, (b + 1) * LANES : (b + 2) * LANES] - smooth
            )

        latest = first_ref[mine * ROWS]
        soonest = last_ref[mine * ROWS]
        holds = False
        for r in range(ROWS):
            a = first_ref[mine * ROWS + r]
            z = last_ref[mine * ROWS + r]
            latest = jnp.maximum(latest, a)
            soonest = jnp.minimum(soonest, z)
            holds = (
                holds
                | ((a > mark - HALF) & (a < mark + SPAN))
                | ((z > mark) & (z < mark + SPAN + HALF))
            )

        @pl.when((latest + HALF > mark) | (soonest - HALF < mark + SPAN))
        def _():
            row = lax.broadcasted_iota(jnp.int32, (ROWS, LANES), 0)
            first = jnp.zeros((ROWS, LANES), jnp.int32)
            last = jnp.zeros((ROWS, LANES), jnp.int32)
            for r in range(ROWS):
                first = jnp.where(row == r, first_ref[mine * ROWS + r] - mark, first)
                last = jnp.where(row == r, last_ref[mine * ROWS + r] - mark, last)
            low_centre = first + HALF
            high_centre = last - HALF - 1

            @pl.when(holds)
            def _():
                def gather(b, sums):
                    v = x_ref[:, aligned(at + (b - 1) * LANES, LANES)]
                    moment = lane + (b - 1) * LANES
                    new = []
                    for centre, (s0, s1, s2) in zip(
                        (low_centre, high_centre), (sums[:3], sums[3:])
                    ):
                        j = moment - centre
                        w = jnp.where((j >= -HALF) & (j <= HALF), v, 0.0)
                        f = jnp.clip(j, -HALF, HALF).astype(jnp.float32)
                        new += [s0 + w, s1 + w * f, s2 + w * (f * f - CENTRE_SQ)]
                    return tuple(new)

                zero = jnp.zeros((ROWS, LANES), jnp.float32)
                sums = lax.fori_loop(0, BLOCKS + 2, gather, (zero,) * 6)
                sums = [
                    jnp.broadcast_to(jnp.sum(s, axis=1, keepdims=True), (ROWS, LANES))
                    * (1.0 / scale)
                    for s, scale in zip(sums, (float(TAPS), SECOND, FOURTH) * 2)
                ]

                def mend(b, carry):
                    to = aligned(out_at + b * LANES, LANES)
                    moment = lane + b * LANES
                    smooth = fit_ref[0, :, to]
                    slope = fit_ref[1, :, to]
                    for centre, (level, tilt, bend), side in (
                        (low_centre, sums[:3], -1),
                        (high_centre, sums[3:], 1),
                    ):
                        j = moment - centre
                        held = (j * side >= 1) & (j * side <= HALF)
                        f = jnp.clip(j, -HALF, HALF).astype(jnp.float32)
                        bent = level + tilt * f + bend * (f * f - CENTRE_SQ)
                        smooth = jnp.where(held, bent, smooth)
                        slope = jnp.where(held, HALF * (tilt + 2.0 * f * bend), slope)
                    fit_ref[0, :, to] = smooth
                    fit_ref[1, :, to] = slope
                    return carry

                lax.fori_loop(0, BLOCKS, mend, 0)

            def mask(b, carry):
                to = aligned(out_at + b * LANES, LANES)
                moment = lane + b * LANES
                inside = (moment >= first) & (moment < last)
                smooth = jnp.where(inside, fit_ref[0, :, to], 0.0)
                fit_ref[0, :, to] = smooth
                fit_ref[1, :, to] = jnp.where(inside, fit_ref[1, :, to], 0.0)
                resid_ref[k, :, aligned(piece_at + b * LANES, LANES)] = jnp.where(
                    inside, x_ref[:, aligned(at + b * LANES, LANES)] - smooth, 0.0
                )
                return carry

            lax.fori_loop(0, BLOCKS, mask, 0)

        give(n, 0).start()
        give(n, 1).start()
        for kk in range(GROUPS):

            @pl.when((k == kk) & (n % per == per - 1))
            def _():
                piece(kk).start()

        return carry

    lax.fori_loop(0, count, body, 0)
    for kk in range(GROUPS):
        piece(kk).wait()

    def drain(n, carry):
        give(n, 0).wait()
        give(n, 1).wait()
        return carry

    lax.fori_loop(0, count, drain, 0)


def fit_steps(base, count, first, last, signal, taps, halos, held):
    rows, width = signal.shape
    ends = halos is not None
    chain = held is not None
    smem = pl.BlockSpec(memory_space=pltpu.SMEM)
    loose = pl.BlockSpec(memory_space=pl.ANY)
    args = [first, last, signal, taps] + list(halos or ()) + list(held or ())
    aliases = {len(args) - 2: 0, len(args) - 1: 1} if chain else {}
    wide = jax.ShapeDtypeStruct((rows, width), jnp.float32)
    part = jax.ShapeDtypeStruct((rows, count // GROUPS * SPAN), jnp.float32)
    edge = jax.ShapeDtypeStruct((rows, LANES), jnp.float32)
    out_shape = [wide, wide] + [part] * GROUPS + ([] if ends else [edge] * 2)
    return pl.pallas_call(
        functools.partial(fit_kernel, base, count, ends, chain),
        in_specs=[smem, smem] + [loose] * (len(args) - 2),
        out_specs=[loose] * 6 + ([] if ends else [pl.BlockSpec(memory_space=pltpu.VMEM)] * 2),
        out_shape=out_shape,
        scratch_shapes=[
            pltpu.VMEM((rows, count * SPAN + (4 if ends else 2) * LANES), jnp.float32),
            pltpu.VMEM((2, rows, count * SPAN), jnp.float32),
            pltpu.VMEM((GROUPS, rows, count // GROUPS * SPAN), jnp.float32),
            pltpu.VMEM(taps.shape, taps.dtype),
            pltpu.SemaphoreType.DMA((count,)),
            pltpu.SemaphoreType.DMA((2, count)),
            pltpu.SemaphoreType.DMA((GROUPS,)),
            pltpu.SemaphoreType.DMA((5,)),
        ],
        input_output_aliases=aliases,
        compiler_params=pltpu.CompilerParams(vmem_limit_bytes=12 * MIB),
        cost_estimate=pl.CostEstimate(
            flops=count * 3 * rows * BLOCKS * 256 * 256 * 2,
            bytes_accessed=count * rows * SPAN * 4 * 4,
            transcendentals=0,
        ),
    )(*args)


def gram_kernel(spread, *refs):
    parts, refs = refs[:GROUPS], refs[GROUPS:]
    if spread:
        so_far_ref, refs = refs[0], refs[1:]
    out_ref, stack_ref = refs
    mine = lax.axis_index("series")
    for k in range(GROUPS):
        at = pl.multiple_of((mine + GROUPS - k) % GROUPS * ROWS, ROWS)
        x = parts[k][...]
        a = x.astype(jnp.bfloat16)
        b = (x - a.astype(jnp.float32)).astype(jnp.bfloat16)
        stack_ref[pl.ds(at, ROWS)] = a
        stack_ref[pl.ds(64 + at, ROWS)] = a
        stack_ref[pl.ds(128 + at, ROWS)] = b
        stack_ref[pl.ds(192 + at, ROWS)] = b
    both = lax.dot_general(
        stack_ref[64:192],
        stack_ref[...],
        (((1,), (1,)), ((), ())),
        preferred_element_type=jnp.float32,
    )
    gram = both[:64, :128] + (both[64:, :128] + both[:64, 128:] + both[64:, 128:])
    low = lax.broadcasted_iota(jnp.int32, (8, LANES), 1) < 64
    for g in range(GROUPS):
        rows = jnp.where(low, gram[16 * g : 16 * g + 8], gram[16 * g + 8 : 16 * g + 16])
        if spread:
            rows = rows + so_far_ref[g]
            for n in range(spread):
                out_ref[n, g] = rows
        else:
            out_ref[g] = rows


def gram_of(parts, so_far, spread):
    width = parts[0].shape[1]
    vmem = pl.BlockSpec(memory_space=pltpu.VMEM)
    args = list(parts) + ([so_far] if spread else [])
    lead = (spread,) if spread else ()
    return pl.pallas_call(
        functools.partial(gram_kernel, spread),
        in_specs=[vmem] * len(args),
        out_specs=vmem,
        out_shape=jax.ShapeDtypeStruct((*lead, GROUPS, 8, LANES), jnp.float32),
        scratch_shapes=[pltpu.VMEM((256, width), jnp.bfloat16)],
        compiler_params=pltpu.CompilerParams(vmem_limit_bytes=12 * MIB),
        cost_estimate=pl.CostEstimate(
            flops=128 * 256 * width * 2, bytes_accessed=64 * width * 4, transcendentals=0
        ),
        name="gram_last" if spread else "gram_first",
    )(*args)


def packed(rows):
    return jnp.concatenate([rows[:8], rows[8:]], axis=1)


def exchanged(pieces):
    parts = [pieces[0]]
    for k in (2, 1, 3):
        pairs = [(s, (s + k) % GROUPS) for s in range(GROUPS)]
        parts.append(lax.ppermute(pieces[k], "series", pairs))
    return [parts[0], parts[2], parts[1], parts[3]]


def shards(taps, signal, valid_start, valid_end):
    rows, width = signal.shape
    steps = width // SPAN
    devices = lax.axis_size(TIME)
    taps = jnp.asarray(taps, jnp.bfloat16)
    mine = lax.axis_index("series")

    first = lax.dynamic_slice_in_dim(valid_start, mine * rows, rows)[:, None]
    last = lax.dynamic_slice_in_dim(valid_end, mine * rows, rows)[:, None]
    shared = jnp.minimum(last, valid_end[None, :]) - jnp.maximum(first, valid_start[None, :])
    shared = packed(shared.astype(jnp.float32))

    quarter = steps // 4
    out = fit_steps(quarter, steps // 2, valid_start, valid_end, signal, taps, None, None)
    held, front, back = out[:2], out[6], out[7]
    parts = exchanged(out[2:6])
    left = lax.ppermute(back, TIME, [(t, t + 1) for t in range(devices - 1)])
    right = lax.ppermute(front, TIME, [(t + 1, t) for t in range(devices - 1)])
    out = fit_steps(
        3 * quarter, steps // 2, valid_start, valid_end, signal, taps, (left, right), held
    )
    held = out[:2]
    gram = gram_of(parts, None, 0)
    parts = exchanged(out[2:6])
    copies = gram_of(parts, gram, devices).reshape(devices * GROUPS, 8, LANES)
    copies = lax.all_to_all(copies, (*TIME, "series"), 0, 0, tiled=True)
    cov = jnp.sum(copies, axis=0) / shared
    return (*held, jnp.concatenate([cov[:, :64], cov[:, 64:]], axis=0))


def solution(mesh):
    split = Mesh(mesh.devices.reshape(4, 4, 2, GROUPS), (*TIME, "series"))
    return jax.shard_map(
        functools.partial(shards, filter_matrix()),
        mesh=split,
        in_specs=(P("series", TIME), P(), P()),
        out_specs=(P("series", TIME), P("series", TIME), P("series", None)),
        check_vma=False,
    )
```

time: 246 us -> 74.4 us (0.30)
  between operations: 86.5 us -> 0.73 us
  other arithmetic: 69.5 us -> 0.9 us
  blocking collectives: 54.3 us -> 0 us
  waiting for transfers between devices: 0.01 us -> 22.1 us
  starting transfers between devices: 6.83 us -> 28 us
  local copies, waits for them, and re-layouts: 24.7 us -> 4.04 us
  Pallas kernels: 0 us -> 18.4 us
    add x5 -> x0, other arithmetic: 59.7 us -> none  [the longest x1 19.9 us: shards(): bend = bend + window * (curved[m] / fourth)]
    all_to_all x3 -> x0, blocking collectives: 54.3 us -> none  [the longest x1 29.2 us: shards(): lax.all_to_all(resid, 'series', split_axis=1, concat_axis=0, tiled=True)]
    pallas_call x0 -> x4, Pallas kernels: none -> 18.4 us  [the longest x2 15.3 us: fit_steps(): pl.pallas_call(functools.partial(fit_kernel, base, count, ends, chain), i...]
    all_to_all x0 -> x1, waiting for transfers between devices: none -> 13.9 us  [shards(): copies = lax.all_to_all(copies, (*TIME, 'series'), 0, 0, tiled=True)]
    ppermute x2 -> x8, starting transfers between devices: 6.83 us -> 17.6 us  [the longest x6 12.5 us: exchanged(): parts.append(lax.ppermute(pieces[k], 'series', pairs))]
    all_to_all x0 -> x1, starting transfers between devices: none -> 10.4 us  [shards(): copies = lax.all_to_all(copies, (*TIME, 'series'), 0, 0, tiled=True)]
    gather x6 -> x0, local copies, waits for them, and re-layouts: 9.45 us -> none  [held_value(): return jnp.take_along_axis(field, spot, axis=1)]
    ppermute x2 -> x8, waiting for transfers between devices: 0.01 us -> 8.25 us  [the longest x6 8.25 us: exchanged(): parts.append(lax.ppermute(pieces[k], 'series', pairs))]
  transfers between devices with their start and end apart: 2 -> 9, of which waited for: 0 -> 3; matrix products, arithmetic and copies ran while one was open for 6% -> 0% of each run, Pallas kernels for 0% -> 12%
where the time goes in v1:
time: 74.4 us; the launch traced here: 74.1 us
  starting transfers between devices  28 us (38%)
  waiting for transfers between devices  22.1 us (30%)
  Pallas kernels  18.4 us (25%)
  local copies, waits for them, and re-layouts  4.04 us (5%)
  other arithmetic  0.9 us (1%)
    pallas_call x2, Pallas kernels, fit_steps(): pl.pallas_call(functools.partial(fit_kernel, base, count, ends, chain), i...  15.3 us
    all_to_all x1, waiting for transfers between devices, shards(): copies = lax.all_to_all(copies, (*TIME, 'series'), 0, 0, tiled=True)  13.9 us
    ppermute x6, starting transfers between devices, exchanged(): parts.append(lax.ppermute(pieces[k], 'series', pairs))  12.5 us
    all_to_all x1, starting transfers between devices, shards(): copies = lax.all_to_all(copies, (*TIME, 'series'), 0, 0, tiled=True)  10.4 us
    ppermute x6, waiting for transfers between devices, exchanged(): parts.append(lax.ppermute(pieces[k], 'series', pairs))  8.25 us
    unnamed x12, local copies, waits for them, and re-layouts  3.81 us
    ppermute x1, starting transfers between devices, shards(): left = lax.ppermute(back, TIME, [(t, t + 1) for t in range(devices - 1)])  3.1 us
    pallas_call x2, Pallas kernels, gram_of(): pl.pallas_call(functools.partial(gram_kernel, spread), in_specs=[vmem] *...  3.06 us
  transfers between devices with their start and end apart: 9, of which 3 were waited for; matrix products, arithmetic and copies ran while one was open for 0% of the time, Pallas kernels for 12%

profile of v1, /device:TPU:1, one launch (start us, length us, event | category | flops | bytes accessed | tf_op | source)
XLA Modules:
  0.0 74.1 jit_solution(13975252740612034052)
XLA Ops:
  0.6 1.6 %copy-done = f32[16,32768]{1,0:T(8,128)S(1)} copy-done((f32[16,32768]{1,0:T(8,128)S(1)}, f32[16,32768]{1,0:T(8,128)}, u32[]{:S(2)}) %copy-start) | copy-done | bytes 2097176
  2.2 0.9 %copy-done.1 = bf16[256,256]{1,0:T(8,128)(2,1)S(1)} copy-done((bf16[256,256]{1,0:T(8,128)(2,1)S(1)}, bf16[256,256]{1,0:T(8,128)(2,1)}, u32[]{:S(2)}) %copy-start.1) | copy-done | bytes 131096
  3.1 0.7 copy-done.2
  3.8 0.7 copy-done.4
  4.4 7.6 %shard_map.67 = (f32[16,32768]{1,0:T(8,128)}, f32[16,32768]{1,0:T(8,128)}, f32[16,4096]{1,0:T(8,128)S(1)}, f32[16,4096]{1,0:T(8,128)S(1)}, f32[16,4096]{1,0:T(8,...) custom-call(s32[64]{0:T(128)S(1)} %copy-done.2, s32[64]{0:T(128)S(1)} %copy-done.4, ...), custom_call_target="tpu_custom_call" | custom-call | flops 805306368 | bytes 4194304 | tf_op jit(solution)/shard_map/pallas_call | solution.py:282
  12.0 2.7 %collective-permute-start.5 = (f32[16,4096]{1,0:T(8,128)S(1)}, f32[16,4096]{1,0:T(8,128)S(1)}, u32[]{:S(2)}, u32[]{:S(2)}) collective-permute-start(f32[16,4096]{1,0:T(8,128)S(1)} %get-tuple-element.28), channel_id=1, source_target_pairs={{0,1},{1,2},{2,3},{3,0},{4,5},{5,6},{6,7},{7,4},{8,9},{9,10},{10,1... | collective-permute-start | bytes 786440 | tf_op jit(solution)/shard_map/ppermute | solution.py:367
  14.8 3.1 %collective-permute-start = (f32[16,128]{1,0:T(8,128)S(1)}, f32[16,128]{1,0:T(8,128)S(1)}, u32[]{:S(2)}, u32[]{:S(2)}) collective-permute-start(f32[16,128]{1,0:T(8,128)S(1)} %get-tuple-element.17), channel_id=1, source_target_pairs={{0,4},{4,8},{8,12},{12,16},{16,20},{20,24},{24,28},{28,32},{32,36}... | collective-permute-start | bytes 24584 | tf_op jit(solution)/shard_map/ppermute | solution.py:387
  17.9 1.9 %collective-permute-start.1 = (f32[16,128]{1,0:T(8,128)S(1)}, f32[16,128]{1,0:T(8,128)S(1)}, u32[]{:S(2)}, u32[]{:S(2)}) collective-permute-start(f32[16,128]{1,0:T(8,128)S(1)} %get-tuple-element.18), channel_id=1, source_target_pairs={{4,0},{8,4},{12,8},{16,12},{20,16},{24,20},{28,24},{32,28},{36,32}... | collective-permute-start | bytes 24584 | tf_op jit(solution)/shard_map/ppermute | solution.py:388
  19.8 4.4 %collective-permute-start.6 = (f32[16,4096]{1,0:T(8,128)S(1)}, f32[16,4096]{1,0:T(8,128)S(1)}, u32[]{:S(2)}, u32[]{:S(2)}) collective-permute-start(f32[16,4096]{1,0:T(8,128)S(1)} %get-tuple-element.29), channel_id=1, source_target_pairs={{0,2},{1,3},{2,0},{3,1},{4,6},{5,7},{6,4},{7,5},{8,10},{9,11},{10,... | collective-permute-start | bytes 786440 | tf_op jit(solution)/shard_map/ppermute | solution.py:367
  24.2 0.0 collective-permute-start.7
  24.3 0.0 collective-permute-done.refs_4_
  24.3 0.0 collective-permute-done.1.refs_5_
  24.3 7.7 %shard_map.68 = (f32[16,32768]{1,0:T(8,128)}, f32[16,32768]{1,0:T(8,128)}, f32[16,4096]{1,0:T(8,128)S(1)}, f32[16,4096]{1,0:T(8,128)S(1)}, f32[16,4096]{1,0:T(8,128)S(1)}, /*index=5*/f32[16,4096]{1,0:T(8,128)S(1)}) custom-call(s32[64]{0:T(128)S(1)} %copy-done.2, s32[64]{0:T(128)S(1)} %copy-done.4, ...), custom_call_target="tpu_custom_call", output_to_operand_aliasing={{0}: (6, {}), {1}: (7, {})} | custom-call | flops 805306368 | bytes 4194304 | tf_op jit(solution)/shard_map/pallas_call | solution.py:282
  32.0 0.0 copy-start.3
  32.0 0.0 copy-start.5
  32.0 1.5 %collective-permute-start.2 = (f32[16,4096]{1,0:T(8,128)S(1)}, f32[16,4096]{1,0:T(8,128)S(1)}, u32[]{:S(2)}, u32[]{:S(2)}) collective-permute-start(f32[16,4096]{1,0:T(8,128)S(1)} %get-tuple-element.24), channel_id=1, source_target_pairs={{0,1},{1,2},{2,3},{3,0},{4,5},{5,6},{6,7},{7,4},{8,9},{9,10},{10,1... | collective-permute-start | bytes 786440 | tf_op jit(solution)/shard_map/ppermute | solution.py:367
  33.5 1.9 %collective-permute-start.3 = (f32[16,4096]{1,0:T(8,128)S(1)}, f32[16,4096]{1,0:T(8,128)S(1)}, u32[]{:S(2)}, u32[]{:S(2)}) collective-permute-start(f32[16,4096]{1,0:T(8,128)S(1)} %get-tuple-element.25), channel_id=1, source_target_pairs={{0,2},{1,3},{2,0},{3,1},{4,6},{5,7},{6,4},{7,5},{8,10},{9,11},{10,... | collective-permute-start | bytes 786440 | tf_op jit(solution)/shard_map/ppermute | solution.py:367
  35.4 2.0 %collective-permute-start.4 = (f32[16,4096]{1,0:T(8,128)S(1)}, f32[16,4096]{1,0:T(8,128)S(1)}, u32[]{:S(2)}, u32[]{:S(2)}) collective-permute-start(f32[16,4096]{1,0:T(8,128)S(1)} %get-tuple-element.26), channel_id=1, source_target_pairs={{0,3},{1,0},{2,1},{3,2},{4,7},{5,4},{6,5},{7,6},{8,11},{9,8},{10,9... | collective-permute-start | bytes 786440 | tf_op jit(solution)/shard_map/ppermute | solution.py:367
  37.4 0.0 collective-permute-done.6.refs_2_
  37.4 1.1 %gram_first.1.refs_4_ = f32[4,8,128]{2,1,0:T(8,128)S(1)} custom-call(f32[16,4096]{1,0:T(8,128)S(1)} %get-tuple-element.27.refs_0_, f32[16,4096]{1,0:T(8,128)S(1)} %collective-permute-done.5.refs_1_, f32[16,4096]{1,0:T(8,128)S(1)} %collective-permute-done.6.refs_2_, f32[16,4096]{1,0:T(8,128)S(1)} %collective-permute-done.7.refs_3_), custom_call_target="tpu_custom_call" | custom-call | flops 268435456 | bytes 1048576 | tf_op jit(solution)/shard_map/gram_first/pallas_call | solution.py:345
  38.5 7.3 %collective-permute-done.2.refs_1_ = f32[16,4096]{1,0:T(8,128)S(1)} collective-permute-done((f32[16,4096]{1,0:T(8,128)S(1)}, f32[16,4096]{1,0:T(8,128)S(1)}, u32[]{:S(2)}, u32[]{:S(2)}) %collective-permute-start.2) | collective-permute-done | bytes 262176 | tf_op jit(solution)/shard_map/ppermute | solution.py:367
  45.8 0.9 %collective-permute-done.4.refs_3_ = f32[16,4096]{1,0:T(8,128)S(1)} collective-permute-done((f32[16,4096]{1,0:T(8,128)S(1)}, f32[16,4096]{1,0:T(8,128)S(1)}, u32[]{:S(2)}, u32[]{:S(2)}) %collective-permute-start.4) | collective-permute-done | bytes 262176 | tf_op jit(solution)/shard_map/ppermute | solution.py:367
  46.7 2.0 %gram_last.1 = f32[32,4,8,128]{3,2,1,0:T(8,128)} custom-call(f32[16,4096]{1,0:T(8,128)S(1)} %get-tuple-element.23.refs_0_, f32[16,4096]{1,0:T(8,128)S(1)} %collective-permute-done.2.refs_1_, f32[16,4096]{1,0:T(8,128)S(1)} %collective-permute-done.3.refs_2_, f32[16,4096]{1,0:T(8,128)S(1)} %collective-permute-done.4.refs_3_, f32[4,8,128]{2,1,0:T(8,128)S(1)} %gram_first.1.refs_4_), custom_call_target="tpu_custom_call" | custom-call | flops 268435456 | bytes 1048576 | tf_op jit(solution)/shard_map/gram_last/pallas_call | solution.py:345
  48.7 10.4 %all-to-all-start = ((f32[128,8,128]{2,1,0:T(8,128)}), f32[128,8,128]{2,1,0:T(8,128)S(1)}, u32[]{:S(2)}, u32[]{:S(2)}) async-start(f32[128,8,128]{2,1,0:T(8,128)} %bitcast), calls=%async_computation | async-start | bytes 1048576 | tf_op jit(solution)/shard_map/all_to_all | solution.py:396
  59.1 0.1 dynamic_slice.7
  59.2 0.1 dynamic_slice.6
  59.3 0.1 subtract_convert_fusion
  59.4 13.9 %all-to-all-done = f32[128,8,128]{2,1,0:T(8,128)S(1)} async-done(((f32[128,8,128]{2,1,0:T(8,128)}), f32[128,8,128]{2,1,0:T(8,128)S(1)}, u32[]{:S(2)}, u32[]{:S(2)}) %all-to-all-start) | async-done | bytes 524320 | tf_op jit(solution)/shard_map/all_to_all | solution.py:396
  73.2 0.1 reduce_sum.9
  73.3 0.1 maximum_divide_fusion
  73.4 0.1 fusion.1
  73.5 0.6 pad_maximum_fusion
  (10 shorter events, 0.0 us)
Async XLA Ops:
  0.6 1.6 %copy-start = (f32[16,32768]{1,0:T(8,128)S(1)}, f32[16,32768]{1,0:T(8,128)}, u32[]{:S(2)}) copy-start(f32[16,32768]{1,0:T(8,128)} %refs_2_.3) | copy-start | bytes 6291460
  2.2 0.9 %copy-start.1 = (bf16[256,256]{1,0:T(8,128)(2,1)S(1)}, bf16[256,256]{1,0:T(8,128)(2,1)}, u32[]{:S(2)}) copy-start(bf16[256,256]{1,0:T(8,128)(2,1)} %constant.14.clone.refs_3_) | copy-start | bytes 393220
  3.1 0.7 copy-start.2
  3.8 0.7 copy-start.4
  12.0 23.3 %collective-permute-start.5 = (f32[16,4096]{1,0:T(8,128)S(1)}, f32[16,4096]{1,0:T(8,128)S(1)}, u32[]{:S(2)}, u32[]{:S(2)}) collective-permute-start(f32[16,4096]{1,0:T(8,128)S(1)} %get-tuple-element.28), channel_id=1, source_target_pairs={{0,1},{1,2},{2,3},{3,0},{4,5},{5,6},{6,7},{7,4},{8,9},{9,10},{10,1... | collective-permute-start | bytes 786440 | tf_op jit(solution)/shard_map/ppermute | solution.py:367
  14.8 9.5 %collective-permute-start = (f32[16,128]{1,0:T(8,128)S(1)}, f32[16,128]{1,0:T(8,128)S(1)}, u32[]{:S(2)}, u32[]{:S(2)}) collective-permute-start(f32[16,128]{1,0:T(8,128)S(1)} %get-tuple-element.17), channel_id=1, source_target_pairs={{0,4},{4,8},{8,12},{12,16},{16,20},{20,24},{24,28},{28,32},{32,36}... | collective-permute-start | bytes 24584 | tf_op jit(solution)/shard_map/ppermute | solution.py:387
  17.9 6.4 %collective-permute-start.1 = (f32[16,128]{1,0:T(8,128)S(1)}, f32[16,128]{1,0:T(8,128)S(1)}, u32[]{:S(2)}, u32[]{:S(2)}) collective-permute-start(f32[16,128]{1,0:T(8,128)S(1)} %get-tuple-element.18), channel_id=1, source_target_pairs={{4,0},{8,4},{12,8},{16,12},{20,16},{24,20},{28,24},{32,28},{36,32}... | collective-permute-start | bytes 24584 | tf_op jit(solution)/shard_map/ppermute | solution.py:388
  19.8 17.6 %collective-permute-start.6 = (f32[16,4096]{1,0:T(8,128)S(1)}, f32[16,4096]{1,0:T(8,128)S(1)}, u32[]{:S(2)}, u32[]{:S(2)}) collective-permute-start(f32[16,4096]{1,0:T(8,128)S(1)} %get-tuple-element.29), channel_id=1, source_target_pairs={{0,2},{1,3},{2,0},{3,1},{4,6},{5,7},{6,4},{7,5},{8,10},{9,11},{10,... | collective-permute-start | bytes 786440 | tf_op jit(solution)/shard_map/ppermute | solution.py:367
  24.2 13.1 %collective-permute-start.7 = (f32[16,4096]{1,0:T(8,128)S(1)}, f32[16,4096]{1,0:T(8,128)S(1)}, u32[]{:S(2)}, u32[]{:S(2)}) collective-permute-start(f32[16,4096]{1,0:T(8,128)S(1)} %get-tuple-element.30), channel_id=1, source_target_pairs={{0,3},{1,0},{2,1},{3,2},{4,7},{5,4},{6,5},{7,6},{8,11},{9,8},{10,9... | collective-permute-start | bytes 786440 | tf_op jit(solution)/shard_map/ppermute | solution.py:367
  32.0 27.1 %copy-start.3 = (s32[64]{0:T(128)S(1)}, s32[64]{0:T(128)}, u32[]{:S(2)}) copy-start(s32[64]{0:T(128)} %refs_0_.3) | copy-start | bytes 772
  32.0 27.2 %copy-start.5 = (s32[64]{0:T(128)S(1)}, s32[64]{0:T(128)}, u32[]{:S(2)}) copy-start(s32[64]{0:T(128)} %refs_1_.3) | copy-start | bytes 772
  32.0 13.8 %collective-permute-start.2 = (f32[16,4096]{1,0:T(8,128)S(1)}, f32[16,4096]{1,0:T(8,128)S(1)}, u32[]{:S(2)}, u32[]{:S(2)}) collective-permute-start(f32[16,4096]{1,0:T(8,128)S(1)} %get-tuple-element.24), channel_id=1, source_target_pairs={{0,1},{1,2},{2,3},{3,0},{4,5},{5,6},{6,7},{7,4},{8,9},{9,10},{10,1... | collective-permute-start | bytes 786440 | tf_op jit(solution)/shard_map/ppermute | solution.py:367
  33.5 12.3 %collective-permute-start.3 = (f32[16,4096]{1,0:T(8,128)S(1)}, f32[16,4096]{1,0:T(8,128)S(1)}, u32[]{:S(2)}, u32[]{:S(2)}) collective-permute-start(f32[16,4096]{1,0:T(8,128)S(1)} %get-tuple-element.25), channel_id=1, source_target_pairs={{0,2},{1,3},{2,0},{3,1},{4,6},{5,7},{6,4},{7,5},{8,10},{9,11},{10,... | collective-permute-start | bytes 786440 | tf_op jit(solution)/shard_map/ppermute | solution.py:367
  35.4 11.3 %collective-permute-start.4 = (f32[16,4096]{1,0:T(8,128)S(1)}, f32[16,4096]{1,0:T(8,128)S(1)}, u32[]{:S(2)}, u32[]{:S(2)}) collective-permute-start(f32[16,4096]{1,0:T(8,128)S(1)} %get-tuple-element.26), channel_id=1, source_target_pairs={{0,3},{1,0},{2,1},{3,2},{4,7},{5,4},{6,5},{7,6},{8,11},{9,8},{10,9... | collective-permute-start | bytes 786440 | tf_op jit(solution)/shard_map/ppermute | solution.py:367
  48.7 24.5 %all-to-all-start = ((f32[128,8,128]{2,1,0:T(8,128)}), f32[128,8,128]{2,1,0:T(8,128)S(1)}, u32[]{:S(2)}, u32[]{:S(2)}) async-start(f32[128,8,128]{2,1,0:T(8,128)} %bitcast), calls=%async_computation | async-start | bytes 1048576 | tf_op jit(solution)/shard_map/all_to_all | solution.py:396

commit v2 on v1

--- a/solution.py
+++ b/solution.py
@@ -50,7 +50,7 @@
 
 def fit_kernel(base, count, ends, chain, *refs):
     refs = list(refs)
-    first_ref, last_ref, signal_ref, taps_hbm = refs[:4]
+    first_hbm, last_hbm, signal_ref, taps_hbm = refs[:4]
     refs = refs[4:]
     if ends:
         halo_refs, refs = refs[:2], refs[2:]
@@ -60,7 +60,8 @@
     outs, refs = refs[2:6], refs[6:]
     if not ends:
         edge_refs, refs = refs[:2], refs[2:]
-    x_ref, fit_ref, resid_ref, taps_ref, in_sems, out_sems, piece_sems, side_sems = refs
+    x_ref, fit_ref, resid_ref, taps_ref, first_ref, last_ref = refs[:6]
+    in_sems, out_sems, piece_sems, side_sems = refs[6:]
 
     width = signal_ref.shape[1]
     total = width // SPAN
@@ -87,6 +88,8 @@
             signal_ref.at[:, pl.ds((base + count) % total * SPAN, LANES)],
             x_ref.at[:, pl.ds(tail, LANES)],
         ),
+        (first_hbm, first_ref),
+        (last_hbm, last_ref),
         (taps_hbm, taps_ref),
     ]
     if ends:
@@ -100,11 +103,11 @@
             (signal_ref.at[:, pl.ds(width - LANES, LANES)], edge_refs[1]),
         ]
     sides = [pltpu.make_async_copy(a, b, side_sems.at[n]) for n, (a, b) in enumerate(sides)]
-    for copy in sides[:3]:
+    for copy in sides[:5]:
         copy.start()
     for n in range(count):
         fetch(n).start()
-    for copy in sides[3:]:
+    for copy in sides[5:]:
         copy.start()
 
     def give(n, kind):
@@ -124,6 +127,13 @@
     for copy in sides:
         copy.wait()
     fetch(0).wait()
+
+    row = lax.broadcasted_iota(jnp.int32, (ROWS, LANES), 0)
+    first = jnp.zeros((ROWS, LANES), jnp.int32)
+    last = jnp.zeros((ROWS, LANES), jnp.int32)
+    for r in range(ROWS):
+        first = jnp.where(row == r, first_ref[mine * ROWS + r], first)
+        last = jnp.where(row == r, last_ref[mine * ROWS + r], last)
 
     def body(n, carry):
         at = place(n)
@@ -153,97 +163,74 @@
             jnp.concatenate(rows, axis=0), taps_ref[...], preferred_element_type=jnp.float32
         )
         fit = fit[:height] + (fit[height : 2 * height] + fit[2 * height :])
+        since = first - mark
+        until = last - mark
         for b in range(BLOCKS):
             part = fit[b * ROWS : (b + 1) * ROWS]
+            moment = lane + b * LANES
+            inside = (moment >= since) & (moment < until)
             smooth = part[:, :LANES] * SMOOTH_SCALE
-            fit_ref[0, :, aligned(out_at + b * LANES, LANES)] = smooth
-            fit_ref[1, :, aligned(out_at + b * LANES, LANES)] = part[:, LANES:] * SLOPE_SCALE
-            resid_ref[k, :, aligned(piece_at + b * LANES, LANES)] = (
-                x[:, (b + 1) * LANES : (b + 2) * LANES] - smooth
-            )
-
-        latest = first_ref[mine * ROWS]
-        soonest = last_ref[mine * ROWS]
+            resid = x[:, (b + 1) * LANES : (b + 2) * LANES] - smooth
+            to = aligned(out_at + b * LANES, LANES)
+            fit_ref[0, :, to] = jnp.where(inside, smooth, 0.0)
+            fit_ref[1, :, to] = jnp.where(inside, part[:, LANES:] * SLOPE_SCALE, 0.0)
+            resid_ref[k, :, aligned(piece_at + b * LANES, LANES)] = jnp.where(inside, resid, 0.0)
+
+        def starts_here(a):
+            return (a > mark - HALF) & (a < mark + SPAN)
+
+        def stops_here(z):
+            return (z > mark) & (z < mark + SPAN + HALF)
+
         holds = False
         for r in range(ROWS):
-            a = first_ref[mine * ROWS + r]
-            z = last_ref[mine * ROWS + r]
-            latest = jnp.maximum(latest, a)
-            soonest = jnp.minimum(soonest, z)
-            holds = (
-                holds
-                | ((a > mark - HALF) & (a < mark + SPAN))
-                | ((z > mark) & (z < mark + SPAN + HALF))
-            )
-
-        @pl.when((latest + HALF > mark) | (soonest - HALF < mark + SPAN))
+            holds = holds | starts_here(first_ref[mine * ROWS + r])
+            holds = holds | stops_here(last_ref[mine * ROWS + r])
+
+        @pl.when(holds)
         def _():
-            row = lax.broadcasted_iota(jnp.int32, (ROWS, LANES), 0)
-            first = jnp.zeros((ROWS, LANES), jnp.int32)
-            last = jnp.zeros((ROWS, LANES), jnp.int32)
-            for r in range(ROWS):
-                first = jnp.where(row == r, first_ref[mine * ROWS + r] - mark, first)
-                last = jnp.where(row == r, last_ref[mine * ROWS + r] - mark, last)
-            low_centre = first + HALF
-            high_centre = last - HALF - 1
-
-            @pl.when(holds)
-            def _():
-                def gather(b, sums):
-                    v = x_ref[:, aligned(at + (b - 1) * LANES, LANES)]
-                    moment = lane + (b - 1) * LANES
-                    new = []
-                    for centre, (s0, s1, s2) in zip(
-                        (low_centre, high_centre), (sums[:3], sums[3:])
-                    ):
-                        j = moment - centre
-                        w = jnp.where((j >= -HALF) & (j <= HALF), v, 0.0)
-                        f = jnp.clip(j, -HALF, HALF).astype(jnp.float32)
-                        new += [s0 + w, s1 + w * f, s2 + w * (f * f - CENTRE_SQ)]
-                    return tuple(new)
-
-                zero = jnp.zeros((ROWS, LANES), jnp.float32)
-                sums = lax.fori_loop(0, BLOCKS + 2, gather, (zero,) * 6)
-                sums = [
-                    jnp.broadcast_to(jnp.sum(s, axis=1, keepdims=True), (ROWS, LANES))
-                    * (1.0 / scale)
-                    for s, scale in zip(sums, (float(TAPS), SECOND, FOURTH) * 2)
-                ]
-
-                def mend(b, carry):
-                    to = aligned(out_at + b * LANES, LANES)
-                    moment = lane + b * LANES
-                    smooth = fit_ref[0, :, to]
-                    slope = fit_ref[1, :, to]
-                    for centre, (level, tilt, bend), side in (
-                        (low_centre, sums[:3], -1),
-                        (high_centre, sums[3:], 1),
-                    ):
-                        j = moment - centre
-                        held = (j * side >= 1) & (j * side <= HALF)
-                        f = jnp.clip(j, -HALF, HALF).astype(jnp.float32)
-                        bent = level + tilt * f + bend * (f * f - CENTRE_SQ)
-                        smooth = jnp.where(held, bent, smooth)
-                        slope = jnp.where(held, HALF * (tilt + 2.0 * f * bend), slope)
-                    fit_ref[0, :, to] = smooth
-                    fit_ref[1, :, to] = slope
-                    return carry
-
-                lax.fori_loop(0, BLOCKS, mend, 0)
-
-            def mask(b, carry):
-                to = aligned(out_at + b * LANES, LANES)
-                moment = lane + b * LANES
-                inside = (moment >= first) & (moment < last)
-                smooth = jnp.where(inside, fit_ref[0, :, to], 0.0)
-                fit_ref[0, :, to] = smooth
-                fit_ref[1, :, to] = jnp.where(inside, fit_ref[1, :, to], 0.0)
-                resid_ref[k, :, aligned(piece_at + b * LANES, LANES)] = jnp.where(
-                    inside, x_ref[:, aligned(at + b * LANES, LANES)] - smooth, 0.0
-                )
+            def mend(r, left, centre, side):
+                b = (left + LANES) // LANES - 1
+                v = x_ref[:, aligned(at + b * LANES, 2 * LANES)]
+                j = lax.broadcasted_iota(jnp.int32, (ROWS, 2 * LANES), 1) + (b * LANES - centre)
+                w = jnp.where((j >= -HALF) & (j <= HALF), v, 0.0)
+                f = jnp.clip(j, -HALF, HALF).astype(jnp.float32)
+                level = jnp.sum(w, axis=1, keepdims=True) * (1.0 / TAPS)
+                tilt = jnp.sum(w * f, axis=1, keepdims=True) * (1.0 / SECOND)
+                curve = f * f - CENTRE_SQ
+                bend = jnp.sum(w * curve, axis=1, keepdims=True) * (1.0 / FOURTH)
+                smooth = level + tilt * f + bend * curve
+                slope = HALF * (tilt + 2.0 * f * bend)
+                held = (j * side >= 1) & (j * side <= HALF)
+                for h in range(2):
+
+                    @pl.when((b + h >= 0) & (b + h < BLOCKS))
+                    def _():
+                        part = slice(h * LANES, (h + 1) * LANES)
+                        mine_held = held[:, part] & (row == r)
+                        to = aligned(out_at + (b + h) * LANES, LANES)
+                        fit_ref[0, :, to] = jnp.where(mine_held, smooth[:, part], fit_ref[0, :, to])
+                        fit_ref[1, :, to] = jnp.where(mine_held, slope[:, part], fit_ref[1, :, to])
+                        to = aligned(piece_at + (b + h) * LANES, LANES)
+                        resid_ref[k, :, to] = jnp.where(
+                            mine_held, v[:, part] - smooth[:, part], resid_ref[k, :, to]
+                        )
+
+            def series(r, carry):
+                a = first_ref[mine * ROWS + r]
+                z = last_ref[mine * ROWS + r]
+
+                @pl.when(starts_here(a))
+                def _():
+                    mend(r, a - mark, a - mark + HALF, -1)
+
+                @pl.when(stops_here(z))
+                def _():
+                    mend(r, z - mark - TAPS, z - mark - HALF - 1, 1)
+
                 return carry
 
-            lax.fori_loop(0, BLOCKS, mask, 0)
+            lax.fori_loop(0, ROWS, series, 0)
 
         give(n, 0).start()
         give(n, 1).start()
@@ -271,9 +258,10 @@
     rows, width = signal.shape
     ends = halos is not None
     chain = held is not None
-    smem = pl.BlockSpec(memory_space=pltpu.SMEM)
+    hbm = pl.BlockSpec(memory_space=pltpu.HBM)
     loose = pl.BlockSpec(memory_space=pl.ANY)
-    args = [first, last, signal, taps] + list(halos or ()) + list(held or ())
+    args = [pltpu.with_memory_space_constraint(a, pltpu.HBM) for a in (first, last, signal, taps)]
+    args += list(halos or ()) + list(held or ())
     aliases = {len(args) - 2: 0, len(args) - 1: 1} if chain else {}
     wide = jax.ShapeDtypeStruct((rows, width), jnp.float32)
     part = jax.ShapeDtypeStruct((rows, count // GROUPS * SPAN), jnp.float32)
@@ -281,18 +269,20 @@
     out_shape = [wide, wide] + [part] * GROUPS + ([] if ends else [edge] * 2)
     return pl.pallas_call(
         functools.partial(fit_kernel, base, count, ends, chain),
-        in_specs=[smem, smem] + [loose] * (len(args) - 2),
-        out_specs=[loose] * 6 + ([] if ends else [pl.BlockSpec(memory_space=pltpu.VMEM)] * 2),
+        in_specs=[hbm] * 4 + [loose] * len(halos or ()) + [hbm] * len(held or ()),
+        out_specs=[hbm] * 2 + [loose] * GROUPS + [loose] * (0 if ends else 2),
         out_shape=out_shape,
         scratch_shapes=[
             pltpu.VMEM((rows, count * SPAN + (4 if ends else 2) * LANES), jnp.float32),
             pltpu.VMEM((2, rows, count * SPAN), jnp.float32),
             pltpu.VMEM((GROUPS, rows, count // GROUPS * SPAN), jnp.float32),
             pltpu.VMEM(taps.shape, taps.dtype),
+            pltpu.SMEM(first.shape, jnp.int32),
+            pltpu.SMEM(last.shape, jnp.int32),
             pltpu.SemaphoreType.DMA((count,)),
             pltpu.SemaphoreType.DMA((2, count)),
             pltpu.SemaphoreType.DMA((GROUPS,)),
-            pltpu.SemaphoreType.DMA((5,)),
+            pltpu.SemaphoreType.DMA((7,)),
         ],
         input_output_aliases=aliases,
         compiler_params=pltpu.CompilerParams(vmem_limit_bytes=12 * MIB),

time: 74.4 us -> 67.7 us (0.910)
  local copies, waits for them, and re-layouts: 4.04 us -> 0.24 us
  Pallas kernels: 18.4 us -> 14.8 us
    unnamed x12 -> x4, local copies, waits for them, and re-layouts: 3.81 us -> 0.01 us
    pallas_call x2, Pallas kernels: 15.3 us -> 11.7 us  [fit_steps(): pl.pallas_call(functools.partial(fit_kernel, base, count, ends, chain), i...]
    all_to_all x1, starting transfers between devices: 10.4 us -> 11.3 us  [shards(): copies = lax.all_to_all(copies, (*TIME, 'series'), 0, 0, tiled=True)]
  transfers between devices with their start and end apart: 9 -> 9, of which waited for: 3 -> 3; matrix products, arithmetic and copies ran while one was open for 0% -> 0% of each run, Pallas kernels for 12% -> 10%
where the time goes in v2:
time: 67.7 us; the launch traced here: 67.5 us
  starting transfers between devices  28.6 us (42%)
  waiting for transfers between devices  22.2 us (33%)
  Pallas kernels  14.8 us (22%)
  other arithmetic  0.9 us (1%)
  between operations  0.72 us (1%)
    all_to_all x1, waiting for transfers between devices, shards(): copies = lax.all_to_all(copies, (*TIME, 'series'), 0, 0, tiled=True)  13.9 us
    ppermute x6, starting transfers between devices, exchanged(): parts.append(lax.ppermute(pieces[k], 'series', pairs))  12.2 us
    pallas_call x2, Pallas kernels, fit_steps(): pl.pallas_call(functools.partial(fit_kernel, base, count, ends, chain), i...  11.7 us
    all_to_all x1, starting transfers between devices, shards(): copies = lax.all_to_all(copies, (*TIME, 'series'), 0, 0, tiled=True)  11.3 us
    ppermute x6, waiting for transfers between devices, exchanged(): parts.append(lax.ppermute(pieces[k], 'series', pairs))  8.35 us
    ppermute x1, starting transfers between devices, shards(): left = lax.ppermute(back, TIME, [(t, t + 1) for t in range(devices - 1)])  3.28 us
    pallas_call x2, Pallas kernels, gram_of(): pl.pallas_call(functools.partial(gram_kernel, spread), in_specs=[vmem] *...  3.07 us
    ppermute x1, starting transfers between devices, shards(): right = lax.ppermute(front, TIME, [(t + 1, t) for t in range(devices - 1)])  1.92 us
  transfers between devices with their start and end apart: 9, of which 3 were waited for; matrix products, arithmetic and copies ran while one was open for 0% of the time, Pallas kernels for 10%

profile of v2, /device:TPU:1, one launch (start us, length us, event | category | flops | bytes accessed | tf_op | source)
XLA Modules:
  0.0 67.5 jit_solution(2418060742920566804)
XLA Ops:
  0.6 5.8 %shard_map.67 = (f32[16,32768]{1,0:T(8,128)}, f32[16,32768]{1,0:T(8,128)}, f32[16,4096]{1,0:T(8,128)S(1)}, f32[16,4096]{1,0:T(8,128)S(1)}, f32[16,4096]{1,0:T(8,...) custom-call(s32[64]{0:T(128)} %refs_0_.3, s32[64]{0:T(128)} %refs_1_.3, ...), custom_call_target="tpu_custom_call" | custom-call | flops 805306368 | bytes 4194304 | tf_op jit(solution)/shard_map/pallas_call | solution.py:270
  6.4 2.7 %collective-permute-start.5 = (f32[16,4096]{1,0:T(8,128)S(1)}, f32[16,4096]{1,0:T(8,128)S(1)}, u32[]{:S(2)}, u32[]{:S(2)}) collective-permute-start(f32[16,4096]{1,0:T(8,128)S(1)} %get-tuple-element.28), channel_id=1, source_target_pairs={{0,1},{1,2},{2,3},{3,0},{4,5},{5,6},{6,7},{7,4},{8,9},{9,10},{10,1... | collective-permute-start | bytes 786440 | tf_op jit(solution)/shard_map/ppermute | solution.py:357
  9.1 3.3 %collective-permute-start = (f32[16,128]{1,0:T(8,128)S(1)}, f32[16,128]{1,0:T(8,128)S(1)}, u32[]{:S(2)}, u32[]{:S(2)}) collective-permute-start(f32[16,128]{1,0:T(8,128)S(1)} %get-tuple-element.17), channel_id=1, source_target_pairs={{0,4},{4,8},{8,12},{12,16},{16,20},{20,24},{24,28},{28,32},{32,36}... | collective-permute-start | bytes 24584 | tf_op jit(solution)/shard_map/ppermute | solution.py:377
  12.4 1.9 %collective-permute-start.1 = (f32[16,128]{1,0:T(8,128)S(1)}, f32[16,128]{1,0:T(8,128)S(1)}, u32[]{:S(2)}, u32[]{:S(2)}) collective-permute-start(f32[16,128]{1,0:T(8,128)S(1)} %get-tuple-element.18), channel_id=1, source_target_pairs={{4,0},{8,4},{12,8},{16,12},{20,16},{24,20},{28,24},{32,28},{36,32}... | collective-permute-start | bytes 24584 | tf_op jit(solution)/shard_map/ppermute | solution.py:378
  14.3 4.1 %collective-permute-start.6 = (f32[16,4096]{1,0:T(8,128)S(1)}, f32[16,4096]{1,0:T(8,128)S(1)}, u32[]{:S(2)}, u32[]{:S(2)}) collective-permute-start(f32[16,4096]{1,0:T(8,128)S(1)} %get-tuple-element.29), channel_id=1, source_target_pairs={{0,2},{1,3},{2,0},{3,1},{4,6},{5,7},{6,4},{7,5},{8,10},{9,11},{10,... | collective-permute-start | bytes 786440 | tf_op jit(solution)/shard_map/ppermute | solution.py:357
  18.4 0.0 collective-permute-start.7
  18.4 0.0 collective-permute-done.refs_4_
  18.4 0.0 collective-permute-done.1.refs_5_
  18.4 5.9 %shard_map.68 = (f32[16,32768]{1,0:T(8,128)}, f32[16,32768]{1,0:T(8,128)}, f32[16,4096]{1,0:T(8,128)S(1)}, f32[16,4096]{1,0:T(8,128)S(1)}, f32[16,4096]{1,0:T(8,128)S(1)}, /*index=5*/f32[16,4096]{1,0:T(8,128)S(1)}) custom-call(s32[64]{0:T(128)} %refs_0_.3, s32[64]{0:T(128)} %refs_1_.3, ...), custom_call_target="tpu_custom_call", output_to_operand_aliasing={{0}: (6, {}), {1}: (7, {})} | custom-call | flops 805306368 | bytes 4194304 | tf_op jit(solution)/shard_map/pallas_call | solution.py:270
  24.4 0.0 copy-start
  24.4 0.0 copy-start.1
  24.4 1.5 %collective-permute-start.2 = (f32[16,4096]{1,0:T(8,128)S(1)}, f32[16,4096]{1,0:T(8,128)S(1)}, u32[]{:S(2)}, u32[]{:S(2)}) collective-permute-start(f32[16,4096]{1,0:T(8,128)S(1)} %get-tuple-element.24), channel_id=1, source_target_pairs={{0,1},{1,2},{2,3},{3,0},{4,5},{5,6},{6,7},{7,4},{8,9},{9,10},{10,1... | collective-permute-start | bytes 786440 | tf_op jit(solution)/shard_map/ppermute | solution.py:357
  25.9 1.9 %collective-permute-start.3 = (f32[16,4096]{1,0:T(8,128)S(1)}, f32[16,4096]{1,0:T(8,128)S(1)}, u32[]{:S(2)}, u32[]{:S(2)}) collective-permute-start(f32[16,4096]{1,0:T(8,128)S(1)} %get-tuple-element.25), channel_id=1, source_target_pairs={{0,2},{1,3},{2,0},{3,1},{4,6},{5,7},{6,4},{7,5},{8,10},{9,11},{10,... | collective-permute-start | bytes 786440 | tf_op jit(solution)/shard_map/ppermute | solution.py:357
  27.8 0.0 collective-permute-done.5.refs_1_
  27.8 2.0 %collective-permute-start.4 = (f32[16,4096]{1,0:T(8,128)S(1)}, f32[16,4096]{1,0:T(8,128)S(1)}, u32[]{:S(2)}, u32[]{:S(2)}) collective-permute-start(f32[16,4096]{1,0:T(8,128)S(1)} %get-tuple-element.26), channel_id=1, source_target_pairs={{0,3},{1,0},{2,1},{3,2},{4,7},{5,4},{6,5},{7,6},{8,11},{9,8},{10,9... | collective-permute-start | bytes 786440 | tf_op jit(solution)/shard_map/ppermute | solution.py:357
  29.8 0.0 collective-permute-done.6.refs_2_
  29.8 0.0 collective-permute-done.7.refs_3_
  29.8 1.1 %gram_first.1.refs_4_ = f32[4,8,128]{2,1,0:T(8,128)S(1)} custom-call(f32[16,4096]{1,0:T(8,128)S(1)} %get-tuple-element.27.refs_0_, f32[16,4096]{1,0:T(8,128)S(1)} %collective-permute-done.5.refs_1_, f32[16,4096]{1,0:T(8,128)S(1)} %collective-permute-done.6.refs_2_, f32[16,4096]{1,0:T(8,128)S(1)} %collective-permute-done.7.refs_3_), custom_call_target="tpu_custom_call" | custom-call | flops 268435456 | bytes 1048576 | tf_op jit(solution)/shard_map/gram_first/pallas_call | solution.py:335
  30.9 7.4 %collective-permute-done.2.refs_1_ = f32[16,4096]{1,0:T(8,128)S(1)} collective-permute-done((f32[16,4096]{1,0:T(8,128)S(1)}, f32[16,4096]{1,0:T(8,128)S(1)}, u32[]{:S(2)}, u32[]{:S(2)}) %collective-permute-start.2) | collective-permute-done | bytes 262176 | tf_op jit(solution)/shard_map/ppermute | solution.py:357
  38.3 0.0 collective-permute-done.3.refs_2_
  38.3 0.9 %collective-permute-done.4.refs_3_ = f32[16,4096]{1,0:T(8,128)S(1)} collective-permute-done((f32[16,4096]{1,0:T(8,128)S(1)}, f32[16,4096]{1,0:T(8,128)S(1)}, u32[]{:S(2)}, u32[]{:S(2)}) %collective-permute-start.4) | collective-permute-done | bytes 262176 | tf_op jit(solution)/shard_map/ppermute | solution.py:357
  39.2 2.0 %gram_last.1 = f32[32,4,8,128]{3,2,1,0:T(8,128)} custom-call(f32[16,4096]{1,0:T(8,128)S(1)} %get-tuple-element.23.refs_0_, f32[16,4096]{1,0:T(8,128)S(1)} %collective-permute-done.2.refs_1_, f32[16,4096]{1,0:T(8,128)S(1)} %collective-permute-done.3.refs_2_, f32[16,4096]{1,0:T(8,128)S(1)} %collective-permute-done.4.refs_3_, f32[4,8,128]{2,1,0:T(8,128)S(1)} %gram_first.1.refs_4_), custom_call_target="tpu_custom_call" | custom-call | flops 268435456 | bytes 1048576 | tf_op jit(solution)/shard_map/gram_last/pallas_call | solution.py:335
  41.2 11.3 %all-to-all-start = ((f32[128,8,128]{2,1,0:T(8,128)}), f32[128,8,128]{2,1,0:T(8,128)S(1)}, u32[]{:S(2)}, u32[]{:S(2)}) async-start(f32[128,8,128]{2,1,0:T(8,128)} %bitcast), calls=%async_computation | async-start | bytes 1048576 | tf_op jit(solution)/shard_map/all_to_all | solution.py:386
  52.5 0.0 copy-done
  52.5 0.1 dynamic_slice.7
  52.6 0.1 dynamic_slice.6
  52.6 0.1 subtract_convert_fusion
  52.7 13.9 %all-to-all-done = f32[128,8,128]{2,1,0:T(8,128)S(1)} async-done(((f32[128,8,128]{2,1,0:T(8,128)}), f32[128,8,128]{2,1,0:T(8,128)S(1)}, u32[]{:S(2)}, u32[]{:S(2)}) %all-to-all-start) | async-done | bytes 524320 | tf_op jit(solution)/shard_map/all_to_all | solution.py:386
  66.6 0.1 reduce_sum.9
  66.7 0.1 maximum_divide_fusion
  66.8 0.1 fusion.1
  66.9 0.6 pad_maximum_fusion
  (2 shorter events, 0.0 us)
Async XLA Ops:
  6.4 21.4 %collective-permute-start.5 = (f32[16,4096]{1,0:T(8,128)S(1)}, f32[16,4096]{1,0:T(8,128)S(1)}, u32[]{:S(2)}, u32[]{:S(2)}) collective-permute-start(f32[16,4096]{1,0:T(8,128)S(1)} %get-tuple-element.28), channel_id=1, source_target_pairs={{0,1},{1,2},{2,3},{3,0},{4,5},{5,6},{6,7},{7,4},{8,9},{9,10},{10,1... | collective-permute-start | bytes 786440 | tf_op jit(solution)/shard_map/ppermute | solution.py:357
  9.1 9.4 %collective-permute-start = (f32[16,128]{1,0:T(8,128)S(1)}, f32[16,128]{1,0:T(8,128)S(1)}, u32[]{:S(2)}, u32[]{:S(2)}) collective-permute-start(f32[16,128]{1,0:T(8,128)S(1)} %get-tuple-element.17), channel_id=1, source_target_pairs={{0,4},{4,8},{8,12},{12,16},{16,20},{20,24},{24,28},{28,32},{32,36}... | collective-permute-start | bytes 24584 | tf_op jit(solution)/shard_map/ppermute | solution.py:377
  12.4 6.1 %collective-permute-start.1 = (f32[16,128]{1,0:T(8,128)S(1)}, f32[16,128]{1,0:T(8,128)S(1)}, u32[]{:S(2)}, u32[]{:S(2)}) collective-permute-start(f32[16,128]{1,0:T(8,128)S(1)} %get-tuple-element.18), channel_id=1, source_target_pairs={{4,0},{8,4},{12,8},{16,12},{20,16},{24,20},{28,24},{32,28},{36,32}... | collective-permute-start | bytes 24584 | tf_op jit(solution)/shard_map/ppermute | solution.py:378
  14.3 15.5 %collective-permute-start.6 = (f32[16,4096]{1,0:T(8,128)S(1)}, f32[16,4096]{1,0:T(8,128)S(1)}, u32[]{:S(2)}, u32[]{:S(2)}) collective-permute-start(f32[16,4096]{1,0:T(8,128)S(1)} %get-tuple-element.29), channel_id=1, source_target_pairs={{0,2},{1,3},{2,0},{3,1},{4,6},{5,7},{6,4},{7,5},{8,10},{9,11},{10,... | collective-permute-start | bytes 786440 | tf_op jit(solution)/shard_map/ppermute | solution.py:357
  18.4 11.3 %collective-permute-start.7 = (f32[16,4096]{1,0:T(8,128)S(1)}, f32[16,4096]{1,0:T(8,128)S(1)}, u32[]{:S(2)}, u32[]{:S(2)}) collective-permute-start(f32[16,4096]{1,0:T(8,128)S(1)} %get-tuple-element.30), channel_id=1, source_target_pairs={{0,3},{1,0},{2,1},{3,2},{4,7},{5,4},{6,5},{7,6},{8,11},{9,8},{10,9... | collective-permute-start | bytes 786440 | tf_op jit(solution)/shard_map/ppermute | solution.py:357
  24.4 28.1 %copy-start = (s32[64]{0:T(128)S(1)}, s32[64]{0:T(128)}, u32[]{:S(2)}) copy-start(s32[64]{0:T(128)} %refs_0_.3) | copy-start | bytes 772
  24.4 28.2 %copy-start.1 = (s32[64]{0:T(128)S(1)}, s32[64]{0:T(128)}, u32[]{:S(2)}) copy-start(s32[64]{0:T(128)} %refs_1_.3) | copy-start | bytes 772
  24.4 13.9 %collective-permute-start.2 = (f32[16,4096]{1,0:T(8,128)S(1)}, f32[16,4096]{1,0:T(8,128)S(1)}, u32[]{:S(2)}, u32[]{:S(2)}) collective-permute-start(f32[16,4096]{1,0:T(8,128)S(1)} %get-tuple-element.24), channel_id=1, source_target_pairs={{0,1},{1,2},{2,3},{3,0},{4,5},{5,6},{6,7},{7,4},{8,9},{9,10},{10,1... | collective-permute-start | bytes 786440 | tf_op jit(solution)/shard_map/ppermute | solution.py:357
  25.9 12.4 %collective-permute-start.3 = (f32[16,4096]{1,0:T(8,128)S(1)}, f32[16,4096]{1,0:T(8,128)S(1)}, u32[]{:S(2)}, u32[]{:S(2)}) collective-permute-start(f32[16,4096]{1,0:T(8,128)S(1)} %get-tuple-element.25), channel_id=1, source_target_pairs={{0,2},{1,3},{2,0},{3,1},{4,6},{5,7},{6,4},{7,5},{8,10},{9,11},{10,... | collective-permute-start | bytes 786440 | tf_op jit(solution)/shard_map/ppermute | solution.py:357
  27.8 11.4 %collective-permute-start.4 = (f32[16,4096]{1,0:T(8,128)S(1)}, f32[16,4096]{1,0:T(8,128)S(1)}, u32[]{:S(2)}, u32[]{:S(2)}) collective-permute-start(f32[16,4096]{1,0:T(8,128)S(1)} %get-tuple-element.26), channel_id=1, source_target_pairs={{0,3},{1,0},{2,1},{3,2},{4,7},{5,4},{6,5},{7,6},{8,11},{9,8},{10,9... | collective-permute-start | bytes 786440 | tf_op jit(solution)/shard_map/ppermute | solution.py:357
  41.2 25.4 %all-to-all-start = ((f32[128,8,128]{2,1,0:T(8,128)}), f32[128,8,128]{2,1,0:T(8,128)S(1)}, u32[]{:S(2)}, u32[]{:S(2)}) async-start(f32[128,8,128]{2,1,0:T(8,128)} %bitcast), calls=%async_computation | async-start | bytes 1048576 | tf_op jit(solution)/shard_map/all_to_all | solution.py:386

commit v3 on v2

v3 whole, which is shorter than its diff:
```python
import functools

import jax
import jax.numpy as jnp
import numpy as np
from jax import lax
from jax.experimental import pallas as pl
from jax.experimental.pallas import tpu as pltpu
from jax.sharding import Mesh
from jax.sharding import PartitionSpec as P


HALF = 16
TAPS = 2 * HALF + 1
ROWS = 16
GROUPS = 4
LANES = 128
TIME = ("y", "z", "core")
MIB = 1 << 20

SECOND = float(sum(j * j for j in range(-HALF, HALF + 1)))
CENTRE_SQ = SECOND / TAPS
FOURTH = float(sum((j * j - CENTRE_SQ) ** 2 for j in range(-HALF, HALF + 1)))
SMOOTH_SCALE = 2048.0 / 2387.0
SLOPE_SCALE = HALF * 16.0 / SECOND


def filter_matrix():
    place = np.concatenate([np.arange(128), np.arange(128, 192), np.arange(-64, 0)])
    j = place[:, None] - np.arange(LANES)[None, :]
    near = np.abs(j) <= HALF
    smooth = np.where(near, (163 - j * j) / 2048.0, 0.0)
    slope = np.where(near, j / 16.0, 0.0)
    return np.concatenate([smooth, slope], axis=1).astype(np.float32)


def thirds(x):
    a = x.astype(jnp.bfloat16)
    rest = x - a.astype(jnp.float32)
    b = rest.astype(jnp.bfloat16)
    c = (rest - b.astype(jnp.float32)).astype(jnp.bfloat16)
    return a, b, c


def aligned(start, size):
    return pl.ds(pl.multiple_of(start, LANES), size)


def fit_kernel(plan, fits, resids, ends, edges, chain, *refs):
    base, span, count = plan
    blocks = span // LANES
    refs = list(refs)
    first_hbm, last_hbm, signal_ref, taps_hbm = refs[:4]
    refs = refs[4:]
    if ends:
        halo_refs, refs = refs[:2], refs[2:]
    if chain:
        refs = refs[2:]
    if fits:
        fit_hbm, refs = refs[:2], refs[2:]
    if resids:
        outs, refs = refs[:GROUPS], refs[GROUPS:]
    if edges:
        edge_refs, refs = refs[:2], refs[2:]
    x_ref, taps_ref, first_ref, last_ref, in_sems, side_sems = refs[:6]
    refs = refs[6:]
    if fits:
        fit_ref, out_sems = refs[:2]
        refs = refs[2:]
    if resids:
        resid_ref, piece_sems = refs

    width = signal_ref.shape[1]
    per = count // GROUPS
    half = count // 2
    mine = lax.axis_index("series")
    begin = lax.axis_index(TIME) * width

    def place(n):
        return LANES + n * span + (2 * LANES * (n // half) if ends else 0)

    def source(n):
        return lax.rem(base + n * span, width) if ends else base + n * span

    def fetch(n):
        return pltpu.make_async_copy(
            signal_ref.at[:, aligned(source(n), span)],
            x_ref.at[:, aligned(place(n), span)],
            in_sems.at[n],
        )

    middle = place(half)
    tail = place(count - 1) + span
    after = (base + count * span) % width
    sides = [
        (signal_ref.at[:, pl.ds(base - LANES, LANES)], x_ref.at[:, pl.ds(0, LANES)]),
        (signal_ref.at[:, pl.ds(after, LANES)], x_ref.at[:, pl.ds(tail, LANES)]),
        (first_hbm, first_ref),
        (last_hbm, last_ref),
        (taps_hbm, taps_ref),
    ]
    if ends:
        sides += [
            (halo_refs[0], x_ref.at[:, pl.ds(middle - LANES, LANES)]),
            (halo_refs[1], x_ref.at[:, pl.ds(middle - 2 * LANES, LANES)]),
        ]
    if edges:
        sides += [
            (signal_ref.at[:, pl.ds(0, LANES)], edge_refs[0]),
            (signal_ref.at[:, pl.ds(width - LANES, LANES)], edge_refs[1]),
        ]
    sides = [pltpu.make_async_copy(a, b, side_sems.at[n]) for n, (a, b) in enumerate(sides)]
    for copy in sides[:5]:
        copy.start()
    for n in range(count):
        fetch(n).start()
    for copy in sides[5:]:
        copy.start()

    def give(n, kind):
        return pltpu.make_async_copy(
            fit_ref.at[kind, :, aligned(n * span, span)],
            fit_hbm[kind].at[:, aligned(source(n), span)],
            out_sems.at[kind, n],
        )

    def piece(k):
        return pltpu.make_async_copy(resid_ref.at[k], outs[k], piece_sems.at[k])

    lane = lax.broadcasted_iota(jnp.int32, (ROWS, LANES), 1)
    low = lane < 64
    height = ROWS * blocks
    late = len(sides) - (2 if edges else 0)

    for copy in sides[:late]:
        copy.wait()
    fetch(0).wait()

    row = lax.broadcasted_iota(jnp.int32, (ROWS, LANES), 0)
    first = jnp.zeros((ROWS, LANES), jnp.int32)
    last = jnp.zeros((ROWS, LANES), jnp.int32)
    for r in range(ROWS):
        first = jnp.where(row == r, first_ref[mine * ROWS + r], first)
        last = jnp.where(row == r, last_ref[mine * ROWS + r], last)

    def body(n, carry):
        at = place(n)
        k = (n // per + GROUPS - mine) % GROUPS
        mark = begin + source(n)
        out_at = n * span
        piece_at = n % per * span

        @pl.when(n + 1 < count)
        def _():
            fetch(n + 1).wait()

        x = x_ref[:, aligned(at - LANES, span + 2 * LANES)]
        parts = thirds(x)

        def cut(m, b):
            return parts[m][:, b * LANES : (b + 1) * LANES]

        rows = [
            jnp.concatenate(
                [cut(m, b + 1), jnp.where(low, cut(m, b + 2), cut(m, b))], axis=1
            )
            for m in range(3)
            for b in range(blocks)
        ]
        fit = jnp.dot(
            jnp.concatenate(rows, axis=0), taps_ref[...], preferred_element_type=jnp.float32
        )
        fit = fit[:height] + (fit[height : 2 * height] + fit[2 * height :])
        since = first - mark
        until = last - mark
        for b in range(blocks):
            part = fit[b * ROWS : (b + 1) * ROWS]
            moment = lane + b * LANES
            inside = (moment >= since) & (moment < until)
            smooth = part[:, :LANES] * SMOOTH_SCALE
            if fits:
                to = aligned(out_at + b * LANES, LANES)
                fit_ref[0, :, to] = jnp.where(inside, smooth, 0.0)
                fit_ref[1, :, to] = jnp.where(inside, part[:, LANES:] * SLOPE_SCALE, 0.0)
            if resids:
                resid = x[:, (b + 1) * LANES : (b + 2) * LANES] - smooth
                resid_ref[k, :, aligned(piece_at + b * LANES, LANES)] = jnp.where(inside, resid, 0.0)

        def starts_here(a):
            return (a > mark - HALF) & (a < mark + span)

        def stops_here(z):
            return (z > mark) & (z < mark + span + HALF)

        holds = False
        for r in range(ROWS):
            holds = holds | starts_here(first_ref[mine * ROWS + r])
            holds = holds | stops_here(last_ref[mine * ROWS + r])

        @pl.when(holds)
        def _():
            def mend(r, left, centre, side):
                b = (left + LANES) // LANES - 1
                v = x_ref[:, aligned(at + b * LANES, 2 * LANES)]
                j = lax.broadcasted_iota(jnp.int32, (ROWS, 2 * LANES), 1) + (b * LANES - centre)
                w = jnp.where((j >= -HALF) & (j <= HALF), v, 0.0)
                f = jnp.clip(j, -HALF, HALF).astype(jnp.float32)
                level = jnp.sum(w, axis=1, keepdims=True) * (1.0 / TAPS)
                tilt = jnp.sum(w * f, axis=1, keepdims=True) * (1.0 / SECOND)
                curve = f * f - CENTRE_SQ
                bend = jnp.sum(w * curve, axis=1, keepdims=True) * (1.0 / FOURTH)
                smooth = level + tilt * f + bend * curve
                slope = HALF * (tilt + 2.0 * f * bend)
                held = (j * side >= 1) & (j * side <= HALF)
                for h in range(2):

                    @pl.when((b + h >= 0) & (b + h < blocks))
                    def _():
                        part = slice(h * LANES, (h + 1) * LANES)
                        to = held[:, part] & (row == r)
                        if fits:
                            at_fit = aligned(out_at + (b + h) * LANES, LANES)
                            fit_ref[0, :, at_fit] = jnp.where(
                                to, smooth[:, part], fit_ref[0, :, at_fit]
                            )
                            fit_ref[1, :, at_fit] = jnp.where(
                                to, slope[:, part], fit_ref[1, :, at_fit]
                            )
                        if resids:
                            at_piece = aligned(piece_at + (b + h) * LANES, LANES)
                            resid_ref[k, :, at_piece] = jnp.where(
                                to, v[:, part] - smooth[:, part], resid_ref[k, :, at_piece]
                            )

            def series(r, carry):
                a = first_ref[mine * ROWS + r]
                z = last_ref[mine * ROWS + r]

                @pl.when(starts_here(a))
                def _():
                    mend(r, a - mark, a - mark + HALF, -1)

                @pl.when(stops_here(z))
                def _():
                    mend(r, z - mark - TAPS, z - mark - HALF - 1, 1)

                return carry

            lax.fori_loop(0, ROWS, series, 0)

        if fits:
            give(n, 0).start()
            give(n, 1).start()
        if resids:
            for kk in range(GROUPS):

                @pl.when((k == kk) & (n % per == per - 1))
                def _():
                    piece(kk).start()

        return carry

    lax.fori_loop(0, count, body, 0)
    for copy in sides[late:]:
        copy.wait()
    if resids:
        for kk in range(GROUPS):
            piece(kk).wait()
    if fits:
        for n in range(count):
            give(n, 0).wait()
            give(n, 1).wait()


def fit_steps(plan, first, last, signal, taps, fits, resids, halos, edges, held):
    _, span, count = plan
    rows, width = signal.shape
    ends = halos is not None
    chain = held is not None
    hbm = pl.BlockSpec(memory_space=pltpu.HBM)
    loose = pl.BlockSpec(memory_space=pl.ANY)
    args = [pltpu.with_memory_space_constraint(a, pltpu.HBM) for a in (first, last, signal, taps)]
    args += list(halos or ()) + list(held or ())
    aliases = {len(args) - 2: 0, len(args) - 1: 1} if chain else {}
    wide = jax.ShapeDtypeStruct((rows, width), jnp.float32)
    part = jax.ShapeDtypeStruct((rows, count // GROUPS * span), jnp.float32)
    edge = jax.ShapeDtypeStruct((rows, LANES), jnp.float32)
    out_shape = [wide] * (2 * fits) + [part] * (GROUPS * resids) + [edge] * (2 * edges)
    scratch = [
        pltpu.VMEM((rows, count * span + (4 if ends else 2) * LANES), jnp.float32),
        pltpu.VMEM(taps.shape, taps.dtype),
        pltpu.SMEM(first.shape, jnp.int32),
        pltpu.SMEM(last.shape, jnp.int32),
        pltpu.SemaphoreType.DMA((count,)),
        pltpu.SemaphoreType.DMA((9,)),
    ]
    if fits:
        scratch += [
            pltpu.VMEM((2, rows, count * span), jnp.float32),
            pltpu.SemaphoreType.DMA((2, count)),
        ]
    if resids:
        scratch += [
            pltpu.VMEM((GROUPS, rows, count // GROUPS * span), jnp.float32),
            pltpu.SemaphoreType.DMA((GROUPS,)),
        ]
    return pl.pallas_call(
        functools.partial(fit_kernel, plan, fits, resids, ends, edges, chain),
        in_specs=[hbm] * 4 + [loose] * len(halos or ()) + [hbm] * len(held or ()),
        out_specs=[hbm] * (2 * fits) + [loose] * (GROUPS * resids + 2 * edges),
        out_shape=out_shape,
        scratch_shapes=scratch,
        input_output_aliases=aliases,
        compiler_params=pltpu.CompilerParams(vmem_limit_bytes=12 * MIB),
        cost_estimate=pl.CostEstimate(
            flops=count * 3 * rows * span * 256 * 4,
            bytes_accessed=count * rows * span * 4 * 4,
            transcendentals=0,
        ),
    )(*args)


def gram_kernel(add, spread, *refs):
    parts, refs = refs[:GROUPS], refs[GROUPS:]
    if add:
        so_far_ref, refs = refs[0], refs[1:]
    out_ref, stack_ref = refs
    mine = lax.axis_index("series")
    for k in range(GROUPS):
        at = pl.multiple_of((mine + GROUPS - k) % GROUPS * ROWS, ROWS)
        x = parts[k][...]
        a = x.astype(jnp.bfloat16)
        b = (x - a.astype(jnp.float32)).astype(jnp.bfloat16)
        stack_ref[pl.ds(at, ROWS)] = a
        stack_ref[pl.ds(64 + at, ROWS)] = a
        stack_ref[pl.ds(128 + at, ROWS)] = b
        stack_ref[pl.ds(192 + at, ROWS)] = b
    both = lax.dot_general(
        stack_ref[64:192],
        stack_ref[...],
        (((1,), (1,)), ((), ())),
        preferred_element_type=jnp.float32,
    )
    gram = both[:64, :128] + (both[64:, :128] + both[:64, 128:] + both[64:, 128:])
    low = lax.broadcasted_iota(jnp.int32, (8, LANES), 1) < 64
    for g in range(GROUPS):
        rows = jnp.where(low, gram[16 * g : 16 * g + 8], gram[16 * g + 8 : 16 * g + 16])
        if add:
            rows = rows + so_far_ref[g]
        if spread:
            for n in range(spread):
                out_ref[n, g] = rows
        else:
            out_ref[g] = rows


def gram_of(parts, so_far, spread):
    width = parts[0].shape[1]
    vmem = pl.BlockSpec(memory_space=pltpu.VMEM)
    args = list(parts) + ([] if so_far is None else [so_far])
    lead = (spread,) if spread else ()
    return pl.pallas_call(
        functools.partial(gram_kernel, so_far is not None, spread),
        in_specs=[vmem] * len(args),
        out_specs=vmem,
        out_shape=jax.ShapeDtypeStruct((*lead, GROUPS, 8, LANES), jnp.float32),
        scratch_shapes=[pltpu.VMEM((256, width), jnp.bfloat16)],
        compiler_params=pltpu.CompilerParams(vmem_limit_bytes=12 * MIB),
        cost_estimate=pl.CostEstimate(
            flops=128 * 256 * width * 2, bytes_accessed=64 * width * 4, transcendentals=0
        ),
    )(*args)


def packed(rows):
    return jnp.concatenate([rows[:8], rows[8:]], axis=1)


def exchanged(pieces):
    parts = [pieces[0]]
    for k in (2, 1, 3):
        pairs = [(s, (s + k) % GROUPS) for s in range(GROUPS)]
        parts.append(lax.ppermute(pieces[k], "series", pairs))
    return [parts[0], parts[2], parts[1], parts[3]]


def shards(taps, signal, valid_start, valid_end):
    rows, width = signal.shape
    devices = lax.axis_size(TIME)
    taps = jnp.asarray(taps, jnp.bfloat16)
    mine = lax.axis_index("series")
    edge = width // 16
    early, mid, late = (
        (edge, edge * 3 // 2, 4),
        (edge * 7, edge, 8),
        (edge * 15, edge // 2, 4),
    )

    def fit(plan, fits, resids, halos=None, edges=False, held=None):
        return fit_steps(
            plan, valid_start, valid_end, signal, taps, fits, resids, halos, edges, held
        )

    first = lax.dynamic_slice_in_dim(valid_start, mine * rows, rows)[:, None]
    last = lax.dynamic_slice_in_dim(valid_end, mine * rows, rows)[:, None]
    shared = jnp.minimum(last, valid_end[None, :]) - jnp.maximum(first, valid_start[None, :])
    shared = packed(shared.astype(jnp.float32))

    *pieces, front, back = fit(early, False, True, edges=True)
    parts = exchanged(pieces)
    *pieces, = fit(mid, True, True)
    held, pieces = pieces[:2], pieces[2:]
    parts_mid = exchanged(pieces)
    left = lax.ppermute(back, TIME, [(t, t + 1) for t in range(devices - 1)])
    right = lax.ppermute(front, TIME, [(t + 1, t) for t in range(devices - 1)])
    gram = gram_of(parts, None, None)
    pieces = fit(late, True, True, halos=(left, right), held=held)
    held, pieces = pieces[:2], pieces[2:]
    parts = exchanged(pieces)
    gram = gram_of(parts_mid, gram, None)
    copies = gram_of(parts, gram, devices).reshape(devices * GROUPS, 8, LANES)
    copies = lax.all_to_all(copies, (*TIME, "series"), 0, 0, tiled=True)
    held = fit(early, True, False, held=held)
    cov = jnp.sum(copies, axis=0) / shared
    return (*held, jnp.concatenate([cov[:, :64], cov[:, 64:]], axis=0))


def solution(mesh):
    split = Mesh(mesh.devices.reshape(4, 4, 2, GROUPS), (*TIME, "series"))
    return jax.shard_map(
        functools.partial(shards, filter_matrix()),
        mesh=split,
        in_specs=(P("series", TIME), P(), P()),
        out_specs=(P("series", TIME), P("series", TIME), P("series", None)),
        check_vma=False,
    )
```

time: 67.7 us -> 73.3 us (1.083)
  Pallas kernels: 14.8 us -> 21.6 us
  waiting for transfers between devices: 22.2 us -> 18.1 us
  starting transfers between devices: 28.6 us -> 31.3 us
    pallas_call x4 -> x7, Pallas kernels: 14.8 us -> 21.6 us  [the longest x4 18.5 us: fit_steps(): pl.pallas_call(functools.partial(fit_kernel, plan, fits, resids, ends, ed...]
    all_to_all x1, waiting for transfers between devices: 13.9 us -> 9.12 us  [shards(): copies = lax.all_to_all(copies, (*TIME, 'series'), 0, 0, tiled=True)]
    ppermute x6 -> x9, waiting for transfers between devices: 8.35 us -> 4.64 us  [exchanged(): parts.append(lax.ppermute(pieces[k], 'series', pairs))]
    ppermute x1, waiting for transfers between devices: 0.01 us -> 3.59 us  [shards(): right = lax.ppermute(front, TIME, [(t + 1, t) for t in range(devices - 1)])]
    ppermute x1, starting transfers between devices: 3.28 us -> 6.03 us  [shards(): left = lax.ppermute(back, TIME, [(t, t + 1) for t in range(devices - 1)])]
    ppermute x1, waiting for transfers between devices: 0.01 us -> 0.77 us  [shards(): left = lax.ppermute(back, TIME, [(t, t + 1) for t in range(devices - 1)])]
    ppermute x6 -> x9, starting transfers between devices: 12.2 us -> 12.8 us  [exchanged(): parts.append(lax.ppermute(pieces[k], 'series', pairs))]
  transfers between devices with their start and end apart: 9 -> 12, of which waited for: 3 -> 4; matrix products, arithmetic and copies ran while one was open for 0% -> 0% of each run, Pallas kernels for 10% -> 21%
where the time goes in v3:
time: 73.3 us; the launch traced here: 73 us
  starting transfers between devices  31.3 us (43%)
  Pallas kernels  21.6 us (29%)
  waiting for transfers between devices  18.1 us (25%)
  other arithmetic  0.9 us (1%)
  between operations  0.78 us (1%)
    pallas_call x4, Pallas kernels, fit_steps(): pl.pallas_call(functools.partial(fit_kernel, plan, fits, resids, ends, ed...  18.5 us
    ppermute x9, starting transfers between devices, exchanged(): parts.append(lax.ppermute(pieces[k], 'series', pairs))  12.8 us
    all_to_all x1, starting transfers between devices, shards(): copies = lax.all_to_all(copies, (*TIME, 'series'), 0, 0, tiled=True)  10.6 us
    all_to_all x1, waiting for transfers between devices, shards(): copies = lax.all_to_all(copies, (*TIME, 'series'), 0, 0, tiled=True)  9.12 us
    ppermute x1, starting transfers between devices, shards(): left = lax.ppermute(back, TIME, [(t, t + 1) for t in range(devices - 1)])  6.03 us
    ppermute x9, waiting for transfers between devices, exchanged(): parts.append(lax.ppermute(pieces[k], 'series', pairs))  4.64 us
    ppermute x1, waiting for transfers between devices, shards(): right = lax.ppermute(front, TIME, [(t + 1, t) for t in range(devices - 1)])  3.59 us
    pallas_call x3, Pallas kernels, gram_of(): pl.pallas_call(functools.partial(gram_kernel, so_far is not None, spread)...  3.16 us
  transfers between devices with their start and end apart: 12, of which 4 were waited for; matrix products, arithmetic and copies ran while one was open for 0% of the time, Pallas kernels for 21%

profile of v3, /device:TPU:1, one launch (start us, length us, event | category | flops | bytes accessed | tf_op | source)
XLA Modules:
  0.0 73.0 jit_solution(16136215550092156234)
XLA Ops:
  0.6 5.0 %shard_map.67 = (f32[16,3072]{1,0:T(8,128)S(1)}, f32[16,3072]{1,0:T(8,128)S(1)}, f32[16,3072]{1,0:T(8,128)S(1)}, f32[16,3072]{1,0:T(8,128)S(1)}, f32[16,128]{1,0:T(8,128)S(1)}, /*index=5*/f32[16,128]{1,0:T(8,128)S(1)}) custom-call(s32[64]{0:T(128)} %refs_0_.7, s32[64]{0:T(128)} %refs_1_.7, f32[16,32768]{1,0:T(8,128)} %refs_2_.7, ...), custom_call_target="tpu_custom_call" | custom-call | flops 603979776 | bytes 3145728 | tf_op jit(solution)/shard_map/pallas_call | solution.py:307
  5.6 2.9 %collective-permute-start.10 = (f32[16,3072]{1,0:T(8,128)S(1)}, f32[16,3072]{1,0:T(8,128)S(1)}, u32[]{:S(2)}, u32[]{:S(2)}) collective-permute-start(f32[16,3072]{1,0:T(8,128)S(1)} %get-tuple-element.42), channel_id=1, source_target_pairs={{0,3},{1,0},{2,1},{3,2},{4,7},{5,4},{6,5},{7,6},{8,11},{9,8},{10,9... | collective-permute-start | bytes 589832 | tf_op jit(solution)/shard_map/ppermute | solution.py:383
  8.5 5.3 %shard_map.68 = (f32[16,32768]{1,0:T(8,128)}, f32[16,32768]{1,0:T(8,128)}, f32[16,4096]{1,0:T(8,128)S(1)}, f32[16,4096]{1,0:T(8,128)S(1)}, f32[16,4096]{1,0:T(8,128)S(1)}, /*index=5*/f32[16,4096]{1,0:T(8,128)S(1)}) custom-call(s32[64]{0:T(128)} %refs_0_.7, s32[64]{0:T(128)} %refs_1_.7, f32[16,32768]{1,0:T(8,128)} %refs_2_.7, ...), custom_call_target="tpu_custom_call" | custom-call | flops 805306368 | bytes 4194304 | tf_op jit(solution)/shard_map/pallas_call | solution.py:307
  13.9 0.1 collective-permute-start.5
  14.0 1.7 %collective-permute-start.6 = (f32[16,4096]{1,0:T(8,128)S(1)}, f32[16,4096]{1,0:T(8,128)S(1)}, u32[]{:S(2)}, u32[]{:S(2)}) collective-permute-start(f32[16,4096]{1,0:T(8,128)S(1)} %get-tuple-element.37), channel_id=1, source_target_pairs={{0,2},{1,3},{2,0},{3,1},{4,6},{5,7},{6,4},{7,5},{8,10},{9,11},{10,... | collective-permute-start | bytes 786440 | tf_op jit(solution)/shard_map/ppermute | solution.py:383
  15.7 1.9 %collective-permute-start.7 = (f32[16,4096]{1,0:T(8,128)S(1)}, f32[16,4096]{1,0:T(8,128)S(1)}, u32[]{:S(2)}, u32[]{:S(2)}) collective-permute-start(f32[16,4096]{1,0:T(8,128)S(1)} %get-tuple-element.38), channel_id=1, source_target_pairs={{0,3},{1,0},{2,1},{3,2},{4,7},{5,4},{6,5},{7,6},{8,11},{9,8},{10,9... | collective-permute-start | bytes 786440 | tf_op jit(solution)/shard_map/ppermute | solution.py:383
  17.5 6.0 %collective-permute-start = (f32[16,128]{1,0:T(8,128)S(1)}, f32[16,128]{1,0:T(8,128)S(1)}, u32[]{:S(2)}, u32[]{:S(2)}) collective-permute-start(f32[16,128]{1,0:T(8,128)S(1)} %get-tuple-element.23), channel_id=1, source_target_pairs={{0,4},{4,8},{8,12},{12,16},{16,20},{20,24},{24,28},{28,32},{32,36}... | collective-permute-start | bytes 24584 | tf_op jit(solution)/shard_map/ppermute | solution.py:414
  23.6 0.8 %collective-permute-done.refs_4_ = f32[16,128]{1,0:T(8,128)S(1)} collective-permute-done((f32[16,128]{1,0:T(8,128)S(1)}, f32[16,128]{1,0:T(8,128)S(1)}, u32[]{:S(2)}, u32[]{:S(2)}) %collective-permute-start) | collective-permute-done | bytes 8224 | tf_op jit(solution)/shard_map/ppermute | solution.py:414
  24.4 1.9 %collective-permute-start.1 = (f32[16,128]{1,0:T(8,128)S(1)}, f32[16,128]{1,0:T(8,128)S(1)}, u32[]{:S(2)}, u32[]{:S(2)}) collective-permute-start(f32[16,128]{1,0:T(8,128)S(1)} %get-tuple-element.24), channel_id=1, source_target_pairs={{4,0},{8,4},{12,8},{16,12},{20,16},{24,20},{28,24},{32,28},{36,32}... | collective-permute-start | bytes 24584 | tf_op jit(solution)/shard_map/ppermute | solution.py:415
  26.3 3.6 %collective-permute-done.1.refs_5_ = f32[16,128]{1,0:T(8,128)S(1)} collective-permute-done((f32[16,128]{1,0:T(8,128)S(1)}, f32[16,128]{1,0:T(8,128)S(1)}, u32[]{:S(2)}, u32[]{:S(2)}) %collective-permute-start.1) | collective-permute-done | bytes 8224 | tf_op jit(solution)/shard_map/ppermute | solution.py:415
  29.9 0.7 %collective-permute-start.8 = (f32[16,3072]{1,0:T(8,128)S(1)}, f32[16,3072]{1,0:T(8,128)S(1)}, u32[]{:S(2)}, u32[]{:S(2)}) collective-permute-start(f32[16,3072]{1,0:T(8,128)S(1)} %get-tuple-element.40), channel_id=1, source_target_pairs={{0,1},{1,2},{2,3},{3,0},{4,5},{5,6},{6,7},{7,4},{8,9},{9,10},{10,1... | collective-permute-start | bytes 589832 | tf_op jit(solution)/shard_map/ppermute | solution.py:383
  30.6 1.9 %collective-permute-start.9 = (f32[16,3072]{1,0:T(8,128)S(1)}, f32[16,3072]{1,0:T(8,128)S(1)}, u32[]{:S(2)}, u32[]{:S(2)}) collective-permute-start(f32[16,3072]{1,0:T(8,128)S(1)} %get-tuple-element.41), channel_id=1, source_target_pairs={{0,2},{1,3},{2,0},{3,1},{4,6},{5,7},{6,4},{7,5},{8,10},{9,11},{10,... | collective-permute-start | bytes 589832 | tf_op jit(solution)/shard_map/ppermute | solution.py:383
  32.5 3.4 %shard_map.69 = (f32[16,32768]{1,0:T(8,128)}, f32[16,32768]{1,0:T(8,128)}, f32[16,1024]{1,0:T(8,128)S(1)}, f32[16,1024]{1,0:T(8,128)S(1)}, f32[16,1024]{1,0:T(8,128)S(1)}, /*index=5*/f32[16,1024]{1,0:T(8,128)S(1)}) custom-call(s32[64]{0:T(128)} %refs_0_.7, s32[64]{0:T(128)} %refs_1_.7, ...), custom_call_target="tpu_custom_call", output_to_operand_aliasing={{0}: (6, {}), {1}: (7, {})} | custom-call | flops 201326592 | bytes 1048576 | tf_op jit(solution)/shard_map/pallas_call | solution.py:307
  35.9 0.0 copy-start.1
  35.9 0.0 copy-start
  35.9 4.6 %collective-permute-done.8.refs_1_ = f32[16,3072]{1,0:T(8,128)S(1)} collective-permute-done((f32[16,3072]{1,0:T(8,128)S(1)}, f32[16,3072]{1,0:T(8,128)S(1)}, u32[]{:S(2)}, u32[]{:S(2)}) %collective-permute-start.8) | collective-permute-done | bytes 196640 | tf_op jit(solution)/shard_map/ppermute | solution.py:383
  40.5 1.5 %collective-permute-start.3 = (f32[16,1024]{1,0:T(8,128)S(1)}, f32[16,1024]{1,0:T(8,128)S(1)}, u32[]{:S(2)}, u32[]{:S(2)}) collective-permute-start(f32[16,1024]{1,0:T(8,128)S(1)} %get-tuple-element.33), channel_id=1, source_target_pairs={{0,2},{1,3},{2,0},{3,1},{4,6},{5,7},{6,4},{7,5},{8,10},{9,11},{10,... | collective-permute-start | bytes 196616 | tf_op jit(solution)/shard_map/ppermute | solution.py:383
  42.1 2.1 %collective-permute-start.4 = (f32[16,1024]{1,0:T(8,128)S(1)}, f32[16,1024]{1,0:T(8,128)S(1)}, u32[]{:S(2)}, u32[]{:S(2)}) collective-permute-start(f32[16,1024]{1,0:T(8,128)S(1)} %get-tuple-element.34), channel_id=1, source_target_pairs={{0,3},{1,0},{2,1},{3,2},{4,7},{5,4},{6,5},{7,6},{8,11},{9,8},{10,9... | collective-permute-start | bytes 196616 | tf_op jit(solution)/shard_map/ppermute | solution.py:383
  44.1 0.8 %shard_map.71.refs_4_ = f32[4,8,128]{2,1,0:T(8,128)S(1)} custom-call(f32[16,3072]{1,0:T(8,128)S(1)} %get-tuple-element.39.refs_0_, f32[16,3072]{1,0:T(8,128)S(1)} %collective-permute-done.8.refs_1_, f32[16,3072]{1,0:T(8,128)S(1)} %collective-permute-done.9.refs_2_, f32[16,3072]{1,0:T(8,128)S(1)} %collective-permute-done.10.refs_3_), custom_call_target="tpu_custom_call" | custom-call | flops 201326592 | bytes 786432 | tf_op jit(solution)/shard_map/pallas_call | solution.py:362
  45.0 1.1 %shard_map.72.refs_4_ = f32[4,8,128]{2,1,0:T(8,128)S(1)} custom-call(f32[16,4096]{1,0:T(8,128)S(1)} %get-tuple-element.35.refs_0_, f32[16,4096]{1,0:T(8,128)S(1)} %collective-permute-done.5.refs_1_, f32[16,4096]{1,0:T(8,128)S(1)} %collective-permute-done.6.refs_2_, f32[16,4096]{1,0:T(8,128)S(1)} %collective-permute-done.7.refs_3_, ...), custom_call_target="tpu_custom_call" | custom-call | flops 268435456 | bytes 1048576 | tf_op jit(solution)/shard_map/pallas_call | solution.py:362
  46.1 0.0 collective-permute-done.4.refs_3_
  46.1 1.2 %shard_map.73 = f32[32,4,8,128]{3,2,1,0:T(8,128)} custom-call(f32[16,1024]{1,0:T(8,128)S(1)} %get-tuple-element.31.refs_0_, f32[16,1024]{1,0:T(8,128)S(1)} %collective-permute-done.2.refs_1_, f32[16,1024]{1,0:T(8,128)S(1)} %collective-permute-done.3.refs_2_, f32[16,1024]{1,0:T(8,128)S(1)} %collective-permute-done.4.refs_3_, f32[4,8,128]{2,1,0:T(8,128)S(1)} %shard_map.72.refs_4_), custom_call_target="tpu_custom_call" | custom-call | flops 67108864 | bytes 262144 | tf_op jit(solution)/shard_map/pallas_call | solution.py:362
  47.4 10.6 %all-to-all-start = ((f32[128,8,128]{2,1,0:T(8,128)}), f32[128,8,128]{2,1,0:T(8,128)S(1)}, u32[]{:S(2)}, u32[]{:S(2)}) async-start(f32[128,8,128]{2,1,0:T(8,128)} %bitcast), calls=%async_computation | async-start | bytes 1048576 | tf_op jit(solution)/shard_map/all_to_all | solution.py:422
  58.0 0.1 dynamic_slice.6
  58.1 0.1 dynamic_slice.7
  58.1 0.1 subtract_convert_fusion
  58.2 4.7 %shard_map.70 = (f32[16,32768]{1,0:T(8,128)}, f32[16,32768]{1,0:T(8,128)}) custom-call(s32[64]{0:T(128)} %refs_0_.7, s32[64]{0:T(128)} %refs_1_.7, f32[16,32768]{1,0:T(8,128)} %refs_2_.7, bf16[256,256]{1,0:T(8,128)(2,1)} %constant.14.clone.refs_3_, f32[16,32768]{1,0:T(8,128)} %get-tuple-element.27.refs_4_, ...), custom_call_target="tpu_custom_call", output_to_operand_aliasing={{0}: (4, {}), {1}: (5, {})} | custom-call | flops 603979776 | bytes 3145728 | tf_op jit(solution)/shard_map/pallas_call | solution.py:307
  63.0 9.1 %all-to-all-done = f32[128,8,128]{2,1,0:T(8,128)S(1)} async-done(((f32[128,8,128]{2,1,0:T(8,128)}), f32[128,8,128]{2,1,0:T(8,128)S(1)}, u32[]{:S(2)}, u32[]{:S(2)}) %all-to-all-start) | async-done | bytes 524320 | tf_op jit(solution)/shard_map/all_to_all | solution.py:422
  72.1 0.1 reduce_sum.9
  72.2 0.1 maximum_divide_fusion
  72.3 0.1 fusion.1
  72.4 0.6 pad_maximum_fusion
  (11 shorter events, 0.0 us)
Async XLA Ops:
  5.6 25.0 %collective-permute-start.10 = (f32[16,3072]{1,0:T(8,128)S(1)}, f32[16,3072]{1,0:T(8,128)S(1)}, u32[]{:S(2)}, u32[]{:S(2)}) collective-permute-start(f32[16,3072]{1,0:T(8,128)S(1)} %get-tuple-element.42), channel_id=1, source_target_pairs={{0,3},{1,0},{2,1},{3,2},{4,7},{5,4},{6,5},{7,6},{8,11},{9,8},{10,9... | collective-permute-start | bytes 589832 | tf_op jit(solution)/shard_map/ppermute | solution.py:383
  13.9 28.2 %collective-permute-start.5 = (f32[16,4096]{1,0:T(8,128)S(1)}, f32[16,4096]{1,0:T(8,128)S(1)}, u32[]{:S(2)}, u32[]{:S(2)}) collective-permute-start(f32[16,4096]{1,0:T(8,128)S(1)} %get-tuple-element.36), channel_id=1, source_target_pairs={{0,1},{1,2},{2,3},{3,0},{4,5},{5,6},{6,7},{7,4},{8,9},{9,10},{10,1... | collective-permute-start | bytes 786440 | tf_op jit(solution)/shard_map/ppermute | solution.py:383
  14.0 31.0 %collective-permute-start.6 = (f32[16,4096]{1,0:T(8,128)S(1)}, f32[16,4096]{1,0:T(8,128)S(1)}, u32[]{:S(2)}, u32[]{:S(2)}) collective-permute-start(f32[16,4096]{1,0:T(8,128)S(1)} %get-tuple-element.37), channel_id=1, source_target_pairs={{0,2},{1,3},{2,0},{3,1},{4,6},{5,7},{6,4},{7,5},{8,10},{9,11},{10,... | collective-permute-start | bytes 786440 | tf_op jit(solution)/shard_map/ppermute | solution.py:383
  15.7 29.3 %collective-permute-start.7 = (f32[16,4096]{1,0:T(8,128)S(1)}, f32[16,4096]{1,0:T(8,128)S(1)}, u32[]{:S(2)}, u32[]{:S(2)}) collective-permute-start(f32[16,4096]{1,0:T(8,128)S(1)} %get-tuple-element.38), channel_id=1, source_target_pairs={{0,3},{1,0},{2,1},{3,2},{4,7},{5,4},{6,5},{7,6},{8,11},{9,8},{10,9... | collective-permute-start | bytes 786440 | tf_op jit(solution)/shard_map/ppermute | solution.py:383
  17.5 6.8 %collective-permute-start = (f32[16,128]{1,0:T(8,128)S(1)}, f32[16,128]{1,0:T(8,128)S(1)}, u32[]{:S(2)}, u32[]{:S(2)}) collective-permute-start(f32[16,128]{1,0:T(8,128)S(1)} %get-tuple-element.23), channel_id=1, source_target_pairs={{0,4},{4,8},{8,12},{12,16},{16,20},{20,24},{24,28},{28,32},{32,36}... | collective-permute-start | bytes 24584 | tf_op jit(solution)/shard_map/ppermute | solution.py:414
  24.4 5.5 %collective-permute-start.1 = (f32[16,128]{1,0:T(8,128)S(1)}, f32[16,128]{1,0:T(8,128)S(1)}, u32[]{:S(2)}, u32[]{:S(2)}) collective-permute-start(f32[16,128]{1,0:T(8,128)S(1)} %get-tuple-element.24), channel_id=1, source_target_pairs={{4,0},{8,4},{12,8},{16,12},{20,16},{24,20},{28,24},{32,28},{36,32}... | collective-permute-start | bytes 24584 | tf_op jit(solution)/shard_map/ppermute | solution.py:415
  29.9 10.7 %collective-permute-start.8 = (f32[16,3072]{1,0:T(8,128)S(1)}, f32[16,3072]{1,0:T(8,128)S(1)}, u32[]{:S(2)}, u32[]{:S(2)}) collective-permute-start(f32[16,3072]{1,0:T(8,128)S(1)} %get-tuple-element.40), channel_id=1, source_target_pairs={{0,1},{1,2},{2,3},{3,0},{4,5},{5,6},{6,7},{7,4},{8,9},{9,10},{10,1... | collective-permute-start | bytes 589832 | tf_op jit(solution)/shard_map/ppermute | solution.py:383
  30.6 9.9 %collective-permute-start.9 = (f32[16,3072]{1,0:T(8,128)S(1)}, f32[16,3072]{1,0:T(8,128)S(1)}, u32[]{:S(2)}, u32[]{:S(2)}) collective-permute-start(f32[16,3072]{1,0:T(8,128)S(1)} %get-tuple-element.41), channel_id=1, source_target_pairs={{0,2},{1,3},{2,0},{3,1},{4,6},{5,7},{6,4},{7,5},{8,10},{9,11},{10,... | collective-permute-start | bytes 589832 | tf_op jit(solution)/shard_map/ppermute | solution.py:383
  35.9 22.1 %copy-start.1 = (s32[64]{0:T(128)S(1)}, s32[64]{0:T(128)}, u32[]{:S(2)}) copy-start(s32[64]{0:T(128)} %refs_1_.7) | copy-start | bytes 772
  35.9 22.2 %copy-start = (s32[64]{0:T(128)S(1)}, s32[64]{0:T(128)}, u32[]{:S(2)}) copy-start(s32[64]{0:T(128)} %refs_0_.7) | copy-start | bytes 772
  40.5 5.6 %collective-permute-start.2 = (f32[16,1024]{1,0:T(8,128)S(1)}, f32[16,1024]{1,0:T(8,128)S(1)}, u32[]{:S(2)}, u32[]{:S(2)}) collective-permute-start(f32[16,1024]{1,0:T(8,128)S(1)} %get-tuple-element.32), channel_id=1, source_target_pairs={{0,1},{1,2},{2,3},{3,0},{4,5},{5,6},{6,7},{7,4},{8,9},{9,10},{10,1... | collective-permute-start | bytes 196616 | tf_op jit(solution)/shard_map/ppermute | solution.py:383
  40.5 5.6 %collective-permute-start.3 = (f32[16,1024]{1,0:T(8,128)S(1)}, f32[16,1024]{1,0:T(8,128)S(1)}, u32[]{:S(2)}, u32[]{:S(2)}) collective-permute-start(f32[16,1024]{1,0:T(8,128)S(1)} %get-tuple-element.33), channel_id=1, source_target_pairs={{0,2},{1,3},{2,0},{3,1},{4,6},{5,7},{6,4},{7,5},{8,10},{9,11},{10,... | collective-permute-start | bytes 196616 | tf_op jit(solution)/shard_map/ppermute | solution.py:383
  42.1 4.1 %collective-permute-start.4 = (f32[16,1024]{1,0:T(8,128)S(1)}, f32[16,1024]{1,0:T(8,128)S(1)}, u32[]{:S(2)}, u32[]{:S(2)}) collective-permute-start(f32[16,1024]{1,0:T(8,128)S(1)} %get-tuple-element.34), channel_id=1, source_target_pairs={{0,3},{1,0},{2,1},{3,2},{4,7},{5,4},{6,5},{7,6},{8,11},{9,8},{10,9... | collective-permute-start | bytes 196616 | tf_op jit(solution)/shard_map/ppermute | solution.py:383
  47.4 24.7 %all-to-all-start = ((f32[128,8,128]{2,1,0:T(8,128)}), f32[128,8,128]{2,1,0:T(8,128)S(1)}, u32[]{:S(2)}, u32[]{:S(2)}) async-start(f32[128,8,128]{2,1,0:T(8,128)} %bitcast), calls=%async_computation | async-start | bytes 1048576 | tf_op jit(solution)/shard_map/all_to_all | solution.py:422

commit v4 on v3

--- a/solution.py
+++ b/solution.py
@@ -46,22 +46,19 @@
     return pl.ds(pl.multiple_of(start, LANES), size)
 
 
-def fit_kernel(plan, fits, resids, ends, edges, chain, *refs):
+def fit_kernel(plan, fits, resids, ends, *refs):
     base, span, count = plan
     blocks = span // LANES
     refs = list(refs)
+    whole = ends and base == 0
     first_hbm, last_hbm, signal_ref, taps_hbm = refs[:4]
     refs = refs[4:]
     if ends:
         halo_refs, refs = refs[:2], refs[2:]
-    if chain:
-        refs = refs[2:]
     if fits:
         fit_hbm, refs = refs[:2], refs[2:]
     if resids:
         outs, refs = refs[:GROUPS], refs[GROUPS:]
-    if edges:
-        edge_refs, refs = refs[:2], refs[2:]
     x_ref, taps_ref, first_ref, last_ref, in_sems, side_sems = refs[:6]
     refs = refs[6:]
     if fits:
@@ -77,10 +74,10 @@
     begin = lax.axis_index(TIME) * width
 
     def place(n):
-        return LANES + n * span + (2 * LANES * (n // half) if ends else 0)
+        return LANES + n * span + (2 * LANES * (n // half) if ends and not whole else 0)
 
     def source(n):
-        return lax.rem(base + n * span, width) if ends else base + n * span
+        return lax.rem(base + n * span, width) if ends and not whole else base + n * span
 
     def fetch(n):
         return pltpu.make_async_copy(
@@ -92,30 +89,23 @@
     middle = place(half)
     tail = place(count - 1) + span
     after = (base + count * span) % width
-    sides = [
-        (signal_ref.at[:, pl.ds(base - LANES, LANES)], x_ref.at[:, pl.ds(0, LANES)]),
-        (signal_ref.at[:, pl.ds(after, LANES)], x_ref.at[:, pl.ds(tail, LANES)]),
-        (first_hbm, first_ref),
-        (last_hbm, last_ref),
-        (taps_hbm, taps_ref),
-    ]
+    sides = [(first_hbm, first_ref), (last_hbm, last_ref), (taps_hbm, taps_ref)]
+    if not whole:
+        sides += [
+            (signal_ref.at[:, pl.ds(base - LANES, LANES)], x_ref.at[:, pl.ds(0, LANES)]),
+            (signal_ref.at[:, pl.ds(after, LANES)], x_ref.at[:, pl.ds(tail, LANES)]),
+        ]
     if ends:
+        at_left, at_right = (0, tail) if whole else (middle - LANES, middle - 2 * LANES)
         sides += [
-            (halo_refs[0], x_ref.at[:, pl.ds(middle - LANES, LANES)]),
-            (halo_refs[1], x_ref.at[:, pl.ds(middle - 2 * LANES, LANES)]),
-        ]
-    if edges:
-        sides += [
-            (signal_ref.at[:, pl.ds(0, LANES)], edge_refs[0]),
-            (signal_ref.at[:, pl.ds(width - LANES, LANES)], edge_refs[1]),
+            (halo_refs[0], x_ref.at[:, pl.ds(at_left, LANES)]),
+            (halo_refs[1], x_ref.at[:, pl.ds(at_right, LANES)]),
         ]
     sides = [pltpu.make_async_copy(a, b, side_sems.at[n]) for n, (a, b) in enumerate(sides)]
-    for copy in sides[:5]:
+    for copy in sides:
         copy.start()
     for n in range(count):
         fetch(n).start()
-    for copy in sides[5:]:
-        copy.start()
 
     def give(n, kind):
         return pltpu.make_async_copy(
@@ -130,9 +120,8 @@
     lane = lax.broadcasted_iota(jnp.int32, (ROWS, LANES), 1)
     low = lane < 64
     height = ROWS * blocks
-    late = len(sides) - (2 if edges else 0)
-
-    for copy in sides[:late]:
+
+    for copy in sides:
         copy.wait()
     fetch(0).wait()
 
@@ -261,8 +250,6 @@
         return carry
 
     lax.fori_loop(0, count, body, 0)
-    for copy in sides[late:]:
-        copy.wait()
     if resids:
         for kk in range(GROUPS):
             piece(kk).wait()
@@ -272,27 +259,26 @@
             give(n, 1).wait()
 
 
-def fit_steps(plan, first, last, signal, taps, fits, resids, halos, edges, held):
-    _, span, count = plan
+def fit_steps(plan, first, last, signal, taps, fits, resids, halos):
+    base, span, count = plan
     rows, width = signal.shape
     ends = halos is not None
-    chain = held is not None
+    margins = 4 if ends and base else 2
+    if not fits:
+        taps = taps[:, :LANES]
     hbm = pl.BlockSpec(memory_space=pltpu.HBM)
     loose = pl.BlockSpec(memory_space=pl.ANY)
     args = [pltpu.with_memory_space_constraint(a, pltpu.HBM) for a in (first, last, signal, taps)]
-    args += list(halos or ()) + list(held or ())
-    aliases = {len(args) - 2: 0, len(args) - 1: 1} if chain else {}
+    args += list(halos or ())
     wide = jax.ShapeDtypeStruct((rows, width), jnp.float32)
     part = jax.ShapeDtypeStruct((rows, count // GROUPS * span), jnp.float32)
-    edge = jax.ShapeDtypeStruct((rows, LANES), jnp.float32)
-    out_shape = [wide] * (2 * fits) + [part] * (GROUPS * resids) + [edge] * (2 * edges)
     scratch = [
-        pltpu.VMEM((rows, count * span + (4 if ends else 2) * LANES), jnp.float32),
+        pltpu.VMEM((rows, count * span + margins * LANES), jnp.float32),
         pltpu.VMEM(taps.shape, taps.dtype),
         pltpu.SMEM(first.shape, jnp.int32),
         pltpu.SMEM(last.shape, jnp.int32),
         pltpu.SemaphoreType.DMA((count,)),
-        pltpu.SemaphoreType.DMA((9,)),
+        pltpu.SemaphoreType.DMA((7,)),
     ]
     if fits:
         scratch += [
@@ -305,13 +291,12 @@
             pltpu.SemaphoreType.DMA((GROUPS,)),
         ]
     return pl.pallas_call(
-        functools.partial(fit_kernel, plan, fits, resids, ends, edges, chain),
-        in_specs=[hbm] * 4 + [loose] * len(halos or ()) + [hbm] * len(held or ()),
-        out_specs=[hbm] * (2 * fits) + [loose] * (GROUPS * resids + 2 * edges),
-        out_shape=out_shape,
+        functools.partial(fit_kernel, plan, fits, resids, ends),
+        in_specs=[hbm] * 4 + [loose] * len(halos or ()),
+        out_specs=[hbm] * (2 * fits) + [loose] * (GROUPS * resids),
+        out_shape=[wide] * (2 * fits) + [part] * (GROUPS * resids),
         scratch_shapes=scratch,
-        input_output_aliases=aliases,
-        compiler_params=pltpu.CompilerParams(vmem_limit_bytes=12 * MIB),
+        compiler_params=pltpu.CompilerParams(vmem_limit_bytes=16 * MIB),
         cost_estimate=pl.CostEstimate(
             flops=count * 3 * rows * span * 256 * 4,
             bytes_accessed=count * rows * span * 4 * 4,
@@ -332,16 +317,15 @@
         a = x.astype(jnp.bfloat16)
         b = (x - a.astype(jnp.float32)).astype(jnp.bfloat16)
         stack_ref[pl.ds(at, ROWS)] = a
-        stack_ref[pl.ds(64 + at, ROWS)] = a
-        stack_ref[pl.ds(128 + at, ROWS)] = b
-        stack_ref[pl.ds(192 + at, ROWS)] = b
+        stack_ref[pl.ds(64 + at, ROWS)] = b
     both = lax.dot_general(
-        stack_ref[64:192],
+        stack_ref[...],
         stack_ref[...],
         (((1,), (1,)), ((), ())),
         preferred_element_type=jnp.float32,
     )
-    gram = both[:64, :128] + (both[64:, :128] + both[:64, 128:] + both[64:, 128:])
+    gram = both[:64] + both[64:]
+    gram = gram + pltpu.roll(gram, 64, 1)
     low = lax.broadcasted_iota(jnp.int32, (8, LANES), 1) < 64
     for g in range(GROUPS):
         rows = jnp.where(low, gram[16 * g : 16 * g + 8], gram[16 * g + 8 : 16 * g + 16])
@@ -364,10 +348,10 @@
         in_specs=[vmem] * len(args),
         out_specs=vmem,
         out_shape=jax.ShapeDtypeStruct((*lead, GROUPS, 8, LANES), jnp.float32),
-        scratch_shapes=[pltpu.VMEM((256, width), jnp.bfloat16)],
+        scratch_shapes=[pltpu.VMEM((128, width), jnp.bfloat16)],
         compiler_params=pltpu.CompilerParams(vmem_limit_bytes=12 * MIB),
         cost_estimate=pl.CostEstimate(
-            flops=128 * 256 * width * 2, bytes_accessed=64 * width * 4, transcendentals=0
+            flops=128 * 128 * width * 2, bytes_accessed=64 * width * 4, transcendentals=0
         ),
     )(*args)
 
@@ -389,40 +373,31 @@
     devices = lax.axis_size(TIME)
     taps = jnp.asarray(taps, jnp.bfloat16)
     mine = lax.axis_index("series")
-    edge = width // 16
-    early, mid, late = (
-        (edge, edge * 3 // 2, 4),
-        (edge * 7, edge, 8),
-        (edge * 15, edge // 2, 4),
-    )
-
-    def fit(plan, fits, resids, halos=None, edges=False, held=None):
-        return fit_steps(
-            plan, valid_start, valid_end, signal, taps, fits, resids, halos, edges, held
-        )
+    span = width // 8
+    early, late, whole = (2 * span, span, 4), (6 * span, span, 4), (0, span, 8)
+
+    def fit(plan, fits, resids, halos=None):
+        return fit_steps(plan, valid_start, valid_end, signal, taps, fits, resids, halos)
 
     first = lax.dynamic_slice_in_dim(valid_start, mine * rows, rows)[:, None]
     last = lax.dynamic_slice_in_dim(valid_end, mine * rows, rows)[:, None]
     shared = jnp.minimum(last, valid_end[None, :]) - jnp.maximum(first, valid_start[None, :])
     shared = packed(shared.astype(jnp.float32))
 
-    *pieces, front, back = fit(early, False, True, edges=True)
-    parts = exchanged(pieces)
-    *pieces, = fit(mid, True, True)
-    held, pieces = pieces[:2], pieces[2:]
-    parts_mid = exchanged(pieces)
-    left = lax.ppermute(back, TIME, [(t, t + 1) for t in range(devices - 1)])
-    right = lax.ppermute(front, TIME, [(t + 1, t) for t in range(devices - 1)])
+    left = lax.ppermute(signal[:, width - LANES :], TIME, [(t, t + 1) for t in range(devices - 1)])
+    right = lax.ppermute(
+        signal[:, :LANES], TIME, [(t + 1, t) for t in range(devices - 1)]
+    )
+    halos = (left, right)
+    parts = exchanged(fit(early, False, True))
+    parts_late = exchanged(fit(late, False, True, halos))
     gram = gram_of(parts, None, None)
-    pieces = fit(late, True, True, halos=(left, right), held=held)
-    held, pieces = pieces[:2], pieces[2:]
-    parts = exchanged(pieces)
-    gram = gram_of(parts_mid, gram, None)
-    copies = gram_of(parts, gram, devices).reshape(devices * GROUPS, 8, LANES)
+    smooth, slope = fit(whole, True, False, halos)
+    copies = gram_of(parts_late, gram, devices)
+    copies = copies.reshape(devices * GROUPS, 8, LANES)
     copies = lax.all_to_all(copies, (*TIME, "series"), 0, 0, tiled=True)
-    held = fit(early, True, False, held=held)
     cov = jnp.sum(copies, axis=0) / shared
-    return (*held, jnp.concatenate([cov[:, :64], cov[:, 64:]], axis=0))
+    return smooth, slope, jnp.concatenate([cov[:, :64], cov[:, 64:]], axis=0)
 
 
 def solution(mesh):

time: 73.3 us -> 65.1 us (0.89)
  starting transfers between devices: 31.3 us -> 25.3 us
  Pallas kernels: 21.6 us -> 16.2 us
  waiting for transfers between devices: 18.1 us -> 20.7 us
    ppermute x9 -> x6, waiting for transfers between devices: 4.64 us -> 13.5 us  [exchanged(): parts.append(lax.ppermute(pieces[k], 'series', pairs))]
    pallas_call x4 -> x3, Pallas kernels: 18.5 us -> 14 us  [fit_steps(): pl.pallas_call(functools.partial(fit_kernel, plan, fits, resids, ends), i...]
    ppermute x2, waiting for transfers between devices: 4.36 us -> 0.01 us  [the longest x1 0.01 us: shards(): lax.ppermute(signal[:, :LANES], TIME, [(t + 1, t) for t in range(devices...]
    ppermute x9 -> x6, starting transfers between devices: 12.8 us -> 9.96 us  [exchanged(): parts.append(lax.ppermute(pieces[k], 'series', pairs))]
    ppermute x2, starting transfers between devices: 7.94 us -> 5.55 us  [the longest x1 3.17 us: shards(): lax.ppermute(signal[:, width - LANES:], TIME, [(t, t + 1) for t in range(...]
    all_to_all x1, waiting for transfers between devices: 9.12 us -> 7.15 us  [shards(): copies = lax.all_to_all(copies, (*TIME, 'series'), 0, 0, tiled=True)]
    pallas_call x3 -> x2, Pallas kernels: 3.16 us -> 2.28 us  [gram_of(): pl.pallas_call(functools.partial(gram_kernel, so_far is not None, spread)...]
    all_to_all x1, starting transfers between devices: 10.6 us -> 9.79 us  [shards(): copies = lax.all_to_all(copies, (*TIME, 'series'), 0, 0, tiled=True)]
  transfers between devices with their start and end apart: 12 -> 9, of which waited for: 4 -> 4; matrix products, arithmetic and copies ran while one was open for 0% -> 1% of each run, Pallas kernels for 21% -> 17%
where the time goes in v4:
time: 65.1 us; the launch traced here: 64.8 us
  starting transfers between devices  25.3 us (39%)
  waiting for transfers between devices  20.7 us (32%)
  Pallas kernels  16.2 us (25%)
  local copies, waits for them, and re-layouts  0.96 us (1%)
  other arithmetic  0.9 us (1%)
  between operations  0.71 us (1%)
    pallas_call x3, Pallas kernels, fit_steps(): pl.pallas_call(functools.partial(fit_kernel, plan, fits, resids, ends), i...  14 us
    ppermute x6, waiting for transfers between devices, exchanged(): parts.append(lax.ppermute(pieces[k], 'series', pairs))  13.5 us
    ppermute x6, starting transfers between devices, exchanged(): parts.append(lax.ppermute(pieces[k], 'series', pairs))  9.96 us
    all_to_all x1, starting transfers between devices, shards(): copies = lax.all_to_all(copies, (*TIME, 'series'), 0, 0, tiled=True)  9.79 us
    all_to_all x1, waiting for transfers between devices, shards(): copies = lax.all_to_all(copies, (*TIME, 'series'), 0, 0, tiled=True)  7.15 us
    ppermute x1, starting transfers between devices, shards(): lax.ppermute(signal[:, width - LANES:], TIME, [(t, t + 1) for t in range(...  3.17 us
    ppermute x1, starting transfers between devices, shards(): lax.ppermute(signal[:, :LANES], TIME, [(t + 1, t) for t in range(devices...  2.38 us
    pallas_call x2, Pallas kernels, gram_of(): pl.pallas_call(functools.partial(gram_kernel, so_far is not None, spread)...  2.28 us
  transfers between devices with their start and end apart: 9, of which 4 were waited for; matrix products, arithmetic and copies ran while one was open for 1% of the time, Pallas kernels for 17%

profile of v4, /device:TPU:1, one launch (start us, length us, event | category | flops | bytes accessed | tf_op | source)
XLA Modules:
  0.0 64.8 jit_solution(6649528408842271118)
XLA Ops:
  0.6 3.6 %shard_map.69 = (f32[16,4096]{1,0:T(8,128)S(1)}, f32[16,4096]{1,0:T(8,128)S(1)}, f32[16,4096]{1,0:T(8,128)S(1)}, f32[16,4096]{1,0:T(8,128)S(1)}) custom-call(s32[64]{0:T(128)} %refs_0_.5, s32[64]{0:T(128)} %refs_1_.5, f32[16,32768]{1,0:T(8,128)} %refs_2_.5, bf16[256,128]{1,0:T(8,128)(2,1)} %constant.15.refs_3_), custom_call_target="tpu_custom_call" | custom-call | flops 805306368 | bytes 4194304 | tf_op jit(solution)/shard_map/pallas_call | solution.py:293
  4.2 0.0 copy-start
  4.2 0.0 copy-start.1
  4.2 2.6 %collective-permute-start.5 = (f32[16,4096]{1,0:T(8,128)S(1)}, f32[16,4096]{1,0:T(8,128)S(1)}, u32[]{:S(2)}, u32[]{:S(2)}) collective-permute-start(f32[16,4096]{1,0:T(8,128)S(1)} %get-tuple-element.20), channel_id=1, source_target_pairs={{0,1},{1,2},{2,3},{3,0},{4,5},{5,6},{6,7},{7,4},{8,9},{9,10},{10,1... | collective-permute-start | bytes 786440 | tf_op jit(solution)/shard_map/ppermute | solution.py:367
  6.8 0.7 %fusion = (f32[16,128]{1,0:T(8,128)S(1)}, f32[16,128]{1,0:T(8,128)S(1)}) fusion(f32[16,32768]{1,0:T(8,128)} %refs_2_.5), kind=kLoop, calls=%fused_computation.3 | loop fusion | bytes 32768 | tf_op jit(solution)/shard_map/slice | solution.py:389
  7.5 2.4 %collective-permute-start.1 = (f32[16,128]{1,0:T(8,128)S(1)}, f32[16,128]{1,0:T(8,128)S(1)}, u32[]{:S(2)}, u32[]{:S(2)}) collective-permute-start(f32[16,128]{1,0:T(8,128)S(1)} %get-tuple-element.23), channel_id=1, source_target_pairs={{4,0},{8,4},{12,8},{16,12},{20,16},{24,20},{28,24},{32,28},{36,32}... | collective-permute-start | bytes 24584 | tf_op jit(solution)/shard_map/ppermute | solution.py:388
  9.9 3.2 %collective-permute-start = (f32[16,128]{1,0:T(8,128)S(1)}, f32[16,128]{1,0:T(8,128)S(1)}, u32[]{:S(2)}, u32[]{:S(2)}) collective-permute-start(f32[16,128]{1,0:T(8,128)S(1)} %get-tuple-element.24), channel_id=1, source_target_pairs={{0,4},{4,8},{8,12},{12,16},{16,20},{20,24},{24,28},{28,32},{32,36}... | collective-permute-start | bytes 24584 | tf_op jit(solution)/shard_map/ppermute | solution.py:387
  13.1 3.4 %collective-permute-start.6 = (f32[16,4096]{1,0:T(8,128)S(1)}, f32[16,4096]{1,0:T(8,128)S(1)}, u32[]{:S(2)}, u32[]{:S(2)}) collective-permute-start(f32[16,4096]{1,0:T(8,128)S(1)} %get-tuple-element.21), channel_id=1, source_target_pairs={{0,2},{1,3},{2,0},{3,1},{4,6},{5,7},{6,4},{7,5},{8,10},{9,11},{10,... | collective-permute-start | bytes 786440 | tf_op jit(solution)/shard_map/ppermute | solution.py:367
  16.5 0.1 collective-permute-start.7
  16.6 0.0 collective-permute-done.1.refs_5_
  16.6 0.0 collective-permute-done.refs_4_
  16.6 3.5 %shard_map.68 = (f32[16,4096]{1,0:T(8,128)S(1)}, f32[16,4096]{1,0:T(8,128)S(1)}, f32[16,4096]{1,0:T(8,128)S(1)}, f32[16,4096]{1,0:T(8,128)S(1)}) custom-call(s32[64]{0:T(128)} %refs_0_.5, s32[64]{0:T(128)} %refs_1_.5, f32[16,32768]{1,0:T(8,128)} %refs_2_.5, bf16[256,128]{1,0:T(8,128)(2,1)} %constant.15.refs_3_, f32[16,128]{1,0:T(8,128)S(1)} %collective-permute-done.refs_4_, ...), custom_call_target="tpu_custom_call" | custom-call | flops 805306368 | bytes 4194304 | tf_op jit(solution)/shard_map/pallas_call | solution.py:293
  20.1 1.4 %collective-permute-start.2 = (f32[16,4096]{1,0:T(8,128)S(1)}, f32[16,4096]{1,0:T(8,128)S(1)}, u32[]{:S(2)}, u32[]{:S(2)}) collective-permute-start(f32[16,4096]{1,0:T(8,128)S(1)} %get-tuple-element.16), channel_id=1, source_target_pairs={{0,1},{1,2},{2,3},{3,0},{4,5},{5,6},{6,7},{7,4},{8,9},{9,10},{10,1... | collective-permute-start | bytes 786440 | tf_op jit(solution)/shard_map/ppermute | solution.py:367
  21.5 0.0 collective-permute-start.3
  21.5 0.0 collective-permute-done.5.refs_1_
  21.5 2.5 %collective-permute-start.4 = (f32[16,4096]{1,0:T(8,128)S(1)}, f32[16,4096]{1,0:T(8,128)S(1)}, u32[]{:S(2)}, u32[]{:S(2)}) collective-permute-start(f32[16,4096]{1,0:T(8,128)S(1)} %get-tuple-element.18), channel_id=1, source_target_pairs={{0,3},{1,0},{2,1},{3,2},{4,7},{5,4},{6,5},{7,6},{8,11},{9,8},{10,9... | collective-permute-start | bytes 786440 | tf_op jit(solution)/shard_map/ppermute | solution.py:367
  24.0 0.1 dynamic_slice.7
  24.1 0.1 dynamic_slice.6
  24.2 4.3 %collective-permute-done.7.refs_3_ = f32[16,4096]{1,0:T(8,128)S(1)} collective-permute-done((f32[16,4096]{1,0:T(8,128)S(1)}, f32[16,4096]{1,0:T(8,128)S(1)}, u32[]{:S(2)}, u32[]{:S(2)}) %collective-permute-start.7) | collective-permute-done | bytes 262176 | tf_op jit(solution)/shard_map/ppermute | solution.py:367
  28.5 0.7 %shard_map.70.refs_4_ = f32[4,8,128]{2,1,0:T(8,128)S(1)} custom-call(f32[16,4096]{1,0:T(8,128)S(1)} %get-tuple-element.19.refs_0_, f32[16,4096]{1,0:T(8,128)S(1)} %collective-permute-done.5.refs_1_, f32[16,4096]{1,0:T(8,128)S(1)} %collective-permute-done.6.refs_2_, f32[16,4096]{1,0:T(8,128)S(1)} %collective-permute-done.7.refs_3_), custom_call_target="tpu_custom_call" | custom-call | flops 134217728 | bytes 1048576 | tf_op jit(solution)/shard_map/pallas_call | solution.py:346
  29.2 5.7 %collective-permute-done.2.refs_1_ = f32[16,4096]{1,0:T(8,128)S(1)} collective-permute-done((f32[16,4096]{1,0:T(8,128)S(1)}, f32[16,4096]{1,0:T(8,128)S(1)}, u32[]{:S(2)}, u32[]{:S(2)}) %collective-permute-start.2) | collective-permute-done | bytes 262176 | tf_op jit(solution)/shard_map/ppermute | solution.py:367
  34.9 0.0 collective-permute-done.3.refs_2_
  34.9 3.5 %collective-permute-done.4.refs_3_ = f32[16,4096]{1,0:T(8,128)S(1)} collective-permute-done((f32[16,4096]{1,0:T(8,128)S(1)}, f32[16,4096]{1,0:T(8,128)S(1)}, u32[]{:S(2)}, u32[]{:S(2)}) %collective-permute-start.4) | collective-permute-done | bytes 262176 | tf_op jit(solution)/shard_map/ppermute | solution.py:367
  38.4 1.6 %shard_map.71 = f32[32,4,8,128]{3,2,1,0:T(8,128)} custom-call(f32[16,4096]{1,0:T(8,128)S(1)} %get-tuple-element.15.refs_0_, f32[16,4096]{1,0:T(8,128)S(1)} %collective-permute-done.2.refs_1_, f32[16,4096]{1,0:T(8,128)S(1)} %collective-permute-done.3.refs_2_, f32[16,4096]{1,0:T(8,128)S(1)} %collective-permute-done.4.refs_3_, f32[4,8,128]{2,1,0:T(8,128)S(1)} %shard_map.70.refs_4_), custom_call_target="tpu_custom_call" | custom-call | flops 134217728 | bytes 1048576 | tf_op jit(solution)/shard_map/pallas_call | solution.py:346
  40.0 9.8 %all-to-all-start = ((f32[128,8,128]{2,1,0:T(8,128)}), f32[128,8,128]{2,1,0:T(8,128)S(1)}, u32[]{:S(2)}, u32[]{:S(2)}) async-start(f32[128,8,128]{2,1,0:T(8,128)} %bitcast), calls=%async_computation | async-start | bytes 1048576 | tf_op jit(solution)/shard_map/all_to_all | solution.py:398
  49.8 0.1 subtract_convert_fusion
  49.8 6.9 %shard_map.67 = (f32[16,32768]{1,0:T(8,128)}, f32[16,32768]{1,0:T(8,128)}) custom-call(s32[64]{0:T(128)} %refs_0_.5, s32[64]{0:T(128)} %refs_1_.5, f32[16,32768]{1,0:T(8,128)} %refs_2_.5, bf16[256,256]{1,0:T(8,128)(2,1)} %constant.14.clone.refs_3_, f32[16,128]{1,0:T(8,128)S(1)} %collective-permute-done.refs_4_, f32[16,128]{1,0:T(8,128)S(1)} %collective-permute-done.1.refs_5_), custom_call_target="tpu_custom_call" | custom-call | flops 1610612736 | bytes 8388608 | tf_op jit(solution)/shard_map/pallas_call | solution.py:293
  56.7 7.1 %all-to-all-done = f32[128,8,128]{2,1,0:T(8,128)S(1)} async-done(((f32[128,8,128]{2,1,0:T(8,128)}), f32[128,8,128]{2,1,0:T(8,128)S(1)}, u32[]{:S(2)}, u32[]{:S(2)}) %all-to-all-start) | async-done | bytes 524320 | tf_op jit(solution)/shard_map/all_to_all | solution.py:398
  63.9 0.1 reduce_sum.9
  64.0 0.1 maximum_divide_fusion
  64.1 0.1 fusion.2
  64.2 0.6 pad_maximum_fusion
  (4 shorter events, 0.0 us)
Async XLA Ops:
  4.2 19.8 %copy-start = (s32[64]{0:T(128)S(1)}, s32[64]{0:T(128)}, u32[]{:S(2)}) copy-start(s32[64]{0:T(128)} %refs_0_.5) | copy-start | bytes 772
  4.2 19.9 %copy-start.1 = (s32[64]{0:T(128)S(1)}, s32[64]{0:T(128)}, u32[]{:S(2)}) copy-start(s32[64]{0:T(128)} %refs_1_.5) | copy-start | bytes 772
  4.2 17.3 %collective-permute-start.5 = (f32[16,4096]{1,0:T(8,128)S(1)}, f32[16,4096]{1,0:T(8,128)S(1)}, u32[]{:S(2)}, u32[]{:S(2)}) collective-permute-start(f32[16,4096]{1,0:T(8,128)S(1)} %get-tuple-element.20), channel_id=1, source_target_pairs={{0,1},{1,2},{2,3},{3,0},{4,5},{5,6},{6,7},{7,4},{8,9},{9,10},{10,1... | collective-permute-start | bytes 786440 | tf_op jit(solution)/shard_map/ppermute | solution.py:367
  7.5 9.1 %collective-permute-start.1 = (f32[16,128]{1,0:T(8,128)S(1)}, f32[16,128]{1,0:T(8,128)S(1)}, u32[]{:S(2)}, u32[]{:S(2)}) collective-permute-start(f32[16,128]{1,0:T(8,128)S(1)} %get-tuple-element.23), channel_id=1, source_target_pairs={{4,0},{8,4},{12,8},{16,12},{20,16},{24,20},{28,24},{32,28},{36,32}... | collective-permute-start | bytes 24584 | tf_op jit(solution)/shard_map/ppermute | solution.py:388
  9.9 6.7 %collective-permute-start = (f32[16,128]{1,0:T(8,128)S(1)}, f32[16,128]{1,0:T(8,128)S(1)}, u32[]{:S(2)}, u32[]{:S(2)}) collective-permute-start(f32[16,128]{1,0:T(8,128)S(1)} %get-tuple-element.24), channel_id=1, source_target_pairs={{0,4},{4,8},{8,12},{12,16},{16,20},{20,24},{24,28},{28,32},{32,36}... | collective-permute-start | bytes 24584 | tf_op jit(solution)/shard_map/ppermute | solution.py:387
  13.1 11.1 %collective-permute-start.6 = (f32[16,4096]{1,0:T(8,128)S(1)}, f32[16,4096]{1,0:T(8,128)S(1)}, u32[]{:S(2)}, u32[]{:S(2)}) collective-permute-start(f32[16,4096]{1,0:T(8,128)S(1)} %get-tuple-element.21), channel_id=1, source_target_pairs={{0,2},{1,3},{2,0},{3,1},{4,6},{5,7},{6,4},{7,5},{8,10},{9,11},{10,... | collective-permute-start | bytes 786440 | tf_op jit(solution)/shard_map/ppermute | solution.py:367
  16.5 12.0 %collective-permute-start.7 = (f32[16,4096]{1,0:T(8,128)S(1)}, f32[16,4096]{1,0:T(8,128)S(1)}, u32[]{:S(2)}, u32[]{:S(2)}) collective-permute-start(f32[16,4096]{1,0:T(8,128)S(1)} %get-tuple-element.22), channel_id=1, source_target_pairs={{0,3},{1,0},{2,1},{3,2},{4,7},{5,4},{6,5},{7,6},{8,11},{9,8},{10,9... | collective-permute-start | bytes 786440 | tf_op jit(solution)/shard_map/ppermute | solution.py:367
  20.1 14.8 %collective-permute-start.2 = (f32[16,4096]{1,0:T(8,128)S(1)}, f32[16,4096]{1,0:T(8,128)S(1)}, u32[]{:S(2)}, u32[]{:S(2)}) collective-permute-start(f32[16,4096]{1,0:T(8,128)S(1)} %get-tuple-element.16), channel_id=1, source_target_pairs={{0,1},{1,2},{2,3},{3,0},{4,5},{5,6},{6,7},{7,4},{8,9},{9,10},{10,1... | collective-permute-start | bytes 786440 | tf_op jit(solution)/shard_map/ppermute | solution.py:367
  21.5 13.3 %collective-permute-start.3 = (f32[16,4096]{1,0:T(8,128)S(1)}, f32[16,4096]{1,0:T(8,128)S(1)}, u32[]{:S(2)}, u32[]{:S(2)}) collective-permute-start(f32[16,4096]{1,0:T(8,128)S(1)} %get-tuple-element.17), channel_id=1, source_target_pairs={{0,2},{1,3},{2,0},{3,1},{4,6},{5,7},{6,4},{7,5},{8,10},{9,11},{10,... | collective-permute-start | bytes 786440 | tf_op jit(solution)/shard_map/ppermute | solution.py:367
  21.5 16.9 %collective-permute-start.4 = (f32[16,4096]{1,0:T(8,128)S(1)}, f32[16,4096]{1,0:T(8,128)S(1)}, u32[]{:S(2)}, u32[]{:S(2)}) collective-permute-start(f32[16,4096]{1,0:T(8,128)S(1)} %get-tuple-element.18), channel_id=1, source_target_pairs={{0,3},{1,0},{2,1},{3,2},{4,7},{5,4},{6,5},{7,6},{8,11},{9,8},{10,9... | collective-permute-start | bytes 786440 | tf_op jit(solution)/shard_map/ppermute | solution.py:367
  40.0 23.9 %all-to-all-start = ((f32[128,8,128]{2,1,0:T(8,128)}), f32[128,8,128]{2,1,0:T(8,128)S(1)}, u32[]{:S(2)}, u32[]{:S(2)}) async-start(f32[128,8,128]{2,1,0:T(8,128)} %bitcast), calls=%async_computation | async-start | bytes 1048576 | tf_op jit(solution)/shard_map/all_to_all | solution.py:398

commit v5 on v4

--- a/solution.py
+++ b/solution.py
@@ -46,7 +46,7 @@
     return pl.ds(pl.multiple_of(start, LANES), size)
 
 
-def fit_kernel(plan, fits, resids, ends, *refs):
+def fit_kernel(plan, fits, resids, ends, edges, *refs):
     base, span, count = plan
     blocks = span // LANES
     refs = list(refs)
@@ -59,6 +59,8 @@
         fit_hbm, refs = refs[:2], refs[2:]
     if resids:
         outs, refs = refs[:GROUPS], refs[GROUPS:]
+    if edges:
+        edge_refs, refs = refs[:2], refs[2:]
     x_ref, taps_ref, first_ref, last_ref, in_sems, side_sems = refs[:6]
     refs = refs[6:]
     if fits:
@@ -101,11 +103,19 @@
             (halo_refs[0], x_ref.at[:, pl.ds(at_left, LANES)]),
             (halo_refs[1], x_ref.at[:, pl.ds(at_right, LANES)]),
         ]
+    needed = len(sides)
+    if edges:
+        sides += [
+            (signal_ref.at[:, pl.ds(0, LANES)], edge_refs[0]),
+            (signal_ref.at[:, pl.ds(width - LANES, LANES)], edge_refs[1]),
+        ]
     sides = [pltpu.make_async_copy(a, b, side_sems.at[n]) for n, (a, b) in enumerate(sides)]
-    for copy in sides:
+    for copy in sides[:needed]:
         copy.start()
     for n in range(count):
         fetch(n).start()
+    for copy in sides[needed:]:
+        copy.start()
 
     def give(n, kind):
         return pltpu.make_async_copy(
@@ -121,7 +131,7 @@
     low = lane < 64
     height = ROWS * blocks
 
-    for copy in sides:
+    for copy in sides[:needed]:
         copy.wait()
     fetch(0).wait()
 
@@ -250,6 +260,8 @@
         return carry
 
     lax.fori_loop(0, count, body, 0)
+    for copy in sides[needed:]:
+        copy.wait()
     if resids:
         for kk in range(GROUPS):
             piece(kk).wait()
@@ -259,7 +271,7 @@
             give(n, 1).wait()
 
 
-def fit_steps(plan, first, last, signal, taps, fits, resids, halos):
+def fit_steps(plan, first, last, signal, taps, fits, resids, halos, edges):
     base, span, count = plan
     rows, width = signal.shape
     ends = halos is not None
@@ -272,6 +284,7 @@
     args += list(halos or ())
     wide = jax.ShapeDtypeStruct((rows, width), jnp.float32)
     part = jax.ShapeDtypeStruct((rows, count // GROUPS * span), jnp.float32)
+    edge = jax.ShapeDtypeStruct((rows, LANES), jnp.float32)
     scratch = [
         pltpu.VMEM((rows, count * span + margins * LANES), jnp.float32),
         pltpu.VMEM(taps.shape, taps.dtype),
@@ -291,10 +304,10 @@
             pltpu.SemaphoreType.DMA((GROUPS,)),
         ]
     return pl.pallas_call(
-        functools.partial(fit_kernel, plan, fits, resids, ends),
+        functools.partial(fit_kernel, plan, fits, resids, ends, edges),
         in_specs=[hbm] * 4 + [loose] * len(halos or ()),
-        out_specs=[hbm] * (2 * fits) + [loose] * (GROUPS * resids),
-        out_shape=[wide] * (2 * fits) + [part] * (GROUPS * resids),
+        out_specs=[hbm] * (2 * fits) + [loose] * (GROUPS * resids + 2 * edges),
+        out_shape=[wide] * (2 * fits) + [part] * (GROUPS * resids) + [edge] * (2 * edges),
         scratch_shapes=scratch,
         compiler_params=pltpu.CompilerParams(vmem_limit_bytes=16 * MIB),
         cost_estimate=pl.CostEstimate(
@@ -376,20 +389,19 @@
     span = width // 8
     early, late, whole = (2 * span, span, 4), (6 * span, span, 4), (0, span, 8)
 
-    def fit(plan, fits, resids, halos=None):
-        return fit_steps(plan, valid_start, valid_end, signal, taps, fits, resids, halos)
+    def fit(plan, fits, resids, halos=None, edges=False):
+        return fit_steps(plan, valid_start, valid_end, signal, taps, fits, resids, halos, edges)
 
     first = lax.dynamic_slice_in_dim(valid_start, mine * rows, rows)[:, None]
     last = lax.dynamic_slice_in_dim(valid_end, mine * rows, rows)[:, None]
     shared = jnp.minimum(last, valid_end[None, :]) - jnp.maximum(first, valid_start[None, :])
     shared = packed(shared.astype(jnp.float32))
 
-    left = lax.ppermute(signal[:, width - LANES :], TIME, [(t, t + 1) for t in range(devices - 1)])
-    right = lax.ppermute(
-        signal[:, :LANES], TIME, [(t + 1, t) for t in range(devices - 1)]
-    )
+    *pieces, front, back = fit(early, False, True, edges=True)
+    parts = exchanged(pieces)
+    left = lax.ppermute(back, TIME, [(t, t + 1) for t in range(devices - 1)])
+    right = lax.ppermute(front, TIME, [(t + 1, t) for t in range(devices - 1)])
     halos = (left, right)
-    parts = exchanged(fit(early, False, True))
     parts_late = exchanged(fit(late, False, True, halos))
     gram = gram_of(parts, None, None)
     smooth, slope = fit(whole, True, False, halos)

time: 65.1 us -> 65.2 us (level)
  starting transfers between devices: 25.3 us -> 29.3 us
  waiting for transfers between devices: 20.7 us -> 17.5 us
  local copies, waits for them, and re-layouts: 0.96 us -> 0.24 us
    ppermute x6, waiting for transfers between devices: 13.5 us -> 10.4 us  [exchanged(): parts.append(lax.ppermute(pieces[k], 'series', pairs))]
    all_to_all x1, starting transfers between devices: 9.79 us -> 12.4 us  [shards(): copies = lax.all_to_all(copies, (*TIME, 'series'), 0, 0, tiled=True)]
    ppermute x6, starting transfers between devices: 9.96 us -> 11.5 us  [exchanged(): parts.append(lax.ppermute(pieces[k], 'series', pairs))]
    slice x1 -> x0, local copies, waits for them, and re-layouts: 0.72 us -> none  [shards(): signal[:, :LANES]]
  transfers between devices with their start and end apart: 9 -> 9, of which waited for: 4 -> 4; matrix products, arithmetic and copies ran while one was open for 1% -> 0% of each run, Pallas kernels for 17% -> 17%
where the time goes in v5:
time: 65.2 us; the launch traced here: 64.9 us
  starting transfers between devices  29.3 us (45%)
  waiting for transfers between devices  17.5 us (27%)
  Pallas kernels  16.2 us (25%)
  other arithmetic  0.9 us (1%)
  between operations  0.71 us (1%)
    pallas_call x3, Pallas kernels, fit_steps(): pl.pallas_call(functools.partial(fit_kernel, plan, fits, resids, ends, ed...  14 us
    all_to_all x1, starting transfers between devices, shards(): copies = lax.all_to_all(copies, (*TIME, 'series'), 0, 0, tiled=True)  12.4 us
    ppermute x6, starting transfers between devices, exchanged(): parts.append(lax.ppermute(pieces[k], 'series', pairs))  11.5 us
    ppermute x6, waiting for transfers between devices, exchanged(): parts.append(lax.ppermute(pieces[k], 'series', pairs))  10.4 us
    all_to_all x1, waiting for transfers between devices, shards(): copies = lax.all_to_all(copies, (*TIME, 'series'), 0, 0, tiled=True)  7.14 us
    ppermute x1, starting transfers between devices, shards(): left = lax.ppermute(back, TIME, [(t, t + 1) for t in range(devices - 1)])  3.43 us
    pallas_call x2, Pallas kernels, gram_of(): pl.pallas_call(functools.partial(gram_kernel, so_far is not None, spread)...  2.28 us
    ppermute x1, starting transfers between devices, shards(): right = lax.ppermute(front, TIME, [(t + 1, t) for t in range(devices - 1)])  1.92 us
  transfers between devices with their start and end apart: 9, of which 4 were waited for; matrix products, arithmetic and copies ran while one was open for 0% of the time, Pallas kernels for 17%

profile of v5, /device:TPU:1, one launch (start us, length us, event | category | flops | bytes accessed | tf_op | source)
XLA Modules:
  0.0 64.9 jit_solution(3915155216145442446)
XLA Ops:
  0.6 3.6 %shard_map.67 = (f32[16,4096]{1,0:T(8,128)S(1)}, f32[16,4096]{1,0:T(8,128)S(1)}, f32[16,4096]{1,0:T(8,128)S(1)}, f32[16,4096]{1,0:T(8,128)S(1)}, f32[16,128]{1,0:T(8,128)S(1)}, /*index=5*/f32[16,128]{1,0:T(8,128)S(1)}) custom-call(s32[64]{0:T(128)} %refs_0_.5, s32[64]{0:T(128)} %refs_1_.5, f32[16,32768]{1,0:T(8,128)} %refs_2_.5, ...), custom_call_target="tpu_custom_call" | custom-call | flops 805306368 | bytes 4194304 | tf_op jit(solution)/shard_map/pallas_call | solution.py:306
  4.2 0.0 copy-start
  4.2 0.0 copy-start.1
  4.2 2.6 %collective-permute-start.5 = (f32[16,4096]{1,0:T(8,128)S(1)}, f32[16,4096]{1,0:T(8,128)S(1)}, u32[]{:S(2)}, u32[]{:S(2)}) collective-permute-start(f32[16,4096]{1,0:T(8,128)S(1)} %get-tuple-element.24), channel_id=1, source_target_pairs={{0,1},{1,2},{2,3},{3,0},{4,5},{5,6},{6,7},{7,4},{8,9},{9,10},{10,1... | collective-permute-start | bytes 786440 | tf_op jit(solution)/shard_map/ppermute | solution.py:380
  6.8 3.4 %collective-permute-start = (f32[16,128]{1,0:T(8,128)S(1)}, f32[16,128]{1,0:T(8,128)S(1)}, u32[]{:S(2)}, u32[]{:S(2)}) collective-permute-start(f32[16,128]{1,0:T(8,128)S(1)} %get-tuple-element.15), channel_id=1, source_target_pairs={{0,4},{4,8},{8,12},{12,16},{16,20},{20,24},{24,28},{28,32},{32,36}... | collective-permute-start | bytes 24584 | tf_op jit(solution)/shard_map/ppermute | solution.py:402
  10.2 1.9 %collective-permute-start.1 = (f32[16,128]{1,0:T(8,128)S(1)}, f32[16,128]{1,0:T(8,128)S(1)}, u32[]{:S(2)}, u32[]{:S(2)}) collective-permute-start(f32[16,128]{1,0:T(8,128)S(1)} %get-tuple-element.16), channel_id=1, source_target_pairs={{4,0},{8,4},{12,8},{16,12},{20,16},{24,20},{28,24},{32,28},{36,32}... | collective-permute-start | bytes 24584 | tf_op jit(solution)/shard_map/ppermute | solution.py:403
  12.2 3.6 %collective-permute-start.6 = (f32[16,4096]{1,0:T(8,128)S(1)}, f32[16,4096]{1,0:T(8,128)S(1)}, u32[]{:S(2)}, u32[]{:S(2)}) collective-permute-start(f32[16,4096]{1,0:T(8,128)S(1)} %get-tuple-element.25), channel_id=1, source_target_pairs={{0,2},{1,3},{2,0},{3,1},{4,6},{5,7},{6,4},{7,5},{8,10},{9,11},{10,... | collective-permute-start | bytes 786440 | tf_op jit(solution)/shard_map/ppermute | solution.py:380
  15.7 0.1 collective-permute-start.7
  15.9 0.0 collective-permute-done.refs_4_
  15.9 0.0 collective-permute-done.1.refs_5_
  15.9 3.5 %shard_map.69 = (f32[16,4096]{1,0:T(8,128)S(1)}, f32[16,4096]{1,0:T(8,128)S(1)}, f32[16,4096]{1,0:T(8,128)S(1)}, f32[16,4096]{1,0:T(8,128)S(1)}) custom-call(s32[64]{0:T(128)} %refs_0_.5, s32[64]{0:T(128)} %refs_1_.5, f32[16,32768]{1,0:T(8,128)} %refs_2_.5, bf16[256,128]{1,0:T(8,128)(2,1)} %constant.15.refs_3_, f32[16,128]{1,0:T(8,128)S(1)} %collective-permute-done.refs_4_, ...), custom_call_target="tpu_custom_call" | custom-call | flops 805306368 | bytes 4194304 | tf_op jit(solution)/shard_map/pallas_call | solution.py:306
  19.4 1.4 %collective-permute-start.2 = (f32[16,4096]{1,0:T(8,128)S(1)}, f32[16,4096]{1,0:T(8,128)S(1)}, u32[]{:S(2)}, u32[]{:S(2)}) collective-permute-start(f32[16,4096]{1,0:T(8,128)S(1)} %get-tuple-element.20), channel_id=1, source_target_pairs={{0,1},{1,2},{2,3},{3,0},{4,5},{5,6},{6,7},{7,4},{8,9},{9,10},{10,1... | collective-permute-start | bytes 786440 | tf_op jit(solution)/shard_map/ppermute | solution.py:380
  20.8 1.9 %collective-permute-start.3 = (f32[16,4096]{1,0:T(8,128)S(1)}, f32[16,4096]{1,0:T(8,128)S(1)}, u32[]{:S(2)}, u32[]{:S(2)}) collective-permute-start(f32[16,4096]{1,0:T(8,128)S(1)} %get-tuple-element.21), channel_id=1, source_target_pairs={{0,2},{1,3},{2,0},{3,1},{4,6},{5,7},{6,4},{7,5},{8,10},{9,11},{10,... | collective-permute-start | bytes 786440 | tf_op jit(solution)/shard_map/ppermute | solution.py:380
  22.7 0.0 collective-permute-done.5.refs_1_
  22.7 2.0 %collective-permute-start.4 = (f32[16,4096]{1,0:T(8,128)S(1)}, f32[16,4096]{1,0:T(8,128)S(1)}, u32[]{:S(2)}, u32[]{:S(2)}) collective-permute-start(f32[16,4096]{1,0:T(8,128)S(1)} %get-tuple-element.22), channel_id=1, source_target_pairs={{0,3},{1,0},{2,1},{3,2},{4,7},{5,4},{6,5},{7,6},{8,11},{9,8},{10,9... | collective-permute-start | bytes 786440 | tf_op jit(solution)/shard_map/ppermute | solution.py:380
  24.7 0.1 dynamic_slice.7
  24.7 0.1 dynamic_slice.6
  24.8 0.0 collective-permute-done.6.refs_2_
  24.8 1.4 %collective-permute-done.7.refs_3_ = f32[16,4096]{1,0:T(8,128)S(1)} collective-permute-done((f32[16,4096]{1,0:T(8,128)S(1)}, f32[16,4096]{1,0:T(8,128)S(1)}, u32[]{:S(2)}, u32[]{:S(2)}) %collective-permute-start.7) | collective-permute-done | bytes 262176 | tf_op jit(solution)/shard_map/ppermute | solution.py:380
  26.3 0.7 %shard_map.70.refs_4_ = f32[4,8,128]{2,1,0:T(8,128)S(1)} custom-call(f32[16,4096]{1,0:T(8,128)S(1)} %get-tuple-element.23.refs_0_, f32[16,4096]{1,0:T(8,128)S(1)} %collective-permute-done.5.refs_1_, f32[16,4096]{1,0:T(8,128)S(1)} %collective-permute-done.6.refs_2_, f32[16,4096]{1,0:T(8,128)S(1)} %collective-permute-done.7.refs_3_), custom_call_target="tpu_custom_call" | custom-call | flops 134217728 | bytes 1048576 | tf_op jit(solution)/shard_map/pallas_call | solution.py:359
  27.0 6.7 %collective-permute-done.2.refs_1_ = f32[16,4096]{1,0:T(8,128)S(1)} collective-permute-done((f32[16,4096]{1,0:T(8,128)S(1)}, f32[16,4096]{1,0:T(8,128)S(1)}, u32[]{:S(2)}, u32[]{:S(2)}) %collective-permute-start.2) | collective-permute-done | bytes 262176 | tf_op jit(solution)/shard_map/ppermute | solution.py:380
  33.7 0.0 collective-permute-done.3.refs_2_
  33.7 2.2 %collective-permute-done.4.refs_3_ = f32[16,4096]{1,0:T(8,128)S(1)} collective-permute-done((f32[16,4096]{1,0:T(8,128)S(1)}, f32[16,4096]{1,0:T(8,128)S(1)}, u32[]{:S(2)}, u32[]{:S(2)}) %collective-permute-start.4) | collective-permute-done | bytes 262176 | tf_op jit(solution)/shard_map/ppermute | solution.py:380
  35.9 1.6 %shard_map.71 = f32[32,4,8,128]{3,2,1,0:T(8,128)} custom-call(f32[16,4096]{1,0:T(8,128)S(1)} %get-tuple-element.19.refs_0_, f32[16,4096]{1,0:T(8,128)S(1)} %collective-permute-done.2.refs_1_, f32[16,4096]{1,0:T(8,128)S(1)} %collective-permute-done.3.refs_2_, f32[16,4096]{1,0:T(8,128)S(1)} %collective-permute-done.4.refs_3_, f32[4,8,128]{2,1,0:T(8,128)S(1)} %shard_map.70.refs_4_), custom_call_target="tpu_custom_call" | custom-call | flops 134217728 | bytes 1048576 | tf_op jit(solution)/shard_map/pallas_call | solution.py:359
  37.5 12.4 %all-to-all-start = ((f32[128,8,128]{2,1,0:T(8,128)}), f32[128,8,128]{2,1,0:T(8,128)S(1)}, u32[]{:S(2)}, u32[]{:S(2)}) async-start(f32[128,8,128]{2,1,0:T(8,128)} %bitcast), calls=%async_computation | async-start | bytes 1048576 | tf_op jit(solution)/shard_map/all_to_all | solution.py:410
  49.9 0.1 subtract_convert_fusion
  50.0 6.9 %shard_map.68 = (f32[16,32768]{1,0:T(8,128)}, f32[16,32768]{1,0:T(8,128)}) custom-call(s32[64]{0:T(128)} %refs_0_.5, s32[64]{0:T(128)} %refs_1_.5, f32[16,32768]{1,0:T(8,128)} %refs_2_.5, bf16[256,256]{1,0:T(8,128)(2,1)} %constant.14.clone.refs_3_, f32[16,128]{1,0:T(8,128)S(1)} %collective-permute-done.refs_4_, f32[16,128]{1,0:T(8,128)S(1)} %collective-permute-done.1.refs_5_), custom_call_target="tpu_custom_call" | custom-call | flops 1610612736 | bytes 8388608 | tf_op jit(solution)/shard_map/pallas_call | solution.py:306
  56.8 7.1 %all-to-all-done = f32[128,8,128]{2,1,0:T(8,128)S(1)} async-done(((f32[128,8,128]{2,1,0:T(8,128)}), f32[128,8,128]{2,1,0:T(8,128)S(1)}, u32[]{:S(2)}, u32[]{:S(2)}) %all-to-all-start) | async-done | bytes 524320 | tf_op jit(solution)/shard_map/all_to_all | solution.py:410
  64.0 0.1 reduce_sum.9
  64.1 0.1 maximum_divide_fusion
  64.2 0.1 fusion.1
  64.3 0.6 pad_maximum_fusion
  (3 shorter events, 0.0 us)
Async XLA Ops:
  4.2 20.5 %copy-start = (s32[64]{0:T(128)S(1)}, s32[64]{0:T(128)}, u32[]{:S(2)}) copy-start(s32[64]{0:T(128)} %refs_0_.5) | copy-start | bytes 772
  4.2 20.5 %copy-start.1 = (s32[64]{0:T(128)S(1)}, s32[64]{0:T(128)}, u32[]{:S(2)}) copy-start(s32[64]{0:T(128)} %refs_1_.5) | copy-start | bytes 772
  4.2 18.5 %collective-permute-start.5 = (f32[16,4096]{1,0:T(8,128)S(1)}, f32[16,4096]{1,0:T(8,128)S(1)}, u32[]{:S(2)}, u32[]{:S(2)}) collective-permute-start(f32[16,4096]{1,0:T(8,128)S(1)} %get-tuple-element.24), channel_id=1, source_target_pairs={{0,1},{1,2},{2,3},{3,0},{4,5},{5,6},{6,7},{7,4},{8,9},{9,10},{10,1... | collective-permute-start | bytes 786440 | tf_op jit(solution)/shard_map/ppermute | solution.py:380
  6.8 9.1 %collective-permute-start = (f32[16,128]{1,0:T(8,128)S(1)}, f32[16,128]{1,0:T(8,128)S(1)}, u32[]{:S(2)}, u32[]{:S(2)}) collective-permute-start(f32[16,128]{1,0:T(8,128)S(1)} %get-tuple-element.15), channel_id=1, source_target_pairs={{0,4},{4,8},{8,12},{12,16},{16,20},{20,24},{24,28},{28,32},{32,36}... | collective-permute-start | bytes 24584 | tf_op jit(solution)/shard_map/ppermute | solution.py:402
  10.2 5.6 %collective-permute-start.1 = (f32[16,128]{1,0:T(8,128)S(1)}, f32[16,128]{1,0:T(8,128)S(1)}, u32[]{:S(2)}, u32[]{:S(2)}) collective-permute-start(f32[16,128]{1,0:T(8,128)S(1)} %get-tuple-element.16), channel_id=1, source_target_pairs={{4,0},{8,4},{12,8},{16,12},{20,16},{24,20},{28,24},{32,28},{36,32}... | collective-permute-start | bytes 24584 | tf_op jit(solution)/shard_map/ppermute | solution.py:403
  12.2 12.7 %collective-permute-start.6 = (f32[16,4096]{1,0:T(8,128)S(1)}, f32[16,4096]{1,0:T(8,128)S(1)}, u32[]{:S(2)}, u32[]{:S(2)}) collective-permute-start(f32[16,4096]{1,0:T(8,128)S(1)} %get-tuple-element.25), channel_id=1, source_target_pairs={{0,2},{1,3},{2,0},{3,1},{4,6},{5,7},{6,4},{7,5},{8,10},{9,11},{10,... | collective-permute-start | bytes 786440 | tf_op jit(solution)/shard_map/ppermute | solution.py:380
  15.7 10.5 %collective-permute-start.7 = (f32[16,4096]{1,0:T(8,128)S(1)}, f32[16,4096]{1,0:T(8,128)S(1)}, u32[]{:S(2)}, u32[]{:S(2)}) collective-permute-start(f32[16,4096]{1,0:T(8,128)S(1)} %get-tuple-element.26), channel_id=1, source_target_pairs={{0,3},{1,0},{2,1},{3,2},{4,7},{5,4},{6,5},{7,6},{8,11},{9,8},{10,9... | collective-permute-start | bytes 786440 | tf_op jit(solution)/shard_map/ppermute | solution.py:380
  19.4 14.3 %collective-permute-start.2 = (f32[16,4096]{1,0:T(8,128)S(1)}, f32[16,4096]{1,0:T(8,128)S(1)}, u32[]{:S(2)}, u32[]{:S(2)}) collective-permute-start(f32[16,4096]{1,0:T(8,128)S(1)} %get-tuple-element.20), channel_id=1, source_target_pairs={{0,1},{1,2},{2,3},{3,0},{4,5},{5,6},{6,7},{7,4},{8,9},{9,10},{10,1... | collective-permute-start | bytes 786440 | tf_op jit(solution)/shard_map/ppermute | solution.py:380
  20.8 12.9 %collective-permute-start.3 = (f32[16,4096]{1,0:T(8,128)S(1)}, f32[16,4096]{1,0:T(8,128)S(1)}, u32[]{:S(2)}, u32[]{:S(2)}) collective-permute-start(f32[16,4096]{1,0:T(8,128)S(1)} %get-tuple-element.21), channel_id=1, source_target_pairs={{0,2},{1,3},{2,0},{3,1},{4,6},{5,7},{6,4},{7,5},{8,10},{9,11},{10,... | collective-permute-start | bytes 786440 | tf_op jit(solution)/shard_map/ppermute | solution.py:380
  22.7 13.2 %collective-permute-start.4 = (f32[16,4096]{1,0:T(8,128)S(1)}, f32[16,4096]{1,0:T(8,128)S(1)}, u32[]{:S(2)}, u32[]{:S(2)}) collective-permute-start(f32[16,4096]{1,0:T(8,128)S(1)} %get-tuple-element.22), channel_id=1, source_target_pairs={{0,3},{1,0},{2,1},{3,2},{4,7},{5,4},{6,5},{7,6},{8,11},{9,8},{10,9... | collective-permute-start | bytes 786440 | tf_op jit(solution)/shard_map/ppermute | solution.py:380
  37.5 26.5 %all-to-all-start = ((f32[128,8,128]{2,1,0:T(8,128)}), f32[128,8,128]{2,1,0:T(8,128)S(1)}, u32[]{:S(2)}, u32[]{:S(2)}) async-start(f32[128,8,128]{2,1,0:T(8,128)} %bitcast), calls=%async_computation | async-start | bytes 1048576 | tf_op jit(solution)/shard_map/all_to_all | solution.py:410

commit v6 on v5

--- a/solution.py
+++ b/solution.py
@@ -74,6 +74,7 @@
     half = count // 2
     mine = lax.axis_index("series")
     begin = lax.axis_index(TIME) * width
+    core = lax.axis_index("core")
 
     def place(n):
         return LANES + n * span + (2 * LANES * (n // half) if ends and not whole else 0)
@@ -99,15 +100,16 @@
         ]
     if ends:
         at_left, at_right = (0, tail) if whole else (middle - LANES, middle - 2 * LANES)
+        across = core * (at_left - at_right)
         sides += [
-            (halo_refs[0], x_ref.at[:, pl.ds(at_left, LANES)]),
-            (halo_refs[1], x_ref.at[:, pl.ds(at_right, LANES)]),
+            (halo_refs[0], x_ref.at[:, aligned(at_right + across, LANES)]),
+            (halo_refs[1], x_ref.at[:, aligned(at_left - across, LANES)]),
         ]
     needed = len(sides)
     if edges:
         sides += [
-            (signal_ref.at[:, pl.ds(0, LANES)], edge_refs[0]),
-            (signal_ref.at[:, pl.ds(width - LANES, LANES)], edge_refs[1]),
+            (signal_ref.at[:, aligned((1 - core) * (width - LANES), LANES)], edge_refs[0]),
+            (signal_ref.at[:, aligned(core * (width - LANES), LANES)], edge_refs[1]),
         ]
     sides = [pltpu.make_async_copy(a, b, side_sems.at[n]) for n, (a, b) in enumerate(sides)]
     for copy in sides[:needed]:
@@ -397,11 +399,12 @@
     shared = jnp.minimum(last, valid_end[None, :]) - jnp.maximum(first, valid_start[None, :])
     shared = packed(shared.astype(jnp.float32))
 
-    *pieces, front, back = fit(early, False, True, edges=True)
+    *pieces, near, far = fit(early, False, True, edges=True)
     parts = exchanged(pieces)
-    left = lax.ppermute(back, TIME, [(t, t + 1) for t in range(devices - 1)])
-    right = lax.ppermute(front, TIME, [(t + 1, t) for t in range(devices - 1)])
-    halos = (left, right)
+    near = lax.ppermute(near, TIME, [(t, t ^ 1) for t in range(devices)])
+    pairs = [(t, t + 1) for t in range(1, devices - 1, 2)]
+    far = lax.ppermute(far, TIME, pairs + [(b, a) for a, b in pairs])
+    halos = (near, far)
     parts_late = exchanged(fit(late, False, True, halos))
     gram = gram_of(parts, None, None)
     smooth, slope = fit(whole, True, False, halos)

time: 65.2 us -> 63 us (0.966)
  starting transfers between devices: 29.3 us -> 25.9 us
  waiting for transfers between devices: 17.5 us -> 18.8 us
    ppermute x2, starting transfers between devices: 5.35 us -> 3.43 us  [the longest x1 2.95 us: shards(): far = lax.ppermute(far, TIME, pairs + [(b, a) for a, b in pairs])]
    ppermute x6, starting transfers between devices: 11.5 us -> 10.2 us  [exchanged(): parts.append(lax.ppermute(pieces[k], 'series', pairs))]
    ppermute x6, waiting for transfers between devices: 10.4 us -> 11.7 us  [exchanged(): parts.append(lax.ppermute(pieces[k], 'series', pairs))]
  transfers between devices with their start and end apart: 9 -> 9, of which waited for: 4 -> 5; matrix products, arithmetic and copies ran while one was open for 0% -> 0% of each run, Pallas kernels for 17% -> 18%
where the time goes in v6:
time: 63 us; the launch traced here: 62.8 us
  starting transfers between devices  25.9 us (41%)
  waiting for transfers between devices  18.8 us (30%)
  Pallas kernels  16.2 us (26%)
  other arithmetic  0.9 us (1%)
  between operations  0.7 us (1%)
    pallas_call x3, Pallas kernels, fit_steps(): pl.pallas_call(functools.partial(fit_kernel, plan, fits, resids, ends, ed...  14 us
    all_to_all x1, starting transfers between devices, shards(): copies = lax.all_to_all(copies, (*TIME, 'series'), 0, 0, tiled=True)  12.3 us
    ppermute x6, waiting for transfers between devices, exchanged(): parts.append(lax.ppermute(pieces[k], 'series', pairs))  11.7 us
    ppermute x6, starting transfers between devices, exchanged(): parts.append(lax.ppermute(pieces[k], 'series', pairs))  10.2 us
    all_to_all x1, waiting for transfers between devices, shards(): copies = lax.all_to_all(copies, (*TIME, 'series'), 0, 0, tiled=True)  7.14 us
    ppermute x1, starting transfers between devices, shards(): far = lax.ppermute(far, TIME, pairs + [(b, a) for a, b in pairs])  2.95 us
    pallas_call x2, Pallas kernels, gram_of(): pl.pallas_call(functools.partial(gram_kernel, so_far is not None, spread)...  2.28 us
  transfers between devices with their start and end apart: 9, of which 5 were waited for; matrix products, arithmetic and copies ran while one was open for 0% of the time, Pallas kernels for 18%

profile of v6, /device:TPU:1, one launch (start us, length us, event | category | flops | bytes accessed | tf_op | source)
XLA Modules:
  0.0 62.8 jit_solution(3851014105666962365)
XLA Ops:
  0.6 3.6 %shard_map.67 = (f32[16,4096]{1,0:T(8,128)S(1)}, f32[16,4096]{1,0:T(8,128)S(1)}, f32[16,4096]{1,0:T(8,128)S(1)}, f32[16,4096]{1,0:T(8,128)S(1)}, f32[16,128]{1,0:T(8,128)S(1)}, /*index=5*/f32[16,128]{1,0:T(8,128)S(1)}) custom-call(s32[64]{0:T(128)} %refs_0_.5, s32[64]{0:T(128)} %refs_1_.5, f32[16,32768]{1,0:T(8,128)} %refs_2_.5, ...), custom_call_target="tpu_custom_call" | custom-call | flops 805306368 | bytes 4194304 | tf_op jit(solution)/shard_map/pallas_call | solution.py:308
  4.2 0.0 copy-start
  4.2 0.0 copy-start.1
  4.2 2.6 %collective-permute-start.5 = (f32[16,4096]{1,0:T(8,128)S(1)}, f32[16,4096]{1,0:T(8,128)S(1)}, u32[]{:S(2)}, u32[]{:S(2)}) collective-permute-start(f32[16,4096]{1,0:T(8,128)S(1)} %get-tuple-element.24), channel_id=1, source_target_pairs={{0,1},{1,2},{2,3},{3,0},{4,5},{5,6},{6,7},{7,4},{8,9},{9,10},{10,1... | collective-permute-start | bytes 786440 | tf_op jit(solution)/shard_map/ppermute | solution.py:382
  6.8 0.5 collective-permute-start
  7.3 2.9 %collective-permute-start.1 = (f32[16,128]{1,0:T(8,128)S(1)}, f32[16,128]{1,0:T(8,128)S(1)}, u32[]{:S(2)}, u32[]{:S(2)}) collective-permute-start(f32[16,128]{1,0:T(8,128)S(1)} %get-tuple-element.16), channel_id=1, source_target_pairs={{4,8},{12,16},{20,24},{28,32},{36,40},{44,48},{52,56},{60,64},{68,... | collective-permute-start | bytes 24584 | tf_op jit(solution)/shard_map/ppermute | solution.py:406
  10.2 3.6 %collective-permute-start.6 = (f32[16,4096]{1,0:T(8,128)S(1)}, f32[16,4096]{1,0:T(8,128)S(1)}, u32[]{:S(2)}, u32[]{:S(2)}) collective-permute-start(f32[16,4096]{1,0:T(8,128)S(1)} %get-tuple-element.25), channel_id=1, source_target_pairs={{0,2},{1,3},{2,0},{3,1},{4,6},{5,7},{6,4},{7,5},{8,10},{9,11},{10,... | collective-permute-start | bytes 786440 | tf_op jit(solution)/shard_map/ppermute | solution.py:382
  13.8 0.1 collective-permute-start.7
  13.9 0.0 collective-permute-done.refs_4_
  13.9 0.0 collective-permute-done.1.refs_5_
  13.9 3.5 %shard_map.69 = (f32[16,4096]{1,0:T(8,128)S(1)}, f32[16,4096]{1,0:T(8,128)S(1)}, f32[16,4096]{1,0:T(8,128)S(1)}, f32[16,4096]{1,0:T(8,128)S(1)}) custom-call(s32[64]{0:T(128)} %refs_0_.5, s32[64]{0:T(128)} %refs_1_.5, f32[16,32768]{1,0:T(8,128)} %refs_2_.5, bf16[256,128]{1,0:T(8,128)(2,1)} %constant.15.refs_3_, f32[16,128]{1,0:T(8,128)S(1)} %collective-permute-done.refs_4_, ...), custom_call_target="tpu_custom_call" | custom-call | flops 805306368 | bytes 4194304 | tf_op jit(solution)/shard_map/pallas_call | solution.py:308
  17.5 1.4 %collective-permute-start.2 = (f32[16,4096]{1,0:T(8,128)S(1)}, f32[16,4096]{1,0:T(8,128)S(1)}, u32[]{:S(2)}, u32[]{:S(2)}) collective-permute-start(f32[16,4096]{1,0:T(8,128)S(1)} %get-tuple-element.20), channel_id=1, source_target_pairs={{0,1},{1,2},{2,3},{3,0},{4,5},{5,6},{6,7},{7,4},{8,9},{9,10},{10,1... | collective-permute-start | bytes 786440 | tf_op jit(solution)/shard_map/ppermute | solution.py:382
  18.9 0.2 collective-permute-start.3
  19.0 0.0 collective-permute-done.5.refs_1_
  19.0 2.3 %collective-permute-start.4 = (f32[16,4096]{1,0:T(8,128)S(1)}, f32[16,4096]{1,0:T(8,128)S(1)}, u32[]{:S(2)}, u32[]{:S(2)}) collective-permute-start(f32[16,4096]{1,0:T(8,128)S(1)} %get-tuple-element.22), channel_id=1, source_target_pairs={{0,3},{1,0},{2,1},{3,2},{4,7},{5,4},{6,5},{7,6},{8,11},{9,8},{10,9... | collective-permute-start | bytes 786440 | tf_op jit(solution)/shard_map/ppermute | solution.py:382
  21.4 0.1 dynamic_slice.7
  21.4 0.1 dynamic_slice.6
  21.5 0.0 collective-permute-done.6.refs_2_
  21.5 4.5 %collective-permute-done.7.refs_3_ = f32[16,4096]{1,0:T(8,128)S(1)} collective-permute-done((f32[16,4096]{1,0:T(8,128)S(1)}, f32[16,4096]{1,0:T(8,128)S(1)}, u32[]{:S(2)}, u32[]{:S(2)}) %collective-permute-start.7) | collective-permute-done | bytes 262176 | tf_op jit(solution)/shard_map/ppermute | solution.py:382
  26.1 0.7 %shard_map.70.refs_4_ = f32[4,8,128]{2,1,0:T(8,128)S(1)} custom-call(f32[16,4096]{1,0:T(8,128)S(1)} %get-tuple-element.23.refs_0_, f32[16,4096]{1,0:T(8,128)S(1)} %collective-permute-done.5.refs_1_, f32[16,4096]{1,0:T(8,128)S(1)} %collective-permute-done.6.refs_2_, f32[16,4096]{1,0:T(8,128)S(1)} %collective-permute-done.7.refs_3_), custom_call_target="tpu_custom_call" | custom-call | flops 134217728 | bytes 1048576 | tf_op jit(solution)/shard_map/pallas_call | solution.py:361
  26.8 0.4 collective-permute-done.2.refs_1_
  27.1 4.8 %collective-permute-done.3.refs_2_ = f32[16,4096]{1,0:T(8,128)S(1)} collective-permute-done((f32[16,4096]{1,0:T(8,128)S(1)}, f32[16,4096]{1,0:T(8,128)S(1)}, u32[]{:S(2)}, u32[]{:S(2)}) %collective-permute-start.3) | collective-permute-done | bytes 262176 | tf_op jit(solution)/shard_map/ppermute | solution.py:382
  31.9 2.0 %collective-permute-done.4.refs_3_ = f32[16,4096]{1,0:T(8,128)S(1)} collective-permute-done((f32[16,4096]{1,0:T(8,128)S(1)}, f32[16,4096]{1,0:T(8,128)S(1)}, u32[]{:S(2)}, u32[]{:S(2)}) %collective-permute-start.4) | collective-permute-done | bytes 262176 | tf_op jit(solution)/shard_map/ppermute | solution.py:382
  33.9 1.6 %shard_map.71 = f32[32,4,8,128]{3,2,1,0:T(8,128)} custom-call(f32[16,4096]{1,0:T(8,128)S(1)} %get-tuple-element.19.refs_0_, f32[16,4096]{1,0:T(8,128)S(1)} %collective-permute-done.2.refs_1_, f32[16,4096]{1,0:T(8,128)S(1)} %collective-permute-done.3.refs_2_, f32[16,4096]{1,0:T(8,128)S(1)} %collective-permute-done.4.refs_3_, f32[4,8,128]{2,1,0:T(8,128)S(1)} %shard_map.70.refs_4_), custom_call_target="tpu_custom_call" | custom-call | flops 134217728 | bytes 1048576 | tf_op jit(solution)/shard_map/pallas_call | solution.py:361
  35.5 12.3 %all-to-all-start = ((f32[128,8,128]{2,1,0:T(8,128)}), f32[128,8,128]{2,1,0:T(8,128)S(1)}, u32[]{:S(2)}, u32[]{:S(2)}) async-start(f32[128,8,128]{2,1,0:T(8,128)} %bitcast), calls=%async_computation | async-start | bytes 1048576 | tf_op jit(solution)/shard_map/all_to_all | solution.py:413
  47.8 0.1 subtract_convert_fusion
  47.9 6.9 %shard_map.68 = (f32[16,32768]{1,0:T(8,128)}, f32[16,32768]{1,0:T(8,128)}) custom-call(s32[64]{0:T(128)} %refs_0_.5, s32[64]{0:T(128)} %refs_1_.5, f32[16,32768]{1,0:T(8,128)} %refs_2_.5, bf16[256,256]{1,0:T(8,128)(2,1)} %constant.14.clone.refs_3_, f32[16,128]{1,0:T(8,128)S(1)} %collective-permute-done.refs_4_, f32[16,128]{1,0:T(8,128)S(1)} %collective-permute-done.1.refs_5_), custom_call_target="tpu_custom_call" | custom-call | flops 1610612736 | bytes 8388608 | tf_op jit(solution)/shard_map/pallas_call | solution.py:308
  54.8 7.1 %all-to-all-done = f32[128,8,128]{2,1,0:T(8,128)S(1)} async-done(((f32[128,8,128]{2,1,0:T(8,128)}), f32[128,8,128]{2,1,0:T(8,128)S(1)}, u32[]{:S(2)}, u32[]{:S(2)}) %all-to-all-start) | async-done | bytes 524320 | tf_op jit(solution)/shard_map/all_to_all | solution.py:413
  61.9 0.1 reduce_sum.9
  62.0 0.1 maximum_divide_fusion
  62.1 0.1 fusion.1
  62.2 0.6 pad_maximum_fusion
  (3 shorter events, 0.0 us)
Async XLA Ops:
  4.2 17.2 %copy-start = (s32[64]{0:T(128)S(1)}, s32[64]{0:T(128)}, u32[]{:S(2)}) copy-start(s32[64]{0:T(128)} %refs_0_.5) | copy-start | bytes 772
  4.2 17.2 %copy-start.1 = (s32[64]{0:T(128)S(1)}, s32[64]{0:T(128)}, u32[]{:S(2)}) copy-start(s32[64]{0:T(128)} %refs_1_.5) | copy-start | bytes 772
  4.2 14.8 %collective-permute-start.5 = (f32[16,4096]{1,0:T(8,128)S(1)}, f32[16,4096]{1,0:T(8,128)S(1)}, u32[]{:S(2)}, u32[]{:S(2)}) collective-permute-start(f32[16,4096]{1,0:T(8,128)S(1)} %get-tuple-element.24), channel_id=1, source_target_pairs={{0,1},{1,2},{2,3},{3,0},{4,5},{5,6},{6,7},{7,4},{8,9},{9,10},{10,1... | collective-permute-start | bytes 786440 | tf_op jit(solution)/shard_map/ppermute | solution.py:382
  6.8 7.2 %collective-permute-start = (f32[16,128]{1,0:T(8,128)S(1)}, f32[16,128]{1,0:T(8,128)S(1)}, u32[]{:S(2)}, u32[]{:S(2)}) collective-permute-start(f32[16,128]{1,0:T(8,128)S(1)} %get-tuple-element.15), channel_id=1, source_target_pairs={{0,4},{4,0},{8,12},{12,8},{16,20},{20,16},{24,28},{28,24},{32,36},... | collective-permute-start | bytes 24584 | tf_op jit(solution)/shard_map/ppermute | solution.py:404
  7.3 6.7 %collective-permute-start.1 = (f32[16,128]{1,0:T(8,128)S(1)}, f32[16,128]{1,0:T(8,128)S(1)}, u32[]{:S(2)}, u32[]{:S(2)}) collective-permute-start(f32[16,128]{1,0:T(8,128)S(1)} %get-tuple-element.16), channel_id=1, source_target_pairs={{4,8},{12,16},{20,24},{28,32},{36,40},{44,48},{52,56},{60,64},{68,... | collective-permute-start | bytes 24584 | tf_op jit(solution)/shard_map/ppermute | solution.py:406
  10.2 11.3 %collective-permute-start.6 = (f32[16,4096]{1,0:T(8,128)S(1)}, f32[16,4096]{1,0:T(8,128)S(1)}, u32[]{:S(2)}, u32[]{:S(2)}) collective-permute-start(f32[16,4096]{1,0:T(8,128)S(1)} %get-tuple-element.25), channel_id=1, source_target_pairs={{0,2},{1,3},{2,0},{3,1},{4,6},{5,7},{6,4},{7,5},{8,10},{9,11},{10,... | collective-permute-start | bytes 786440 | tf_op jit(solution)/shard_map/ppermute | solution.py:382
  13.8 12.2 %collective-permute-start.7 = (f32[16,4096]{1,0:T(8,128)S(1)}, f32[16,4096]{1,0:T(8,128)S(1)}, u32[]{:S(2)}, u32[]{:S(2)}) collective-permute-start(f32[16,4096]{1,0:T(8,128)S(1)} %get-tuple-element.26), channel_id=1, source_target_pairs={{0,3},{1,0},{2,1},{3,2},{4,7},{5,4},{6,5},{7,6},{8,11},{9,8},{10,9... | collective-permute-start | bytes 786440 | tf_op jit(solution)/shard_map/ppermute | solution.py:382
  17.5 9.7 %collective-permute-start.2 = (f32[16,4096]{1,0:T(8,128)S(1)}, f32[16,4096]{1,0:T(8,128)S(1)}, u32[]{:S(2)}, u32[]{:S(2)}) collective-permute-start(f32[16,4096]{1,0:T(8,128)S(1)} %get-tuple-element.20), channel_id=1, source_target_pairs={{0,1},{1,2},{2,3},{3,0},{4,5},{5,6},{6,7},{7,4},{8,9},{9,10},{10,1... | collective-permute-start | bytes 786440 | tf_op jit(solution)/shard_map/ppermute | solution.py:382
  18.9 13.0 %collective-permute-start.3 = (f32[16,4096]{1,0:T(8,128)S(1)}, f32[16,4096]{1,0:T(8,128)S(1)}, u32[]{:S(2)}, u32[]{:S(2)}) collective-permute-start(f32[16,4096]{1,0:T(8,128)S(1)} %get-tuple-element.21), channel_id=1, source_target_pairs={{0,2},{1,3},{2,0},{3,1},{4,6},{5,7},{6,4},{7,5},{8,10},{9,11},{10,... | collective-permute-start | bytes 786440 | tf_op jit(solution)/shard_map/ppermute | solution.py:382
  19.0 14.9 %collective-permute-start.4 = (f32[16,4096]{1,0:T(8,128)S(1)}, f32[16,4096]{1,0:T(8,128)S(1)}, u32[]{:S(2)}, u32[]{:S(2)}) collective-permute-start(f32[16,4096]{1,0:T(8,128)S(1)} %get-tuple-element.22), channel_id=1, source_target_pairs={{0,3},{1,0},{2,1},{3,2},{4,7},{5,4},{6,5},{7,6},{8,11},{9,8},{10,9... | collective-permute-start | bytes 786440 | tf_op jit(solution)/shard_map/ppermute | solution.py:382
  35.5 26.4 %all-to-all-start = ((f32[128,8,128]{2,1,0:T(8,128)}), f32[128,8,128]{2,1,0:T(8,128)S(1)}, u32[]{:S(2)}, u32[]{:S(2)}) async-start(f32[128,8,128]{2,1,0:T(8,128)} %bitcast), calls=%async_computation | async-start | bytes 1048576 | tf_op jit(solution)/shard_map/all_to_all | solution.py:413

commit v7 on v6

--- a/solution.py
+++ b/solution.py
@@ -388,8 +388,9 @@
     devices = lax.axis_size(TIME)
     taps = jnp.asarray(taps, jnp.bfloat16)
     mine = lax.axis_index("series")
-    span = width // 8
-    early, late, whole = (2 * span, span, 4), (6 * span, span, 4), (0, span, 8)
+    unit = width // 32
+    early, mid = (2 * unit, 3 * unit, GROUPS), (14 * unit, 4 * unit, GROUPS)
+    late, whole = (30 * unit, unit, GROUPS), (0, 4 * unit, 8)
 
     def fit(plan, fits, resids, halos=None, edges=False):
         return fit_steps(plan, valid_start, valid_end, signal, taps, fits, resids, halos, edges)
@@ -401,16 +402,18 @@
 
     *pieces, near, far = fit(early, False, True, edges=True)
     parts = exchanged(pieces)
+    parts_mid = exchanged(fit(mid, False, True))
     near = lax.ppermute(near, TIME, [(t, t ^ 1) for t in range(devices)])
     pairs = [(t, t + 1) for t in range(1, devices - 1, 2)]
     far = lax.ppermute(far, TIME, pairs + [(b, a) for a, b in pairs])
     halos = (near, far)
-    parts_late = exchanged(fit(late, False, True, halos))
     gram = gram_of(parts, None, None)
-    smooth, slope = fit(whole, True, False, halos)
-    copies = gram_of(parts_late, gram, devices)
+    parts = exchanged(fit(late, False, True, halos))
+    gram = gram_of(parts_mid, gram, None)
+    copies = gram_of(parts, gram, devices)
     copies = copies.reshape(devices * GROUPS, 8, LANES)
     copies = lax.all_to_all(copies, (*TIME, "series"), 0, 0, tiled=True)
+    smooth, slope = fit(whole, True, False, halos)
     cov = jnp.sum(copies, axis=0) / shared
     return smooth, slope, jnp.concatenate([cov[:, :64], cov[:, 64:]], axis=0)
 

time: 63 us -> 69.9 us (1.11)
  starting transfers between devices: 25.9 us -> 33.2 us
  waiting for transfers between devices: 18.8 us -> 14.5 us
  Pallas kernels: 16.2 us -> 20 us
    ppermute x6 -> x9, waiting for transfers between devices: 11.7 us -> 5.74 us  [exchanged(): parts.append(lax.ppermute(pieces[k], 'series', pairs))]
    ppermute x6 -> x9, starting transfers between devices: 10.2 us -> 15.9 us  [exchanged(): parts.append(lax.ppermute(pieces[k], 'series', pairs))]
    pallas_call x3 -> x4, Pallas kernels: 14 us -> 17.5 us  [fit_steps(): pl.pallas_call(functools.partial(fit_kernel, plan, fits, resids, ends, ed...]
    ppermute x1, starting transfers between devices: 2.95 us -> 5.31 us  [shards(): far = lax.ppermute(far, TIME, pairs + [(b, a) for a, b in pairs])]
    ppermute x1, waiting for transfers between devices: 0.01 us -> 1.61 us  [shards(): far = lax.ppermute(far, TIME, pairs + [(b, a) for a, b in pairs])]
    all_to_all x1, starting transfers between devices: 12.3 us -> 11.2 us  [shards(): copies = lax.all_to_all(copies, (*TIME, 'series'), 0, 0, tiled=True)]
    pallas_call x2 -> x3, Pallas kernels: 2.28 us -> 2.5 us  [gram_of(): pl.pallas_call(functools.partial(gram_kernel, so_far is not None, spread)...]
  transfers between devices with their start and end apart: 9 -> 12, of which waited for: 5 -> 5; matrix products, arithmetic and copies ran while one was open for 0% -> 0% of each run, Pallas kernels for 18% -> 20%
where the time goes in v7:
time: 69.9 us; the launch traced here: 69.6 us
  starting transfers between devices  33.2 us (47%)
  Pallas kernels  20 us (29%)
  waiting for transfers between devices  14.5 us (21%)
  other arithmetic  0.9 us (1%)
  between operations  0.75 us (1%)
    pallas_call x4, Pallas kernels, fit_steps(): pl.pallas_call(functools.partial(fit_kernel, plan, fits, resids, ends, ed...  17.5 us
    ppermute x9, starting transfers between devices, exchanged(): parts.append(lax.ppermute(pieces[k], 'series', pairs))  15.9 us
    all_to_all x1, starting transfers between devices, shards(): copies = lax.all_to_all(copies, (*TIME, 'series'), 0, 0, tiled=True)  11.2 us
    all_to_all x1, waiting for transfers between devices, shards(): copies = lax.all_to_all(copies, (*TIME, 'series'), 0, 0, tiled=True)  7.15 us
    ppermute x9, waiting for transfers between devices, exchanged(): parts.append(lax.ppermute(pieces[k], 'series', pairs))  5.74 us
    ppermute x1, starting transfers between devices, shards(): far = lax.ppermute(far, TIME, pairs + [(b, a) for a, b in pairs])  5.31 us
    pallas_call x3, Pallas kernels, gram_of(): pl.pallas_call(functools.partial(gram_kernel, so_far is not None, spread)...  2.5 us
    ppermute x1, waiting for transfers between devices, shards(): far = lax.ppermute(far, TIME, pairs + [(b, a) for a, b in pairs])  1.61 us
  transfers between devices with their start and end apart: 12, of which 5 were waited for; matrix products, arithmetic and copies ran while one was open for 0% of the time, Pallas kernels for 20%

profile of v7, /device:TPU:1, one launch (start us, length us, event | category | flops | bytes accessed | tf_op | source)
XLA Modules:
  0.0 69.6 jit_solution(23030838019041365)
XLA Ops:
  0.6 5.0 %shard_map.67 = (f32[16,3072]{1,0:T(8,128)S(1)}, f32[16,3072]{1,0:T(8,128)S(1)}, f32[16,3072]{1,0:T(8,128)S(1)}, f32[16,3072]{1,0:T(8,128)S(1)}, f32[16,128]{1,0:T(8,128)S(1)}, /*index=5*/f32[16,128]{1,0:T(8,128)S(1)}) custom-call(s32[64]{0:T(128)} %refs_0_.7, s32[64]{0:T(128)} %refs_1_.7, f32[16,32768]{1,0:T(8,128)} %refs_2_.7, ...), custom_call_target="tpu_custom_call" | custom-call | flops 603979776 | bytes 3145728 | tf_op jit(solution)/shard_map/pallas_call | solution.py:308
  5.6 0.0 copy-start.1
  5.6 2.1 %collective-permute-start.8 = (f32[16,3072]{1,0:T(8,128)S(1)}, f32[16,3072]{1,0:T(8,128)S(1)}, u32[]{:S(2)}, u32[]{:S(2)}) collective-permute-start(f32[16,3072]{1,0:T(8,128)S(1)} %get-tuple-element.32), channel_id=1, source_target_pairs={{0,1},{1,2},{2,3},{3,0},{4,5},{5,6},{6,7},{7,4},{8,9},{9,10},{10,1... | collective-permute-start | bytes 589832 | tf_op jit(solution)/shard_map/ppermute | solution.py:382
  7.7 3.1 %shard_map.70 = (f32[16,4096]{1,0:T(8,128)S(1)}, f32[16,4096]{1,0:T(8,128)S(1)}, f32[16,4096]{1,0:T(8,128)S(1)}, f32[16,4096]{1,0:T(8,128)S(1)}) custom-call(s32[64]{0:T(128)} %refs_0_.7, s32[64]{0:T(128)} %refs_1_.7, f32[16,32768]{1,0:T(8,128)} %refs_2_.7, bf16[256,128]{1,0:T(8,128)(2,1)} %constant.15.refs_3_), custom_call_target="tpu_custom_call" | custom-call | flops 805306368 | bytes 4194304 | tf_op jit(solution)/shard_map/pallas_call | solution.py:308
  10.8 1.3 %collective-permute-start.5 = (f32[16,4096]{1,0:T(8,128)S(1)}, f32[16,4096]{1,0:T(8,128)S(1)}, u32[]{:S(2)}, u32[]{:S(2)}) collective-permute-start(f32[16,4096]{1,0:T(8,128)S(1)} %get-tuple-element.28), channel_id=1, source_target_pairs={{0,1},{1,2},{2,3},{3,0},{4,5},{5,6},{6,7},{7,4},{8,9},{9,10},{10,1... | collective-permute-start | bytes 786440 | tf_op jit(solution)/shard_map/ppermute | solution.py:382
  12.1 0.8 %collective-permute-start = (f32[16,128]{1,0:T(8,128)S(1)}, f32[16,128]{1,0:T(8,128)S(1)}, u32[]{:S(2)}, u32[]{:S(2)}) collective-permute-start(f32[16,128]{1,0:T(8,128)S(1)} %get-tuple-element.19), channel_id=1, source_target_pairs={{0,4},{4,0},{8,12},{12,8},{16,20},{20,16},{24,28},{28,24},{32,36},... | collective-permute-start | bytes 24584 | tf_op jit(solution)/shard_map/ppermute | solution.py:406
  12.9 1.3 %collective-permute-start.6 = (f32[16,4096]{1,0:T(8,128)S(1)}, f32[16,4096]{1,0:T(8,128)S(1)}, u32[]{:S(2)}, u32[]{:S(2)}) collective-permute-start(f32[16,4096]{1,0:T(8,128)S(1)} %get-tuple-element.29), channel_id=1, source_target_pairs={{0,2},{1,3},{2,0},{3,1},{4,6},{5,7},{6,4},{7,5},{8,10},{9,11},{10,... | collective-permute-start | bytes 786440 | tf_op jit(solution)/shard_map/ppermute | solution.py:382
  14.2 2.1 %collective-permute-start.7 = (f32[16,4096]{1,0:T(8,128)S(1)}, f32[16,4096]{1,0:T(8,128)S(1)}, u32[]{:S(2)}, u32[]{:S(2)}) collective-permute-start(f32[16,4096]{1,0:T(8,128)S(1)} %get-tuple-element.30), channel_id=1, source_target_pairs={{0,3},{1,0},{2,1},{3,2},{4,7},{5,4},{6,5},{7,6},{8,11},{9,8},{10,9... | collective-permute-start | bytes 786440 | tf_op jit(solution)/shard_map/ppermute | solution.py:382
  16.3 5.3 %collective-permute-start.1 = (f32[16,128]{1,0:T(8,128)S(1)}, f32[16,128]{1,0:T(8,128)S(1)}, u32[]{:S(2)}, u32[]{:S(2)}) collective-permute-start(f32[16,128]{1,0:T(8,128)S(1)} %get-tuple-element.20), channel_id=1, source_target_pairs={{4,8},{12,16},{20,24},{28,32},{36,40},{44,48},{52,56},{60,64},{68,... | collective-permute-start | bytes 24584 | tf_op jit(solution)/shard_map/ppermute | solution.py:408
  21.6 1.6 %collective-permute-done.1.refs_5_ = f32[16,128]{1,0:T(8,128)S(1)} collective-permute-done((f32[16,128]{1,0:T(8,128)S(1)}, f32[16,128]{1,0:T(8,128)S(1)}, u32[]{:S(2)}, u32[]{:S(2)}) %collective-permute-start.1) | collective-permute-done | bytes 8224 | tf_op jit(solution)/shard_map/ppermute | solution.py:408
  23.2 0.0 collective-permute-start.9
  23.2 2.1 %collective-permute-start.10 = (f32[16,3072]{1,0:T(8,128)S(1)}, f32[16,3072]{1,0:T(8,128)S(1)}, u32[]{:S(2)}, u32[]{:S(2)}) collective-permute-start(f32[16,3072]{1,0:T(8,128)S(1)} %get-tuple-element.34), channel_id=1, source_target_pairs={{0,3},{1,0},{2,1},{3,2},{4,7},{5,4},{6,5},{7,6},{8,11},{9,8},{10,9... | collective-permute-start | bytes 589832 | tf_op jit(solution)/shard_map/ppermute | solution.py:382
  25.3 2.6 %shard_map.69 = (f32[16,1024]{1,0:T(8,128)S(1)}, f32[16,1024]{1,0:T(8,128)S(1)}, f32[16,1024]{1,0:T(8,128)S(1)}, f32[16,1024]{1,0:T(8,128)S(1)}) custom-call(s32[64]{0:T(128)} %refs_0_.7, s32[64]{0:T(128)} %refs_1_.7, f32[16,32768]{1,0:T(8,128)} %refs_2_.7, bf16[256,128]{1,0:T(8,128)(2,1)} %constant.15.refs_3_, f32[16,128]{1,0:T(8,128)S(1)} %collective-permute-done.refs_4_, ...), custom_call_target="tpu_custom_call" | custom-call | flops 201326592 | bytes 1048576 | tf_op jit(solution)/shard_map/pallas_call | solution.py:308
  27.9 2.4 %collective-permute-done.9.refs_2_ = f32[16,3072]{1,0:T(8,128)S(1)} collective-permute-done((f32[16,3072]{1,0:T(8,128)S(1)}, f32[16,3072]{1,0:T(8,128)S(1)}, u32[]{:S(2)}, u32[]{:S(2)}) %collective-permute-start.9) | collective-permute-done | bytes 196640 | tf_op jit(solution)/shard_map/ppermute | solution.py:382
  30.3 2.8 %collective-permute-start.2 = (f32[16,1024]{1,0:T(8,128)S(1)}, f32[16,1024]{1,0:T(8,128)S(1)}, u32[]{:S(2)}, u32[]{:S(2)}) collective-permute-start(f32[16,1024]{1,0:T(8,128)S(1)} %get-tuple-element.24), channel_id=1, source_target_pairs={{0,1},{1,2},{2,3},{3,0},{4,5},{5,6},{6,7},{7,4},{8,9},{9,10},{10,1... | collective-permute-start | bytes 196616 | tf_op jit(solution)/shard_map/ppermute | solution.py:382
  33.2 2.7 %collective-permute-done.10.refs_3_ = f32[16,3072]{1,0:T(8,128)S(1)} collective-permute-done((f32[16,3072]{1,0:T(8,128)S(1)}, f32[16,3072]{1,0:T(8,128)S(1)}, u32[]{:S(2)}, u32[]{:S(2)}) %collective-permute-start.10) | collective-permute-done | bytes 196640 | tf_op jit(solution)/shard_map/ppermute | solution.py:382
  35.9 2.1 %collective-permute-start.3 = (f32[16,1024]{1,0:T(8,128)S(1)}, f32[16,1024]{1,0:T(8,128)S(1)}, u32[]{:S(2)}, u32[]{:S(2)}) collective-permute-start(f32[16,1024]{1,0:T(8,128)S(1)} %get-tuple-element.25), channel_id=1, source_target_pairs={{0,2},{1,3},{2,0},{3,1},{4,6},{5,7},{6,4},{7,5},{8,10},{9,11},{10,... | collective-permute-start | bytes 196616 | tf_op jit(solution)/shard_map/ppermute | solution.py:382
  38.0 2.1 %collective-permute-start.4 = (f32[16,1024]{1,0:T(8,128)S(1)}, f32[16,1024]{1,0:T(8,128)S(1)}, u32[]{:S(2)}, u32[]{:S(2)}) collective-permute-start(f32[16,1024]{1,0:T(8,128)S(1)} %get-tuple-element.26), channel_id=1, source_target_pairs={{0,3},{1,0},{2,1},{3,2},{4,7},{5,4},{6,5},{7,6},{8,11},{9,8},{10,9... | collective-permute-start | bytes 196616 | tf_op jit(solution)/shard_map/ppermute | solution.py:382
  40.0 0.1 dynamic_slice.7
  40.1 0.1 dynamic_slice.6
  40.2 0.6 shard_map.71.refs_4_
  40.8 0.7 %shard_map.72.refs_4_ = f32[4,8,128]{2,1,0:T(8,128)S(1)} custom-call(f32[16,4096]{1,0:T(8,128)S(1)} %get-tuple-element.27.refs_0_, f32[16,4096]{1,0:T(8,128)S(1)} %collective-permute-done.5.refs_1_, f32[16,4096]{1,0:T(8,128)S(1)} %collective-permute-done.6.refs_2_, f32[16,4096]{1,0:T(8,128)S(1)} %collective-permute-done.7.refs_3_, ...), custom_call_target="tpu_custom_call" | custom-call | flops 134217728 | bytes 1048576 | tf_op jit(solution)/shard_map/pallas_call | solution.py:361
  41.5 0.6 collective-permute-done.4.refs_3_
  42.1 1.2 %shard_map.73 = f32[32,4,8,128]{3,2,1,0:T(8,128)} custom-call(f32[16,1024]{1,0:T(8,128)S(1)} %get-tuple-element.23.refs_0_, f32[16,1024]{1,0:T(8,128)S(1)} %collective-permute-done.2.refs_1_, f32[16,1024]{1,0:T(8,128)S(1)} %collective-permute-done.3.refs_2_, f32[16,1024]{1,0:T(8,128)S(1)} %collective-permute-done.4.refs_3_, f32[4,8,128]{2,1,0:T(8,128)S(1)} %shard_map.72.refs_4_), custom_call_target="tpu_custom_call" | custom-call | flops 33554432 | bytes 262144 | tf_op jit(solution)/shard_map/pallas_call | solution.py:361
  43.3 11.2 %all-to-all-start = ((f32[128,8,128]{2,1,0:T(8,128)}), f32[128,8,128]{2,1,0:T(8,128)S(1)}, u32[]{:S(2)}, u32[]{:S(2)}) async-start(f32[128,8,128]{2,1,0:T(8,128)} %bitcast), calls=%async_computation | async-start | bytes 1048576 | tf_op jit(solution)/shard_map/all_to_all | solution.py:415
  54.6 0.1 subtract_convert_fusion
  54.6 6.9 %shard_map.68 = (f32[16,32768]{1,0:T(8,128)}, f32[16,32768]{1,0:T(8,128)}) custom-call(s32[64]{0:T(128)} %refs_0_.7, s32[64]{0:T(128)} %refs_1_.7, f32[16,32768]{1,0:T(8,128)} %refs_2_.7, bf16[256,256]{1,0:T(8,128)(2,1)} %constant.14.clone.refs_3_, f32[16,128]{1,0:T(8,128)S(1)} %collective-permute-done.refs_4_, f32[16,128]{1,0:T(8,128)S(1)} %collective-permute-done.1.refs_5_), custom_call_target="tpu_custom_call" | custom-call | flops 1610612736 | bytes 8388608 | tf_op jit(solution)/shard_map/pallas_call | solution.py:308
  61.5 7.1 %all-to-all-done = f32[128,8,128]{2,1,0:T(8,128)S(1)} async-done(((f32[128,8,128]{2,1,0:T(8,128)}), f32[128,8,128]{2,1,0:T(8,128)S(1)}, u32[]{:S(2)}, u32[]{:S(2)}) %all-to-all-start) | async-done | bytes 524320 | tf_op jit(solution)/shard_map/all_to_all | solution.py:415
  68.7 0.1 reduce_sum.9
  68.8 0.1 maximum_divide_fusion
  68.9 0.1 fusion.1
  69.0 0.6 pad_maximum_fusion
  (11 shorter events, 0.0 us)
Async XLA Ops:
  5.6 34.4 %copy-start = (s32[64]{0:T(128)S(1)}, s32[64]{0:T(128)}, u32[]{:S(2)}) copy-start(s32[64]{0:T(128)} %refs_0_.7) | copy-start | bytes 772
  5.6 34.5 %copy-start.1 = (s32[64]{0:T(128)S(1)}, s32[64]{0:T(128)}, u32[]{:S(2)}) copy-start(s32[64]{0:T(128)} %refs_1_.7) | copy-start | bytes 772
  5.6 17.6 %collective-permute-start.8 = (f32[16,3072]{1,0:T(8,128)S(1)}, f32[16,3072]{1,0:T(8,128)S(1)}, u32[]{:S(2)}, u32[]{:S(2)}) collective-permute-start(f32[16,3072]{1,0:T(8,128)S(1)} %get-tuple-element.32), channel_id=1, source_target_pairs={{0,1},{1,2},{2,3},{3,0},{4,5},{5,6},{6,7},{7,4},{8,9},{9,10},{10,1... | collective-permute-start | bytes 589832 | tf_op jit(solution)/shard_map/ppermute | solution.py:382
  10.8 27.2 %collective-permute-start.5 = (f32[16,4096]{1,0:T(8,128)S(1)}, f32[16,4096]{1,0:T(8,128)S(1)}, u32[]{:S(2)}, u32[]{:S(2)}) collective-permute-start(f32[16,4096]{1,0:T(8,128)S(1)} %get-tuple-element.28), channel_id=1, source_target_pairs={{0,1},{1,2},{2,3},{3,0},{4,5},{5,6},{6,7},{7,4},{8,9},{9,10},{10,1... | collective-permute-start | bytes 786440 | tf_op jit(solution)/shard_map/ppermute | solution.py:382
  12.1 4.2 %collective-permute-start = (f32[16,128]{1,0:T(8,128)S(1)}, f32[16,128]{1,0:T(8,128)S(1)}, u32[]{:S(2)}, u32[]{:S(2)}) collective-permute-start(f32[16,128]{1,0:T(8,128)S(1)} %get-tuple-element.19), channel_id=1, source_target_pairs={{0,4},{4,0},{8,12},{12,8},{16,20},{20,16},{24,28},{28,24},{32,36},... | collective-permute-start | bytes 24584 | tf_op jit(solution)/shard_map/ppermute | solution.py:406
  12.9 27.9 %collective-permute-start.6 = (f32[16,4096]{1,0:T(8,128)S(1)}, f32[16,4096]{1,0:T(8,128)S(1)}, u32[]{:S(2)}, u32[]{:S(2)}) collective-permute-start(f32[16,4096]{1,0:T(8,128)S(1)} %get-tuple-element.29), channel_id=1, source_target_pairs={{0,2},{1,3},{2,0},{3,1},{4,6},{5,7},{6,4},{7,5},{8,10},{9,11},{10,... | collective-permute-start | bytes 786440 | tf_op jit(solution)/shard_map/ppermute | solution.py:382
  14.2 26.6 %collective-permute-start.7 = (f32[16,4096]{1,0:T(8,128)S(1)}, f32[16,4096]{1,0:T(8,128)S(1)}, u32[]{:S(2)}, u32[]{:S(2)}) collective-permute-start(f32[16,4096]{1,0:T(8,128)S(1)} %get-tuple-element.30), channel_id=1, source_target_pairs={{0,3},{1,0},{2,1},{3,2},{4,7},{5,4},{6,5},{7,6},{8,11},{9,8},{10,9... | collective-permute-start | bytes 786440 | tf_op jit(solution)/shard_map/ppermute | solution.py:382
  16.3 6.9 %collective-permute-start.1 = (f32[16,128]{1,0:T(8,128)S(1)}, f32[16,128]{1,0:T(8,128)S(1)}, u32[]{:S(2)}, u32[]{:S(2)}) collective-permute-start(f32[16,128]{1,0:T(8,128)S(1)} %get-tuple-element.20), channel_id=1, source_target_pairs={{4,8},{12,16},{20,24},{28,32},{36,40},{44,48},{52,56},{60,64},{68,... | collective-permute-start | bytes 24584 | tf_op jit(solution)/shard_map/ppermute | solution.py:408
  23.2 7.1 %collective-permute-start.9 = (f32[16,3072]{1,0:T(8,128)S(1)}, f32[16,3072]{1,0:T(8,128)S(1)}, u32[]{:S(2)}, u32[]{:S(2)}) collective-permute-start(f32[16,3072]{1,0:T(8,128)S(1)} %get-tuple-element.33), channel_id=1, source_target_pairs={{0,2},{1,3},{2,0},{3,1},{4,6},{5,7},{6,4},{7,5},{8,10},{9,11},{10,... | collective-permute-start | bytes 589832 | tf_op jit(solution)/shard_map/ppermute | solution.py:382
  23.2 12.7 %collective-permute-start.10 = (f32[16,3072]{1,0:T(8,128)S(1)}, f32[16,3072]{1,0:T(8,128)S(1)}, u32[]{:S(2)}, u32[]{:S(2)}) collective-permute-start(f32[16,3072]{1,0:T(8,128)S(1)} %get-tuple-element.34), channel_id=1, source_target_pairs={{0,3},{1,0},{2,1},{3,2},{4,7},{5,4},{6,5},{7,6},{8,11},{9,8},{10,9... | collective-permute-start | bytes 589832 | tf_op jit(solution)/shard_map/ppermute | solution.py:382
  30.3 11.2 %collective-permute-start.2 = (f32[16,1024]{1,0:T(8,128)S(1)}, f32[16,1024]{1,0:T(8,128)S(1)}, u32[]{:S(2)}, u32[]{:S(2)}) collective-permute-start(f32[16,1024]{1,0:T(8,128)S(1)} %get-tuple-element.24), channel_id=1, source_target_pairs={{0,1},{1,2},{2,3},{3,0},{4,5},{5,6},{6,7},{7,4},{8,9},{9,10},{10,1... | collective-permute-start | bytes 196616 | tf_op jit(solution)/shard_map/ppermute | solution.py:382
  35.9 5.6 %collective-permute-start.3 = (f32[16,1024]{1,0:T(8,128)S(1)}, f32[16,1024]{1,0:T(8,128)S(1)}, u32[]{:S(2)}, u32[]{:S(2)}) collective-permute-start(f32[16,1024]{1,0:T(8,128)S(1)} %get-tuple-element.25), channel_id=1, source_target_pairs={{0,2},{1,3},{2,0},{3,1},{4,6},{5,7},{6,4},{7,5},{8,10},{9,11},{10,... | collective-permute-start | bytes 196616 | tf_op jit(solution)/shard_map/ppermute | solution.py:382
  38.0 4.2 %collective-permute-start.4 = (f32[16,1024]{1,0:T(8,128)S(1)}, f32[16,1024]{1,0:T(8,128)S(1)}, u32[]{:S(2)}, u32[]{:S(2)}) collective-permute-start(f32[16,1024]{1,0:T(8,128)S(1)} %get-tuple-element.26), channel_id=1, source_target_pairs={{0,3},{1,0},{2,1},{3,2},{4,7},{5,4},{6,5},{7,6},{8,11},{9,8},{10,9... | collective-permute-start | bytes 196616 | tf_op jit(solution)/shard_map/ppermute | solution.py:382
  43.3 25.3 %all-to-all-start = ((f32[128,8,128]{2,1,0:T(8,128)}), f32[128,8,128]{2,1,0:T(8,128)S(1)}, u32[]{:S(2)}, u32[]{:S(2)}) async-start(f32[128,8,128]{2,1,0:T(8,128)} %bitcast), calls=%async_computation | async-start | bytes 1048576 | tf_op jit(solution)/shard_map/all_to_all | solution.py:415

commit v8 on v7

--- a/solution.py
+++ b/solution.py
@@ -67,7 +67,7 @@
         fit_ref, out_sems = refs[:2]
         refs = refs[2:]
     if resids:
-        resid_ref, piece_sems = refs
+        resid_ref = refs[0]
 
     width = signal_ref.shape[1]
     per = count // GROUPS
@@ -126,9 +126,6 @@
             out_sems.at[kind, n],
         )
 
-    def piece(k):
-        return pltpu.make_async_copy(resid_ref.at[k], outs[k], piece_sems.at[k])
-
     lane = lax.broadcasted_iota(jnp.int32, (ROWS, LANES), 1)
     low = lane < 64
     height = ROWS * blocks
@@ -252,13 +249,6 @@
         if fits:
             give(n, 0).start()
             give(n, 1).start()
-        if resids:
-            for kk in range(GROUPS):
-
-                @pl.when((k == kk) & (n % per == per - 1))
-                def _():
-                    piece(kk).start()
-
         return carry
 
     lax.fori_loop(0, count, body, 0)
@@ -266,7 +256,7 @@
         copy.wait()
     if resids:
         for kk in range(GROUPS):
-            piece(kk).wait()
+            outs[kk][...] = resid_ref[kk]
     if fits:
         for n in range(count):
             give(n, 0).wait()
@@ -281,6 +271,7 @@
     if not fits:
         taps = taps[:, :LANES]
     hbm = pl.BlockSpec(memory_space=pltpu.HBM)
+    vmem = pl.BlockSpec(memory_space=pltpu.VMEM)
     loose = pl.BlockSpec(memory_space=pl.ANY)
     args = [pltpu.with_memory_space_constraint(a, pltpu.HBM) for a in (first, last, signal, taps)]
     args += list(halos or ())
@@ -301,14 +292,11 @@
             pltpu.SemaphoreType.DMA((2, count)),
         ]
     if resids:
-        scratch += [
-            pltpu.VMEM((GROUPS, rows, count // GROUPS * span), jnp.float32),
-            pltpu.SemaphoreType.DMA((GROUPS,)),
-        ]
+        scratch += [pltpu.VMEM((GROUPS, rows, count // GROUPS * span), jnp.float32)]
     return pl.pallas_call(
         functools.partial(fit_kernel, plan, fits, resids, ends, edges),
         in_specs=[hbm] * 4 + [loose] * len(halos or ()),
-        out_specs=[hbm] * (2 * fits) + [loose] * (GROUPS * resids + 2 * edges),
+        out_specs=[hbm] * (2 * fits) + [vmem] * (GROUPS * resids) + [loose] * (2 * edges),
         out_shape=[wide] * (2 * fits) + [part] * (GROUPS * resids) + [edge] * (2 * edges),
         scratch_shapes=scratch,
         compiler_params=pltpu.CompilerParams(vmem_limit_bytes=16 * MIB),

time: 69.9 us -> 68.4 us (0.979)
  Pallas kernels: 20 us -> 18 us
  waiting for transfers between devices: 14.5 us -> 15.2 us
    pallas_call x4, Pallas kernels: 17.5 us -> 15.5 us  [fit_steps(): pl.pallas_call(functools.partial(fit_kernel, plan, fits, resids, ends, ed...]
  transfers between devices with their start and end apart: 12 -> 12, of which waited for: 5 -> 5; matrix products, arithmetic and copies ran while one was open for 0% -> 0% of each run, Pallas kernels for 20% -> 19%
where the time goes in v8:
time: 68.4 us; the launch traced here: 68.1 us
  starting transfers between devices  33 us (48%)
  Pallas kernels  18 us (26%)
  waiting for transfers between devices  15.2 us (22%)
  other arithmetic  0.9 us (1%)
  between operations  0.75 us (1%)
    ppermute x9, starting transfers between devices, exchanged(): parts.append(lax.ppermute(pieces[k], 'series', pairs))  15.7 us
    pallas_call x4, Pallas kernels, fit_steps(): pl.pallas_call(functools.partial(fit_kernel, plan, fits, resids, ends, ed...  15.5 us
    all_to_all x1, starting transfers between devices, shards(): copies = lax.all_to_all(copies, (*TIME, 'series'), 0, 0, tiled=True)  11.2 us
    all_to_all x1, waiting for transfers between devices, shards(): copies = lax.all_to_all(copies, (*TIME, 'series'), 0, 0, tiled=True)  7.15 us
    ppermute x9, waiting for transfers between devices, exchanged(): parts.append(lax.ppermute(pieces[k], 'series', pairs))  6.42 us
    ppermute x1, starting transfers between devices, shards(): far = lax.ppermute(far, TIME, pairs + [(b, a) for a, b in pairs])  5.31 us
    pallas_call x3, Pallas kernels, gram_of(): pl.pallas_call(functools.partial(gram_kernel, so_far is not None, spread)...  2.5 us
    ppermute x1, waiting for transfers between devices, shards(): far = lax.ppermute(far, TIME, pairs + [(b, a) for a, b in pairs])  1.61 us
  transfers between devices with their start and end apart: 12, of which 5 were waited for; matrix products, arithmetic and copies ran while one was open for 0% of the time, Pallas kernels for 19%

profile of v8, /device:TPU:1, one launch (start us, length us, event | category | flops | bytes accessed | tf_op | source)
XLA Modules:
  0.0 68.1 jit_solution(2737356080658862914)
XLA Ops:
  0.6 3.6 %shard_map.67 = (f32[16,3072]{1,0:T(8,128)S(1)}, f32[16,3072]{1,0:T(8,128)S(1)}, f32[16,3072]{1,0:T(8,128)S(1)}, f32[16,3072]{1,0:T(8,128)S(1)}, f32[16,128]{1,0:T(8,128)S(1)}, /*index=5*/f32[16,128]{1,0:T(8,128)S(1)}) custom-call(s32[64]{0:T(128)} %refs_0_.7, s32[64]{0:T(128)} %refs_1_.7, f32[16,32768]{1,0:T(8,128)} %refs_2_.7, ...), custom_call_target="tpu_custom_call" | custom-call | flops 603979776 | bytes 3145728 | tf_op jit(solution)/shard_map/pallas_call | solution.py:296
  4.3 0.0 copy-start
  4.3 2.1 %collective-permute-start.8 = (f32[16,3072]{1,0:T(8,128)S(1)}, f32[16,3072]{1,0:T(8,128)S(1)}, u32[]{:S(2)}, u32[]{:S(2)}) collective-permute-start(f32[16,3072]{1,0:T(8,128)S(1)} %get-tuple-element.32), channel_id=1, source_target_pairs={{0,1},{1,2},{2,3},{3,0},{4,5},{5,6},{6,7},{7,4},{8,9},{9,10},{10,1... | collective-permute-start | bytes 589832 | tf_op jit(solution)/shard_map/ppermute | solution.py:370
  6.4 2.9 %shard_map.70 = (f32[16,4096]{1,0:T(8,128)S(1)}, f32[16,4096]{1,0:T(8,128)S(1)}, f32[16,4096]{1,0:T(8,128)S(1)}, f32[16,4096]{1,0:T(8,128)S(1)}) custom-call(s32[64]{0:T(128)} %refs_0_.7, s32[64]{0:T(128)} %refs_1_.7, f32[16,32768]{1,0:T(8,128)} %refs_2_.7, bf16[256,128]{1,0:T(8,128)(2,1)} %constant.15.refs_3_), custom_call_target="tpu_custom_call" | custom-call | flops 805306368 | bytes 4194304 | tf_op jit(solution)/shard_map/pallas_call | solution.py:296
  9.3 1.3 %collective-permute-start.5 = (f32[16,4096]{1,0:T(8,128)S(1)}, f32[16,4096]{1,0:T(8,128)S(1)}, u32[]{:S(2)}, u32[]{:S(2)}) collective-permute-start(f32[16,4096]{1,0:T(8,128)S(1)} %get-tuple-element.28), channel_id=1, source_target_pairs={{0,1},{1,2},{2,3},{3,0},{4,5},{5,6},{6,7},{7,4},{8,9},{9,10},{10,1... | collective-permute-start | bytes 786440 | tf_op jit(solution)/shard_map/ppermute | solution.py:370
  10.6 0.8 %collective-permute-start = (f32[16,128]{1,0:T(8,128)S(1)}, f32[16,128]{1,0:T(8,128)S(1)}, u32[]{:S(2)}, u32[]{:S(2)}) collective-permute-start(f32[16,128]{1,0:T(8,128)S(1)} %get-tuple-element.19), channel_id=1, source_target_pairs={{0,4},{4,0},{8,12},{12,8},{16,20},{20,16},{24,28},{28,24},{32,36},... | collective-permute-start | bytes 24584 | tf_op jit(solution)/shard_map/ppermute | solution.py:394
  11.4 1.3 %collective-permute-start.6 = (f32[16,4096]{1,0:T(8,128)S(1)}, f32[16,4096]{1,0:T(8,128)S(1)}, u32[]{:S(2)}, u32[]{:S(2)}) collective-permute-start(f32[16,4096]{1,0:T(8,128)S(1)} %get-tuple-element.29), channel_id=1, source_target_pairs={{0,2},{1,3},{2,0},{3,1},{4,6},{5,7},{6,4},{7,5},{8,10},{9,11},{10,... | collective-permute-start | bytes 786440 | tf_op jit(solution)/shard_map/ppermute | solution.py:370
  12.7 2.1 %collective-permute-start.7 = (f32[16,4096]{1,0:T(8,128)S(1)}, f32[16,4096]{1,0:T(8,128)S(1)}, u32[]{:S(2)}, u32[]{:S(2)}) collective-permute-start(f32[16,4096]{1,0:T(8,128)S(1)} %get-tuple-element.30), channel_id=1, source_target_pairs={{0,3},{1,0},{2,1},{3,2},{4,7},{5,4},{6,5},{7,6},{8,11},{9,8},{10,9... | collective-permute-start | bytes 786440 | tf_op jit(solution)/shard_map/ppermute | solution.py:370
  14.8 5.3 %collective-permute-start.1 = (f32[16,128]{1,0:T(8,128)S(1)}, f32[16,128]{1,0:T(8,128)S(1)}, u32[]{:S(2)}, u32[]{:S(2)}) collective-permute-start(f32[16,128]{1,0:T(8,128)S(1)} %get-tuple-element.20), channel_id=1, source_target_pairs={{4,8},{12,16},{20,24},{28,32},{36,40},{44,48},{52,56},{60,64},{68,... | collective-permute-start | bytes 24584 | tf_op jit(solution)/shard_map/ppermute | solution.py:396
  20.1 1.6 %collective-permute-done.1.refs_5_ = f32[16,128]{1,0:T(8,128)S(1)} collective-permute-done((f32[16,128]{1,0:T(8,128)S(1)}, f32[16,128]{1,0:T(8,128)S(1)}, u32[]{:S(2)}, u32[]{:S(2)}) %collective-permute-start.1) | collective-permute-done | bytes 8224 | tf_op jit(solution)/shard_map/ppermute | solution.py:396
  21.7 0.0 collective-permute-start.9
  21.7 2.1 %collective-permute-start.10 = (f32[16,3072]{1,0:T(8,128)S(1)}, f32[16,3072]{1,0:T(8,128)S(1)}, u32[]{:S(2)}, u32[]{:S(2)}) collective-permute-start(f32[16,3072]{1,0:T(8,128)S(1)} %get-tuple-element.34), channel_id=1, source_target_pairs={{0,3},{1,0},{2,1},{3,2},{4,7},{5,4},{6,5},{7,6},{8,11},{9,8},{10,9... | collective-permute-start | bytes 589832 | tf_op jit(solution)/shard_map/ppermute | solution.py:370
  23.8 2.1 %shard_map.69 = (f32[16,1024]{1,0:T(8,128)S(1)}, f32[16,1024]{1,0:T(8,128)S(1)}, f32[16,1024]{1,0:T(8,128)S(1)}, f32[16,1024]{1,0:T(8,128)S(1)}) custom-call(s32[64]{0:T(128)} %refs_0_.7, s32[64]{0:T(128)} %refs_1_.7, f32[16,32768]{1,0:T(8,128)} %refs_2_.7, bf16[256,128]{1,0:T(8,128)(2,1)} %constant.15.refs_3_, f32[16,128]{1,0:T(8,128)S(1)} %collective-permute-done.refs_4_, ...), custom_call_target="tpu_custom_call" | custom-call | flops 201326592 | bytes 1048576 | tf_op jit(solution)/shard_map/pallas_call | solution.py:296
  25.9 3.1 %collective-permute-done.9.refs_2_ = f32[16,3072]{1,0:T(8,128)S(1)} collective-permute-done((f32[16,3072]{1,0:T(8,128)S(1)}, f32[16,3072]{1,0:T(8,128)S(1)}, u32[]{:S(2)}, u32[]{:S(2)}) %collective-permute-start.9) | collective-permute-done | bytes 196640 | tf_op jit(solution)/shard_map/ppermute | solution.py:370
  29.0 2.7 %collective-permute-start.2 = (f32[16,1024]{1,0:T(8,128)S(1)}, f32[16,1024]{1,0:T(8,128)S(1)}, u32[]{:S(2)}, u32[]{:S(2)}) collective-permute-start(f32[16,1024]{1,0:T(8,128)S(1)} %get-tuple-element.24), channel_id=1, source_target_pairs={{0,1},{1,2},{2,3},{3,0},{4,5},{5,6},{6,7},{7,4},{8,9},{9,10},{10,1... | collective-permute-start | bytes 196616 | tf_op jit(solution)/shard_map/ppermute | solution.py:370
  31.7 2.7 %collective-permute-done.10.refs_3_ = f32[16,3072]{1,0:T(8,128)S(1)} collective-permute-done((f32[16,3072]{1,0:T(8,128)S(1)}, f32[16,3072]{1,0:T(8,128)S(1)}, u32[]{:S(2)}, u32[]{:S(2)}) %collective-permute-start.10) | collective-permute-done | bytes 196640 | tf_op jit(solution)/shard_map/ppermute | solution.py:370
  34.4 2.1 %collective-permute-start.3 = (f32[16,1024]{1,0:T(8,128)S(1)}, f32[16,1024]{1,0:T(8,128)S(1)}, u32[]{:S(2)}, u32[]{:S(2)}) collective-permute-start(f32[16,1024]{1,0:T(8,128)S(1)} %get-tuple-element.25), channel_id=1, source_target_pairs={{0,2},{1,3},{2,0},{3,1},{4,6},{5,7},{6,4},{7,5},{8,10},{9,11},{10,... | collective-permute-start | bytes 196616 | tf_op jit(solution)/shard_map/ppermute | solution.py:370
  36.5 2.1 %collective-permute-start.4 = (f32[16,1024]{1,0:T(8,128)S(1)}, f32[16,1024]{1,0:T(8,128)S(1)}, u32[]{:S(2)}, u32[]{:S(2)}) collective-permute-start(f32[16,1024]{1,0:T(8,128)S(1)} %get-tuple-element.26), channel_id=1, source_target_pairs={{0,3},{1,0},{2,1},{3,2},{4,7},{5,4},{6,5},{7,6},{8,11},{9,8},{10,9... | collective-permute-start | bytes 196616 | tf_op jit(solution)/shard_map/ppermute | solution.py:370
  38.5 0.1 dynamic_slice.7
  38.6 0.1 dynamic_slice.6
  38.7 0.6 shard_map.71.refs_4_
  39.3 0.7 %shard_map.72.refs_4_ = f32[4,8,128]{2,1,0:T(8,128)S(1)} custom-call(f32[16,4096]{1,0:T(8,128)S(1)} %get-tuple-element.27.refs_0_, f32[16,4096]{1,0:T(8,128)S(1)} %collective-permute-done.5.refs_1_, f32[16,4096]{1,0:T(8,128)S(1)} %collective-permute-done.6.refs_2_, f32[16,4096]{1,0:T(8,128)S(1)} %collective-permute-done.7.refs_3_, ...), custom_call_target="tpu_custom_call" | custom-call | flops 134217728 | bytes 1048576 | tf_op jit(solution)/shard_map/pallas_call | solution.py:349
  40.0 0.6 collective-permute-done.4.refs_3_
  40.6 1.2 %shard_map.73 = f32[32,4,8,128]{3,2,1,0:T(8,128)} custom-call(f32[16,1024]{1,0:T(8,128)S(1)} %get-tuple-element.23.refs_0_, f32[16,1024]{1,0:T(8,128)S(1)} %collective-permute-done.2.refs_1_, f32[16,1024]{1,0:T(8,128)S(1)} %collective-permute-done.3.refs_2_, f32[16,1024]{1,0:T(8,128)S(1)} %collective-permute-done.4.refs_3_, f32[4,8,128]{2,1,0:T(8,128)S(1)} %shard_map.72.refs_4_), custom_call_target="tpu_custom_call" | custom-call | flops 33554432 | bytes 262144 | tf_op jit(solution)/shard_map/pallas_call | solution.py:349
  41.8 11.2 %all-to-all-start = ((f32[128,8,128]{2,1,0:T(8,128)}), f32[128,8,128]{2,1,0:T(8,128)S(1)}, u32[]{:S(2)}, u32[]{:S(2)}) async-start(f32[128,8,128]{2,1,0:T(8,128)} %bitcast), calls=%async_computation | async-start | bytes 1048576 | tf_op jit(solution)/shard_map/all_to_all | solution.py:403
  53.1 0.1 subtract_convert_fusion
  53.1 6.9 %shard_map.68 = (f32[16,32768]{1,0:T(8,128)}, f32[16,32768]{1,0:T(8,128)}) custom-call(s32[64]{0:T(128)} %refs_0_.7, s32[64]{0:T(128)} %refs_1_.7, f32[16,32768]{1,0:T(8,128)} %refs_2_.7, bf16[256,256]{1,0:T(8,128)(2,1)} %constant.14.clone.refs_3_, f32[16,128]{1,0:T(8,128)S(1)} %collective-permute-done.refs_4_, f32[16,128]{1,0:T(8,128)S(1)} %collective-permute-done.1.refs_5_), custom_call_target="tpu_custom_call" | custom-call | flops 1610612736 | bytes 8388608 | tf_op jit(solution)/shard_map/pallas_call | solution.py:296
  60.0 7.1 %all-to-all-done = f32[128,8,128]{2,1,0:T(8,128)S(1)} async-done(((f32[128,8,128]{2,1,0:T(8,128)}), f32[128,8,128]{2,1,0:T(8,128)S(1)}, u32[]{:S(2)}, u32[]{:S(2)}) %all-to-all-start) | async-done | bytes 524320 | tf_op jit(solution)/shard_map/all_to_all | solution.py:403
  67.2 0.1 reduce_sum.9
  67.3 0.1 maximum_divide_fusion
  67.4 0.1 fusion.1
  67.5 0.6 pad_maximum_fusion
  (11 shorter events, 0.0 us)
Async XLA Ops:
  4.3 34.3 %copy-start = (s32[64]{0:T(128)S(1)}, s32[64]{0:T(128)}, u32[]{:S(2)}) copy-start(s32[64]{0:T(128)} %refs_0_.7) | copy-start | bytes 772
  4.3 34.3 %copy-start.1 = (s32[64]{0:T(128)S(1)}, s32[64]{0:T(128)}, u32[]{:S(2)}) copy-start(s32[64]{0:T(128)} %refs_1_.7) | copy-start | bytes 772
  4.3 17.4 %collective-permute-start.8 = (f32[16,3072]{1,0:T(8,128)S(1)}, f32[16,3072]{1,0:T(8,128)S(1)}, u32[]{:S(2)}, u32[]{:S(2)}) collective-permute-start(f32[16,3072]{1,0:T(8,128)S(1)} %get-tuple-element.32), channel_id=1, source_target_pairs={{0,1},{1,2},{2,3},{3,0},{4,5},{5,6},{6,7},{7,4},{8,9},{9,10},{10,1... | collective-permute-start | bytes 589832 | tf_op jit(solution)/shard_map/ppermute | solution.py:370
  9.3 27.2 %collective-permute-start.5 = (f32[16,4096]{1,0:T(8,128)S(1)}, f32[16,4096]{1,0:T(8,128)S(1)}, u32[]{:S(2)}, u32[]{:S(2)}) collective-permute-start(f32[16,4096]{1,0:T(8,128)S(1)} %get-tuple-element.28), channel_id=1, source_target_pairs={{0,1},{1,2},{2,3},{3,0},{4,5},{5,6},{6,7},{7,4},{8,9},{9,10},{10,1... | collective-permute-start | bytes 786440 | tf_op jit(solution)/shard_map/ppermute | solution.py:370
  10.6 4.2 %collective-permute-start = (f32[16,128]{1,0:T(8,128)S(1)}, f32[16,128]{1,0:T(8,128)S(1)}, u32[]{:S(2)}, u32[]{:S(2)}) collective-permute-start(f32[16,128]{1,0:T(8,128)S(1)} %get-tuple-element.19), channel_id=1, source_target_pairs={{0,4},{4,0},{8,12},{12,8},{16,20},{20,16},{24,28},{28,24},{32,36},... | collective-permute-start | bytes 24584 | tf_op jit(solution)/shard_map/ppermute | solution.py:394
  11.4 27.9 %collective-permute-start.6 = (f32[16,4096]{1,0:T(8,128)S(1)}, f32[16,4096]{1,0:T(8,128)S(1)}, u32[]{:S(2)}, u32[]{:S(2)}) collective-permute-start(f32[16,4096]{1,0:T(8,128)S(1)} %get-tuple-element.29), channel_id=1, source_target_pairs={{0,2},{1,3},{2,0},{3,1},{4,6},{5,7},{6,4},{7,5},{8,10},{9,11},{10,... | collective-permute-start | bytes 786440 | tf_op jit(solution)/shard_map/ppermute | solution.py:370
  12.7 26.6 %collective-permute-start.7 = (f32[16,4096]{1,0:T(8,128)S(1)}, f32[16,4096]{1,0:T(8,128)S(1)}, u32[]{:S(2)}, u32[]{:S(2)}) collective-permute-start(f32[16,4096]{1,0:T(8,128)S(1)} %get-tuple-element.30), channel_id=1, source_target_pairs={{0,3},{1,0},{2,1},{3,2},{4,7},{5,4},{6,5},{7,6},{8,11},{9,8},{10,9... | collective-permute-start | bytes 786440 | tf_op jit(solution)/shard_map/ppermute | solution.py:370
  14.8 6.9 %collective-permute-start.1 = (f32[16,128]{1,0:T(8,128)S(1)}, f32[16,128]{1,0:T(8,128)S(1)}, u32[]{:S(2)}, u32[]{:S(2)}) collective-permute-start(f32[16,128]{1,0:T(8,128)S(1)} %get-tuple-element.20), channel_id=1, source_target_pairs={{4,8},{12,16},{20,24},{28,32},{36,40},{44,48},{52,56},{60,64},{68,... | collective-permute-start | bytes 24584 | tf_op jit(solution)/shard_map/ppermute | solution.py:396
  21.7 7.3 %collective-permute-start.9 = (f32[16,3072]{1,0:T(8,128)S(1)}, f32[16,3072]{1,0:T(8,128)S(1)}, u32[]{:S(2)}, u32[]{:S(2)}) collective-permute-start(f32[16,3072]{1,0:T(8,128)S(1)} %get-tuple-element.33), channel_id=1, source_target_pairs={{0,2},{1,3},{2,0},{3,1},{4,6},{5,7},{6,4},{7,5},{8,10},{9,11},{10,... | collective-permute-start | bytes 589832 | tf_op jit(solution)/shard_map/ppermute | solution.py:370
  21.7 12.7 %collective-permute-start.10 = (f32[16,3072]{1,0:T(8,128)S(1)}, f32[16,3072]{1,0:T(8,128)S(1)}, u32[]{:S(2)}, u32[]{:S(2)}) collective-permute-start(f32[16,3072]{1,0:T(8,128)S(1)} %get-tuple-element.34), channel_id=1, source_target_pairs={{0,3},{1,0},{2,1},{3,2},{4,7},{5,4},{6,5},{7,6},{8,11},{9,8},{10,9... | collective-permute-start | bytes 589832 | tf_op jit(solution)/shard_map/ppermute | solution.py:370
  29.0 11.1 %collective-permute-start.2 = (f32[16,1024]{1,0:T(8,128)S(1)}, f32[16,1024]{1,0:T(8,128)S(1)}, u32[]{:S(2)}, u32[]{:S(2)}) collective-permute-start(f32[16,1024]{1,0:T(8,128)S(1)} %get-tuple-element.24), channel_id=1, source_target_pairs={{0,1},{1,2},{2,3},{3,0},{4,5},{5,6},{6,7},{7,4},{8,9},{9,10},{10,1... | collective-permute-start | bytes 196616 | tf_op jit(solution)/shard_map/ppermute | solution.py:370
  34.4 5.6 %collective-permute-start.3 = (f32[16,1024]{1,0:T(8,128)S(1)}, f32[16,1024]{1,0:T(8,128)S(1)}, u32[]{:S(2)}, u32[]{:S(2)}) collective-permute-start(f32[16,1024]{1,0:T(8,128)S(1)} %get-tuple-element.25), channel_id=1, source_target_pairs={{0,2},{1,3},{2,0},{3,1},{4,6},{5,7},{6,4},{7,5},{8,10},{9,11},{10,... | collective-permute-start | bytes 196616 | tf_op jit(solution)/shard_map/ppermute | solution.py:370
  36.5 4.2 %collective-permute-start.4 = (f32[16,1024]{1,0:T(8,128)S(1)}, f32[16,1024]{1,0:T(8,128)S(1)}, u32[]{:S(2)}, u32[]{:S(2)}) collective-permute-start(f32[16,1024]{1,0:T(8,128)S(1)} %get-tuple-element.26), channel_id=1, source_target_pairs={{0,3},{1,0},{2,1},{3,2},{4,7},{5,4},{6,5},{7,6},{8,11},{9,8},{10,9... | collective-permute-start | bytes 196616 | tf_op jit(solution)/shard_map/ppermute | solution.py:370
  41.8 25.3 %all-to-all-start = ((f32[128,8,128]{2,1,0:T(8,128)}), f32[128,8,128]{2,1,0:T(8,128)S(1)}, u32[]{:S(2)}, u32[]{:S(2)}) async-start(f32[128,8,128]{2,1,0:T(8,128)} %bitcast), calls=%async_computation | async-start | bytes 1048576 | tf_op jit(solution)/shard_map/all_to_all | solution.py:403

commit v9 on v8

--- a/solution.py
+++ b/solution.py
@@ -377,7 +377,7 @@
     taps = jnp.asarray(taps, jnp.bfloat16)
     mine = lax.axis_index("series")
     unit = width // 32
-    early, mid = (2 * unit, 3 * unit, GROUPS), (14 * unit, 4 * unit, GROUPS)
+    early, mid = (2 * unit, 4 * unit, GROUPS), (18 * unit, 3 * unit, GROUPS)
     late, whole = (30 * unit, unit, GROUPS), (0, 4 * unit, 8)
 
     def fit(plan, fits, resids, halos=None, edges=False):
@@ -385,7 +385,8 @@
 
     first = lax.dynamic_slice_in_dim(valid_start, mine * rows, rows)[:, None]
     last = lax.dynamic_slice_in_dim(valid_end, mine * rows, rows)[:, None]
-    shared = jnp.minimum(last, valid_end[None, :]) - jnp.maximum(first, valid_start[None, :])
+    shared = jnp.minimum(last, valid_end[None, :])
+    shared = shared - jnp.maximum(first, valid_start[None, :])
     shared = packed(shared.astype(jnp.float32))
 
     *pieces, near, far = fit(early, False, True, edges=True)

time: 68.4 us -> 64 us (0.936)
  starting transfers between devices: 33 us -> 30.3 us
  waiting for transfers between devices: 15.2 us -> 13.5 us
    ppermute x9, waiting for transfers between devices: 6.42 us -> 3.9 us  [exchanged(): parts.append(lax.ppermute(pieces[k], 'series', pairs))]
    ppermute x9, starting transfers between devices: 15.7 us -> 13.2 us  [exchanged(): parts.append(lax.ppermute(pieces[k], 'series', pairs))]
    ppermute x1, starting transfers between devices: 5.31 us -> 4.24 us  [shards(): far = lax.ppermute(far, TIME, pairs + [(b, a) for a, b in pairs])]
    all_to_all x1, starting transfers between devices: 11.2 us -> 12.1 us  [shards(): copies = lax.all_to_all(copies, (*TIME, 'series'), 0, 0, tiled=True)]
    ppermute x1, waiting for transfers between devices: 0.01 us -> 0.83 us  [shards(): near = lax.ppermute(near, TIME, [(t, t ^ 1) for t in range(devices)])]
  transfers between devices with their start and end apart: 12 -> 12, of which waited for: 5 -> 5; matrix products, arithmetic and copies ran while one was open for 0% -> 0% of each run, Pallas kernels for 19% -> 22%
where the time goes in v9:
time: 64 us; the launch traced here: 63.7 us
  starting transfers between devices  30.3 us (47%)
  Pallas kernels  18 us (28%)
  waiting for transfers between devices  13.5 us (21%)
  other arithmetic  0.9 us (1%)
  between operations  0.77 us (1%)
    pallas_call x4, Pallas kernels, fit_steps(): pl.pallas_call(functools.partial(fit_kernel, plan, fits, resids, ends, ed...  15.5 us
    ppermute x9, starting transfers between devices, exchanged(): parts.append(lax.ppermute(pieces[k], 'series', pairs))  13.2 us
    all_to_all x1, starting transfers between devices, shards(): copies = lax.all_to_all(copies, (*TIME, 'series'), 0, 0, tiled=True)  12.1 us
    all_to_all x1, waiting for transfers between devices, shards(): copies = lax.all_to_all(copies, (*TIME, 'series'), 0, 0, tiled=True)  7.15 us
    ppermute x1, starting transfers between devices, shards(): far = lax.ppermute(far, TIME, pairs + [(b, a) for a, b in pairs])  4.24 us
    ppermute x9, waiting for transfers between devices, exchanged(): parts.append(lax.ppermute(pieces[k], 'series', pairs))  3.9 us
    pallas_call x3, Pallas kernels, gram_of(): pl.pallas_call(functools.partial(gram_kernel, so_far is not None, spread)...  2.49 us
    ppermute x1, waiting for transfers between devices, shards(): far = lax.ppermute(far, TIME, pairs + [(b, a) for a, b in pairs])  1.61 us
  transfers between devices with their start and end apart: 12, of which 5 were waited for; matrix products, arithmetic and copies ran while one was open for 0% of the time, Pallas kernels for 22%

profile of v9, /device:TPU:1, one launch (start us, length us, event | category | flops | bytes accessed | tf_op | source)
XLA Modules:
  0.0 63.7 jit_solution(17007175663702918061)
XLA Ops:
  0.6 2.7 %shard_map.70 = (f32[16,3072]{1,0:T(8,128)S(1)}, f32[16,3072]{1,0:T(8,128)S(1)}, f32[16,3072]{1,0:T(8,128)S(1)}, f32[16,3072]{1,0:T(8,128)S(1)}) custom-call(s32[64]{0:T(128)} %refs_0_.7, s32[64]{0:T(128)} %refs_1_.7, f32[16,32768]{1,0:T(8,128)} %refs_2_.7, bf16[256,128]{1,0:T(8,128)(2,1)} %constant.15.refs_3_), custom_call_target="tpu_custom_call" | custom-call | flops 603979776 | bytes 3145728 | tf_op jit(solution)/shard_map/pallas_call | solution.py:296
  3.3 0.0 copy-start
  3.3 0.0 copy-start.1
  3.4 2.1 %collective-permute-start.5 = (f32[16,3072]{1,0:T(8,128)S(1)}, f32[16,3072]{1,0:T(8,128)S(1)}, u32[]{:S(2)}, u32[]{:S(2)}) collective-permute-start(f32[16,3072]{1,0:T(8,128)S(1)} %get-tuple-element.28), channel_id=1, source_target_pairs={{0,1},{1,2},{2,3},{3,0},{4,5},{5,6},{6,7},{7,4},{8,9},{9,10},{10,1... | collective-permute-start | bytes 589832 | tf_op jit(solution)/shard_map/ppermute | solution.py:370
  5.5 3.9 %shard_map.67 = (f32[16,4096]{1,0:T(8,128)S(1)}, f32[16,4096]{1,0:T(8,128)S(1)}, f32[16,4096]{1,0:T(8,128)S(1)}, f32[16,4096]{1,0:T(8,128)S(1)}, f32[16,128]{1,0:T(8,128)S(1)}, /*index=5*/f32[16,128]{1,0:T(8,128)S(1)}) custom-call(s32[64]{0:T(128)} %refs_0_.7, s32[64]{0:T(128)} %refs_1_.7, f32[16,32768]{1,0:T(8,128)} %refs_2_.7, ...), custom_call_target="tpu_custom_call" | custom-call | flops 805306368 | bytes 4194304 | tf_op jit(solution)/shard_map/pallas_call | solution.py:296
  9.3 2.2 %collective-permute-start.8 = (f32[16,4096]{1,0:T(8,128)S(1)}, f32[16,4096]{1,0:T(8,128)S(1)}, u32[]{:S(2)}, u32[]{:S(2)}) collective-permute-start(f32[16,4096]{1,0:T(8,128)S(1)} %get-tuple-element.32), channel_id=1, source_target_pairs={{0,1},{1,2},{2,3},{3,0},{4,5},{5,6},{6,7},{7,4},{8,9},{9,10},{10,1... | collective-permute-start | bytes 786440 | tf_op jit(solution)/shard_map/ppermute | solution.py:370
  11.6 2.5 %collective-permute-start.10 = (f32[16,4096]{1,0:T(8,128)S(1)}, f32[16,4096]{1,0:T(8,128)S(1)}, u32[]{:S(2)}, u32[]{:S(2)}) collective-permute-start(f32[16,4096]{1,0:T(8,128)S(1)} %get-tuple-element.34), channel_id=1, source_target_pairs={{0,3},{1,0},{2,1},{3,2},{4,7},{5,4},{6,5},{7,6},{8,11},{9,8},{10,9... | collective-permute-start | bytes 786440 | tf_op jit(solution)/shard_map/ppermute | solution.py:370
  14.0 0.7 %collective-permute-start = (f32[16,128]{1,0:T(8,128)S(1)}, f32[16,128]{1,0:T(8,128)S(1)}, u32[]{:S(2)}, u32[]{:S(2)}) collective-permute-start(f32[16,128]{1,0:T(8,128)S(1)} %get-tuple-element.19), channel_id=1, source_target_pairs={{0,4},{4,0},{8,12},{12,8},{16,20},{20,16},{24,28},{28,24},{32,36},... | collective-permute-start | bytes 24584 | tf_op jit(solution)/shard_map/ppermute | solution.py:395
  14.8 0.8 %collective-permute-done.refs_4_ = f32[16,128]{1,0:T(8,128)S(1)} collective-permute-done((f32[16,128]{1,0:T(8,128)S(1)}, f32[16,128]{1,0:T(8,128)S(1)}, u32[]{:S(2)}, u32[]{:S(2)}) %collective-permute-start) | collective-permute-done | bytes 8224 | tf_op jit(solution)/shard_map/ppermute | solution.py:395
  15.6 4.2 %collective-permute-start.1 = (f32[16,128]{1,0:T(8,128)S(1)}, f32[16,128]{1,0:T(8,128)S(1)}, u32[]{:S(2)}, u32[]{:S(2)}) collective-permute-start(f32[16,128]{1,0:T(8,128)S(1)} %get-tuple-element.20), channel_id=1, source_target_pairs={{4,8},{12,16},{20,24},{28,32},{36,40},{44,48},{52,56},{60,64},{68,... | collective-permute-start | bytes 24584 | tf_op jit(solution)/shard_map/ppermute | solution.py:397
  19.8 1.6 %collective-permute-done.1.refs_5_ = f32[16,128]{1,0:T(8,128)S(1)} collective-permute-done((f32[16,128]{1,0:T(8,128)S(1)}, f32[16,128]{1,0:T(8,128)S(1)}, u32[]{:S(2)}, u32[]{:S(2)}) %collective-permute-start.1) | collective-permute-done | bytes 8224 | tf_op jit(solution)/shard_map/ppermute | solution.py:397
  21.5 1.3 %collective-permute-start.6 = (f32[16,3072]{1,0:T(8,128)S(1)}, f32[16,3072]{1,0:T(8,128)S(1)}, u32[]{:S(2)}, u32[]{:S(2)}) collective-permute-start(f32[16,3072]{1,0:T(8,128)S(1)} %get-tuple-element.29), channel_id=1, source_target_pairs={{0,2},{1,3},{2,0},{3,1},{4,6},{5,7},{6,4},{7,5},{8,10},{9,11},{10,... | collective-permute-start | bytes 589832 | tf_op jit(solution)/shard_map/ppermute | solution.py:370
  22.8 2.3 %collective-permute-start.7 = (f32[16,3072]{1,0:T(8,128)S(1)}, f32[16,3072]{1,0:T(8,128)S(1)}, u32[]{:S(2)}, u32[]{:S(2)}) collective-permute-start(f32[16,3072]{1,0:T(8,128)S(1)} %get-tuple-element.30), channel_id=1, source_target_pairs={{0,3},{1,0},{2,1},{3,2},{4,7},{5,4},{6,5},{7,6},{8,11},{9,8},{10,9... | collective-permute-start | bytes 589832 | tf_op jit(solution)/shard_map/ppermute | solution.py:370
  25.1 2.1 %shard_map.69 = (f32[16,1024]{1,0:T(8,128)S(1)}, f32[16,1024]{1,0:T(8,128)S(1)}, f32[16,1024]{1,0:T(8,128)S(1)}, f32[16,1024]{1,0:T(8,128)S(1)}) custom-call(s32[64]{0:T(128)} %refs_0_.7, s32[64]{0:T(128)} %refs_1_.7, f32[16,32768]{1,0:T(8,128)} %refs_2_.7, bf16[256,128]{1,0:T(8,128)(2,1)} %constant.15.refs_3_, f32[16,128]{1,0:T(8,128)S(1)} %collective-permute-done.refs_4_, ...), custom_call_target="tpu_custom_call" | custom-call | flops 201326592 | bytes 1048576 | tf_op jit(solution)/shard_map/pallas_call | solution.py:296
  27.2 0.1 collective-permute-start.2
  27.3 1.2 %collective-permute-start.3 = (f32[16,1024]{1,0:T(8,128)S(1)}, f32[16,1024]{1,0:T(8,128)S(1)}, u32[]{:S(2)}, u32[]{:S(2)}) collective-permute-start(f32[16,1024]{1,0:T(8,128)S(1)} %get-tuple-element.25), channel_id=1, source_target_pairs={{0,2},{1,3},{2,0},{3,1},{4,6},{5,7},{6,4},{7,5},{8,10},{9,11},{10,... | collective-permute-start | bytes 196616 | tf_op jit(solution)/shard_map/ppermute | solution.py:370
  28.4 1.6 %collective-permute-start.4 = (f32[16,1024]{1,0:T(8,128)S(1)}, f32[16,1024]{1,0:T(8,128)S(1)}, u32[]{:S(2)}, u32[]{:S(2)}) collective-permute-start(f32[16,1024]{1,0:T(8,128)S(1)} %get-tuple-element.26), channel_id=1, source_target_pairs={{0,3},{1,0},{2,1},{3,2},{4,7},{5,4},{6,5},{7,6},{8,11},{9,8},{10,9... | collective-permute-start | bytes 196616 | tf_op jit(solution)/shard_map/ppermute | solution.py:370
  30.0 0.1 dynamic_slice.7
  30.1 0.1 dynamic_slice.6
  30.1 0.7 %shard_map.71.refs_4_ = f32[4,8,128]{2,1,0:T(8,128)S(1)} custom-call(f32[16,4096]{1,0:T(8,128)S(1)} %get-tuple-element.31.refs_0_, f32[16,4096]{1,0:T(8,128)S(1)} %collective-permute-done.8.refs_1_, f32[16,4096]{1,0:T(8,128)S(1)} %collective-permute-done.9.refs_2_, f32[16,4096]{1,0:T(8,128)S(1)} %collective-permute-done.10.refs_3_), custom_call_target="tpu_custom_call" | custom-call | flops 134217728 | bytes 1048576 | tf_op jit(solution)/shard_map/pallas_call | solution.py:349
  30.9 2.4 %collective-permute-done.7.refs_3_ = f32[16,3072]{1,0:T(8,128)S(1)} collective-permute-done((f32[16,3072]{1,0:T(8,128)S(1)}, f32[16,3072]{1,0:T(8,128)S(1)}, u32[]{:S(2)}, u32[]{:S(2)}) %collective-permute-start.7) | collective-permute-done | bytes 196640 | tf_op jit(solution)/shard_map/ppermute | solution.py:370
  33.3 0.6 shard_map.72.refs_4_
  33.9 1.5 %collective-permute-done.4.refs_3_ = f32[16,1024]{1,0:T(8,128)S(1)} collective-permute-done((f32[16,1024]{1,0:T(8,128)S(1)}, f32[16,1024]{1,0:T(8,128)S(1)}, u32[]{:S(2)}, u32[]{:S(2)}) %collective-permute-start.4) | collective-permute-done | bytes 65568 | tf_op jit(solution)/shard_map/ppermute | solution.py:370
  35.4 1.2 %shard_map.73 = f32[32,4,8,128]{3,2,1,0:T(8,128)} custom-call(f32[16,1024]{1,0:T(8,128)S(1)} %get-tuple-element.23.refs_0_, f32[16,1024]{1,0:T(8,128)S(1)} %collective-permute-done.2.refs_1_, f32[16,1024]{1,0:T(8,128)S(1)} %collective-permute-done.3.refs_2_, f32[16,1024]{1,0:T(8,128)S(1)} %collective-permute-done.4.refs_3_, f32[4,8,128]{2,1,0:T(8,128)S(1)} %shard_map.72.refs_4_), custom_call_target="tpu_custom_call" | custom-call | flops 33554432 | bytes 262144 | tf_op jit(solution)/shard_map/pallas_call | solution.py:349
  36.6 12.1 %all-to-all-start = ((f32[128,8,128]{2,1,0:T(8,128)}), f32[128,8,128]{2,1,0:T(8,128)S(1)}, u32[]{:S(2)}, u32[]{:S(2)}) async-start(f32[128,8,128]{2,1,0:T(8,128)} %bitcast), calls=%async_computation | async-start | bytes 1048576 | tf_op jit(solution)/shard_map/all_to_all | solution.py:404
  48.7 0.1 subtract_convert_fusion
  48.8 6.9 %shard_map.68 = (f32[16,32768]{1,0:T(8,128)}, f32[16,32768]{1,0:T(8,128)}) custom-call(s32[64]{0:T(128)} %refs_0_.7, s32[64]{0:T(128)} %refs_1_.7, f32[16,32768]{1,0:T(8,128)} %refs_2_.7, bf16[256,256]{1,0:T(8,128)(2,1)} %constant.14.clone.refs_3_, f32[16,128]{1,0:T(8,128)S(1)} %collective-permute-done.refs_4_, f32[16,128]{1,0:T(8,128)S(1)} %collective-permute-done.1.refs_5_), custom_call_target="tpu_custom_call" | custom-call | flops 1610612736 | bytes 8388608 | tf_op jit(solution)/shard_map/pallas_call | solution.py:296
  55.7 7.1 %all-to-all-done = f32[128,8,128]{2,1,0:T(8,128)S(1)} async-done(((f32[128,8,128]{2,1,0:T(8,128)}), f32[128,8,128]{2,1,0:T(8,128)S(1)}, u32[]{:S(2)}, u32[]{:S(2)}) %all-to-all-start) | async-done | bytes 524320 | tf_op jit(solution)/shard_map/all_to_all | solution.py:404
  62.8 0.1 reduce_sum.9
  63.0 0.1 maximum_divide_fusion
  63.0 0.1 fusion.1
  63.1 0.6 pad_maximum_fusion
  (11 shorter events, 0.0 us)
Async XLA Ops:
  3.3 26.7 %copy-start = (s32[64]{0:T(128)S(1)}, s32[64]{0:T(128)}, u32[]{:S(2)}) copy-start(s32[64]{0:T(128)} %refs_0_.7) | copy-start | bytes 772
  3.3 26.7 %copy-start.1 = (s32[64]{0:T(128)S(1)}, s32[64]{0:T(128)}, u32[]{:S(2)}) copy-start(s32[64]{0:T(128)} %refs_1_.7) | copy-start | bytes 772
  3.4 19.4 %collective-permute-start.5 = (f32[16,3072]{1,0:T(8,128)S(1)}, f32[16,3072]{1,0:T(8,128)S(1)}, u32[]{:S(2)}, u32[]{:S(2)}) collective-permute-start(f32[16,3072]{1,0:T(8,128)S(1)} %get-tuple-element.28), channel_id=1, source_target_pairs={{0,1},{1,2},{2,3},{3,0},{4,5},{5,6},{6,7},{7,4},{8,9},{9,10},{10,1... | collective-permute-start | bytes 589832 | tf_op jit(solution)/shard_map/ppermute | solution.py:370
  9.3 17.8 %collective-permute-start.8 = (f32[16,4096]{1,0:T(8,128)S(1)}, f32[16,4096]{1,0:T(8,128)S(1)}, u32[]{:S(2)}, u32[]{:S(2)}) collective-permute-start(f32[16,4096]{1,0:T(8,128)S(1)} %get-tuple-element.32), channel_id=1, source_target_pairs={{0,1},{1,2},{2,3},{3,0},{4,5},{5,6},{6,7},{7,4},{8,9},{9,10},{10,1... | collective-permute-start | bytes 786440 | tf_op jit(solution)/shard_map/ppermute | solution.py:370
  11.5 15.7 %collective-permute-start.9 = (f32[16,4096]{1,0:T(8,128)S(1)}, f32[16,4096]{1,0:T(8,128)S(1)}, u32[]{:S(2)}, u32[]{:S(2)}) collective-permute-start(f32[16,4096]{1,0:T(8,128)S(1)} %get-tuple-element.33), channel_id=1, source_target_pairs={{0,2},{1,3},{2,0},{3,1},{4,6},{5,7},{6,4},{7,5},{8,10},{9,11},{10,... | collective-permute-start | bytes 786440 | tf_op jit(solution)/shard_map/ppermute | solution.py:370
  11.6 16.9 %collective-permute-start.10 = (f32[16,4096]{1,0:T(8,128)S(1)}, f32[16,4096]{1,0:T(8,128)S(1)}, u32[]{:S(2)}, u32[]{:S(2)}) collective-permute-start(f32[16,4096]{1,0:T(8,128)S(1)} %get-tuple-element.34), channel_id=1, source_target_pairs={{0,3},{1,0},{2,1},{3,2},{4,7},{5,4},{6,5},{7,6},{8,11},{9,8},{10,9... | collective-permute-start | bytes 786440 | tf_op jit(solution)/shard_map/ppermute | solution.py:370
  14.0 1.6 %collective-permute-start = (f32[16,128]{1,0:T(8,128)S(1)}, f32[16,128]{1,0:T(8,128)S(1)}, u32[]{:S(2)}, u32[]{:S(2)}) collective-permute-start(f32[16,128]{1,0:T(8,128)S(1)} %get-tuple-element.19), channel_id=1, source_target_pairs={{0,4},{4,0},{8,12},{12,8},{16,20},{20,16},{24,28},{28,24},{32,36},... | collective-permute-start | bytes 24584 | tf_op jit(solution)/shard_map/ppermute | solution.py:395
  15.6 5.9 %collective-permute-start.1 = (f32[16,128]{1,0:T(8,128)S(1)}, f32[16,128]{1,0:T(8,128)S(1)}, u32[]{:S(2)}, u32[]{:S(2)}) collective-permute-start(f32[16,128]{1,0:T(8,128)S(1)} %get-tuple-element.20), channel_id=1, source_target_pairs={{4,8},{12,16},{20,24},{28,32},{36,40},{44,48},{52,56},{60,64},{68,... | collective-permute-start | bytes 24584 | tf_op jit(solution)/shard_map/ppermute | solution.py:397
  21.5 9.4 %collective-permute-start.6 = (f32[16,3072]{1,0:T(8,128)S(1)}, f32[16,3072]{1,0:T(8,128)S(1)}, u32[]{:S(2)}, u32[]{:S(2)}) collective-permute-start(f32[16,3072]{1,0:T(8,128)S(1)} %get-tuple-element.29), channel_id=1, source_target_pairs={{0,2},{1,3},{2,0},{3,1},{4,6},{5,7},{6,4},{7,5},{8,10},{9,11},{10,... | collective-permute-start | bytes 589832 | tf_op jit(solution)/shard_map/ppermute | solution.py:370
  22.8 10.5 %collective-permute-start.7 = (f32[16,3072]{1,0:T(8,128)S(1)}, f32[16,3072]{1,0:T(8,128)S(1)}, u32[]{:S(2)}, u32[]{:S(2)}) collective-permute-start(f32[16,3072]{1,0:T(8,128)S(1)} %get-tuple-element.30), channel_id=1, source_target_pairs={{0,3},{1,0},{2,1},{3,2},{4,7},{5,4},{6,5},{7,6},{8,11},{9,8},{10,9... | collective-permute-start | bytes 589832 | tf_op jit(solution)/shard_map/ppermute | solution.py:370
  27.2 6.7 %collective-permute-start.2 = (f32[16,1024]{1,0:T(8,128)S(1)}, f32[16,1024]{1,0:T(8,128)S(1)}, u32[]{:S(2)}, u32[]{:S(2)}) collective-permute-start(f32[16,1024]{1,0:T(8,128)S(1)} %get-tuple-element.24), channel_id=1, source_target_pairs={{0,1},{1,2},{2,3},{3,0},{4,5},{5,6},{6,7},{7,4},{8,9},{9,10},{10,1... | collective-permute-start | bytes 196616 | tf_op jit(solution)/shard_map/ppermute | solution.py:370
  27.3 6.6 %collective-permute-start.3 = (f32[16,1024]{1,0:T(8,128)S(1)}, f32[16,1024]{1,0:T(8,128)S(1)}, u32[]{:S(2)}, u32[]{:S(2)}) collective-permute-start(f32[16,1024]{1,0:T(8,128)S(1)} %get-tuple-element.25), channel_id=1, source_target_pairs={{0,2},{1,3},{2,0},{3,1},{4,6},{5,7},{6,4},{7,5},{8,10},{9,11},{10,... | collective-permute-start | bytes 196616 | tf_op jit(solution)/shard_map/ppermute | solution.py:370
  28.4 6.9 %collective-permute-start.4 = (f32[16,1024]{1,0:T(8,128)S(1)}, f32[16,1024]{1,0:T(8,128)S(1)}, u32[]{:S(2)}, u32[]{:S(2)}) collective-permute-start(f32[16,1024]{1,0:T(8,128)S(1)} %get-tuple-element.26), channel_id=1, source_target_pairs={{0,3},{1,0},{2,1},{3,2},{4,7},{5,4},{6,5},{7,6},{8,11},{9,8},{10,9... | collective-permute-start | bytes 196616 | tf_op jit(solution)/shard_map/ppermute | solution.py:370
  36.6 26.2 %all-to-all-start = ((f32[128,8,128]{2,1,0:T(8,128)}), f32[128,8,128]{2,1,0:T(8,128)S(1)}, u32[]{:S(2)}, u32[]{:S(2)}) async-start(f32[128,8,128]{2,1,0:T(8,128)} %bitcast), calls=%async_computation | async-start | bytes 1048576 | tf_op jit(solution)/shard_map/all_to_all | solution.py:404

commit v10 on v9

v10 whole, which is shorter than its diff:
```python
import functools

import jax
import jax.numpy as jnp
import numpy as np
from jax import lax
from jax.experimental import pallas as pl
from jax.experimental.pallas import tpu as pltpu
from jax.sharding import Mesh
from jax.sharding import PartitionSpec as P


HALF = 16
TAPS = 2 * HALF + 1
ROWS = 16
GROUPS = 4
LANES = 128
TIME = ("y", "z", "core")
MIB = 1 << 20

SECOND = float(sum(j * j for j in range(-HALF, HALF + 1)))
CENTRE_SQ = SECOND / TAPS
FOURTH = float(sum((j * j - CENTRE_SQ) ** 2 for j in range(-HALF, HALF + 1)))
SMOOTH_SCALE = 2048.0 / 2387.0
SLOPE_SCALE = HALF * 16.0 / SECOND


def filter_matrix():
    place = np.concatenate([np.arange(128), np.arange(128, 192), np.arange(-64, 0)])
    j = place[:, None] - np.arange(LANES)[None, :]
    near = np.abs(j) <= HALF
    smooth = np.where(near, (163 - j * j) / 2048.0, 0.0)
    slope = np.where(near, j / 16.0, 0.0)
    return np.concatenate([smooth, slope], axis=1).astype(np.float32)


def thirds(x):
    a = x.astype(jnp.bfloat16)
    rest = x - a.astype(jnp.float32)
    b = rest.astype(jnp.bfloat16)
    c = (rest - b.astype(jnp.float32)).astype(jnp.bfloat16)
    return a, b, c


def aligned(start, size):
    return pl.ds(pl.multiple_of(start, LANES), size)


def ends_of(group, first_ref, last_ref):
    row = lax.broadcasted_iota(jnp.int32, (ROWS, LANES), 0)
    first = jnp.zeros((ROWS, LANES), jnp.int32)
    last = jnp.zeros((ROWS, LANES), jnp.int32)
    for r in range(ROWS):
        first = jnp.where(row == r, first_ref[group * ROWS + r], first)
        last = jnp.where(row == r, last_ref[group * ROWS + r], last)
    return first, last


def fit_span(span, mark, group, samples, tables, to_fit, to_resid):
    blocks = span // LANES
    height = ROWS * blocks
    x_ref, at = samples
    taps_ref, first_ref, last_ref, first, last = tables
    if to_fit:
        fit_ref, out_at = to_fit
    if to_resid:
        resid_ref, k, piece_at = to_resid
    lane = lax.broadcasted_iota(jnp.int32, (ROWS, LANES), 1)
    row = lax.broadcasted_iota(jnp.int32, (ROWS, LANES), 0)
    low = lane < 64

    x = x_ref[:, aligned(at - LANES, span + 2 * LANES)]
    parts = thirds(x)

    def cut(m, b):
        return parts[m][:, b * LANES : (b + 1) * LANES]

    rows = [
        jnp.concatenate([cut(m, b + 1), jnp.where(low, cut(m, b + 2), cut(m, b))], axis=1)
        for m in range(3)
        for b in range(blocks)
    ]
    fit = jnp.dot(
        jnp.concatenate(rows, axis=0), taps_ref[...], preferred_element_type=jnp.float32
    )
    fit = fit[:height] + (fit[height : 2 * height] + fit[2 * height :])
    since = first - mark
    until = last - mark
    for b in range(blocks):
        part = fit[b * ROWS : (b + 1) * ROWS]
        moment = lane + b * LANES
        inside = (moment >= since) & (moment < until)
        smooth = part[:, :LANES] * SMOOTH_SCALE
        if to_fit:
            to = aligned(out_at + b * LANES, LANES)
            fit_ref[0, :, to] = jnp.where(inside, smooth, 0.0)
            fit_ref[1, :, to] = jnp.where(inside, part[:, LANES:] * SLOPE_SCALE, 0.0)
        if to_resid:
            resid = x[:, (b + 1) * LANES : (b + 2) * LANES] - smooth
            resid_ref[k, :, aligned(piece_at + b * LANES, LANES)] = jnp.where(inside, resid, 0.0)

    def starts_here(a):
        return (a > mark - HALF) & (a < mark + span)

    def stops_here(z):
        return (z > mark) & (z < mark + span + HALF)

    holds = False
    for r in range(ROWS):
        holds = holds | starts_here(first_ref[group * ROWS + r])
        holds = holds | stops_here(last_ref[group * ROWS + r])

    @pl.when(holds)
    def _():
        def mend(r, left, centre, side):
            b = (left + LANES) // LANES - 1
            v = x_ref[:, aligned(at + b * LANES, 2 * LANES)]
            j = lax.broadcasted_iota(jnp.int32, (ROWS, 2 * LANES), 1) + (b * LANES - centre)
            w = jnp.where((j >= -HALF) & (j <= HALF), v, 0.0)
            f = jnp.clip(j, -HALF, HALF).astype(jnp.float32)
            level = jnp.sum(w, axis=1, keepdims=True) * (1.0 / TAPS)
            tilt = jnp.sum(w * f, axis=1, keepdims=True) * (1.0 / SECOND)
            curve = f * f - CENTRE_SQ
            bend = jnp.sum(w * curve, axis=1, keepdims=True) * (1.0 / FOURTH)
            smooth = level + tilt * f + bend * curve
            slope = HALF * (tilt + 2.0 * f * bend)
            held = (j * side >= 1) & (j * side <= HALF)
            for h in range(2):

                @pl.when((b + h >= 0) & (b + h < blocks))
                def _():
                    part = slice(h * LANES, (h + 1) * LANES)
                    to = held[:, part] & (row == r)
                    if to_fit:
                        at_fit = aligned(out_at + (b + h) * LANES, LANES)
                        fit_ref[0, :, at_fit] = jnp.where(
                            to, smooth[:, part], fit_ref[0, :, at_fit]
                        )
                        fit_ref[1, :, at_fit] = jnp.where(to, slope[:, part], fit_ref[1, :, at_fit])
                    if to_resid:
                        at_piece = aligned(piece_at + (b + h) * LANES, LANES)
                        resid_ref[k, :, at_piece] = jnp.where(
                            to, v[:, part] - smooth[:, part], resid_ref[k, :, at_piece]
                        )

        def series(r, carry):
            a = first_ref[group * ROWS + r]
            z = last_ref[group * ROWS + r]

            @pl.when(starts_here(a))
            def _():
                mend(r, a - mark, a - mark + HALF, -1)

            @pl.when(stops_here(z))
            def _():
                mend(r, z - mark - TAPS, z - mark - HALF - 1, 1)

            return carry

        lax.fori_loop(0, ROWS, series, 0)


def cut_kernel(plan, signal_ref, *refs):
    base, span, _ = plan
    pieces, edges, sems = refs[:GROUPS], refs[GROUPS : GROUPS + 2], refs[-1]
    width = signal_ref.shape[1]
    mine = lax.axis_index("series")
    core = lax.axis_index("core")
    copies = [
        pltpu.make_async_copy(
            signal_ref.at[
                :, aligned(base - LANES + (mine + k) % GROUPS * span, span + 2 * LANES)
            ],
            pieces[k],
            sems.at[k],
        )
        for k in (2, 1, 3, 0)
    ]
    for n, start in enumerate(((1 - core) * (width - LANES), core * (width - LANES))):
        copies.append(
            pltpu.make_async_copy(
                signal_ref.at[:, aligned(start, LANES)], edges[n], sems.at[GROUPS + n]
            )
        )
    for copy in copies:
        copy.start()
    for copy in copies:
        copy.wait()


def cut_chunk(plan, signal):
    rows, _ = signal.shape
    part = jax.ShapeDtypeStruct((rows, plan[1] + 2 * LANES), jnp.float32)
    edge = jax.ShapeDtypeStruct((rows, LANES), jnp.float32)
    return pl.pallas_call(
        functools.partial(cut_kernel, plan),
        in_specs=[pl.BlockSpec(memory_space=pltpu.HBM)],
        out_specs=[pl.BlockSpec(memory_space=pltpu.VMEM)] * (GROUPS + 2),
        out_shape=[part] * GROUPS + [edge] * 2,
        scratch_shapes=[pltpu.SemaphoreType.DMA((GROUPS + 2,))],
        compiler_params=pltpu.CompilerParams(vmem_limit_bytes=8 * MIB),
        cost_estimate=pl.CostEstimate(
            flops=0, bytes_accessed=rows * plan[1] * 32, transcendentals=0
        ),
        name="cut_early",
    )(pltpu.with_memory_space_constraint(signal, pltpu.HBM))


def fit_kernel(plan, fits, resids, ends, *refs):
    base, span, count = plan
    refs = list(refs)
    whole = ends and base == 0
    first_hbm, last_hbm, signal_ref, taps_hbm = refs[:4]
    refs = refs[4:]
    if ends:
        halo_refs, refs = refs[:2], refs[2:]
    if fits:
        fit_hbm, refs = refs[:2], refs[2:]
    if resids:
        outs, refs = refs[:GROUPS], refs[GROUPS:]
    x_ref, taps_ref, first_ref, last_ref, in_sems, side_sems = refs[:6]
    refs = refs[6:]
    if fits:
        fit_ref, out_sems = refs[:2]
        refs = refs[2:]
    if resids:
        resid_ref = refs[0]

    width = signal_ref.shape[1]
    per = count // GROUPS
    half = count // 2
    mine = lax.axis_index("series")
    begin = lax.axis_index(TIME) * width
    core = lax.axis_index("core")

    def place(n):
        return LANES + n * span + (2 * LANES * (n // half) if ends and not whole else 0)

    def source(n):
        return lax.rem(base + n * span, width) if ends and not whole else base + n * span

    def fetch(n):
        return pltpu.make_async_copy(
            signal_ref.at[:, aligned(source(n), span)],
            x_ref.at[:, aligned(place(n), span)],
            in_sems.at[n],
        )

    middle = place(half)
    tail = place(count - 1) + span
    after = (base + count * span) % width
    sides = [(first_hbm, first_ref), (last_hbm, last_ref), (taps_hbm, taps_ref)]
    if not whole:
        sides += [
            (signal_ref.at[:, pl.ds(base - LANES, LANES)], x_ref.at[:, pl.ds(0, LANES)]),
            (signal_ref.at[:, pl.ds(after, LANES)], x_ref.at[:, pl.ds(tail, LANES)]),
        ]
    if ends:
        at_left, at_right = (0, tail) if whole else (middle - LANES, middle - 2 * LANES)
        across = core * (at_left - at_right)
        sides += [
            (halo_refs[0], x_ref.at[:, aligned(at_right + across, LANES)]),
            (halo_refs[1], x_ref.at[:, aligned(at_left - across, LANES)]),
        ]
    sides = [pltpu.make_async_copy(a, b, side_sems.at[n]) for n, (a, b) in enumerate(sides)]
    for copy in sides:
        copy.start()
    for n in range(count):
        fetch(n).start()

    def give(n, kind):
        return pltpu.make_async_copy(
            fit_ref.at[kind, :, aligned(n * span, span)],
            fit_hbm[kind].at[:, aligned(source(n), span)],
            out_sems.at[kind, n],
        )

    for copy in sides:
        copy.wait()
    fetch(0).wait()

    first, last = ends_of(mine, first_ref, last_ref)

    def body(n, carry):
        k = (n // per + GROUPS - mine) % GROUPS

        @pl.when(n + 1 < count)
        def _():
            fetch(n + 1).wait()

        fit_span(
            span,
            begin + source(n),
            mine,
            (x_ref, place(n)),
            (taps_ref, first_ref, last_ref, first, last),
            (fit_ref, n * span) if fits else None,
            (resid_ref, k, n % per * span) if resids else None,
        )
        if fits:
            give(n, 0).start()
            give(n, 1).start()
        return carry

    lax.fori_loop(0, count, body, 0)
    if resids:
        for kk in range(GROUPS):
            outs[kk][...] = resid_ref[kk]
    if fits:
        for n in range(count):
            give(n, 0).wait()
            give(n, 1).wait()


def fit_steps(plan, first, last, signal, taps, fits, resids, halos):
    base, span, count = plan
    rows, width = signal.shape
    ends = halos is not None
    margins = 4 if ends and base else 2
    if not fits:
        taps = taps[:, :LANES]
    hbm = pl.BlockSpec(memory_space=pltpu.HBM)
    vmem = pl.BlockSpec(memory_space=pltpu.VMEM)
    loose = pl.BlockSpec(memory_space=pl.ANY)
    args = [pltpu.with_memory_space_constraint(a, pltpu.HBM) for a in (first, last, signal, taps)]
    args += list(halos or ())
    wide = jax.ShapeDtypeStruct((rows, width), jnp.float32)
    part = jax.ShapeDtypeStruct((rows, count // GROUPS * span), jnp.float32)
    scratch = [
        pltpu.VMEM((rows, count * span + margins * LANES), jnp.float32),
        pltpu.VMEM(taps.shape, taps.dtype),
        pltpu.SMEM(first.shape, jnp.int32),
        pltpu.SMEM(last.shape, jnp.int32),
        pltpu.SemaphoreType.DMA((count,)),
        pltpu.SemaphoreType.DMA((7,)),
    ]
    if fits:
        scratch += [
            pltpu.VMEM((2, rows, count * span), jnp.float32),
            pltpu.SemaphoreType.DMA((2, count)),
        ]
    if resids:
        scratch += [pltpu.VMEM((GROUPS, rows, count // GROUPS * span), jnp.float32)]
    return pl.pallas_call(
        functools.partial(fit_kernel, plan, fits, resids, ends),
        in_specs=[hbm] * 4 + [loose] * len(halos or ()),
        out_specs=[hbm] * (2 * fits) + [vmem] * (GROUPS * resids),
        out_shape=[wide] * (2 * fits) + [part] * (GROUPS * resids),
        scratch_shapes=scratch,
        compiler_params=pltpu.CompilerParams(vmem_limit_bytes=16 * MIB),
        cost_estimate=pl.CostEstimate(
            flops=count * 3 * rows * span * 256 * 4,
            bytes_accessed=count * rows * span * 4 * 4,
            transcendentals=0,
        ),
    )(*args)


def stacked(stack_ref, group, x):
    at = pl.multiple_of(group * ROWS, ROWS)
    a = x.astype(jnp.bfloat16)
    stack_ref[pl.ds(at, ROWS)] = a
    stack_ref[pl.ds(64 + at, ROWS)] = (x - a.astype(jnp.float32)).astype(jnp.bfloat16)


def product(stack_ref, so_far_ref, spread, out_ref):
    both = lax.dot_general(
        stack_ref[...],
        stack_ref[...],
        (((1,), (1,)), ((), ())),
        preferred_element_type=jnp.float32,
    )
    gram = both[:64] + both[64:]
    gram = gram + pltpu.roll(gram, 64, 1)
    low = lax.broadcasted_iota(jnp.int32, (8, LANES), 1) < 64
    for g in range(GROUPS):
        rows = jnp.where(low, gram[16 * g : 16 * g + 8], gram[16 * g + 8 : 16 * g + 16])
        if so_far_ref is not None:
            rows = rows + so_far_ref[g]
        if spread:
            for n in range(spread):
                out_ref[n, g] = rows
        else:
            out_ref[g] = rows


def raw_gram_kernel(plan, width, first_hbm, last_hbm, taps_hbm, *refs):
    base, span, _ = plan
    pieces, refs = refs[:GROUPS], refs[GROUPS:]
    out_ref, x_ref, resid_ref, stack_ref, taps_ref, first_ref, last_ref, sems = refs
    mine = lax.axis_index("series")
    mark = lax.axis_index(TIME) * width + base + mine * span
    copies = [
        pltpu.make_async_copy(a, b, sems.at[n])
        for n, (a, b) in enumerate(
            ((first_hbm, first_ref), (last_hbm, last_ref), (taps_hbm, taps_ref))
        )
    ]
    for copy in copies:
        copy.start()
    for k in range(GROUPS):
        x_ref[k] = pieces[k][...]
    for copy in copies:
        copy.wait()

    def body(k, carry):
        group = (mine + GROUPS - k) % GROUPS
        first, last = ends_of(group, first_ref, last_ref)
        fit_span(
            span,
            mark,
            group,
            (x_ref.at[k], LANES),
            (taps_ref, first_ref, last_ref, first, last),
            None,
            (resid_ref, 0, 0),
        )
        stacked(stack_ref, group, resid_ref[0])
        return carry

    lax.fori_loop(0, GROUPS, body, 0)
    product(stack_ref, None, None, out_ref)


def raw_gram_of(plan, width, first, last, taps, pieces):
    _, span, _ = plan
    taps = taps[:, :LANES]
    hbm = pl.BlockSpec(memory_space=pltpu.HBM)
    vmem = pl.BlockSpec(memory_space=pltpu.VMEM)
    args = [pltpu.with_memory_space_constraint(a, pltpu.HBM) for a in (first, last, taps)]
    return pl.pallas_call(
        functools.partial(raw_gram_kernel, plan, width),
        in_specs=[hbm] * 3 + [vmem] * GROUPS,
        out_specs=vmem,
        out_shape=jax.ShapeDtypeStruct((GROUPS, 8, LANES), jnp.float32),
        scratch_shapes=[
            pltpu.VMEM((GROUPS, ROWS, span + 2 * LANES), jnp.float32),
            pltpu.VMEM((1, ROWS, span), jnp.float32),
            pltpu.VMEM((128, span), jnp.bfloat16),
            pltpu.VMEM(taps.shape, taps.dtype),
            pltpu.SMEM(first.shape, jnp.int32),
            pltpu.SMEM(last.shape, jnp.int32),
            pltpu.SemaphoreType.DMA((3,)),
        ],
        compiler_params=pltpu.CompilerParams(vmem_limit_bytes=16 * MIB),
        cost_estimate=pl.CostEstimate(
            flops=GROUPS * 3 * ROWS * span * 256 * 4,
            bytes_accessed=GROUPS * ROWS * span * 8,
            transcendentals=0,
        ),
    )(*args, *pieces)


def gram_kernel(add, spread, *refs):
    parts, refs = refs[:GROUPS], refs[GROUPS:]
    if add:
        so_far_ref, refs = refs[0], refs[1:]
    out_ref, stack_ref = refs
    mine = lax.axis_index("series")
    for k in range(GROUPS):
        stacked(stack_ref, (mine + GROUPS - k) % GROUPS, parts[k][...])
    product(stack_ref, so_far_ref if add else None, spread, out_ref)


def gram_of(parts, so_far, spread):
    width = parts[0].shape[1]
    vmem = pl.BlockSpec(memory_space=pltpu.VMEM)
    args = list(parts) + ([] if so_far is None else [so_far])
    lead = (spread,) if spread else ()
    return pl.pallas_call(
        functools.partial(gram_kernel, so_far is not None, spread),
        in_specs=[vmem] * len(args),
        out_specs=vmem,
        out_shape=jax.ShapeDtypeStruct((*lead, GROUPS, 8, LANES), jnp.float32),
        scratch_shapes=[pltpu.VMEM((128, width), jnp.bfloat16)],
        compiler_params=pltpu.CompilerParams(vmem_limit_bytes=12 * MIB),
        cost_estimate=pl.CostEstimate(
            flops=128 * 128 * width * 2, bytes_accessed=64 * width * 4, transcendentals=0
        ),
    )(*args)


def packed(rows):
    return jnp.concatenate([rows[:8], rows[8:]], axis=1)


def exchanged(pieces):
    parts = [pieces[0]]
    for k in (2, 1, 3):
        pairs = [(s, (s + k) % GROUPS) for s in range(GROUPS)]
        parts.append(lax.ppermute(pieces[k], "series", pairs))
    return [parts[0], parts[2], parts[1], parts[3]]


def shards(taps, signal, valid_start, valid_end):
    rows, width = signal.shape
    devices = lax.axis_size(TIME)
    taps = jnp.asarray(taps, jnp.bfloat16)
    mine = lax.axis_index("series")
    unit = width // 32
    early, mid = (2 * unit, 4 * unit, GROUPS), (18 * unit, 3 * unit, GROUPS)
    late, whole = (30 * unit, unit, GROUPS), (0, 4 * unit, 8)

    def fit(plan, fits, resids, halos=None):
        return fit_steps(plan, valid_start, valid_end, signal, taps, fits, resids, halos)

    first = lax.dynamic_slice_in_dim(valid_start, mine * rows, rows)[:, None]
    last = lax.dynamic_slice_in_dim(valid_end, mine * rows, rows)[:, None]
    shared = jnp.minimum(last, valid_end[None, :])
    shared = shared - jnp.maximum(first, valid_start[None, :])
    shared = packed(shared.astype(jnp.float32))

    *pieces, near, far = cut_chunk(early, signal)
    parts = exchanged(pieces)
    parts_mid = exchanged(fit(mid, False, True))
    near = lax.ppermute(near, TIME, [(t, t ^ 1) for t in range(devices)])
    pairs = [(t, t + 1) for t in range(1, devices - 1, 2)]
    far = lax.ppermute(far, TIME, pairs + [(b, a) for a, b in pairs])
    halos = (near, far)
    gram = raw_gram_of(early, width, valid_start, valid_end, taps, parts)
    parts = exchanged(fit(late, False, True, halos))
    gram = gram_of(parts_mid, gram, None)
    copies = gram_of(parts, gram, devices)
    copies = copies.reshape(devices * GROUPS, 8, LANES)
    copies = lax.all_to_all(copies, (*TIME, "series"), 0, 0, tiled=True)
    smooth, slope = fit(whole, True, False, halos)
    cov = jnp.sum(copies, axis=0) / shared
    return smooth, slope, jnp.concatenate([cov[:, :64], cov[:, 64:]], axis=0)


def solution(mesh):
    split = Mesh(mesh.devices.reshape(4, 4, 2, GROUPS), (*TIME, "series"))
    return jax.shard_map(
        functools.partial(shards, filter_matrix()),
        mesh=split,
        in_specs=(P("series", TIME), P(), P()),
        out_specs=(P("series", TIME), P("series", TIME), P("series", None)),
        check_vma=False,
    )
```

time: 64 us -> 61.3 us (0.958)
  waiting for transfers between devices: 13.5 us -> 11.2 us
    ppermute x9, waiting for transfers between devices: 3.9 us -> 1.34 us  [exchanged(): parts.append(lax.ppermute(pieces[k], 'series', pairs))]
    ppermute x9, starting transfers between devices: 13.2 us -> 11.7 us  [exchanged(): parts.append(lax.ppermute(pieces[k], 'series', pairs))]
    ppermute x1, starting transfers between devices: 0.73 us -> 1.8 us  [shards(): near = lax.ppermute(near, TIME, [(t, t ^ 1) for t in range(devices)])]
    pallas_call x4 -> x5, Pallas kernels: 15.5 us -> 16.3 us  [the longest x3 11.1 us: fit_steps(): pl.pallas_call(functools.partial(fit_kernel, plan, fits, resids, ends), i...]
    pallas_call x3 -> x2, Pallas kernels: 2.49 us -> 1.76 us  [gram_of(): pl.pallas_call(functools.partial(gram_kernel, so_far is not None, spread)...]
  transfers between devices with their start and end apart: 12 -> 12, of which waited for: 5 -> 6; matrix products, arithmetic and copies ran while one was open for 0% -> 0% of each run, Pallas kernels for 22% -> 23%
where the time goes in v10:
time: 61.3 us; the launch traced here: 61 us
  starting transfers between devices  29.8 us (49%)
  Pallas kernels  18.1 us (30%)
  waiting for transfers between devices  11.2 us (18%)
  other arithmetic  0.9 us (1%)
  between operations  0.78 us (1%)
    all_to_all x1, starting transfers between devices, shards(): copies = lax.all_to_all(copies, (*TIME, 'series'), 0, 0, tiled=True)  12.1 us
    ppermute x9, starting transfers between devices, exchanged(): parts.append(lax.ppermute(pieces[k], 'series', pairs))  11.7 us
    pallas_call x3, Pallas kernels, fit_steps(): pl.pallas_call(functools.partial(fit_kernel, plan, fits, resids, ends), i...  11.1 us
    all_to_all x1, waiting for transfers between devices, shards(): copies = lax.all_to_all(copies, (*TIME, 'series'), 0, 0, tiled=True)  7.42 us
    ppermute x1, starting transfers between devices, shards(): far = lax.ppermute(far, TIME, pairs + [(b, a) for a, b in pairs])  4.25 us
    pallas_call x1, Pallas kernels, raw_gram_of(): pl.pallas_call(functools.partial(raw_gram_kernel, plan, width), in_specs=...  3.9 us
    ppermute x1, starting transfers between devices, shards(): near = lax.ppermute(near, TIME, [(t, t ^ 1) for t in range(devices)])  1.8 us
    pallas_call x2, Pallas kernels, gram_of(): pl.pallas_call(functools.partial(gram_kernel, so_far is not None, spread)...  1.76 us
  transfers between devices with their start and end apart: 12, of which 6 were waited for; matrix products, arithmetic and copies ran while one was open for 0% of the time, Pallas kernels for 23%

profile of v10, /device:TPU:1, one launch (start us, length us, event | category | flops | bytes accessed | tf_op | source)
XLA Modules:
  0.0 61.0 jit_solution(1935493725710396800)
XLA Ops:
  0.7 2.6 %shard_map.69 = (f32[16,3072]{1,0:T(8,128)S(1)}, f32[16,3072]{1,0:T(8,128)S(1)}, f32[16,3072]{1,0:T(8,128)S(1)}, f32[16,3072]{1,0:T(8,128)S(1)}) custom-call(s32[64]{0:T(128)} %first_hbm.1, s32[64]{0:T(128)} %last_hbm.1, f32[16,32768]{1,0:T(8,128)} %refs_2_.5, bf16[256,128]{1,0:T(8,128)(2,1)} %constant.15.refs_3_.taps_hbm), custom_call_target="tpu_custom_call" | custom-call | flops 603979776 | bytes 3145728 | tf_op jit(solution)/shard_map/pallas_call | solution.py:344
  3.2 2.1 %collective-permute-start.5 = (f32[16,3072]{1,0:T(8,128)S(1)}, f32[16,3072]{1,0:T(8,128)S(1)}, u32[]{:S(2)}, u32[]{:S(2)}) collective-permute-start(f32[16,3072]{1,0:T(8,128)S(1)} %get-tuple-element.28), channel_id=1, source_target_pairs={{0,1},{1,2},{2,3},{3,0},{4,5},{5,6},{6,7},{7,4},{8,9},{9,10},{10,1... | collective-permute-start | bytes 589832 | tf_op jit(solution)/shard_map/ppermute | solution.py:491
  5.3 1.3 %cut_early.1 = (f32[16,4352]{1,0:T(8,128)S(1)}, f32[16,4352]{1,0:T(8,128)S(1)}, f32[16,4352]{1,0:T(8,128)S(1)}, f32[16,4352]{1,0:T(8,128)S(1)}, f32[16,128]{1,0:T(8,128)S(1)}, /*index=5*/f32[16,128]{1,0:T(8,128)S(1)}) custom-call(f32[16,32768]{1,0:T(8,128)} %refs_2_.5), custom_call_target="tpu_custom_call" | custom-call | bytes 2097152 | tf_op jit(solution)/shard_map/cut_early/pallas_call | solution.py:195
  6.6 1.8 %collective-permute-start.8 = (f32[16,4352]{1,0:T(8,128)S(1)}, f32[16,4352]{1,0:T(8,128)S(1)}, u32[]{:S(2)}, u32[]{:S(2)}) collective-permute-start(f32[16,4352]{1,0:T(8,128)S(1)} %get-tuple-element.32), channel_id=1, source_target_pairs={{0,1},{1,2},{2,3},{3,0},{4,5},{5,6},{6,7},{7,4},{8,9},{9,10},{10,1... | collective-permute-start | bytes 835592 | tf_op jit(solution)/shard_map/ppermute | solution.py:491
  8.4 0.9 %collective-permute-start.9 = (f32[16,4352]{1,0:T(8,128)S(1)}, f32[16,4352]{1,0:T(8,128)S(1)}, u32[]{:S(2)}, u32[]{:S(2)}) collective-permute-start(f32[16,4352]{1,0:T(8,128)S(1)} %get-tuple-element.33), channel_id=1, source_target_pairs={{0,2},{1,3},{2,0},{3,1},{4,6},{5,7},{6,4},{7,5},{8,10},{9,11},{10,... | collective-permute-start | bytes 835592 | tf_op jit(solution)/shard_map/ppermute | solution.py:491
  9.2 2.0 %collective-permute-start.10 = (f32[16,4352]{1,0:T(8,128)S(1)}, f32[16,4352]{1,0:T(8,128)S(1)}, u32[]{:S(2)}, u32[]{:S(2)}) collective-permute-start(f32[16,4352]{1,0:T(8,128)S(1)} %get-tuple-element.34), channel_id=1, source_target_pairs={{0,3},{1,0},{2,1},{3,2},{4,7},{5,4},{6,5},{7,6},{8,11},{9,8},{10,9... | collective-permute-start | bytes 835592 | tf_op jit(solution)/shard_map/ppermute | solution.py:491
  11.2 1.8 %collective-permute-start = (f32[16,128]{1,0:T(8,128)S(1)}, f32[16,128]{1,0:T(8,128)S(1)}, u32[]{:S(2)}, u32[]{:S(2)}) collective-permute-start(f32[16,128]{1,0:T(8,128)S(1)} %get-tuple-element.19), channel_id=1, source_target_pairs={{0,4},{4,0},{8,12},{12,8},{16,20},{20,16},{24,28},{28,24},{32,36},... | collective-permute-start | bytes 24584 | tf_op jit(solution)/shard_map/ppermute | solution.py:516
  13.0 0.8 %collective-permute-done.refs_4_ = f32[16,128]{1,0:T(8,128)S(1)} collective-permute-done((f32[16,128]{1,0:T(8,128)S(1)}, f32[16,128]{1,0:T(8,128)S(1)}, u32[]{:S(2)}, u32[]{:S(2)}) %collective-permute-start) | collective-permute-done | bytes 8224 | tf_op jit(solution)/shard_map/ppermute | solution.py:516
  13.8 4.2 %collective-permute-start.1 = (f32[16,128]{1,0:T(8,128)S(1)}, f32[16,128]{1,0:T(8,128)S(1)}, u32[]{:S(2)}, u32[]{:S(2)}) collective-permute-start(f32[16,128]{1,0:T(8,128)S(1)} %get-tuple-element.20), channel_id=1, source_target_pairs={{4,8},{12,16},{20,24},{28,32},{36,40},{44,48},{52,56},{60,64},{68,... | collective-permute-start | bytes 24584 | tf_op jit(solution)/shard_map/ppermute | solution.py:518
  18.1 1.6 %collective-permute-done.1.refs_5_ = f32[16,128]{1,0:T(8,128)S(1)} collective-permute-done((f32[16,128]{1,0:T(8,128)S(1)}, f32[16,128]{1,0:T(8,128)S(1)}, u32[]{:S(2)}, u32[]{:S(2)}) %collective-permute-start.1) | collective-permute-done | bytes 8224 | tf_op jit(solution)/shard_map/ppermute | solution.py:518
  19.7 0.4 collective-permute-start.6
  20.1 1.6 %collective-permute-start.7 = (f32[16,3072]{1,0:T(8,128)S(1)}, f32[16,3072]{1,0:T(8,128)S(1)}, u32[]{:S(2)}, u32[]{:S(2)}) collective-permute-start(f32[16,3072]{1,0:T(8,128)S(1)} %get-tuple-element.30), channel_id=1, source_target_pairs={{0,3},{1,0},{2,1},{3,2},{4,7},{5,4},{6,5},{7,6},{8,11},{9,8},{10,9... | collective-permute-start | bytes 589832 | tf_op jit(solution)/shard_map/ppermute | solution.py:491
  21.7 0.1 dynamic_slice.7
  21.8 0.1 dynamic_slice.6
  21.8 2.0 %shard_map.68 = (f32[16,1024]{1,0:T(8,128)S(1)}, f32[16,1024]{1,0:T(8,128)S(1)}, f32[16,1024]{1,0:T(8,128)S(1)}, f32[16,1024]{1,0:T(8,128)S(1)}) custom-call(s32[64]{0:T(128)} %first_hbm.1, s32[64]{0:T(128)} %last_hbm.1, f32[16,32768]{1,0:T(8,128)} %refs_2_.5, bf16[256,128]{1,0:T(8,128)(2,1)} %constant.15.refs_3_.taps_hbm, ...), custom_call_target="tpu_custom_call" | custom-call | flops 201326592 | bytes 1048576 | tf_op jit(solution)/shard_map/pallas_call | solution.py:344
  23.8 0.1 collective-permute-start.2
  23.9 0.2 collective-permute-done.9.refs_2_
  24.0 2.3 %collective-permute-start.3 = (f32[16,1024]{1,0:T(8,128)S(1)}, f32[16,1024]{1,0:T(8,128)S(1)}, u32[]{:S(2)}, u32[]{:S(2)}) collective-permute-start(f32[16,1024]{1,0:T(8,128)S(1)} %get-tuple-element.25), channel_id=1, source_target_pairs={{0,2},{1,3},{2,0},{3,1},{4,6},{5,7},{6,4},{7,5},{8,10},{9,11},{10,... | collective-permute-start | bytes 196616 | tf_op jit(solution)/shard_map/ppermute | solution.py:491
  26.4 0.6 %collective-permute-start.4 = (f32[16,1024]{1,0:T(8,128)S(1)}, f32[16,1024]{1,0:T(8,128)S(1)}, u32[]{:S(2)}, u32[]{:S(2)}) collective-permute-start(f32[16,1024]{1,0:T(8,128)S(1)} %get-tuple-element.26), channel_id=1, source_target_pairs={{0,3},{1,0},{2,1},{3,2},{4,7},{5,4},{6,5},{7,6},{8,11},{9,8},{10,9... | collective-permute-start | bytes 196616 | tf_op jit(solution)/shard_map/ppermute | solution.py:491
  27.0 3.9 %shard_map.70.refs_4_ = f32[4,8,128]{2,1,0:T(8,128)S(1)} custom-call(s32[64]{0:T(128)} %first_hbm.1, s32[64]{0:T(128)} %last_hbm.1, bf16[256,128]{1,0:T(8,128)(2,1)} %constant.15.refs_3_.taps_hbm, f32[16,4352]{1,0:T(8,128)S(1)} %get-tuple-element.31.refs_0_, f32[16,4352]{1,0:T(8,128)S(1)} %collective-permute-done.8.refs_1_, ...), custom_call_target="tpu_custom_call" | custom-call | flops 805306368 | bytes 2097152 | tf_op jit(solution)/shard_map/pallas_call | solution.py:431
  30.9 0.1 collective-permute-done.7.refs_3_
  31.0 0.6 shard_map.71.refs_4_
  31.6 1.1 %collective-permute-done.4.refs_3_ = f32[16,1024]{1,0:T(8,128)S(1)} collective-permute-done((f32[16,1024]{1,0:T(8,128)S(1)}, f32[16,1024]{1,0:T(8,128)S(1)}, u32[]{:S(2)}, u32[]{:S(2)}) %collective-permute-start.4) | collective-permute-done | bytes 65568 | tf_op jit(solution)/shard_map/ppermute | solution.py:491
  32.7 1.2 %shard_map.72 = f32[32,4,8,128]{3,2,1,0:T(8,128)} custom-call(f32[16,1024]{1,0:T(8,128)S(1)} %get-tuple-element.23.refs_0_, f32[16,1024]{1,0:T(8,128)S(1)} %collective-permute-done.2.refs_1_, f32[16,1024]{1,0:T(8,128)S(1)} %collective-permute-done.3.refs_2_, f32[16,1024]{1,0:T(8,128)S(1)} %collective-permute-done.4.refs_3_, f32[4,8,128]{2,1,0:T(8,128)S(1)} %shard_map.71.refs_4_), custom_call_target="tpu_custom_call" | custom-call | flops 33554432 | bytes 262144 | tf_op jit(solution)/shard_map/pallas_call | solution.py:470
  33.9 12.1 %all-to-all-start = ((f32[128,8,128]{2,1,0:T(8,128)}), f32[128,8,128]{2,1,0:T(8,128)S(1)}, u32[]{:S(2)}, u32[]{:S(2)}) async-start(f32[128,8,128]{2,1,0:T(8,128)} %bitcast), calls=%async_computation | async-start | bytes 1048576 | tf_op jit(solution)/shard_map/all_to_all | solution.py:525
  46.0 0.1 subtract_convert_fusion
  46.1 6.6 %shard_map.67 = (f32[16,32768]{1,0:T(8,128)}, f32[16,32768]{1,0:T(8,128)}) custom-call(s32[64]{0:T(128)} %first_hbm.1, s32[64]{0:T(128)} %last_hbm.1, f32[16,32768]{1,0:T(8,128)} %refs_2_.5, bf16[256,256]{1,0:T(8,128)(2,1)} %constant.14.clone.refs_3_, f32[16,128]{1,0:T(8,128)S(1)} %collective-permute-done.refs_4_, f32[16,128]{1,0:T(8,128)S(1)} %collective-permute-done.1.refs_5_), custom_call_target="tpu_custom_call" | custom-call | flops 1610612736 | bytes 8388608 | tf_op jit(solution)/shard_map/pallas_call | solution.py:344
  52.7 7.4 %all-to-all-done = f32[128,8,128]{2,1,0:T(8,128)S(1)} async-done(((f32[128,8,128]{2,1,0:T(8,128)}), f32[128,8,128]{2,1,0:T(8,128)S(1)}, u32[]{:S(2)}, u32[]{:S(2)}) %all-to-all-start) | async-done | bytes 524320 | tf_op jit(solution)/shard_map/all_to_all | solution.py:525
  60.1 0.1 reduce_sum.9
  60.2 0.1 maximum_divide_fusion
  60.3 0.1 fusion.1
  60.4 0.6 pad_maximum_fusion
  (15 shorter events, 0.0 us)
Async XLA Ops:
  0.6 21.1 %copy-start.2 = (s32[64]{0:T(128)S(1)}, s32[64]{0:T(128)}, u32[]{:S(2)}) copy-start(s32[64]{0:T(128)} %last_hbm.1) | copy-start | bytes 772
  0.6 21.0 %copy-start = (s32[64]{0:T(128)S(1)}, s32[64]{0:T(128)}, u32[]{:S(2)}) copy-start(s32[64]{0:T(128)} %first_hbm.1) | copy-start | bytes 772
  3.2 16.9 %collective-permute-start.5 = (f32[16,3072]{1,0:T(8,128)S(1)}, f32[16,3072]{1,0:T(8,128)S(1)}, u32[]{:S(2)}, u32[]{:S(2)}) collective-permute-start(f32[16,3072]{1,0:T(8,128)S(1)} %get-tuple-element.28), channel_id=1, source_target_pairs={{0,1},{1,2},{2,3},{3,0},{4,5},{5,6},{6,7},{7,4},{8,9},{9,10},{10,1... | collective-permute-start | bytes 589832 | tf_op jit(solution)/shard_map/ppermute | solution.py:491
  6.6 17.2 %collective-permute-start.8 = (f32[16,4352]{1,0:T(8,128)S(1)}, f32[16,4352]{1,0:T(8,128)S(1)}, u32[]{:S(2)}, u32[]{:S(2)}) collective-permute-start(f32[16,4352]{1,0:T(8,128)S(1)} %get-tuple-element.32), channel_id=1, source_target_pairs={{0,1},{1,2},{2,3},{3,0},{4,5},{5,6},{6,7},{7,4},{8,9},{9,10},{10,1... | collective-permute-start | bytes 835592 | tf_op jit(solution)/shard_map/ppermute | solution.py:491
  8.4 15.7 %collective-permute-start.9 = (f32[16,4352]{1,0:T(8,128)S(1)}, f32[16,4352]{1,0:T(8,128)S(1)}, u32[]{:S(2)}, u32[]{:S(2)}) collective-permute-start(f32[16,4352]{1,0:T(8,128)S(1)} %get-tuple-element.33), channel_id=1, source_target_pairs={{0,2},{1,3},{2,0},{3,1},{4,6},{5,7},{6,4},{7,5},{8,10},{9,11},{10,... | collective-permute-start | bytes 835592 | tf_op jit(solution)/shard_map/ppermute | solution.py:491
  9.2 17.1 %collective-permute-start.10 = (f32[16,4352]{1,0:T(8,128)S(1)}, f32[16,4352]{1,0:T(8,128)S(1)}, u32[]{:S(2)}, u32[]{:S(2)}) collective-permute-start(f32[16,4352]{1,0:T(8,128)S(1)} %get-tuple-element.34), channel_id=1, source_target_pairs={{0,3},{1,0},{2,1},{3,2},{4,7},{5,4},{6,5},{7,6},{8,11},{9,8},{10,9... | collective-permute-start | bytes 835592 | tf_op jit(solution)/shard_map/ppermute | solution.py:491
  11.2 2.6 %collective-permute-start = (f32[16,128]{1,0:T(8,128)S(1)}, f32[16,128]{1,0:T(8,128)S(1)}, u32[]{:S(2)}, u32[]{:S(2)}) collective-permute-start(f32[16,128]{1,0:T(8,128)S(1)} %get-tuple-element.19), channel_id=1, source_target_pairs={{0,4},{4,0},{8,12},{12,8},{16,20},{20,16},{24,28},{28,24},{32,36},... | collective-permute-start | bytes 24584 | tf_op jit(solution)/shard_map/ppermute | solution.py:516
  13.8 5.9 %collective-permute-start.1 = (f32[16,128]{1,0:T(8,128)S(1)}, f32[16,128]{1,0:T(8,128)S(1)}, u32[]{:S(2)}, u32[]{:S(2)}) collective-permute-start(f32[16,128]{1,0:T(8,128)S(1)} %get-tuple-element.20), channel_id=1, source_target_pairs={{4,8},{12,16},{20,24},{28,32},{36,40},{44,48},{52,56},{60,64},{68,... | collective-permute-start | bytes 24584 | tf_op jit(solution)/shard_map/ppermute | solution.py:518
  19.7 11.2 %collective-permute-start.6 = (f32[16,3072]{1,0:T(8,128)S(1)}, f32[16,3072]{1,0:T(8,128)S(1)}, u32[]{:S(2)}, u32[]{:S(2)}) collective-permute-start(f32[16,3072]{1,0:T(8,128)S(1)} %get-tuple-element.29), channel_id=1, source_target_pairs={{0,2},{1,3},{2,0},{3,1},{4,6},{5,7},{6,4},{7,5},{8,10},{9,11},{10,... | collective-permute-start | bytes 589832 | tf_op jit(solution)/shard_map/ppermute | solution.py:491
  20.1 10.9 %collective-permute-start.7 = (f32[16,3072]{1,0:T(8,128)S(1)}, f32[16,3072]{1,0:T(8,128)S(1)}, u32[]{:S(2)}, u32[]{:S(2)}) collective-permute-start(f32[16,3072]{1,0:T(8,128)S(1)} %get-tuple-element.30), channel_id=1, source_target_pairs={{0,3},{1,0},{2,1},{3,2},{4,7},{5,4},{6,5},{7,6},{8,11},{9,8},{10,9... | collective-permute-start | bytes 589832 | tf_op jit(solution)/shard_map/ppermute | solution.py:491
  23.8 7.8 %collective-permute-start.2 = (f32[16,1024]{1,0:T(8,128)S(1)}, f32[16,1024]{1,0:T(8,128)S(1)}, u32[]{:S(2)}, u32[]{:S(2)}) collective-permute-start(f32[16,1024]{1,0:T(8,128)S(1)} %get-tuple-element.24), channel_id=1, source_target_pairs={{0,1},{1,2},{2,3},{3,0},{4,5},{5,6},{6,7},{7,4},{8,9},{9,10},{10,1... | collective-permute-start | bytes 196616 | tf_op jit(solution)/shard_map/ppermute | solution.py:491
  24.0 7.5 %collective-permute-start.3 = (f32[16,1024]{1,0:T(8,128)S(1)}, f32[16,1024]{1,0:T(8,128)S(1)}, u32[]{:S(2)}, u32[]{:S(2)}) collective-permute-start(f32[16,1024]{1,0:T(8,128)S(1)} %get-tuple-element.25), channel_id=1, source_target_pairs={{0,2},{1,3},{2,0},{3,1},{4,6},{5,7},{6,4},{7,5},{8,10},{9,11},{10,... | collective-permute-start | bytes 196616 | tf_op jit(solution)/shard_map/ppermute | solution.py:491
  26.4 6.3 %collective-permute-start.4 = (f32[16,1024]{1,0:T(8,128)S(1)}, f32[16,1024]{1,0:T(8,128)S(1)}, u32[]{:S(2)}, u32[]{:S(2)}) collective-permute-start(f32[16,1024]{1,0:T(8,128)S(1)} %get-tuple-element.26), channel_id=1, source_target_pairs={{0,3},{1,0},{2,1},{3,2},{4,7},{5,4},{6,5},{7,6},{8,11},{9,8},{10,9... | collective-permute-start | bytes 196616 | tf_op jit(solution)/shard_map/ppermute | solution.py:491
  27.0 19.0 %copy-start.1 = (s32[64]{0:T(128)S(1)}, s32[64]{0:T(128)}, u32[]{:S(2)}) copy-start(s32[64]{0:T(128)} %first_hbm.1) | copy-start | bytes 772
  27.0 19.0 %copy-start.3 = (s32[64]{0:T(128)S(1)}, s32[64]{0:T(128)}, u32[]{:S(2)}) copy-start(s32[64]{0:T(128)} %last_hbm.1) | copy-start | bytes 772
  33.9 26.2 %all-to-all-start = ((f32[128,8,128]{2,1,0:T(8,128)}), f32[128,8,128]{2,1,0:T(8,128)S(1)}, u32[]{:S(2)}, u32[]{:S(2)}) async-start(f32[128,8,128]{2,1,0:T(8,128)} %bitcast), calls=%async_computation | async-start | bytes 1048576 | tf_op jit(solution)/shard_map/all_to_all | solution.py:525

commit v11 on v10

--- a/solution.py
+++ b/solution.py
@@ -157,47 +157,63 @@
 
             return carry
 
-        lax.fori_loop(0, ROWS, series, 0)
+        def bunch(q, carry):
+            some = False
+            for r in range(4):
+                some = some | starts_here(first_ref[group * ROWS + 4 * q + r])
+                some = some | stops_here(last_ref[group * ROWS + 4 * q + r])
+
+            @pl.when(some)
+            def _():
+                lax.fori_loop(4 * q, 4 * q + 4, series, 0)
+
+            return carry
+
+        lax.fori_loop(0, ROWS // 4, bunch, 0)
 
 
 def cut_kernel(plan, signal_ref, *refs):
     base, span, _ = plan
-    pieces, edges, sems = refs[:GROUPS], refs[GROUPS : GROUPS + 2], refs[-1]
+    pieces, edges, (side_ref, sems) = refs[:GROUPS], refs[GROUPS : GROUPS + 2], refs[-2:]
     width = signal_ref.shape[1]
     mine = lax.axis_index("series")
     core = lax.axis_index("core")
-    copies = [
-        pltpu.make_async_copy(
-            signal_ref.at[
-                :, aligned(base - LANES + (mine + k) % GROUPS * span, span + 2 * LANES)
-            ],
-            pieces[k],
-            sems.at[k],
+    copies = []
+
+    def move(start, size, to):
+        copy = pltpu.make_async_copy(
+            signal_ref.at[:, aligned(start, size)], to, sems.at[len(copies)]
         )
-        for k in (2, 1, 3, 0)
-    ]
-    for n, start in enumerate(((1 - core) * (width - LANES), core * (width - LANES))):
-        copies.append(
-            pltpu.make_async_copy(
-                signal_ref.at[:, aligned(start, LANES)], edges[n], sems.at[GROUPS + n]
-            )
-        )
-    for copy in copies:
         copy.start()
+        copies.append(copy)
+
+    for k in (2, 1, 3, 0):
+        start = base + (mine + k) % GROUPS * span
+        move(start - LANES, LANES, side_ref.at[2 * k])
+        move(start + span, LANES, side_ref.at[2 * k + 1])
+        move(start, span, pieces[k].at[:, pl.ds(0, span)])
+    move((1 - core) * (width - LANES), LANES, edges[0])
+    move(core * (width - LANES), LANES, edges[1])
     for copy in copies:
         copy.wait()
+    low = lax.broadcasted_iota(jnp.int32, edges[0].shape, 1) < 64
+    for k in range(GROUPS):
+        pieces[k][:, span:] = jnp.where(low, side_ref[2 * k + 1], side_ref[2 * k])
 
 
 def cut_chunk(plan, signal):
     rows, _ = signal.shape
-    part = jax.ShapeDtypeStruct((rows, plan[1] + 2 * LANES), jnp.float32)
+    part = jax.ShapeDtypeStruct((rows, plan[1] + LANES), jnp.float32)
     edge = jax.ShapeDtypeStruct((rows, LANES), jnp.float32)
     return pl.pallas_call(
         functools.partial(cut_kernel, plan),
         in_specs=[pl.BlockSpec(memory_space=pltpu.HBM)],
         out_specs=[pl.BlockSpec(memory_space=pltpu.VMEM)] * (GROUPS + 2),
         out_shape=[part] * GROUPS + [edge] * 2,
-        scratch_shapes=[pltpu.SemaphoreType.DMA((GROUPS + 2,))],
+        scratch_shapes=[
+            pltpu.VMEM((2 * GROUPS, rows, LANES), jnp.float32),
+            pltpu.SemaphoreType.DMA((3 * GROUPS + 2,)),
+        ],
         compiler_params=pltpu.CompilerParams(vmem_limit_bytes=8 * MIB),
         cost_estimate=pl.CostEstimate(
             flops=0, bytes_accessed=rows * plan[1] * 32, transcendentals=0
@@ -399,7 +415,8 @@
     for copy in copies:
         copy.start()
     for k in range(GROUPS):
-        x_ref[k] = pieces[k][...]
+        x_ref[k, :, :LANES] = pieces[k][:, span:]
+        x_ref[k, :, LANES:] = pieces[k][...]
     for copy in copies:
         copy.wait()
 

time: 61.3 us -> 61 us (level)
  transfers between devices with their start and end apart: 12 -> 12, of which waited for: 6 -> 5; matrix products, arithmetic and copies ran while one was open for 0% -> 0% of each run, Pallas kernels for 23% -> 23%
where the time goes in v11:
time: 61 us; the launch traced here: 60.6 us
  starting transfers between devices  29.4 us (48%)
  Pallas kernels  17.6 us (29%)
  waiting for transfers between devices  11.7 us (19%)
  other arithmetic  0.9 us (1%)
  between operations  0.79 us (1%)
    ppermute x9, starting transfers between devices, exchanged(): parts.append(lax.ppermute(pieces[k], 'series', pairs))  11.8 us
    all_to_all x1, starting transfers between devices, shards(): copies = lax.all_to_all(copies, (*TIME, 'series'), 0, 0, tiled=True)  11.7 us
    pallas_call x3, Pallas kernels, fit_steps(): pl.pallas_call(functools.partial(fit_kernel, plan, fits, resids, ends), i...  10.8 us
    all_to_all x1, waiting for transfers between devices, shards(): copies = lax.all_to_all(copies, (*TIME, 'series'), 0, 0, tiled=True)  7.76 us
    ppermute x1, starting transfers between devices, shards(): far = lax.ppermute(far, TIME, pairs + [(b, a) for a, b in pairs])  4.08 us
    pallas_call x1, Pallas kernels, raw_gram_of(): pl.pallas_call(functools.partial(raw_gram_kernel, plan, width), in_specs=...  3.61 us
    ppermute x1, starting transfers between devices, shards(): near = lax.ppermute(near, TIME, [(t, t ^ 1) for t in range(devices)])  1.81 us
    pallas_call x2, Pallas kernels, gram_of(): pl.pallas_call(functools.partial(gram_kernel, so_far is not None, spread)...  1.76 us
  transfers between devices with their start and end apart: 12, of which 5 were waited for; matrix products, arithmetic and copies ran while one was open for 0% of the time, Pallas kernels for 23%

profile of v11, /device:TPU:1, one launch (start us, length us, event | category | flops | bytes accessed | tf_op | source)
XLA Modules:
  0.0 60.6 jit_solution(2808895433124839894)
XLA Ops:
  0.6 0.0 copy-start.2
  0.7 2.6 %shard_map.69 = (f32[16,3072]{1,0:T(8,128)S(1)}, f32[16,3072]{1,0:T(8,128)S(1)}, f32[16,3072]{1,0:T(8,128)S(1)}, f32[16,3072]{1,0:T(8,128)S(1)}) custom-call(s32[64]{0:T(128)} %first_hbm.1, s32[64]{0:T(128)} %last_hbm.1, f32[16,32768]{1,0:T(8,128)} %refs_2_.5, bf16[256,128]{1,0:T(8,128)(2,1)} %constant.15.refs_3_.taps_hbm), custom_call_target="tpu_custom_call" | custom-call | flops 603979776 | bytes 3145728 | tf_op jit(solution)/shard_map/pallas_call | solution.py:360
  3.2 2.1 %collective-permute-start.5 = (f32[16,3072]{1,0:T(8,128)S(1)}, f32[16,3072]{1,0:T(8,128)S(1)}, u32[]{:S(2)}, u32[]{:S(2)}) collective-permute-start(f32[16,3072]{1,0:T(8,128)S(1)} %get-tuple-element.28), channel_id=1, source_target_pairs={{0,1},{1,2},{2,3},{3,0},{4,5},{5,6},{6,7},{7,4},{8,9},{9,10},{10,1... | collective-permute-start | bytes 589832 | tf_op jit(solution)/shard_map/ppermute | solution.py:508
  5.3 1.4 %cut_early.1 = (f32[16,4224]{1,0:T(8,128)S(1)}, f32[16,4224]{1,0:T(8,128)S(1)}, f32[16,4224]{1,0:T(8,128)S(1)}, f32[16,4224]{1,0:T(8,128)S(1)}, f32[16,128]{1,0:T(8,128)S(1)}, /*index=5*/f32[16,128]{1,0:T(8,128)S(1)}) custom-call(f32[16,32768]{1,0:T(8,128)} %refs_2_.5), custom_call_target="tpu_custom_call" | custom-call | bytes 2097152 | tf_op jit(solution)/shard_map/cut_early/pallas_call | solution.py:208
  6.8 1.6 %collective-permute-start.8 = (f32[16,4224]{1,0:T(8,128)S(1)}, f32[16,4224]{1,0:T(8,128)S(1)}, u32[]{:S(2)}, u32[]{:S(2)}) collective-permute-start(f32[16,4224]{1,0:T(8,128)S(1)} %get-tuple-element.32), channel_id=1, source_target_pairs={{0,1},{1,2},{2,3},{3,0},{4,5},{5,6},{6,7},{7,4},{8,9},{9,10},{10,1... | collective-permute-start | bytes 811016 | tf_op jit(solution)/shard_map/ppermute | solution.py:508
  8.4 1.0 %collective-permute-start.9 = (f32[16,4224]{1,0:T(8,128)S(1)}, f32[16,4224]{1,0:T(8,128)S(1)}, u32[]{:S(2)}, u32[]{:S(2)}) collective-permute-start(f32[16,4224]{1,0:T(8,128)S(1)} %get-tuple-element.33), channel_id=1, source_target_pairs={{0,2},{1,3},{2,0},{3,1},{4,6},{5,7},{6,4},{7,5},{8,10},{9,11},{10,... | collective-permute-start | bytes 811016 | tf_op jit(solution)/shard_map/ppermute | solution.py:508
  9.4 2.0 %collective-permute-start.10 = (f32[16,4224]{1,0:T(8,128)S(1)}, f32[16,4224]{1,0:T(8,128)S(1)}, u32[]{:S(2)}, u32[]{:S(2)}) collective-permute-start(f32[16,4224]{1,0:T(8,128)S(1)} %get-tuple-element.34), channel_id=1, source_target_pairs={{0,3},{1,0},{2,1},{3,2},{4,7},{5,4},{6,5},{7,6},{8,11},{9,8},{10,9... | collective-permute-start | bytes 811016 | tf_op jit(solution)/shard_map/ppermute | solution.py:508
  11.4 1.8 %collective-permute-start = (f32[16,128]{1,0:T(8,128)S(1)}, f32[16,128]{1,0:T(8,128)S(1)}, u32[]{:S(2)}, u32[]{:S(2)}) collective-permute-start(f32[16,128]{1,0:T(8,128)S(1)} %get-tuple-element.19), channel_id=1, source_target_pairs={{0,4},{4,0},{8,12},{12,8},{16,20},{20,16},{24,28},{28,24},{32,36},... | collective-permute-start | bytes 24584 | tf_op jit(solution)/shard_map/ppermute | solution.py:533
  13.2 0.8 %collective-permute-done.refs_4_ = f32[16,128]{1,0:T(8,128)S(1)} collective-permute-done((f32[16,128]{1,0:T(8,128)S(1)}, f32[16,128]{1,0:T(8,128)S(1)}, u32[]{:S(2)}, u32[]{:S(2)}) %collective-permute-start) | collective-permute-done | bytes 8224 | tf_op jit(solution)/shard_map/ppermute | solution.py:533
  14.0 4.1 %collective-permute-start.1 = (f32[16,128]{1,0:T(8,128)S(1)}, f32[16,128]{1,0:T(8,128)S(1)}, u32[]{:S(2)}, u32[]{:S(2)}) collective-permute-start(f32[16,128]{1,0:T(8,128)S(1)} %get-tuple-element.20), channel_id=1, source_target_pairs={{4,8},{12,16},{20,24},{28,32},{36,40},{44,48},{52,56},{60,64},{68,... | collective-permute-start | bytes 24584 | tf_op jit(solution)/shard_map/ppermute | solution.py:535
  18.1 1.6 %collective-permute-done.1.refs_5_ = f32[16,128]{1,0:T(8,128)S(1)} collective-permute-done((f32[16,128]{1,0:T(8,128)S(1)}, f32[16,128]{1,0:T(8,128)S(1)}, u32[]{:S(2)}, u32[]{:S(2)}) %collective-permute-start.1) | collective-permute-done | bytes 8224 | tf_op jit(solution)/shard_map/ppermute | solution.py:535
  19.7 0.4 collective-permute-start.6
  20.1 1.6 %collective-permute-start.7 = (f32[16,3072]{1,0:T(8,128)S(1)}, f32[16,3072]{1,0:T(8,128)S(1)}, u32[]{:S(2)}, u32[]{:S(2)}) collective-permute-start(f32[16,3072]{1,0:T(8,128)S(1)} %get-tuple-element.30), channel_id=1, source_target_pairs={{0,3},{1,0},{2,1},{3,2},{4,7},{5,4},{6,5},{7,6},{8,11},{9,8},{10,9... | collective-permute-start | bytes 589832 | tf_op jit(solution)/shard_map/ppermute | solution.py:508
  21.7 0.1 dynamic_slice.7
  21.8 0.1 dynamic_slice.6
  21.8 2.0 %shard_map.68 = (f32[16,1024]{1,0:T(8,128)S(1)}, f32[16,1024]{1,0:T(8,128)S(1)}, f32[16,1024]{1,0:T(8,128)S(1)}, f32[16,1024]{1,0:T(8,128)S(1)}) custom-call(s32[64]{0:T(128)} %first_hbm.1, s32[64]{0:T(128)} %last_hbm.1, f32[16,32768]{1,0:T(8,128)} %refs_2_.5, bf16[256,128]{1,0:T(8,128)(2,1)} %constant.15.refs_3_.taps_hbm, ...), custom_call_target="tpu_custom_call" | custom-call | flops 201326592 | bytes 1048576 | tf_op jit(solution)/shard_map/pallas_call | solution.py:360
  23.8 0.1 collective-permute-start.2
  23.9 2.5 %collective-permute-start.3 = (f32[16,1024]{1,0:T(8,128)S(1)}, f32[16,1024]{1,0:T(8,128)S(1)}, u32[]{:S(2)}, u32[]{:S(2)}) collective-permute-start(f32[16,1024]{1,0:T(8,128)S(1)} %get-tuple-element.25), channel_id=1, source_target_pairs={{0,2},{1,3},{2,0},{3,1},{4,6},{5,7},{6,4},{7,5},{8,10},{9,11},{10,... | collective-permute-start | bytes 196616 | tf_op jit(solution)/shard_map/ppermute | solution.py:508
  26.4 0.6 %collective-permute-start.4 = (f32[16,1024]{1,0:T(8,128)S(1)}, f32[16,1024]{1,0:T(8,128)S(1)}, u32[]{:S(2)}, u32[]{:S(2)}) collective-permute-start(f32[16,1024]{1,0:T(8,128)S(1)} %get-tuple-element.26), channel_id=1, source_target_pairs={{0,3},{1,0},{2,1},{3,2},{4,7},{5,4},{6,5},{7,6},{8,11},{9,8},{10,9... | collective-permute-start | bytes 196616 | tf_op jit(solution)/shard_map/ppermute | solution.py:508
  27.0 3.6 %shard_map.70.refs_4_ = f32[4,8,128]{2,1,0:T(8,128)S(1)} custom-call(s32[64]{0:T(128)} %first_hbm.1, s32[64]{0:T(128)} %last_hbm.1, bf16[256,128]{1,0:T(8,128)(2,1)} %constant.15.refs_3_.taps_hbm, f32[16,4224]{1,0:T(8,128)S(1)} %get-tuple-element.31.refs_0_, f32[16,4224]{1,0:T(8,128)S(1)} %collective-permute-done.8.refs_1_, ...), custom_call_target="tpu_custom_call" | custom-call | flops 805306368 | bytes 2097152 | tf_op jit(solution)/shard_map/pallas_call | solution.py:448
  30.6 0.2 collective-permute-done.7.refs_3_
  30.8 0.6 shard_map.71.refs_4_
  31.4 1.3 %collective-permute-done.4.refs_3_ = f32[16,1024]{1,0:T(8,128)S(1)} collective-permute-done((f32[16,1024]{1,0:T(8,128)S(1)}, f32[16,1024]{1,0:T(8,128)S(1)}, u32[]{:S(2)}, u32[]{:S(2)}) %collective-permute-start.4) | collective-permute-done | bytes 65568 | tf_op jit(solution)/shard_map/ppermute | solution.py:508
  32.7 1.2 %shard_map.72 = f32[32,4,8,128]{3,2,1,0:T(8,128)} custom-call(f32[16,1024]{1,0:T(8,128)S(1)} %get-tuple-element.23.refs_0_, f32[16,1024]{1,0:T(8,128)S(1)} %collective-permute-done.2.refs_1_, f32[16,1024]{1,0:T(8,128)S(1)} %collective-permute-done.3.refs_2_, f32[16,1024]{1,0:T(8,128)S(1)} %collective-permute-done.4.refs_3_, f32[4,8,128]{2,1,0:T(8,128)S(1)} %shard_map.71.refs_4_), custom_call_target="tpu_custom_call" | custom-call | flops 33554432 | bytes 262144 | tf_op jit(solution)/shard_map/pallas_call | solution.py:487
  33.9 11.7 %all-to-all-start = ((f32[128,8,128]{2,1,0:T(8,128)}), f32[128,8,128]{2,1,0:T(8,128)S(1)}, u32[]{:S(2)}, u32[]{:S(2)}) async-start(f32[128,8,128]{2,1,0:T(8,128)} %bitcast), calls=%async_computation | async-start | bytes 1048576 | tf_op jit(solution)/shard_map/all_to_all | solution.py:542
  45.6 0.1 subtract_convert_fusion
  45.7 6.2 %shard_map.67 = (f32[16,32768]{1,0:T(8,128)}, f32[16,32768]{1,0:T(8,128)}) custom-call(s32[64]{0:T(128)} %first_hbm.1, s32[64]{0:T(128)} %last_hbm.1, f32[16,32768]{1,0:T(8,128)} %refs_2_.5, bf16[256,256]{1,0:T(8,128)(2,1)} %constant.14.clone.refs_3_, f32[16,128]{1,0:T(8,128)S(1)} %collective-permute-done.refs_4_, f32[16,128]{1,0:T(8,128)S(1)} %collective-permute-done.1.refs_5_), custom_call_target="tpu_custom_call" | custom-call | flops 1610612736 | bytes 8388608 | tf_op jit(solution)/shard_map/pallas_call | solution.py:360
  52.0 7.8 %all-to-all-done = f32[128,8,128]{2,1,0:T(8,128)S(1)} async-done(((f32[128,8,128]{2,1,0:T(8,128)}), f32[128,8,128]{2,1,0:T(8,128)S(1)}, u32[]{:S(2)}, u32[]{:S(2)}) %all-to-all-start) | async-done | bytes 524320 | tf_op jit(solution)/shard_map/all_to_all | solution.py:542
  59.7 0.1 reduce_sum.9
  59.9 0.1 maximum_divide_fusion
  59.9 0.1 fusion.1
  60.0 0.6 %pad_maximum_fusion = f32[16,64]{1,0:T(8,128)} fusion(f32[8,64]{1,0:T(8,128)S(1)} %get-tuple-element.38, f32[8,64]{1,0:T(8,128)S(1)} %get-tuple-element.37), kind=kLoop, calls=%fused_computation | loop fusion | flops 1024 | bytes 8192 | tf_op jit(solution)/shard_map/concatenate | solution.py:545
  (15 shorter events, 0.0 us)
Async XLA Ops:
  0.6 21.1 %copy-start.2 = (s32[64]{0:T(128)S(1)}, s32[64]{0:T(128)}, u32[]{:S(2)}) copy-start(s32[64]{0:T(128)} %last_hbm.1) | copy-start | bytes 772
  0.6 21.0 %copy-start = (s32[64]{0:T(128)S(1)}, s32[64]{0:T(128)}, u32[]{:S(2)}) copy-start(s32[64]{0:T(128)} %first_hbm.1) | copy-start | bytes 772
  3.2 16.8 %collective-permute-start.5 = (f32[16,3072]{1,0:T(8,128)S(1)}, f32[16,3072]{1,0:T(8,128)S(1)}, u32[]{:S(2)}, u32[]{:S(2)}) collective-permute-start(f32[16,3072]{1,0:T(8,128)S(1)} %get-tuple-element.28), channel_id=1, source_target_pairs={{0,1},{1,2},{2,3},{3,0},{4,5},{5,6},{6,7},{7,4},{8,9},{9,10},{10,1... | collective-permute-start | bytes 589832 | tf_op jit(solution)/shard_map/ppermute | solution.py:508
  6.8 17.0 %collective-permute-start.8 = (f32[16,4224]{1,0:T(8,128)S(1)}, f32[16,4224]{1,0:T(8,128)S(1)}, u32[]{:S(2)}, u32[]{:S(2)}) collective-permute-start(f32[16,4224]{1,0:T(8,128)S(1)} %get-tuple-element.32), channel_id=1, source_target_pairs={{0,1},{1,2},{2,3},{3,0},{4,5},{5,6},{6,7},{7,4},{8,9},{9,10},{10,1... | collective-permute-start | bytes 811016 | tf_op jit(solution)/shard_map/ppermute | solution.py:508
  8.4 15.5 %collective-permute-start.9 = (f32[16,4224]{1,0:T(8,128)S(1)}, f32[16,4224]{1,0:T(8,128)S(1)}, u32[]{:S(2)}, u32[]{:S(2)}) collective-permute-start(f32[16,4224]{1,0:T(8,128)S(1)} %get-tuple-element.33), channel_id=1, source_target_pairs={{0,2},{1,3},{2,0},{3,1},{4,6},{5,7},{6,4},{7,5},{8,10},{9,11},{10,... | collective-permute-start | bytes 811016 | tf_op jit(solution)/shard_map/ppermute | solution.py:508
  9.4 17.0 %collective-permute-start.10 = (f32[16,4224]{1,0:T(8,128)S(1)}, f32[16,4224]{1,0:T(8,128)S(1)}, u32[]{:S(2)}, u32[]{:S(2)}) collective-permute-start(f32[16,4224]{1,0:T(8,128)S(1)} %get-tuple-element.34), channel_id=1, source_target_pairs={{0,3},{1,0},{2,1},{3,2},{4,7},{5,4},{6,5},{7,6},{8,11},{9,8},{10,9... | collective-permute-start | bytes 811016 | tf_op jit(solution)/shard_map/ppermute | solution.py:508
  11.4 2.6 %collective-permute-start = (f32[16,128]{1,0:T(8,128)S(1)}, f32[16,128]{1,0:T(8,128)S(1)}, u32[]{:S(2)}, u32[]{:S(2)}) collective-permute-start(f32[16,128]{1,0:T(8,128)S(1)} %get-tuple-element.19), channel_id=1, source_target_pairs={{0,4},{4,0},{8,12},{12,8},{16,20},{20,16},{24,28},{28,24},{32,36},... | collective-permute-start | bytes 24584 | tf_op jit(solution)/shard_map/ppermute | solution.py:533
  14.0 5.7 %collective-permute-start.1 = (f32[16,128]{1,0:T(8,128)S(1)}, f32[16,128]{1,0:T(8,128)S(1)}, u32[]{:S(2)}, u32[]{:S(2)}) collective-permute-start(f32[16,128]{1,0:T(8,128)S(1)} %get-tuple-element.20), channel_id=1, source_target_pairs={{4,8},{12,16},{20,24},{28,32},{36,40},{44,48},{52,56},{60,64},{68,... | collective-permute-start | bytes 24584 | tf_op jit(solution)/shard_map/ppermute | solution.py:535
  19.7 10.9 %collective-permute-start.6 = (f32[16,3072]{1,0:T(8,128)S(1)}, f32[16,3072]{1,0:T(8,128)S(1)}, u32[]{:S(2)}, u32[]{:S(2)}) collective-permute-start(f32[16,3072]{1,0:T(8,128)S(1)} %get-tuple-element.29), channel_id=1, source_target_pairs={{0,2},{1,3},{2,0},{3,1},{4,6},{5,7},{6,4},{7,5},{8,10},{9,11},{10,... | collective-permute-start | bytes 589832 | tf_op jit(solution)/shard_map/ppermute | solution.py:508
  20.1 10.7 %collective-permute-start.7 = (f32[16,3072]{1,0:T(8,128)S(1)}, f32[16,3072]{1,0:T(8,128)S(1)}, u32[]{:S(2)}, u32[]{:S(2)}) collective-permute-start(f32[16,3072]{1,0:T(8,128)S(1)} %get-tuple-element.30), channel_id=1, source_target_pairs={{0,3},{1,0},{2,1},{3,2},{4,7},{5,4},{6,5},{7,6},{8,11},{9,8},{10,9... | collective-permute-start | bytes 589832 | tf_op jit(solution)/shard_map/ppermute | solution.py:508
  23.8 7.6 %collective-permute-start.2 = (f32[16,1024]{1,0:T(8,128)S(1)}, f32[16,1024]{1,0:T(8,128)S(1)}, u32[]{:S(2)}, u32[]{:S(2)}) collective-permute-start(f32[16,1024]{1,0:T(8,128)S(1)} %get-tuple-element.24), channel_id=1, source_target_pairs={{0,1},{1,2},{2,3},{3,0},{4,5},{5,6},{6,7},{7,4},{8,9},{9,10},{10,1... | collective-permute-start | bytes 196616 | tf_op jit(solution)/shard_map/ppermute | solution.py:508
  23.9 7.5 %collective-permute-start.3 = (f32[16,1024]{1,0:T(8,128)S(1)}, f32[16,1024]{1,0:T(8,128)S(1)}, u32[]{:S(2)}, u32[]{:S(2)}) collective-permute-start(f32[16,1024]{1,0:T(8,128)S(1)} %get-tuple-element.25), channel_id=1, source_target_pairs={{0,2},{1,3},{2,0},{3,1},{4,6},{5,7},{6,4},{7,5},{8,10},{9,11},{10,... | collective-permute-start | bytes 196616 | tf_op jit(solution)/shard_map/ppermute | solution.py:508
  26.4 6.4 %collective-permute-start.4 = (f32[16,1024]{1,0:T(8,128)S(1)}, f32[16,1024]{1,0:T(8,128)S(1)}, u32[]{:S(2)}, u32[]{:S(2)}) collective-permute-start(f32[16,1024]{1,0:T(8,128)S(1)} %get-tuple-element.26), channel_id=1, source_target_pairs={{0,3},{1,0},{2,1},{3,2},{4,7},{5,4},{6,5},{7,6},{8,11},{9,8},{10,9... | collective-permute-start | bytes 196616 | tf_op jit(solution)/shard_map/ppermute | solution.py:508
  27.0 18.6 %copy-start.1 = (s32[64]{0:T(128)S(1)}, s32[64]{0:T(128)}, u32[]{:S(2)}) copy-start(s32[64]{0:T(128)} %first_hbm.1) | copy-start | bytes 772
  27.0 18.7 %copy-start.3 = (s32[64]{0:T(128)S(1)}, s32[64]{0:T(128)}, u32[]{:S(2)}) copy-start(s32[64]{0:T(128)} %last_hbm.1) | copy-start | bytes 772
  33.9 25.8 %all-to-all-start = ((f32[128,8,128]{2,1,0:T(8,128)}), f32[128,8,128]{2,1,0:T(8,128)S(1)}, u32[]{:S(2)}, u32[]{:S(2)}) async-start(f32[128,8,128]{2,1,0:T(8,128)} %bitcast), calls=%async_computation | async-start | bytes 1048576 | tf_op jit(solution)/shard_map/all_to_all | solution.py:542

commit v12 on v11

--- a/solution.py
+++ b/solution.py
@@ -222,14 +222,15 @@
     )(pltpu.with_memory_space_constraint(signal, pltpu.HBM))
 
 
-def fit_kernel(plan, fits, resids, ends, *refs):
+def fit_kernel(plan, fits, resids, ends, chain, *refs):
     base, span, count = plan
     refs = list(refs)
-    whole = ends and base == 0
     first_hbm, last_hbm, signal_ref, taps_hbm = refs[:4]
     refs = refs[4:]
     if ends:
         halo_refs, refs = refs[:2], refs[2:]
+    if chain:
+        refs = refs[2:]
     if fits:
         fit_hbm, refs = refs[:2], refs[2:]
     if resids:
@@ -250,10 +251,10 @@
     core = lax.axis_index("core")
 
     def place(n):
-        return LANES + n * span + (2 * LANES * (n // half) if ends and not whole else 0)
+        return LANES + n * span + (2 * LANES * (n // half) if ends else 0)
 
     def source(n):
-        return lax.rem(base + n * span, width) if ends and not whole else base + n * span
+        return lax.rem(base + n * span, width) if ends else base + n * span
 
     def fetch(n):
         return pltpu.make_async_copy(
@@ -265,14 +266,15 @@
     middle = place(half)
     tail = place(count - 1) + span
     after = (base + count * span) % width
-    sides = [(first_hbm, first_ref), (last_hbm, last_ref), (taps_hbm, taps_ref)]
-    if not whole:
-        sides += [
-            (signal_ref.at[:, pl.ds(base - LANES, LANES)], x_ref.at[:, pl.ds(0, LANES)]),
-            (signal_ref.at[:, pl.ds(after, LANES)], x_ref.at[:, pl.ds(tail, LANES)]),
-        ]
+    sides = [
+        (first_hbm, first_ref),
+        (last_hbm, last_ref),
+        (taps_hbm, taps_ref),
+        (signal_ref.at[:, pl.ds(base - LANES, LANES)], x_ref.at[:, pl.ds(0, LANES)]),
+        (signal_ref.at[:, pl.ds(after, LANES)], x_ref.at[:, pl.ds(tail, LANES)]),
+    ]
     if ends:
-        at_left, at_right = (0, tail) if whole else (middle - LANES, middle - 2 * LANES)
+        at_left, at_right = middle - LANES, middle - 2 * LANES
         across = core * (at_left - at_right)
         sides += [
             (halo_refs[0], x_ref.at[:, aligned(at_right + across, LANES)]),
@@ -328,18 +330,19 @@
             give(n, 1).wait()
 
 
-def fit_steps(plan, first, last, signal, taps, fits, resids, halos):
-    base, span, count = plan
+def fit_steps(plan, first, last, signal, taps, fits, resids, halos, held):
+    _, span, count = plan
     rows, width = signal.shape
     ends = halos is not None
-    margins = 4 if ends and base else 2
+    margins = 4 if ends else 2
     if not fits:
         taps = taps[:, :LANES]
     hbm = pl.BlockSpec(memory_space=pltpu.HBM)
     vmem = pl.BlockSpec(memory_space=pltpu.VMEM)
     loose = pl.BlockSpec(memory_space=pl.ANY)
     args = [pltpu.with_memory_space_constraint(a, pltpu.HBM) for a in (first, last, signal, taps)]
-    args += list(halos or ())
+    args += list(halos or ()) + list(held or ())
+    aliases = {len(args) - 2: 0, len(args) - 1: 1} if held else {}
     wide = jax.ShapeDtypeStruct((rows, width), jnp.float32)
     part = jax.ShapeDtypeStruct((rows, count // GROUPS * span), jnp.float32)
     scratch = [
@@ -358,11 +361,12 @@
     if resids:
         scratch += [pltpu.VMEM((GROUPS, rows, count // GROUPS * span), jnp.float32)]
     return pl.pallas_call(
-        functools.partial(fit_kernel, plan, fits, resids, ends),
-        in_specs=[hbm] * 4 + [loose] * len(halos or ()),
+        functools.partial(fit_kernel, plan, fits, resids, ends, bool(held)),
+        in_specs=[hbm] * 4 + [loose] * len(halos or ()) + [hbm] * len(held or ()),
         out_specs=[hbm] * (2 * fits) + [vmem] * (GROUPS * resids),
         out_shape=[wide] * (2 * fits) + [part] * (GROUPS * resids),
         scratch_shapes=scratch,
+        input_output_aliases=aliases,
         compiler_params=pltpu.CompilerParams(vmem_limit_bytes=16 * MIB),
         cost_estimate=pl.CostEstimate(
             flops=count * 3 * rows * span * 256 * 4,
@@ -497,10 +501,6 @@
     )(*args)
 
 
-def packed(rows):
-    return jnp.concatenate([rows[:8], rows[8:]], axis=1)
-
-
 def exchanged(pieces):
     parts = [pieces[0]]
     for k in (2, 1, 3):
@@ -516,33 +516,40 @@
     mine = lax.axis_index("series")
     unit = width // 32
     early, mid = (2 * unit, 4 * unit, GROUPS), (18 * unit, 3 * unit, GROUPS)
-    late, whole = (30 * unit, unit, GROUPS), (0, 4 * unit, 8)
-
-    def fit(plan, fits, resids, halos=None):
-        return fit_steps(plan, valid_start, valid_end, signal, taps, fits, resids, halos)
+    late = (30 * unit, unit, GROUPS)
+
+    def fit(plan, resids, halos=None, held=None):
+        out = fit_steps(plan, valid_start, valid_end, signal, taps, True, resids, halos, held)
+        return out[:2], out[2:]
 
     first = lax.dynamic_slice_in_dim(valid_start, mine * rows, rows)[:, None]
     last = lax.dynamic_slice_in_dim(valid_end, mine * rows, rows)[:, None]
     shared = jnp.minimum(last, valid_end[None, :])
     shared = shared - jnp.maximum(first, valid_start[None, :])
-    shared = packed(shared.astype(jnp.float32))
+    shared = shared.astype(jnp.float32)
 
     *pieces, near, far = cut_chunk(early, signal)
     parts = exchanged(pieces)
-    parts_mid = exchanged(fit(mid, False, True))
+    held, pieces = fit(mid, True)
+    parts_mid = exchanged(pieces)
     near = lax.ppermute(near, TIME, [(t, t ^ 1) for t in range(devices)])
     pairs = [(t, t + 1) for t in range(1, devices - 1, 2)]
     far = lax.ppermute(far, TIME, pairs + [(b, a) for a, b in pairs])
     halos = (near, far)
     gram = raw_gram_of(early, width, valid_start, valid_end, taps, parts)
-    parts = exchanged(fit(late, False, True, halos))
+    held, pieces = fit(late, True, halos, held)
+    parts = exchanged(pieces)
     gram = gram_of(parts_mid, gram, None)
-    copies = gram_of(parts, gram, devices)
-    copies = copies.reshape(devices * GROUPS, 8, LANES)
-    copies = lax.all_to_all(copies, (*TIME, "series"), 0, 0, tiled=True)
-    smooth, slope = fit(whole, True, False, halos)
-    cov = jnp.sum(copies, axis=0) / shared
-    return smooth, slope, jnp.concatenate([cov[:, :64], cov[:, 64:]], axis=0)
+    copies = gram_of(parts, gram, devices // 2)
+    copies = copies.reshape(devices * GROUPS, 4, LANES)
+    copies = lax.all_to_all(copies, (*TIME[:2], "series", "core"), 0, 0, tiled=True)
+    (smooth, slope), _ = fit(early, False, held=held)
+    own = jnp.sum(copies, axis=0)
+    other = lax.ppermute(own, "core", [(0, 1), (1, 0)])
+    lead = lax.axis_index("core") == 0
+    p, q = jnp.where(lead, own, other), jnp.where(lead, other, own)
+    gram = jnp.concatenate([p[:, :64], q[:, :64], p[:, 64:], q[:, 64:]], axis=0)
+    return smooth, slope, gram / shared
 
 
 def solution(mesh):

time: 61 us -> 62.8 us (1.030)
  waiting for transfers between devices: 11.7 us -> 13 us
  starting transfers between devices: 29.4 us -> 30.3 us
    all_to_all x1, waiting for transfers between devices: 7.76 us -> 10.9 us  [shards(): lax.all_to_all(copies, (*TIME[:2], 'series', 'core'), 0, 0, tiled=True)]
    ppermute x9, waiting for transfers between devices: 1.53 us -> 0.02 us  [exchanged(): parts.append(lax.ppermute(pieces[k], 'series', pairs))]
    ppermute x0 -> x1, starting transfers between devices: none -> 0.81 us  [shards(): other = lax.ppermute(own, 'core', [(0, 1), (1, 0)])]
  transfers between devices with their start and end apart: 12 -> 13, of which waited for: 5 -> 3; matrix products, arithmetic and copies ran while one was open for 0% -> 0% of each run, Pallas kernels for 23% -> 21%
where the time goes in v12:
time: 62.8 us; the launch traced here: 62.5 us
  starting transfers between devices  30.3 us (48%)
  Pallas kernels  17.4 us (28%)
  waiting for transfers between devices  13 us (21%)
  other arithmetic  0.83 us (1%)
  between operations  0.8 us (1%)
    ppermute x9, starting transfers between devices, exchanged(): parts.append(lax.ppermute(pieces[k], 'series', pairs))  12.4 us
    all_to_all x1, starting transfers between devices, shards(): lax.all_to_all(copies, (*TIME[:2], 'series', 'core'), 0, 0, tiled=True)  11.2 us
    all_to_all x1, waiting for transfers between devices, shards(): lax.all_to_all(copies, (*TIME[:2], 'series', 'core'), 0, 0, tiled=True)  10.9 us
    pallas_call x3, Pallas kernels, fit_steps(): pl.pallas_call(functools.partial(fit_kernel, plan, fits, resids, ends, bo...  10.7 us
    ppermute x1, starting transfers between devices, shards(): far = lax.ppermute(far, TIME, pairs + [(b, a) for a, b in pairs])  4.08 us
    pallas_call x1, Pallas kernels, raw_gram_of(): pl.pallas_call(functools.partial(raw_gram_kernel, plan, width), in_specs=...  3.61 us
    ppermute x1, starting transfers between devices, shards(): near = lax.ppermute(near, TIME, [(t, t ^ 1) for t in range(devices)])  1.81 us
    pallas_call x2, Pallas kernels, gram_of(): pl.pallas_call(functools.partial(gram_kernel, so_far is not None, spread)...  1.63 us
  transfers between devices with their start and end apart: 13, of which 3 were waited for; matrix products, arithmetic and copies ran while one was open for 0% of the time, Pallas kernels for 21%

profile of v12, /device:TPU:1, one launch (start us, length us, event | category | flops | bytes accessed | tf_op | source)
XLA Modules:
  0.0 62.5 jit_solution(15520475003008352096)
XLA Ops:
  0.6 3.5 %shard_map.67 = (f32[16,32768]{1,0:T(8,128)}, f32[16,32768]{1,0:T(8,128)}, f32[16,3072]{1,0:T(8,128)S(1)}, f32[16,3072]{1,0:T(8,128)S(1)}, f32[16,3072]{1,0:T(8,128)S(1)}, /*index=5*/f32[16,3072]{1,0:T(8,128)S(1)}) custom-call(s32[64]{0:T(128)} %first_hbm.1, s32[64]{0:T(128)} %last_hbm.1, f32[16,32768]{1,0:T(8,128)} %refs_2_.5, ...), custom_call_target="tpu_custom_call" | custom-call | flops 603979776 | bytes 3145728 | tf_op jit(solution)/shard_map/pallas_call | solution.py:363
  4.2 2.1 %collective-permute-start.5 = (f32[16,3072]{1,0:T(8,128)S(1)}, f32[16,3072]{1,0:T(8,128)S(1)}, u32[]{:S(2)}, u32[]{:S(2)}) collective-permute-start(f32[16,3072]{1,0:T(8,128)S(1)} %get-tuple-element.36), channel_id=1, source_target_pairs={{0,1},{1,2},{2,3},{3,0},{4,5},{5,6},{6,7},{7,4},{8,9},{9,10},{10,1... | collective-permute-start | bytes 589832 | tf_op jit(solution)/shard_map/ppermute | solution.py:508
  6.3 1.4 %cut_early.1 = (f32[16,4224]{1,0:T(8,128)S(1)}, f32[16,4224]{1,0:T(8,128)S(1)}, f32[16,4224]{1,0:T(8,128)S(1)}, f32[16,4224]{1,0:T(8,128)S(1)}, f32[16,128]{1,0:T(8,128)S(1)}, /*index=5*/f32[16,128]{1,0:T(8,128)S(1)}) custom-call(f32[16,32768]{1,0:T(8,128)} %refs_2_.5), custom_call_target="tpu_custom_call" | custom-call | bytes 2097152 | tf_op jit(solution)/shard_map/cut_early/pallas_call | solution.py:208
  7.7 1.4 %collective-permute-start.10 = (f32[16,4224]{1,0:T(8,128)S(1)}, f32[16,4224]{1,0:T(8,128)S(1)}, u32[]{:S(2)}, u32[]{:S(2)}) collective-permute-start(f32[16,4224]{1,0:T(8,128)S(1)} %get-tuple-element.42), channel_id=1, source_target_pairs={{0,3},{1,0},{2,1},{3,2},{4,7},{5,4},{6,5},{7,6},{8,11},{9,8},{10,9... | collective-permute-start | bytes 811016 | tf_op jit(solution)/shard_map/ppermute | solution.py:508
  9.0 0.3 collective-permute-start.8
  9.4 2.3 %collective-permute-start.9 = (f32[16,4224]{1,0:T(8,128)S(1)}, f32[16,4224]{1,0:T(8,128)S(1)}, u32[]{:S(2)}, u32[]{:S(2)}) collective-permute-start(f32[16,4224]{1,0:T(8,128)S(1)} %get-tuple-element.41), channel_id=1, source_target_pairs={{0,2},{1,3},{2,0},{3,1},{4,6},{5,7},{6,4},{7,5},{8,10},{9,11},{10,... | collective-permute-start | bytes 811016 | tf_op jit(solution)/shard_map/ppermute | solution.py:508
  11.7 1.8 %collective-permute-start = (f32[16,128]{1,0:T(8,128)S(1)}, f32[16,128]{1,0:T(8,128)S(1)}, u32[]{:S(2)}, u32[]{:S(2)}) collective-permute-start(f32[16,128]{1,0:T(8,128)S(1)} %get-tuple-element.23), channel_id=1, source_target_pairs={{0,4},{4,0},{8,12},{12,8},{16,20},{20,16},{24,28},{28,24},{32,36},... | collective-permute-start | bytes 24584 | tf_op jit(solution)/shard_map/ppermute | solution.py:535
  13.5 0.8 %collective-permute-done.refs_4_ = f32[16,128]{1,0:T(8,128)S(1)} collective-permute-done((f32[16,128]{1,0:T(8,128)S(1)}, f32[16,128]{1,0:T(8,128)S(1)}, u32[]{:S(2)}, u32[]{:S(2)}) %collective-permute-start) | collective-permute-done | bytes 8224 | tf_op jit(solution)/shard_map/ppermute | solution.py:535
  14.3 4.1 %collective-permute-start.1 = (f32[16,128]{1,0:T(8,128)S(1)}, f32[16,128]{1,0:T(8,128)S(1)}, u32[]{:S(2)}, u32[]{:S(2)}) collective-permute-start(f32[16,128]{1,0:T(8,128)S(1)} %get-tuple-element.24), channel_id=1, source_target_pairs={{4,8},{12,16},{20,24},{28,32},{36,40},{44,48},{52,56},{60,64},{68,... | collective-permute-start | bytes 24584 | tf_op jit(solution)/shard_map/ppermute | solution.py:537
  18.4 1.3 %collective-permute-done.1.refs_5_ = f32[16,128]{1,0:T(8,128)S(1)} collective-permute-done((f32[16,128]{1,0:T(8,128)S(1)}, f32[16,128]{1,0:T(8,128)S(1)}, u32[]{:S(2)}, u32[]{:S(2)}) %collective-permute-start.1) | collective-permute-done | bytes 8224 | tf_op jit(solution)/shard_map/ppermute | solution.py:537
  19.7 0.7 %collective-permute-start.6 = (f32[16,3072]{1,0:T(8,128)S(1)}, f32[16,3072]{1,0:T(8,128)S(1)}, u32[]{:S(2)}, u32[]{:S(2)}) collective-permute-start(f32[16,3072]{1,0:T(8,128)S(1)} %get-tuple-element.37), channel_id=1, source_target_pairs={{0,2},{1,3},{2,0},{3,1},{4,6},{5,7},{6,4},{7,5},{8,10},{9,11},{10,... | collective-permute-start | bytes 589832 | tf_op jit(solution)/shard_map/ppermute | solution.py:508
  20.4 2.8 %collective-permute-start.7 = (f32[16,3072]{1,0:T(8,128)S(1)}, f32[16,3072]{1,0:T(8,128)S(1)}, u32[]{:S(2)}, u32[]{:S(2)}) collective-permute-start(f32[16,3072]{1,0:T(8,128)S(1)} %get-tuple-element.38), channel_id=1, source_target_pairs={{0,3},{1,0},{2,1},{3,2},{4,7},{5,4},{6,5},{7,6},{8,11},{9,8},{10,9... | collective-permute-start | bytes 589832 | tf_op jit(solution)/shard_map/ppermute | solution.py:508
  23.2 2.7 %shard_map.68 = (f32[16,32768]{1,0:T(8,128)}, f32[16,32768]{1,0:T(8,128)}, f32[16,1024]{1,0:T(8,128)S(1)}, f32[16,1024]{1,0:T(8,128)S(1)}, f32[16,1024]{1,0:T(8,128)S(1)}, /*index=5*/f32[16,1024]{1,0:T(8,128)S(1)}) custom-call(s32[64]{0:T(128)} %first_hbm.1, s32[64]{0:T(128)} %last_hbm.1, ...), custom_call_target="tpu_custom_call", output_to_operand_aliasing={{0}: (6, {}), {1}: (7, {})} | custom-call | flops 201326592 | bytes 1048576 | tf_op jit(solution)/shard_map/pallas_call | solution.py:363
  25.9 0.0 collective-permute-done.10.refs_3_
  26.0 0.1 collective-permute-start.2
  26.0 0.0 collective-permute-done.8.refs_1_
  26.1 1.2 %collective-permute-start.3 = (f32[16,1024]{1,0:T(8,128)S(1)}, f32[16,1024]{1,0:T(8,128)S(1)}, u32[]{:S(2)}, u32[]{:S(2)}) collective-permute-start(f32[16,1024]{1,0:T(8,128)S(1)} %get-tuple-element.33), channel_id=1, source_target_pairs={{0,2},{1,3},{2,0},{3,1},{4,6},{5,7},{6,4},{7,5},{8,10},{9,11},{10,... | collective-permute-start | bytes 196616 | tf_op jit(solution)/shard_map/ppermute | solution.py:508
  27.2 0.0 collective-permute-done.9.refs_2_
  27.2 1.6 %collective-permute-start.4 = (f32[16,1024]{1,0:T(8,128)S(1)}, f32[16,1024]{1,0:T(8,128)S(1)}, u32[]{:S(2)}, u32[]{:S(2)}) collective-permute-start(f32[16,1024]{1,0:T(8,128)S(1)} %get-tuple-element.34), channel_id=1, source_target_pairs={{0,3},{1,0},{2,1},{3,2},{4,7},{5,4},{6,5},{7,6},{8,11},{9,8},{10,9... | collective-permute-start | bytes 196616 | tf_op jit(solution)/shard_map/ppermute | solution.py:508
  28.8 3.6 %shard_map.70.refs_4_ = f32[4,8,128]{2,1,0:T(8,128)S(1)} custom-call(s32[64]{0:T(128)} %first_hbm.1, s32[64]{0:T(128)} %last_hbm.1, bf16[256,128]{1,0:T(8,128)(2,1)} %constant.20.taps_hbm, f32[16,4224]{1,0:T(8,128)S(1)} %get-tuple-element.39.refs_0_, f32[16,4224]{1,0:T(8,128)S(1)} %collective-permute-done.8.refs_1_, ...), custom_call_target="tpu_custom_call" | custom-call | flops 805306368 | bytes 2097152 | tf_op jit(solution)/shard_map/pallas_call | solution.py:452
  32.4 0.0 collective-permute-done.6.refs_2_
  32.4 0.6 shard_map.71.refs_4_
  33.1 1.0 %shard_map.72 = f32[16,4,8,128]{3,2,1,0:T(8,128)} custom-call(f32[16,1024]{1,0:T(8,128)S(1)} %get-tuple-element.31.refs_0_, f32[16,1024]{1,0:T(8,128)S(1)} %collective-permute-done.2.refs_1_, f32[16,1024]{1,0:T(8,128)S(1)} %collective-permute-done.3.refs_2_, f32[16,1024]{1,0:T(8,128)S(1)} %collective-permute-done.4.refs_3_, f32[4,8,128]{2,1,0:T(8,128)S(1)} %shard_map.71.refs_4_), custom_call_target="tpu_custom_call" | custom-call | flops 33554432 | bytes 262144 | tf_op jit(solution)/shard_map/pallas_call | solution.py:491
  34.1 11.2 %all-to-all-start = ((f32[128,4,128]{2,1,0:T(4,128)}), f32[128,4,128]{2,1,0:T(4,128)S(1)}, u32[]{:S(2)}, u32[]{:S(2)}) async-start(f32[128,4,128]{2,1,0:T(4,128)} %bitcast), calls=%async_computation | async-start | bytes 524288 | tf_op jit(solution)/shard_map/all_to_all | solution.py:545
  45.3 0.1 dynamic_slice.6
  45.4 0.1 dynamic_slice.7
  45.5 10.9 %all-to-all-done = f32[128,4,128]{2,1,0:T(4,128)S(1)} async-done(((f32[128,4,128]{2,1,0:T(4,128)}), f32[128,4,128]{2,1,0:T(4,128)S(1)}, u32[]{:S(2)}, u32[]{:S(2)}) %all-to-all-start) | async-done | bytes 262176 | tf_op jit(solution)/shard_map/all_to_all | solution.py:545
  56.3 0.1 reduce_sum.9
  56.5 0.8 %collective-permute-start.11 = (f32[4,128]{1,0:T(4,128)S(1)}, f32[4,128]{1,0:T(4,128)S(1)}, u32[]{:S(2)}, u32[]{:S(2)}) collective-permute-start(f32[4,128]{1,0:T(4,128)S(1)} %reduce_sum.9), channel_id=1, source_target_pairs={{0,4},{4,0},{1,5},{5,1},{2,6},{6,2},{3,7},{7,3},{8,12},{12,8},{9,1... | collective-permute-start | bytes 6152 | tf_op jit(solution)/shard_map/ppermute | solution.py:548
  57.3 4.5 %shard_map.69 = (f32[16,32768]{1,0:T(8,128)}, f32[16,32768]{1,0:T(8,128)}) custom-call(s32[64]{0:T(128)} %first_hbm.1, s32[64]{0:T(128)} %last_hbm.1, f32[16,32768]{1,0:T(8,128)} %refs_2_.5, bf16[256,256]{1,0:T(8,128)(2,1)} %constant.19.clone.refs_3_, f32[16,32768]{1,0:T(8,128)} %get-tuple-element.27.refs_4_, ...), custom_call_target="tpu_custom_call", output_to_operand_aliasing={{0}: (4, {}), {1}: (5, {})} | custom-call | flops 805306368 | bytes 4194304 | tf_op jit(solution)/shard_map/pallas_call | solution.py:363
  61.8 0.1 fusion
  61.9 0.7 %maximum_divide_fusion = f32[16,64]{1,0:T(8,128)} fusion(f32[4,64]{1,0:T(4,128)S(1)} %get-tuple-element.49, f32[4,64]{1,0:T(4,128)S(1)} %get-tuple-element.46, f32[4,64]{1,0:T(4,128)S(1)} %get-tuple-element.50, f32[4,64]{1,0:T(4,128)S(1)} %get-tuple-element.45, s32[64]{0:T(128)S(1)} %copy-done.1, s32[16]{0:T(128)S(1)} %dynamic_slice.7, s32[64]{0:T(128)S(1)} %copy-done.3, ...), kind=kLoop, calls=%fused_computation | loop fusion | flops 8192 | bytes 8832 | tf_op jit(solution)/shard_map/div | solution.py:552
  (15 shorter events, 0.0 us)
Async XLA Ops:
  4.2 16.2 %collective-permute-start.5 = (f32[16,3072]{1,0:T(8,128)S(1)}, f32[16,3072]{1,0:T(8,128)S(1)}, u32[]{:S(2)}, u32[]{:S(2)}) collective-permute-start(f32[16,3072]{1,0:T(8,128)S(1)} %get-tuple-element.36), channel_id=1, source_target_pairs={{0,1},{1,2},{2,3},{3,0},{4,5},{5,6},{6,7},{7,4},{8,9},{9,10},{10,1... | collective-permute-start | bytes 589832 | tf_op jit(solution)/shard_map/ppermute | solution.py:508
  7.7 18.3 %collective-permute-start.10 = (f32[16,4224]{1,0:T(8,128)S(1)}, f32[16,4224]{1,0:T(8,128)S(1)}, u32[]{:S(2)}, u32[]{:S(2)}) collective-permute-start(f32[16,4224]{1,0:T(8,128)S(1)} %get-tuple-element.42), channel_id=1, source_target_pairs={{0,3},{1,0},{2,1},{3,2},{4,7},{5,4},{6,5},{7,6},{8,11},{9,8},{10,9... | collective-permute-start | bytes 811016 | tf_op jit(solution)/shard_map/ppermute | solution.py:508
  9.0 17.0 %collective-permute-start.8 = (f32[16,4224]{1,0:T(8,128)S(1)}, f32[16,4224]{1,0:T(8,128)S(1)}, u32[]{:S(2)}, u32[]{:S(2)}) collective-permute-start(f32[16,4224]{1,0:T(8,128)S(1)} %get-tuple-element.40), channel_id=1, source_target_pairs={{0,1},{1,2},{2,3},{3,0},{4,5},{5,6},{6,7},{7,4},{8,9},{9,10},{10,1... | collective-permute-start | bytes 811016 | tf_op jit(solution)/shard_map/ppermute | solution.py:508
  9.4 17.9 %collective-permute-start.9 = (f32[16,4224]{1,0:T(8,128)S(1)}, f32[16,4224]{1,0:T(8,128)S(1)}, u32[]{:S(2)}, u32[]{:S(2)}) collective-permute-start(f32[16,4224]{1,0:T(8,128)S(1)} %get-tuple-element.41), channel_id=1, source_target_pairs={{0,2},{1,3},{2,0},{3,1},{4,6},{5,7},{6,4},{7,5},{8,10},{9,11},{10,... | collective-permute-start | bytes 811016 | tf_op jit(solution)/shard_map/ppermute | solution.py:508
  11.7 2.6 %collective-permute-start = (f32[16,128]{1,0:T(8,128)S(1)}, f32[16,128]{1,0:T(8,128)S(1)}, u32[]{:S(2)}, u32[]{:S(2)}) collective-permute-start(f32[16,128]{1,0:T(8,128)S(1)} %get-tuple-element.23), channel_id=1, source_target_pairs={{0,4},{4,0},{8,12},{12,8},{16,20},{20,16},{24,28},{28,24},{32,36},... | collective-permute-start | bytes 24584 | tf_op jit(solution)/shard_map/ppermute | solution.py:535
  14.3 5.4 %collective-permute-start.1 = (f32[16,128]{1,0:T(8,128)S(1)}, f32[16,128]{1,0:T(8,128)S(1)}, u32[]{:S(2)}, u32[]{:S(2)}) collective-permute-start(f32[16,128]{1,0:T(8,128)S(1)} %get-tuple-element.24), channel_id=1, source_target_pairs={{4,8},{12,16},{20,24},{28,32},{36,40},{44,48},{52,56},{60,64},{68,... | collective-permute-start | bytes 24584 | tf_op jit(solution)/shard_map/ppermute | solution.py:537
  19.7 12.7 %collective-permute-start.6 = (f32[16,3072]{1,0:T(8,128)S(1)}, f32[16,3072]{1,0:T(8,128)S(1)}, u32[]{:S(2)}, u32[]{:S(2)}) collective-permute-start(f32[16,3072]{1,0:T(8,128)S(1)} %get-tuple-element.37), channel_id=1, source_target_pairs={{0,2},{1,3},{2,0},{3,1},{4,6},{5,7},{6,4},{7,5},{8,10},{9,11},{10,... | collective-permute-start | bytes 589832 | tf_op jit(solution)/shard_map/ppermute | solution.py:508
  20.4 12.0 %collective-permute-start.7 = (f32[16,3072]{1,0:T(8,128)S(1)}, f32[16,3072]{1,0:T(8,128)S(1)}, u32[]{:S(2)}, u32[]{:S(2)}) collective-permute-start(f32[16,3072]{1,0:T(8,128)S(1)} %get-tuple-element.38), channel_id=1, source_target_pairs={{0,3},{1,0},{2,1},{3,2},{4,7},{5,4},{6,5},{7,6},{8,11},{9,8},{10,9... | collective-permute-start | bytes 589832 | tf_op jit(solution)/shard_map/ppermute | solution.py:508
  26.0 7.1 %collective-permute-start.2 = (f32[16,1024]{1,0:T(8,128)S(1)}, f32[16,1024]{1,0:T(8,128)S(1)}, u32[]{:S(2)}, u32[]{:S(2)}) collective-permute-start(f32[16,1024]{1,0:T(8,128)S(1)} %get-tuple-element.32), channel_id=1, source_target_pairs={{0,1},{1,2},{2,3},{3,0},{4,5},{5,6},{6,7},{7,4},{8,9},{9,10},{10,1... | collective-permute-start | bytes 196616 | tf_op jit(solution)/shard_map/ppermute | solution.py:508
  26.1 7.0 %collective-permute-start.3 = (f32[16,1024]{1,0:T(8,128)S(1)}, f32[16,1024]{1,0:T(8,128)S(1)}, u32[]{:S(2)}, u32[]{:S(2)}) collective-permute-start(f32[16,1024]{1,0:T(8,128)S(1)} %get-tuple-element.33), channel_id=1, source_target_pairs={{0,2},{1,3},{2,0},{3,1},{4,6},{5,7},{6,4},{7,5},{8,10},{9,11},{10,... | collective-permute-start | bytes 196616 | tf_op jit(solution)/shard_map/ppermute | solution.py:508
  27.2 5.8 %collective-permute-start.4 = (f32[16,1024]{1,0:T(8,128)S(1)}, f32[16,1024]{1,0:T(8,128)S(1)}, u32[]{:S(2)}, u32[]{:S(2)}) collective-permute-start(f32[16,1024]{1,0:T(8,128)S(1)} %get-tuple-element.34), channel_id=1, source_target_pairs={{0,3},{1,0},{2,1},{3,2},{4,7},{5,4},{6,5},{7,6},{8,11},{9,8},{10,9... | collective-permute-start | bytes 196616 | tf_op jit(solution)/shard_map/ppermute | solution.py:508
  28.8 16.5 %copy-start.2 = (s32[64]{0:T(128)S(1)}, s32[64]{0:T(128)}, u32[]{:S(2)}) copy-start(s32[64]{0:T(128)} %last_hbm.1) | copy-start | bytes 772
  28.8 16.6 %copy-start = (s32[64]{0:T(128)S(1)}, s32[64]{0:T(128)}, u32[]{:S(2)}) copy-start(s32[64]{0:T(128)} %first_hbm.1) | copy-start | bytes 772
  34.1 22.2 %all-to-all-start = ((f32[128,4,128]{2,1,0:T(4,128)}), f32[128,4,128]{2,1,0:T(4,128)S(1)}, u32[]{:S(2)}, u32[]{:S(2)}) async-start(f32[128,4,128]{2,1,0:T(4,128)} %bitcast), calls=%async_computation | async-start | bytes 524288 | tf_op jit(solution)/shard_map/all_to_all | solution.py:545
  56.5 5.3 %collective-permute-start.11 = (f32[4,128]{1,0:T(4,128)S(1)}, f32[4,128]{1,0:T(4,128)S(1)}, u32[]{:S(2)}, u32[]{:S(2)}) collective-permute-start(f32[4,128]{1,0:T(4,128)S(1)} %reduce_sum.9), channel_id=1, source_target_pairs={{0,4},{4,0},{1,5},{5,1},{2,6},{6,2},{3,7},{7,3},{8,12},{12,8},{9,1... | collective-permute-start | bytes 6152 | tf_op jit(solution)/shard_map/ppermute | solution.py:548
  57.3 4.6 %copy-start.1 = (s32[64]{0:T(128)S(1)}, s32[64]{0:T(128)}, u32[]{:S(2)}) copy-start(s32[64]{0:T(128)} %first_hbm.1) | copy-start | bytes 772
  57.3 4.6 %copy-start.3 = (s32[64]{0:T(128)S(1)}, s32[64]{0:T(128)}, u32[]{:S(2)}) copy-start(s32[64]{0:T(128)} %last_hbm.1) | copy-start | bytes 772

commit v13 on v11

--- a/solution.py
+++ b/solution.py
@@ -58,7 +58,6 @@
 
 def fit_span(span, mark, group, samples, tables, to_fit, to_resid):
     blocks = span // LANES
-    height = ROWS * blocks
     x_ref, at = samples
     taps_ref, first_ref, last_ref, first, last = tables
     if to_fit:
@@ -69,35 +68,41 @@
     row = lax.broadcasted_iota(jnp.int32, (ROWS, LANES), 0)
     low = lane < 64
 
-    x = x_ref[:, aligned(at - LANES, span + 2 * LANES)]
-    parts = thirds(x)
-
-    def cut(m, b):
-        return parts[m][:, b * LANES : (b + 1) * LANES]
-
-    rows = [
-        jnp.concatenate([cut(m, b + 1), jnp.where(low, cut(m, b + 2), cut(m, b))], axis=1)
-        for m in range(3)
-        for b in range(blocks)
-    ]
-    fit = jnp.dot(
-        jnp.concatenate(rows, axis=0), taps_ref[...], preferred_element_type=jnp.float32
-    )
-    fit = fit[:height] + (fit[height : 2 * height] + fit[2 * height :])
     since = first - mark
     until = last - mark
-    for b in range(blocks):
-        part = fit[b * ROWS : (b + 1) * ROWS]
-        moment = lane + b * LANES
-        inside = (moment >= since) & (moment < until)
-        smooth = part[:, :LANES] * SMOOTH_SCALE
-        if to_fit:
-            to = aligned(out_at + b * LANES, LANES)
-            fit_ref[0, :, to] = jnp.where(inside, smooth, 0.0)
-            fit_ref[1, :, to] = jnp.where(inside, part[:, LANES:] * SLOPE_SCALE, 0.0)
-        if to_resid:
-            resid = x[:, (b + 1) * LANES : (b + 2) * LANES] - smooth
-            resid_ref[k, :, aligned(piece_at + b * LANES, LANES)] = jnp.where(inside, resid, 0.0)
+    group_blocks = 16 if to_fit else 8
+    for begin in range(0, blocks, group_blocks):
+        gather = min(group_blocks, blocks - begin)
+        height = ROWS * gather
+        x = x_ref[:, aligned(at + (begin - 1) * LANES, (gather + 2) * LANES)]
+        parts = thirds(x)
+
+        def cut(m, b):
+            return parts[m][:, b * LANES : (b + 1) * LANES]
+
+        rows = [
+            jnp.concatenate([cut(m, b + 1), jnp.where(low, cut(m, b + 2), cut(m, b))], axis=1)
+            for m in range(3)
+            for b in range(gather)
+        ]
+        fit = jnp.dot(
+            jnp.concatenate(rows, axis=0), taps_ref[...], preferred_element_type=jnp.float32
+        )
+        fit = fit[:height] + (fit[height : 2 * height] + fit[2 * height :])
+        for n in range(gather):
+            b = begin + n
+            part = fit[n * ROWS : (n + 1) * ROWS]
+            moment = lane + b * LANES
+            inside = (moment >= since) & (moment < until)
+            smooth = part[:, :LANES] * SMOOTH_SCALE
+            if to_fit:
+                to = aligned(out_at + b * LANES, LANES)
+                fit_ref[0, :, to] = jnp.where(inside, smooth, 0.0)
+                fit_ref[1, :, to] = jnp.where(inside, part[:, LANES:] * SLOPE_SCALE, 0.0)
+            if to_resid:
+                resid = x[:, (n + 1) * LANES : (n + 2) * LANES] - smooth
+                to = aligned(piece_at + b * LANES, LANES)
+                resid_ref[k, :, to] = jnp.where(inside, resid, 0.0)
 
     def starts_here(a):
         return (a > mark - HALF) & (a < mark + span)
@@ -497,10 +502,6 @@
     )(*args)
 
 
-def packed(rows):
-    return jnp.concatenate([rows[:8], rows[8:]], axis=1)
-
-
 def exchanged(pieces):
     parts = [pieces[0]]
     for k in (2, 1, 3):
@@ -525,7 +526,7 @@
     last = lax.dynamic_slice_in_dim(valid_end, mine * rows, rows)[:, None]
     shared = jnp.minimum(last, valid_end[None, :])
     shared = shared - jnp.maximum(first, valid_start[None, :])
-    shared = packed(shared.astype(jnp.float32))
+    shared = shared.astype(jnp.float32)
 
     *pieces, near, far = cut_chunk(early, signal)
     parts = exchanged(pieces)
@@ -537,12 +538,16 @@
     gram = raw_gram_of(early, width, valid_start, valid_end, taps, parts)
     parts = exchanged(fit(late, False, True, halos))
     gram = gram_of(parts_mid, gram, None)
-    copies = gram_of(parts, gram, devices)
-    copies = copies.reshape(devices * GROUPS, 8, LANES)
-    copies = lax.all_to_all(copies, (*TIME, "series"), 0, 0, tiled=True)
+    copies = gram_of(parts, gram, devices // 2)
+    copies = copies.reshape(devices * GROUPS, 4, LANES)
+    copies = lax.all_to_all(copies, (*TIME[:2], "series", "core"), 0, 0, tiled=True)
     smooth, slope = fit(whole, True, False, halos)
-    cov = jnp.sum(copies, axis=0) / shared
-    return smooth, slope, jnp.concatenate([cov[:, :64], cov[:, 64:]], axis=0)
+    own = jnp.sum(copies, axis=0)
+    other = lax.ppermute(own, "core", [(0, 1), (1, 0)])
+    lead = lax.axis_index("core") == 0
+    p, q = jnp.where(lead, own, other), jnp.where(lead, other, own)
+    gram = jnp.concatenate([p[:, :64], q[:, :64], p[:, 64:], q[:, 64:]], axis=0)
+    return smooth, slope, gram / shared
 
 
 def solution(mesh):

time: 61 us -> 64.8 us (1.062)
  waiting for transfers between devices: 11.7 us -> 15 us
  starting transfers between devices: 29.4 us -> 30.2 us
    all_to_all x1, waiting for transfers between devices: 7.76 us -> 10.8 us  [shards(): lax.all_to_all(copies, (*TIME[:2], 'series', 'core'), 0, 0, tiled=True)]
    ppermute x0 -> x1, starting transfers between devices: none -> 0.82 us  [shards(): other = lax.ppermute(own, 'core', [(0, 1), (1, 0)])]
  transfers between devices with their start and end apart: 12 -> 13, of which waited for: 5 -> 5; matrix products, arithmetic and copies ran while one was open for 0% -> 0% of each run, Pallas kernels for 23% -> 21%
where the time goes in v13:
time: 64.8 us; the launch traced here: 64.5 us
  starting transfers between devices  30.2 us (47%)
  Pallas kernels  17.5 us (27%)
  waiting for transfers between devices  15 us (23%)
  other arithmetic  0.83 us (1%)
  between operations  0.79 us (1%)
    ppermute x9, starting transfers between devices, exchanged(): parts.append(lax.ppermute(pieces[k], 'series', pairs))  11.8 us
    all_to_all x1, starting transfers between devices, shards(): lax.all_to_all(copies, (*TIME[:2], 'series', 'core'), 0, 0, tiled=True)  11.7 us
    all_to_all x1, waiting for transfers between devices, shards(): lax.all_to_all(copies, (*TIME[:2], 'series', 'core'), 0, 0, tiled=True)  10.8 us
    pallas_call x3, Pallas kernels, fit_steps(): pl.pallas_call(functools.partial(fit_kernel, plan, fits, resids, ends), i...  10.8 us
    ppermute x1, starting transfers between devices, shards(): far = lax.ppermute(far, TIME, pairs + [(b, a) for a, b in pairs])  4.06 us
    pallas_call x1, Pallas kernels, raw_gram_of(): pl.pallas_call(functools.partial(raw_gram_kernel, plan, width), in_specs=...  3.63 us
    ppermute x1, starting transfers between devices, shards(): near = lax.ppermute(near, TIME, [(t, t ^ 1) for t in range(devices)])  1.79 us
    ppermute x9, waiting for transfers between devices, exchanged(): parts.append(lax.ppermute(pieces[k], 'series', pairs))  1.7 us
  transfers between devices with their start and end apart: 13, of which 5 were waited for; matrix products, arithmetic and copies ran while one was open for 0% of the time, Pallas kernels for 21%

profile of v13, /device:TPU:1, one launch (start us, length us, event | category | flops | bytes accessed | tf_op | source)
XLA Modules:
  0.0 64.5 jit_solution(15190239276262579305)
XLA Ops:
  0.6 2.6 %shard_map.69 = (f32[16,3072]{1,0:T(8,128)S(1)}, f32[16,3072]{1,0:T(8,128)S(1)}, f32[16,3072]{1,0:T(8,128)S(1)}, f32[16,3072]{1,0:T(8,128)S(1)}) custom-call(s32[64]{0:T(128)} %first_hbm.1, s32[64]{0:T(128)} %last_hbm.1, f32[16,32768]{1,0:T(8,128)} %refs_2_.5, bf16[256,128]{1,0:T(8,128)(2,1)} %constant.20.refs_3_.taps_hbm), custom_call_target="tpu_custom_call" | custom-call | flops 603979776 | bytes 3145728 | tf_op jit(solution)/shard_map/pallas_call | solution.py:365
  3.2 2.1 %collective-permute-start.5 = (f32[16,3072]{1,0:T(8,128)S(1)}, f32[16,3072]{1,0:T(8,128)S(1)}, u32[]{:S(2)}, u32[]{:S(2)}) collective-permute-start(f32[16,3072]{1,0:T(8,128)S(1)} %get-tuple-element.28), channel_id=1, source_target_pairs={{0,1},{1,2},{2,3},{3,0},{4,5},{5,6},{6,7},{7,4},{8,9},{9,10},{10,1... | collective-permute-start | bytes 589832 | tf_op jit(solution)/shard_map/ppermute | solution.py:509
  5.3 1.4 %cut_early.1 = (f32[16,4224]{1,0:T(8,128)S(1)}, f32[16,4224]{1,0:T(8,128)S(1)}, f32[16,4224]{1,0:T(8,128)S(1)}, f32[16,4224]{1,0:T(8,128)S(1)}, f32[16,128]{1,0:T(8,128)S(1)}, /*index=5*/f32[16,128]{1,0:T(8,128)S(1)}) custom-call(f32[16,32768]{1,0:T(8,128)} %refs_2_.5), custom_call_target="tpu_custom_call" | custom-call | bytes 2097152 | tf_op jit(solution)/shard_map/cut_early/pallas_call | solution.py:213
  6.8 1.6 %collective-permute-start.8 = (f32[16,4224]{1,0:T(8,128)S(1)}, f32[16,4224]{1,0:T(8,128)S(1)}, u32[]{:S(2)}, u32[]{:S(2)}) collective-permute-start(f32[16,4224]{1,0:T(8,128)S(1)} %get-tuple-element.32), channel_id=1, source_target_pairs={{0,1},{1,2},{2,3},{3,0},{4,5},{5,6},{6,7},{7,4},{8,9},{9,10},{10,1... | collective-permute-start | bytes 811016 | tf_op jit(solution)/shard_map/ppermute | solution.py:509
  8.3 1.0 %collective-permute-start.9 = (f32[16,4224]{1,0:T(8,128)S(1)}, f32[16,4224]{1,0:T(8,128)S(1)}, u32[]{:S(2)}, u32[]{:S(2)}) collective-permute-start(f32[16,4224]{1,0:T(8,128)S(1)} %get-tuple-element.33), channel_id=1, source_target_pairs={{0,2},{1,3},{2,0},{3,1},{4,6},{5,7},{6,4},{7,5},{8,10},{9,11},{10,... | collective-permute-start | bytes 811016 | tf_op jit(solution)/shard_map/ppermute | solution.py:509
  9.4 2.0 %collective-permute-start.10 = (f32[16,4224]{1,0:T(8,128)S(1)}, f32[16,4224]{1,0:T(8,128)S(1)}, u32[]{:S(2)}, u32[]{:S(2)}) collective-permute-start(f32[16,4224]{1,0:T(8,128)S(1)} %get-tuple-element.34), channel_id=1, source_target_pairs={{0,3},{1,0},{2,1},{3,2},{4,7},{5,4},{6,5},{7,6},{8,11},{9,8},{10,9... | collective-permute-start | bytes 811016 | tf_op jit(solution)/shard_map/ppermute | solution.py:509
  11.4 1.8 %collective-permute-start = (f32[16,128]{1,0:T(8,128)S(1)}, f32[16,128]{1,0:T(8,128)S(1)}, u32[]{:S(2)}, u32[]{:S(2)}) collective-permute-start(f32[16,128]{1,0:T(8,128)S(1)} %get-tuple-element.19), channel_id=1, source_target_pairs={{0,4},{4,0},{8,12},{12,8},{16,20},{20,16},{24,28},{28,24},{32,36},... | collective-permute-start | bytes 24584 | tf_op jit(solution)/shard_map/ppermute | solution.py:534
  13.1 0.8 %collective-permute-done.refs_4_ = f32[16,128]{1,0:T(8,128)S(1)} collective-permute-done((f32[16,128]{1,0:T(8,128)S(1)}, f32[16,128]{1,0:T(8,128)S(1)}, u32[]{:S(2)}, u32[]{:S(2)}) %collective-permute-start) | collective-permute-done | bytes 8224 | tf_op jit(solution)/shard_map/ppermute | solution.py:534
  14.0 4.1 %collective-permute-start.1 = (f32[16,128]{1,0:T(8,128)S(1)}, f32[16,128]{1,0:T(8,128)S(1)}, u32[]{:S(2)}, u32[]{:S(2)}) collective-permute-start(f32[16,128]{1,0:T(8,128)S(1)} %get-tuple-element.20), channel_id=1, source_target_pairs={{4,8},{12,16},{20,24},{28,32},{36,40},{44,48},{52,56},{60,64},{68,... | collective-permute-start | bytes 24584 | tf_op jit(solution)/shard_map/ppermute | solution.py:536
  18.1 1.6 %collective-permute-done.1.refs_5_ = f32[16,128]{1,0:T(8,128)S(1)} collective-permute-done((f32[16,128]{1,0:T(8,128)S(1)}, f32[16,128]{1,0:T(8,128)S(1)}, u32[]{:S(2)}, u32[]{:S(2)}) %collective-permute-start.1) | collective-permute-done | bytes 8224 | tf_op jit(solution)/shard_map/ppermute | solution.py:536
  19.7 0.4 collective-permute-start.6
  20.1 0.0 collective-permute-done.5.refs_1_
  20.1 1.6 %collective-permute-start.7 = (f32[16,3072]{1,0:T(8,128)S(1)}, f32[16,3072]{1,0:T(8,128)S(1)}, u32[]{:S(2)}, u32[]{:S(2)}) collective-permute-start(f32[16,3072]{1,0:T(8,128)S(1)} %get-tuple-element.30), channel_id=1, source_target_pairs={{0,3},{1,0},{2,1},{3,2},{4,7},{5,4},{6,5},{7,6},{8,11},{9,8},{10,9... | collective-permute-start | bytes 589832 | tf_op jit(solution)/shard_map/ppermute | solution.py:509
  21.7 2.0 %shard_map.68 = (f32[16,1024]{1,0:T(8,128)S(1)}, f32[16,1024]{1,0:T(8,128)S(1)}, f32[16,1024]{1,0:T(8,128)S(1)}, f32[16,1024]{1,0:T(8,128)S(1)}) custom-call(s32[64]{0:T(128)} %first_hbm.1, s32[64]{0:T(128)} %last_hbm.1, f32[16,32768]{1,0:T(8,128)} %refs_2_.5, bf16[256,128]{1,0:T(8,128)(2,1)} %constant.20.refs_3_.taps_hbm, ...), custom_call_target="tpu_custom_call" | custom-call | flops 201326592 | bytes 1048576 | tf_op jit(solution)/shard_map/pallas_call | solution.py:365
  23.6 0.1 collective-permute-start.2
  23.7 2.4 %collective-permute-start.3 = (f32[16,1024]{1,0:T(8,128)S(1)}, f32[16,1024]{1,0:T(8,128)S(1)}, u32[]{:S(2)}, u32[]{:S(2)}) collective-permute-start(f32[16,1024]{1,0:T(8,128)S(1)} %get-tuple-element.25), channel_id=1, source_target_pairs={{0,2},{1,3},{2,0},{3,1},{4,6},{5,7},{6,4},{7,5},{8,10},{9,11},{10,... | collective-permute-start | bytes 196616 | tf_op jit(solution)/shard_map/ppermute | solution.py:509
  26.2 0.6 collective-permute-start.4
  26.8 3.6 %shard_map.70.refs_4_ = f32[4,8,128]{2,1,0:T(8,128)S(1)} custom-call(s32[64]{0:T(128)} %first_hbm.1, s32[64]{0:T(128)} %last_hbm.1, bf16[256,128]{1,0:T(8,128)(2,1)} %constant.20.refs_3_.taps_hbm, f32[16,4224]{1,0:T(8,128)S(1)} %get-tuple-element.31.refs_0_, f32[16,4224]{1,0:T(8,128)S(1)} %collective-permute-done.8.refs_1_, ...), custom_call_target="tpu_custom_call" | custom-call | flops 805306368 | bytes 2097152 | tf_op jit(solution)/shard_map/pallas_call | solution.py:453
  30.4 0.4 collective-permute-done.7.refs_3_
  30.8 0.6 shard_map.71.refs_4_
  31.4 1.3 %collective-permute-done.4.refs_3_ = f32[16,1024]{1,0:T(8,128)S(1)} collective-permute-done((f32[16,1024]{1,0:T(8,128)S(1)}, f32[16,1024]{1,0:T(8,128)S(1)}, u32[]{:S(2)}, u32[]{:S(2)}) %collective-permute-start.4) | collective-permute-done | bytes 65568 | tf_op jit(solution)/shard_map/ppermute | solution.py:509
  32.7 1.1 %shard_map.72 = f32[16,4,8,128]{3,2,1,0:T(8,128)} custom-call(f32[16,1024]{1,0:T(8,128)S(1)} %get-tuple-element.23.refs_0_, f32[16,1024]{1,0:T(8,128)S(1)} %collective-permute-done.2.refs_1_, f32[16,1024]{1,0:T(8,128)S(1)} %collective-permute-done.3.refs_2_, f32[16,1024]{1,0:T(8,128)S(1)} %collective-permute-done.4.refs_3_, f32[4,8,128]{2,1,0:T(8,128)S(1)} %shard_map.71.refs_4_), custom_call_target="tpu_custom_call" | custom-call | flops 33554432 | bytes 262144 | tf_op jit(solution)/shard_map/pallas_call | solution.py:492
  33.8 11.7 %all-to-all-start = ((f32[128,4,128]{2,1,0:T(4,128)}), f32[128,4,128]{2,1,0:T(4,128)S(1)}, u32[]{:S(2)}, u32[]{:S(2)}) async-start(f32[128,4,128]{2,1,0:T(4,128)} %bitcast), calls=%async_computation | async-start | bytes 524288 | tf_op jit(solution)/shard_map/all_to_all | solution.py:543
  45.5 0.1 dynamic_slice.7
  45.6 0.1 dynamic_slice.6
  45.6 10.8 %all-to-all-done = f32[128,4,128]{2,1,0:T(4,128)S(1)} async-done(((f32[128,4,128]{2,1,0:T(4,128)}), f32[128,4,128]{2,1,0:T(4,128)S(1)}, u32[]{:S(2)}, u32[]{:S(2)}) %all-to-all-start) | async-done | bytes 262176 | tf_op jit(solution)/shard_map/all_to_all | solution.py:543
  56.5 0.1 reduce_sum.9
  56.6 0.0 copy-start.3
  56.6 0.8 %collective-permute-start.11 = (f32[4,128]{1,0:T(4,128)S(1)}, f32[4,128]{1,0:T(4,128)S(1)}, u32[]{:S(2)}, u32[]{:S(2)}) collective-permute-start(f32[4,128]{1,0:T(4,128)S(1)} %reduce_sum.9), channel_id=1, source_target_pairs={{0,4},{4,0},{1,5},{5,1},{2,6},{6,2},{3,7},{7,3},{8,12},{12,8},{9,1... | collective-permute-start | bytes 6152 | tf_op jit(solution)/shard_map/ppermute | solution.py:546
  57.5 6.2 %shard_map.67 = (f32[16,32768]{1,0:T(8,128)}, f32[16,32768]{1,0:T(8,128)}) custom-call(s32[64]{0:T(128)} %first_hbm.1, s32[64]{0:T(128)} %last_hbm.1, f32[16,32768]{1,0:T(8,128)} %refs_2_.5, bf16[256,256]{1,0:T(8,128)(2,1)} %constant.19.clone.refs_3_, f32[16,128]{1,0:T(8,128)S(1)} %collective-permute-done.refs_4_, f32[16,128]{1,0:T(8,128)S(1)} %collective-permute-done.1.refs_5_), custom_call_target="tpu_custom_call" | custom-call | flops 1610612736 | bytes 8388608 | tf_op jit(solution)/shard_map/pallas_call | solution.py:365
  63.7 0.1 fusion
  63.8 0.7 %maximum_divide_fusion = f32[16,64]{1,0:T(8,128)} fusion(f32[4,64]{1,0:T(4,128)S(1)} %get-tuple-element.41, f32[4,64]{1,0:T(4,128)S(1)} %get-tuple-element.38, f32[4,64]{1,0:T(4,128)S(1)} %get-tuple-element.42, f32[4,64]{1,0:T(4,128)S(1)} %get-tuple-element.37, s32[64]{0:T(128)S(1)} %copy-done.1, s32[16]{0:T(128)S(1)} %dynamic_slice.7, s32[64]{0:T(128)S(1)} %copy-done.3, ...), kind=kLoop, calls=%fused_computation | loop fusion | flops 8192 | bytes 8832 | tf_op jit(solution)/shard_map/div | solution.py:550
  (15 shorter events, 0.0 us)
Async XLA Ops:
  3.2 16.8 %collective-permute-start.5 = (f32[16,3072]{1,0:T(8,128)S(1)}, f32[16,3072]{1,0:T(8,128)S(1)}, u32[]{:S(2)}, u32[]{:S(2)}) collective-permute-start(f32[16,3072]{1,0:T(8,128)S(1)} %get-tuple-element.28), channel_id=1, source_target_pairs={{0,1},{1,2},{2,3},{3,0},{4,5},{5,6},{6,7},{7,4},{8,9},{9,10},{10,1... | collective-permute-start | bytes 589832 | tf_op jit(solution)/shard_map/ppermute | solution.py:509
  6.8 16.9 %collective-permute-start.8 = (f32[16,4224]{1,0:T(8,128)S(1)}, f32[16,4224]{1,0:T(8,128)S(1)}, u32[]{:S(2)}, u32[]{:S(2)}) collective-permute-start(f32[16,4224]{1,0:T(8,128)S(1)} %get-tuple-element.32), channel_id=1, source_target_pairs={{0,1},{1,2},{2,3},{3,0},{4,5},{5,6},{6,7},{7,4},{8,9},{9,10},{10,1... | collective-permute-start | bytes 811016 | tf_op jit(solution)/shard_map/ppermute | solution.py:509
  8.3 15.4 %collective-permute-start.9 = (f32[16,4224]{1,0:T(8,128)S(1)}, f32[16,4224]{1,0:T(8,128)S(1)}, u32[]{:S(2)}, u32[]{:S(2)}) collective-permute-start(f32[16,4224]{1,0:T(8,128)S(1)} %get-tuple-element.33), channel_id=1, source_target_pairs={{0,2},{1,3},{2,0},{3,1},{4,6},{5,7},{6,4},{7,5},{8,10},{9,11},{10,... | collective-permute-start | bytes 811016 | tf_op jit(solution)/shard_map/ppermute | solution.py:509
  9.4 16.8 %collective-permute-start.10 = (f32[16,4224]{1,0:T(8,128)S(1)}, f32[16,4224]{1,0:T(8,128)S(1)}, u32[]{:S(2)}, u32[]{:S(2)}) collective-permute-start(f32[16,4224]{1,0:T(8,128)S(1)} %get-tuple-element.34), channel_id=1, source_target_pairs={{0,3},{1,0},{2,1},{3,2},{4,7},{5,4},{6,5},{7,6},{8,11},{9,8},{10,9... | collective-permute-start | bytes 811016 | tf_op jit(solution)/shard_map/ppermute | solution.py:509
  11.4 2.6 %collective-permute-start = (f32[16,128]{1,0:T(8,128)S(1)}, f32[16,128]{1,0:T(8,128)S(1)}, u32[]{:S(2)}, u32[]{:S(2)}) collective-permute-start(f32[16,128]{1,0:T(8,128)S(1)} %get-tuple-element.19), channel_id=1, source_target_pairs={{0,4},{4,0},{8,12},{12,8},{16,20},{20,16},{24,28},{28,24},{32,36},... | collective-permute-start | bytes 24584 | tf_op jit(solution)/shard_map/ppermute | solution.py:534
  14.0 5.7 %collective-permute-start.1 = (f32[16,128]{1,0:T(8,128)S(1)}, f32[16,128]{1,0:T(8,128)S(1)}, u32[]{:S(2)}, u32[]{:S(2)}) collective-permute-start(f32[16,128]{1,0:T(8,128)S(1)} %get-tuple-element.20), channel_id=1, source_target_pairs={{4,8},{12,16},{20,24},{28,32},{36,40},{44,48},{52,56},{60,64},{68,... | collective-permute-start | bytes 24584 | tf_op jit(solution)/shard_map/ppermute | solution.py:536
  19.7 10.7 %collective-permute-start.6 = (f32[16,3072]{1,0:T(8,128)S(1)}, f32[16,3072]{1,0:T(8,128)S(1)}, u32[]{:S(2)}, u32[]{:S(2)}) collective-permute-start(f32[16,3072]{1,0:T(8,128)S(1)} %get-tuple-element.29), channel_id=1, source_target_pairs={{0,2},{1,3},{2,0},{3,1},{4,6},{5,7},{6,4},{7,5},{8,10},{9,11},{10,... | collective-permute-start | bytes 589832 | tf_op jit(solution)/shard_map/ppermute | solution.py:509
  20.1 10.7 %collective-permute-start.7 = (f32[16,3072]{1,0:T(8,128)S(1)}, f32[16,3072]{1,0:T(8,128)S(1)}, u32[]{:S(2)}, u32[]{:S(2)}) collective-permute-start(f32[16,3072]{1,0:T(8,128)S(1)} %get-tuple-element.30), channel_id=1, source_target_pairs={{0,3},{1,0},{2,1},{3,2},{4,7},{5,4},{6,5},{7,6},{8,11},{9,8},{10,9... | collective-permute-start | bytes 589832 | tf_op jit(solution)/shard_map/ppermute | solution.py:509
  23.6 7.8 %collective-permute-start.2 = (f32[16,1024]{1,0:T(8,128)S(1)}, f32[16,1024]{1,0:T(8,128)S(1)}, u32[]{:S(2)}, u32[]{:S(2)}) collective-permute-start(f32[16,1024]{1,0:T(8,128)S(1)} %get-tuple-element.24), channel_id=1, source_target_pairs={{0,1},{1,2},{2,3},{3,0},{4,5},{5,6},{6,7},{7,4},{8,9},{9,10},{10,1... | collective-permute-start | bytes 196616 | tf_op jit(solution)/shard_map/ppermute | solution.py:509
  23.7 7.7 %collective-permute-start.3 = (f32[16,1024]{1,0:T(8,128)S(1)}, f32[16,1024]{1,0:T(8,128)S(1)}, u32[]{:S(2)}, u32[]{:S(2)}) collective-permute-start(f32[16,1024]{1,0:T(8,128)S(1)} %get-tuple-element.25), channel_id=1, source_target_pairs={{0,2},{1,3},{2,0},{3,1},{4,6},{5,7},{6,4},{7,5},{8,10},{9,11},{10,... | collective-permute-start | bytes 196616 | tf_op jit(solution)/shard_map/ppermute | solution.py:509
  26.2 6.5 %collective-permute-start.4 = (f32[16,1024]{1,0:T(8,128)S(1)}, f32[16,1024]{1,0:T(8,128)S(1)}, u32[]{:S(2)}, u32[]{:S(2)}) collective-permute-start(f32[16,1024]{1,0:T(8,128)S(1)} %get-tuple-element.26), channel_id=1, source_target_pairs={{0,3},{1,0},{2,1},{3,2},{4,7},{5,4},{6,5},{7,6},{8,11},{9,8},{10,9... | collective-permute-start | bytes 196616 | tf_op jit(solution)/shard_map/ppermute | solution.py:509
  26.8 18.7 %copy-start = (s32[64]{0:T(128)S(1)}, s32[64]{0:T(128)}, u32[]{:S(2)}) copy-start(s32[64]{0:T(128)} %first_hbm.1) | copy-start | bytes 772
  26.8 18.8 %copy-start.2 = (s32[64]{0:T(128)S(1)}, s32[64]{0:T(128)}, u32[]{:S(2)}) copy-start(s32[64]{0:T(128)} %last_hbm.1) | copy-start | bytes 772
  33.8 22.7 %all-to-all-start = ((f32[128,4,128]{2,1,0:T(4,128)}), f32[128,4,128]{2,1,0:T(4,128)S(1)}, u32[]{:S(2)}, u32[]{:S(2)}) async-start(f32[128,4,128]{2,1,0:T(4,128)} %bitcast), calls=%async_computation | async-start | bytes 524288 | tf_op jit(solution)/shard_map/all_to_all | solution.py:543
  56.6 7.2 %copy-start.1 = (s32[64]{0:T(128)S(1)}, s32[64]{0:T(128)}, u32[]{:S(2)}) copy-start(s32[64]{0:T(128)} %first_hbm.1) | copy-start | bytes 772
  56.6 7.2 %copy-start.3 = (s32[64]{0:T(128)S(1)}, s32[64]{0:T(128)}, u32[]{:S(2)}) copy-start(s32[64]{0:T(128)} %last_hbm.1) | copy-start | bytes 772
  56.6 7.1 %collective-permute-start.11 = (f32[4,128]{1,0:T(4,128)S(1)}, f32[4,128]{1,0:T(4,128)S(1)}, u32[]{:S(2)}, u32[]{:S(2)}) collective-permute-start(f32[4,128]{1,0:T(4,128)S(1)} %reduce_sum.9), channel_id=1, source_target_pairs={{0,4},{4,0},{1,5},{5,1},{2,6},{6,2},{3,7},{7,3},{8,12},{12,8},{9,1... | collective-permute-start | bytes 6152 | tf_op jit(solution)/shard_map/ppermute | solution.py:546

commit v14 on v12

--- a/solution.py
+++ b/solution.py
@@ -244,14 +244,19 @@
         resid_ref = refs[0]
 
     width = signal_ref.shape[1]
-    per = count // GROUPS
-    half = count // 2
+    per = max(count // GROUPS, 1)
+    seam = (width - base) // span
     mine = lax.axis_index("series")
     begin = lax.axis_index(TIME) * width
     core = lax.axis_index("core")
 
     def place(n):
-        return LANES + n * span + (2 * LANES * (n // half) if ends else 0)
+        at = LANES + n * span
+        if not ends:
+            return at
+        if isinstance(n, int):
+            return at + 2 * LANES * (n >= seam)
+        return at + jnp.where(n >= seam, 2 * LANES, 0)
 
     def source(n):
         return lax.rem(base + n * span, width) if ends else base + n * span
@@ -263,7 +268,7 @@
             in_sems.at[n],
         )
 
-    middle = place(half)
+    middle = place(seam)
     tail = place(count - 1) + span
     after = (base + count * span) % width
     sides = [
@@ -517,10 +522,10 @@
     unit = width // 32
     early, mid = (2 * unit, 4 * unit, GROUPS), (18 * unit, 3 * unit, GROUPS)
     late = (30 * unit, unit, GROUPS)
-
-    def fit(plan, resids, halos=None, held=None):
-        out = fit_steps(plan, valid_start, valid_end, signal, taps, True, resids, halos, held)
-        return out[:2], out[2:]
+    some, rest = (22 * unit, 4 * unit, 2), (30 * unit, 2 * unit, 12)
+
+    def fit(plan, fits, resids, halos=None, held=None):
+        return fit_steps(plan, valid_start, valid_end, signal, taps, fits, resids, halos, held)
 
     first = lax.dynamic_slice_in_dim(valid_start, mine * rows, rows)[:, None]
     last = lax.dynamic_slice_in_dim(valid_end, mine * rows, rows)[:, None]
@@ -530,20 +535,19 @@
 
     *pieces, near, far = cut_chunk(early, signal)
     parts = exchanged(pieces)
-    held, pieces = fit(mid, True)
-    parts_mid = exchanged(pieces)
+    parts_mid = exchanged(fit(mid, False, True))
     near = lax.ppermute(near, TIME, [(t, t ^ 1) for t in range(devices)])
     pairs = [(t, t + 1) for t in range(1, devices - 1, 2)]
     far = lax.ppermute(far, TIME, pairs + [(b, a) for a, b in pairs])
     halos = (near, far)
     gram = raw_gram_of(early, width, valid_start, valid_end, taps, parts)
-    held, pieces = fit(late, True, halos, held)
-    parts = exchanged(pieces)
+    parts = exchanged(fit(late, False, True, halos))
+    held = fit(some, True, False)
     gram = gram_of(parts_mid, gram, None)
     copies = gram_of(parts, gram, devices // 2)
     copies = copies.reshape(devices * GROUPS, 4, LANES)
     copies = lax.all_to_all(copies, (*TIME[:2], "series", "core"), 0, 0, tiled=True)
-    (smooth, slope), _ = fit(early, False, held=held)
+    smooth, slope = fit(rest, True, False, halos, held)
     own = jnp.sum(copies, axis=0)
     other = lax.ppermute(own, "core", [(0, 1), (1, 0)])
     lead = lax.axis_index("core") == 0

time: 62.8 us -> 65 us (1.035)
  Pallas kernels: 17.4 us -> 20.5 us
  waiting for transfers between devices: 13 us -> 12.1 us
    pallas_call x3 -> x4, Pallas kernels: 10.7 us -> 13.8 us  [fit_steps(): pl.pallas_call(functools.partial(fit_kernel, plan, fits, resids, ends, bo...]
    all_to_all x1, waiting for transfers between devices: 10.9 us -> 7.95 us  [shards(): lax.all_to_all(copies, (*TIME[:2], 'series', 'core'), 0, 0, tiled=True)]
    ppermute x9, waiting for transfers between devices: 0.02 us -> 1.7 us  [exchanged(): parts.append(lax.ppermute(pieces[k], 'series', pairs))]
  transfers between devices with their start and end apart: 13 -> 13, of which waited for: 3 -> 5; matrix products, arithmetic and copies ran while one was open for 0% -> 0% of each run, Pallas kernels for 21% -> 26%
where the time goes in v14:
time: 65 us; the launch traced here: 64.6 us
  starting transfers between devices  30.2 us (46%)
  Pallas kernels  20.5 us (32%)
  waiting for transfers between devices  12.1 us (19%)
  other arithmetic  0.83 us (1%)
  between operations  0.79 us (1%)
    pallas_call x4, Pallas kernels, fit_steps(): pl.pallas_call(functools.partial(fit_kernel, plan, fits, resids, ends, bo...  13.8 us
    ppermute x9, starting transfers between devices, exchanged(): parts.append(lax.ppermute(pieces[k], 'series', pairs))  11.8 us
    all_to_all x1, starting transfers between devices, shards(): lax.all_to_all(copies, (*TIME[:2], 'series', 'core'), 0, 0, tiled=True)  11.7 us
    all_to_all x1, waiting for transfers between devices, shards(): lax.all_to_all(copies, (*TIME[:2], 'series', 'core'), 0, 0, tiled=True)  7.95 us
    ppermute x1, starting transfers between devices, shards(): far = lax.ppermute(far, TIME, pairs + [(b, a) for a, b in pairs])  4.07 us
    pallas_call x1, Pallas kernels, raw_gram_of(): pl.pallas_call(functools.partial(raw_gram_kernel, plan, width), in_specs=...  3.61 us
    ppermute x1, starting transfers between devices, shards(): near = lax.ppermute(near, TIME, [(t, t ^ 1) for t in range(devices)])  1.8 us
    ppermute x9, waiting for transfers between devices, exchanged(): parts.append(lax.ppermute(pieces[k], 'series', pairs))  1.7 us
  transfers between devices with their start and end apart: 13, of which 5 were waited for; matrix products, arithmetic and copies ran while one was open for 0% of the time, Pallas kernels for 26%

profile of v14, /device:TPU:1, one launch (start us, length us, event | category | flops | bytes accessed | tf_op | source)
XLA Modules:
  0.0 64.6 jit_solution(584406140843133035)
XLA Ops:
  0.6 2.6 %shard_map.70 = (f32[16,3072]{1,0:T(8,128)S(1)}, f32[16,3072]{1,0:T(8,128)S(1)}, f32[16,3072]{1,0:T(8,128)S(1)}, f32[16,3072]{1,0:T(8,128)S(1)}) custom-call(s32[64]{0:T(128)} %first_hbm.1, s32[64]{0:T(128)} %last_hbm.1, f32[16,32768]{1,0:T(8,128)} %refs_2_.7, bf16[256,128]{1,0:T(8,128)(2,1)} %constant.20.refs_3_.taps_hbm), custom_call_target="tpu_custom_call" | custom-call | flops 603979776 | bytes 3145728 | tf_op jit(solution)/shard_map/pallas_call | solution.py:368
  3.2 2.1 %collective-permute-start.5 = (f32[16,3072]{1,0:T(8,128)S(1)}, f32[16,3072]{1,0:T(8,128)S(1)}, u32[]{:S(2)}, u32[]{:S(2)}) collective-permute-start(f32[16,3072]{1,0:T(8,128)S(1)} %get-tuple-element.32), channel_id=1, source_target_pairs={{0,1},{1,2},{2,3},{3,0},{4,5},{5,6},{6,7},{7,4},{8,9},{9,10},{10,1... | collective-permute-start | bytes 589832 | tf_op jit(solution)/shard_map/ppermute | solution.py:513
  5.3 1.4 %cut_early.1 = (f32[16,4224]{1,0:T(8,128)S(1)}, f32[16,4224]{1,0:T(8,128)S(1)}, f32[16,4224]{1,0:T(8,128)S(1)}, f32[16,4224]{1,0:T(8,128)S(1)}, f32[16,128]{1,0:T(8,128)S(1)}, /*index=5*/f32[16,128]{1,0:T(8,128)S(1)}) custom-call(f32[16,32768]{1,0:T(8,128)} %refs_2_.7), custom_call_target="tpu_custom_call" | custom-call | bytes 2097152 | tf_op jit(solution)/shard_map/cut_early/pallas_call | solution.py:208
  6.8 1.6 %collective-permute-start.8 = (f32[16,4224]{1,0:T(8,128)S(1)}, f32[16,4224]{1,0:T(8,128)S(1)}, u32[]{:S(2)}, u32[]{:S(2)}) collective-permute-start(f32[16,4224]{1,0:T(8,128)S(1)} %get-tuple-element.36), channel_id=1, source_target_pairs={{0,1},{1,2},{2,3},{3,0},{4,5},{5,6},{6,7},{7,4},{8,9},{9,10},{10,1... | collective-permute-start | bytes 811016 | tf_op jit(solution)/shard_map/ppermute | solution.py:513
  8.3 1.0 %collective-permute-start.9 = (f32[16,4224]{1,0:T(8,128)S(1)}, f32[16,4224]{1,0:T(8,128)S(1)}, u32[]{:S(2)}, u32[]{:S(2)}) collective-permute-start(f32[16,4224]{1,0:T(8,128)S(1)} %get-tuple-element.37), channel_id=1, source_target_pairs={{0,2},{1,3},{2,0},{3,1},{4,6},{5,7},{6,4},{7,5},{8,10},{9,11},{10,... | collective-permute-start | bytes 811016 | tf_op jit(solution)/shard_map/ppermute | solution.py:513
  9.4 2.0 %collective-permute-start.10 = (f32[16,4224]{1,0:T(8,128)S(1)}, f32[16,4224]{1,0:T(8,128)S(1)}, u32[]{:S(2)}, u32[]{:S(2)}) collective-permute-start(f32[16,4224]{1,0:T(8,128)S(1)} %get-tuple-element.38), channel_id=1, source_target_pairs={{0,3},{1,0},{2,1},{3,2},{4,7},{5,4},{6,5},{7,6},{8,11},{9,8},{10,9... | collective-permute-start | bytes 811016 | tf_op jit(solution)/shard_map/ppermute | solution.py:513
  11.3 1.8 %collective-permute-start = (f32[16,128]{1,0:T(8,128)S(1)}, f32[16,128]{1,0:T(8,128)S(1)}, u32[]{:S(2)}, u32[]{:S(2)}) collective-permute-start(f32[16,128]{1,0:T(8,128)S(1)} %get-tuple-element.21), channel_id=1, source_target_pairs={{0,4},{4,0},{8,12},{12,8},{16,20},{20,16},{24,28},{28,24},{32,36},... | collective-permute-start | bytes 24584 | tf_op jit(solution)/shard_map/ppermute | solution.py:539
  13.1 0.8 %collective-permute-done.refs_4_ = f32[16,128]{1,0:T(8,128)S(1)} collective-permute-done((f32[16,128]{1,0:T(8,128)S(1)}, f32[16,128]{1,0:T(8,128)S(1)}, u32[]{:S(2)}, u32[]{:S(2)}) %collective-permute-start) | collective-permute-done | bytes 8224 | tf_op jit(solution)/shard_map/ppermute | solution.py:539
  14.0 4.1 %collective-permute-start.1 = (f32[16,128]{1,0:T(8,128)S(1)}, f32[16,128]{1,0:T(8,128)S(1)}, u32[]{:S(2)}, u32[]{:S(2)}) collective-permute-start(f32[16,128]{1,0:T(8,128)S(1)} %get-tuple-element.22), channel_id=1, source_target_pairs={{4,8},{12,16},{20,24},{28,32},{36,40},{44,48},{52,56},{60,64},{68,... | collective-permute-start | bytes 24584 | tf_op jit(solution)/shard_map/ppermute | solution.py:541
  18.0 1.6 %collective-permute-done.1.refs_5_ = f32[16,128]{1,0:T(8,128)S(1)} collective-permute-done((f32[16,128]{1,0:T(8,128)S(1)}, f32[16,128]{1,0:T(8,128)S(1)}, u32[]{:S(2)}, u32[]{:S(2)}) %collective-permute-start.1) | collective-permute-done | bytes 8224 | tf_op jit(solution)/shard_map/ppermute | solution.py:541
  19.7 0.4 collective-permute-start.6
  20.0 1.6 %collective-permute-start.7 = (f32[16,3072]{1,0:T(8,128)S(1)}, f32[16,3072]{1,0:T(8,128)S(1)}, u32[]{:S(2)}, u32[]{:S(2)}) collective-permute-start(f32[16,3072]{1,0:T(8,128)S(1)} %get-tuple-element.34), channel_id=1, source_target_pairs={{0,3},{1,0},{2,1},{3,2},{4,7},{5,4},{6,5},{7,6},{8,11},{9,8},{10,9... | collective-permute-start | bytes 589832 | tf_op jit(solution)/shard_map/ppermute | solution.py:513
  21.7 2.0 %shard_map.69 = (f32[16,1024]{1,0:T(8,128)S(1)}, f32[16,1024]{1,0:T(8,128)S(1)}, f32[16,1024]{1,0:T(8,128)S(1)}, f32[16,1024]{1,0:T(8,128)S(1)}) custom-call(s32[64]{0:T(128)} %first_hbm.1, s32[64]{0:T(128)} %last_hbm.1, f32[16,32768]{1,0:T(8,128)} %refs_2_.7, bf16[256,128]{1,0:T(8,128)(2,1)} %constant.20.refs_3_.taps_hbm, ...), custom_call_target="tpu_custom_call" | custom-call | flops 201326592 | bytes 1048576 | tf_op jit(solution)/shard_map/pallas_call | solution.py:368
  23.6 0.1 collective-permute-start.2
  23.7 2.4 %collective-permute-start.3 = (f32[16,1024]{1,0:T(8,128)S(1)}, f32[16,1024]{1,0:T(8,128)S(1)}, u32[]{:S(2)}, u32[]{:S(2)}) collective-permute-start(f32[16,1024]{1,0:T(8,128)S(1)} %get-tuple-element.29), channel_id=1, source_target_pairs={{0,2},{1,3},{2,0},{3,1},{4,6},{5,7},{6,4},{7,5},{8,10},{9,11},{10,... | collective-permute-start | bytes 196616 | tf_op jit(solution)/shard_map/ppermute | solution.py:513
  26.1 0.0 collective-permute-done.10.refs_3_
  26.2 0.6 collective-permute-start.4
  26.8 3.6 %shard_map.71.refs_4_ = f32[4,8,128]{2,1,0:T(8,128)S(1)} custom-call(s32[64]{0:T(128)} %first_hbm.1, s32[64]{0:T(128)} %last_hbm.1, bf16[256,128]{1,0:T(8,128)(2,1)} %constant.20.refs_3_.taps_hbm, f32[16,4224]{1,0:T(8,128)S(1)} %get-tuple-element.35.refs_0_, f32[16,4224]{1,0:T(8,128)S(1)} %collective-permute-done.8.refs_1_, ...), custom_call_target="tpu_custom_call" | custom-call | flops 805306368 | bytes 2097152 | tf_op jit(solution)/shard_map/pallas_call | solution.py:457
  30.4 0.4 collective-permute-done.7.refs_3_
  30.8 0.6 shard_map.72.refs_4_
  31.4 1.3 %collective-permute-done.4.refs_3_ = f32[16,1024]{1,0:T(8,128)S(1)} collective-permute-done((f32[16,1024]{1,0:T(8,128)S(1)}, f32[16,1024]{1,0:T(8,128)S(1)}, u32[]{:S(2)}, u32[]{:S(2)}) %collective-permute-start.4) | collective-permute-done | bytes 65568 | tf_op jit(solution)/shard_map/ppermute | solution.py:513
  32.7 1.0 %shard_map.73 = f32[16,4,8,128]{3,2,1,0:T(8,128)} custom-call(f32[16,1024]{1,0:T(8,128)S(1)} %get-tuple-element.27.refs_0_, f32[16,1024]{1,0:T(8,128)S(1)} %collective-permute-done.2.refs_1_, f32[16,1024]{1,0:T(8,128)S(1)} %collective-permute-done.3.refs_2_, f32[16,1024]{1,0:T(8,128)S(1)} %collective-permute-done.4.refs_3_, f32[4,8,128]{2,1,0:T(8,128)S(1)} %shard_map.72.refs_4_), custom_call_target="tpu_custom_call" | custom-call | flops 33554432 | bytes 262144 | tf_op jit(solution)/shard_map/pallas_call | solution.py:496
  33.7 11.7 %all-to-all-start = ((f32[128,4,128]{2,1,0:T(4,128)}), f32[128,4,128]{2,1,0:T(4,128)S(1)}, u32[]{:S(2)}, u32[]{:S(2)}) async-start(f32[128,4,128]{2,1,0:T(4,128)} %bitcast), calls=%async_computation | async-start | bytes 524288 | tf_op jit(solution)/shard_map/all_to_all | solution.py:549
  45.5 0.1 dynamic_slice.7
  45.6 0.1 dynamic_slice.6
  45.6 2.9 %shard_map.67 = (f32[16,32768]{1,0:T(8,128)}, f32[16,32768]{1,0:T(8,128)}) custom-call(s32[64]{0:T(128)} %first_hbm.1, s32[64]{0:T(128)} %last_hbm.1, f32[16,32768]{1,0:T(8,128)} %refs_2_.7, bf16[256,256]{1,0:T(8,128)(2,1)} %constant.19.clone.refs_3_), custom_call_target="tpu_custom_call" | custom-call | flops 402653184 | bytes 2097152 | tf_op jit(solution)/shard_map/pallas_call | solution.py:368
  48.5 7.9 %all-to-all-done = f32[128,4,128]{2,1,0:T(4,128)S(1)} async-done(((f32[128,4,128]{2,1,0:T(4,128)}), f32[128,4,128]{2,1,0:T(4,128)S(1)}, u32[]{:S(2)}, u32[]{:S(2)}) %all-to-all-start) | async-done | bytes 262176 | tf_op jit(solution)/shard_map/all_to_all | solution.py:549
  56.5 0.1 reduce_sum.9
  56.6 0.8 %collective-permute-start.11 = (f32[4,128]{1,0:T(4,128)S(1)}, f32[4,128]{1,0:T(4,128)S(1)}, u32[]{:S(2)}, u32[]{:S(2)}) collective-permute-start(f32[4,128]{1,0:T(4,128)S(1)} %reduce_sum.9), channel_id=1, source_target_pairs={{0,4},{4,0},{1,5},{5,1},{2,6},{6,2},{3,7},{7,3},{8,12},{12,8},{9,1... | collective-permute-start | bytes 6152 | tf_op jit(solution)/shard_map/ppermute | solution.py:552
  57.4 6.4 %shard_map.68 = (f32[16,32768]{1,0:T(8,128)}, f32[16,32768]{1,0:T(8,128)}) custom-call(s32[64]{0:T(128)} %first_hbm.1, s32[64]{0:T(128)} %last_hbm.1, f32[16,32768]{1,0:T(8,128)} %refs_2_.7, bf16[256,256]{1,0:T(8,128)(2,1)} %constant.19.clone.refs_3_, f32[16,128]{1,0:T(8,128)S(1)} %collective-permute-done.refs_4_, ...), custom_call_target="tpu_custom_call", output_to_operand_aliasing={{0}: (6, {}), {1}: (7, {})} | custom-call | flops 1207959552 | bytes 6291456 | tf_op jit(solution)/shard_map/pallas_call | solution.py:368
  63.9 0.1 fusion
  64.0 0.7 %maximum_divide_fusion = f32[16,64]{1,0:T(8,128)} fusion(f32[4,64]{1,0:T(4,128)S(1)} %get-tuple-element.45, f32[4,64]{1,0:T(4,128)S(1)} %get-tuple-element.42, f32[4,64]{1,0:T(4,128)S(1)} %get-tuple-element.46, f32[4,64]{1,0:T(4,128)S(1)} %get-tuple-element.41, s32[64]{0:T(128)S(1)} %copy-done.1, s32[16]{0:T(128)S(1)} %dynamic_slice.7, s32[64]{0:T(128)S(1)} %copy-done.3, ...), kind=kLoop, calls=%fused_computation | loop fusion | flops 8192 | bytes 8832 | tf_op jit(solution)/shard_map/div | solution.py:556
  (16 shorter events, 0.0 us)
Async XLA Ops:
  3.2 16.8 %collective-permute-start.5 = (f32[16,3072]{1,0:T(8,128)S(1)}, f32[16,3072]{1,0:T(8,128)S(1)}, u32[]{:S(2)}, u32[]{:S(2)}) collective-permute-start(f32[16,3072]{1,0:T(8,128)S(1)} %get-tuple-element.32), channel_id=1, source_target_pairs={{0,1},{1,2},{2,3},{3,0},{4,5},{5,6},{6,7},{7,4},{8,9},{9,10},{10,1... | collective-permute-start | bytes 589832 | tf_op jit(solution)/shard_map/ppermute | solution.py:513
  6.8 16.9 %collective-permute-start.8 = (f32[16,4224]{1,0:T(8,128)S(1)}, f32[16,4224]{1,0:T(8,128)S(1)}, u32[]{:S(2)}, u32[]{:S(2)}) collective-permute-start(f32[16,4224]{1,0:T(8,128)S(1)} %get-tuple-element.36), channel_id=1, source_target_pairs={{0,1},{1,2},{2,3},{3,0},{4,5},{5,6},{6,7},{7,4},{8,9},{9,10},{10,1... | collective-permute-start | bytes 811016 | tf_op jit(solution)/shard_map/ppermute | solution.py:513
  8.3 15.4 %collective-permute-start.9 = (f32[16,4224]{1,0:T(8,128)S(1)}, f32[16,4224]{1,0:T(8,128)S(1)}, u32[]{:S(2)}, u32[]{:S(2)}) collective-permute-start(f32[16,4224]{1,0:T(8,128)S(1)} %get-tuple-element.37), channel_id=1, source_target_pairs={{0,2},{1,3},{2,0},{3,1},{4,6},{5,7},{6,4},{7,5},{8,10},{9,11},{10,... | collective-permute-start | bytes 811016 | tf_op jit(solution)/shard_map/ppermute | solution.py:513
  9.4 16.8 %collective-permute-start.10 = (f32[16,4224]{1,0:T(8,128)S(1)}, f32[16,4224]{1,0:T(8,128)S(1)}, u32[]{:S(2)}, u32[]{:S(2)}) collective-permute-start(f32[16,4224]{1,0:T(8,128)S(1)} %get-tuple-element.38), channel_id=1, source_target_pairs={{0,3},{1,0},{2,1},{3,2},{4,7},{5,4},{6,5},{7,6},{8,11},{9,8},{10,9... | collective-permute-start | bytes 811016 | tf_op jit(solution)/shard_map/ppermute | solution.py:513
  11.3 2.6 %collective-permute-start = (f32[16,128]{1,0:T(8,128)S(1)}, f32[16,128]{1,0:T(8,128)S(1)}, u32[]{:S(2)}, u32[]{:S(2)}) collective-permute-start(f32[16,128]{1,0:T(8,128)S(1)} %get-tuple-element.21), channel_id=1, source_target_pairs={{0,4},{4,0},{8,12},{12,8},{16,20},{20,16},{24,28},{28,24},{32,36},... | collective-permute-start | bytes 24584 | tf_op jit(solution)/shard_map/ppermute | solution.py:539
  14.0 5.7 %collective-permute-start.1 = (f32[16,128]{1,0:T(8,128)S(1)}, f32[16,128]{1,0:T(8,128)S(1)}, u32[]{:S(2)}, u32[]{:S(2)}) collective-permute-start(f32[16,128]{1,0:T(8,128)S(1)} %get-tuple-element.22), channel_id=1, source_target_pairs={{4,8},{12,16},{20,24},{28,32},{36,40},{44,48},{52,56},{60,64},{68,... | collective-permute-start | bytes 24584 | tf_op jit(solution)/shard_map/ppermute | solution.py:541
  19.7 10.7 %collective-permute-start.6 = (f32[16,3072]{1,0:T(8,128)S(1)}, f32[16,3072]{1,0:T(8,128)S(1)}, u32[]{:S(2)}, u32[]{:S(2)}) collective-permute-start(f32[16,3072]{1,0:T(8,128)S(1)} %get-tuple-element.33), channel_id=1, source_target_pairs={{0,2},{1,3},{2,0},{3,1},{4,6},{5,7},{6,4},{7,5},{8,10},{9,11},{10,... | collective-permute-start | bytes 589832 | tf_op jit(solution)/shard_map/ppermute | solution.py:513
  20.0 10.7 %collective-permute-start.7 = (f32[16,3072]{1,0:T(8,128)S(1)}, f32[16,3072]{1,0:T(8,128)S(1)}, u32[]{:S(2)}, u32[]{:S(2)}) collective-permute-start(f32[16,3072]{1,0:T(8,128)S(1)} %get-tuple-element.34), channel_id=1, source_target_pairs={{0,3},{1,0},{2,1},{3,2},{4,7},{5,4},{6,5},{7,6},{8,11},{9,8},{10,9... | collective-permute-start | bytes 589832 | tf_op jit(solution)/shard_map/ppermute | solution.py:513
  23.6 7.8 %collective-permute-start.2 = (f32[16,1024]{1,0:T(8,128)S(1)}, f32[16,1024]{1,0:T(8,128)S(1)}, u32[]{:S(2)}, u32[]{:S(2)}) collective-permute-start(f32[16,1024]{1,0:T(8,128)S(1)} %get-tuple-element.28), channel_id=1, source_target_pairs={{0,1},{1,2},{2,3},{3,0},{4,5},{5,6},{6,7},{7,4},{8,9},{9,10},{10,1... | collective-permute-start | bytes 196616 | tf_op jit(solution)/shard_map/ppermute | solution.py:513
  23.7 7.7 %collective-permute-start.3 = (f32[16,1024]{1,0:T(8,128)S(1)}, f32[16,1024]{1,0:T(8,128)S(1)}, u32[]{:S(2)}, u32[]{:S(2)}) collective-permute-start(f32[16,1024]{1,0:T(8,128)S(1)} %get-tuple-element.29), channel_id=1, source_target_pairs={{0,2},{1,3},{2,0},{3,1},{4,6},{5,7},{6,4},{7,5},{8,10},{9,11},{10,... | collective-permute-start | bytes 196616 | tf_op jit(solution)/shard_map/ppermute | solution.py:513
  26.2 6.5 %collective-permute-start.4 = (f32[16,1024]{1,0:T(8,128)S(1)}, f32[16,1024]{1,0:T(8,128)S(1)}, u32[]{:S(2)}, u32[]{:S(2)}) collective-permute-start(f32[16,1024]{1,0:T(8,128)S(1)} %get-tuple-element.30), channel_id=1, source_target_pairs={{0,3},{1,0},{2,1},{3,2},{4,7},{5,4},{6,5},{7,6},{8,11},{9,8},{10,9... | collective-permute-start | bytes 196616 | tf_op jit(solution)/shard_map/ppermute | solution.py:513
  26.8 18.7 %copy-start = (s32[64]{0:T(128)S(1)}, s32[64]{0:T(128)}, u32[]{:S(2)}) copy-start(s32[64]{0:T(128)} %first_hbm.1) | copy-start | bytes 772
  26.8 18.8 %copy-start.2 = (s32[64]{0:T(128)S(1)}, s32[64]{0:T(128)}, u32[]{:S(2)}) copy-start(s32[64]{0:T(128)} %last_hbm.1) | copy-start | bytes 772
  33.7 22.7 %all-to-all-start = ((f32[128,4,128]{2,1,0:T(4,128)}), f32[128,4,128]{2,1,0:T(4,128)S(1)}, u32[]{:S(2)}, u32[]{:S(2)}) async-start(f32[128,4,128]{2,1,0:T(4,128)} %bitcast), calls=%async_computation | async-start | bytes 524288 | tf_op jit(solution)/shard_map/all_to_all | solution.py:549
  56.6 7.2 %collective-permute-start.11 = (f32[4,128]{1,0:T(4,128)S(1)}, f32[4,128]{1,0:T(4,128)S(1)}, u32[]{:S(2)}, u32[]{:S(2)}) collective-permute-start(f32[4,128]{1,0:T(4,128)S(1)} %reduce_sum.9), channel_id=1, source_target_pairs={{0,4},{4,0},{1,5},{5,1},{2,6},{6,2},{3,7},{7,3},{8,12},{12,8},{9,1... | collective-permute-start | bytes 6152 | tf_op jit(solution)/shard_map/ppermute | solution.py:552
  57.4 6.5 %copy-start.1 = (s32[64]{0:T(128)S(1)}, s32[64]{0:T(128)}, u32[]{:S(2)}) copy-start(s32[64]{0:T(128)} %first_hbm.1) | copy-start | bytes 772
  57.4 6.5 %copy-start.3 = (s32[64]{0:T(128)S(1)}, s32[64]{0:T(128)}, u32[]{:S(2)}) copy-start(s32[64]{0:T(128)} %last_hbm.1) | copy-start | bytes 772

commit v15 on v11

--- a/solution.py
+++ b/solution.py
@@ -497,10 +497,6 @@
     )(*args)
 
 
-def packed(rows):
-    return jnp.concatenate([rows[:8], rows[8:]], axis=1)
-
-
 def exchanged(pieces):
     parts = [pieces[0]]
     for k in (2, 1, 3):
@@ -515,8 +511,8 @@
     taps = jnp.asarray(taps, jnp.bfloat16)
     mine = lax.axis_index("series")
     unit = width // 32
-    early, mid = (2 * unit, 4 * unit, GROUPS), (18 * unit, 3 * unit, GROUPS)
-    late, whole = (30 * unit, unit, GROUPS), (0, 4 * unit, 8)
+    early, mid = (unit, 4 * unit, GROUPS), (17 * unit, unit * 7 // 2, GROUPS)
+    late, whole = (31 * unit, unit // 2, GROUPS), (0, 8 * unit, 4)
 
     def fit(plan, fits, resids, halos=None):
         return fit_steps(plan, valid_start, valid_end, signal, taps, fits, resids, halos)
@@ -525,7 +521,7 @@
     last = lax.dynamic_slice_in_dim(valid_end, mine * rows, rows)[:, None]
     shared = jnp.minimum(last, valid_end[None, :])
     shared = shared - jnp.maximum(first, valid_start[None, :])
-    shared = packed(shared.astype(jnp.float32))
+    shared = shared.astype(jnp.float32)
 
     *pieces, near, far = cut_chunk(early, signal)
     parts = exchanged(pieces)
@@ -537,12 +533,16 @@
     gram = raw_gram_of(early, width, valid_start, valid_end, taps, parts)
     parts = exchanged(fit(late, False, True, halos))
     gram = gram_of(parts_mid, gram, None)
-    copies = gram_of(parts, gram, devices)
-    copies = copies.reshape(devices * GROUPS, 8, LANES)
-    copies = lax.all_to_all(copies, (*TIME, "series"), 0, 0, tiled=True)
+    copies = gram_of(parts, gram, devices // 2)
+    copies = copies.reshape(devices * GROUPS, 4, LANES)
+    copies = lax.all_to_all(copies, (*TIME[:2], "series", "core"), 0, 0, tiled=True)
     smooth, slope = fit(whole, True, False, halos)
-    cov = jnp.sum(copies, axis=0) / shared
-    return smooth, slope, jnp.concatenate([cov[:, :64], cov[:, 64:]], axis=0)
+    own = jnp.sum(copies, axis=0)
+    other = lax.ppermute(own, "core", [(0, 1), (1, 0)])
+    lead = lax.axis_index("core") == 0
+    p, q = jnp.where(lead, own, other), jnp.where(lead, other, own)
+    gram = jnp.concatenate([p[:, :64], q[:, :64], p[:, 64:], q[:, 64:]], axis=0)
+    return smooth, slope, gram / shared
 
 
 def solution(mesh):

time: 61 us -> 67.2 us (1.10)
  starting transfers between devices: 29.4 us -> 33 us
  waiting for transfers between devices: 11.7 us -> 15.2 us
  Pallas kernels: 17.6 us -> 16.8 us
    all_to_all x1, waiting for transfers between devices: 7.76 us -> 10.8 us  [shards(): lax.all_to_all(copies, (*TIME[:2], 'series', 'core'), 0, 0, tiled=True)]
    all_to_all x1, starting transfers between devices: 11.7 us -> 14.3 us  [shards(): lax.all_to_all(copies, (*TIME[:2], 'series', 'core'), 0, 0, tiled=True)]
    ppermute x0 -> x1, starting transfers between devices: none -> 0.82 us  [shards(): other = lax.ppermute(own, 'core', [(0, 1), (1, 0)])]
  transfers between devices with their start and end apart: 12 -> 13, of which waited for: 5 -> 6; matrix products, arithmetic and copies ran while one was open for 0% -> 0% of each run, Pallas kernels for 23% -> 20%
where the time goes in v15:
time: 67.2 us; the launch traced here: 66.9 us
  starting transfers between devices  33 us (49%)
  Pallas kernels  16.8 us (25%)
  waiting for transfers between devices  15.2 us (23%)
  other arithmetic  0.83 us (1%)
  between operations  0.78 us (1%)
    all_to_all x1, starting transfers between devices, shards(): lax.all_to_all(copies, (*TIME[:2], 'series', 'core'), 0, 0, tiled=True)  14.3 us
    ppermute x9, starting transfers between devices, exchanged(): parts.append(lax.ppermute(pieces[k], 'series', pairs))  11.8 us
    all_to_all x1, waiting for transfers between devices, shards(): lax.all_to_all(copies, (*TIME[:2], 'series', 'core'), 0, 0, tiled=True)  10.8 us
    pallas_call x3, Pallas kernels, fit_steps(): pl.pallas_call(functools.partial(fit_kernel, plan, fits, resids, ends), i...  10.2 us
    ppermute x1, starting transfers between devices, shards(): far = lax.ppermute(far, TIME, pairs + [(b, a) for a, b in pairs])  4.06 us
    pallas_call x1, Pallas kernels, raw_gram_of(): pl.pallas_call(functools.partial(raw_gram_kernel, plan, width), in_specs=...  3.61 us
    ppermute x1, starting transfers between devices, shards(): near = lax.ppermute(near, TIME, [(t, t ^ 1) for t in range(devices)])  2.1 us
    ppermute x9, waiting for transfers between devices, exchanged(): parts.append(lax.ppermute(pieces[k], 'series', pairs))  1.87 us
  transfers between devices with their start and end apart: 13, of which 6 were waited for; matrix products, arithmetic and copies ran while one was open for 0% of the time, Pallas kernels for 20%

profile of v15, /device:TPU:1, one launch (start us, length us, event | category | flops | bytes accessed | tf_op | source)
XLA Modules:
  0.0 66.9 jit_solution(4844000071822484767)
XLA Ops:
  0.6 2.7 %shard_map.69 = (f32[16,3584]{1,0:T(8,128)S(1)}, f32[16,3584]{1,0:T(8,128)S(1)}, f32[16,3584]{1,0:T(8,128)S(1)}, f32[16,3584]{1,0:T(8,128)S(1)}) custom-call(s32[64]{0:T(128)} %first_hbm.1, s32[64]{0:T(128)} %last_hbm.1, f32[16,32768]{1,0:T(8,128)} %refs_2_.5, bf16[256,128]{1,0:T(8,128)(2,1)} %constant.20.refs_3_.taps_hbm), custom_call_target="tpu_custom_call" | custom-call | flops 704643072 | bytes 3670016 | tf_op jit(solution)/shard_map/pallas_call | solution.py:360
  3.4 2.4 %collective-permute-start.5 = (f32[16,3584]{1,0:T(8,128)S(1)}, f32[16,3584]{1,0:T(8,128)S(1)}, u32[]{:S(2)}, u32[]{:S(2)}) collective-permute-start(f32[16,3584]{1,0:T(8,128)S(1)} %get-tuple-element.28), channel_id=1, source_target_pairs={{0,1},{1,2},{2,3},{3,0},{4,5},{5,6},{6,7},{7,4},{8,9},{9,10},{10,1... | collective-permute-start | bytes 688136 | tf_op jit(solution)/shard_map/ppermute | solution.py:504
  5.8 1.4 %cut_early.1 = (f32[16,4224]{1,0:T(8,128)S(1)}, f32[16,4224]{1,0:T(8,128)S(1)}, f32[16,4224]{1,0:T(8,128)S(1)}, f32[16,4224]{1,0:T(8,128)S(1)}, f32[16,128]{1,0:T(8,128)S(1)}, /*index=5*/f32[16,128]{1,0:T(8,128)S(1)}) custom-call(f32[16,32768]{1,0:T(8,128)} %refs_2_.5), custom_call_target="tpu_custom_call" | custom-call | bytes 2097152 | tf_op jit(solution)/shard_map/cut_early/pallas_call | solution.py:208
  7.2 1.3 %collective-permute-start.8 = (f32[16,4224]{1,0:T(8,128)S(1)}, f32[16,4224]{1,0:T(8,128)S(1)}, u32[]{:S(2)}, u32[]{:S(2)}) collective-permute-start(f32[16,4224]{1,0:T(8,128)S(1)} %get-tuple-element.32), channel_id=1, source_target_pairs={{0,1},{1,2},{2,3},{3,0},{4,5},{5,6},{6,7},{7,4},{8,9},{9,10},{10,1... | collective-permute-start | bytes 811016 | tf_op jit(solution)/shard_map/ppermute | solution.py:504
  8.5 1.0 %collective-permute-start.9 = (f32[16,4224]{1,0:T(8,128)S(1)}, f32[16,4224]{1,0:T(8,128)S(1)}, u32[]{:S(2)}, u32[]{:S(2)}) collective-permute-start(f32[16,4224]{1,0:T(8,128)S(1)} %get-tuple-element.33), channel_id=1, source_target_pairs={{0,2},{1,3},{2,0},{3,1},{4,6},{5,7},{6,4},{7,5},{8,10},{9,11},{10,... | collective-permute-start | bytes 811016 | tf_op jit(solution)/shard_map/ppermute | solution.py:504
  9.5 2.0 %collective-permute-start.10 = (f32[16,4224]{1,0:T(8,128)S(1)}, f32[16,4224]{1,0:T(8,128)S(1)}, u32[]{:S(2)}, u32[]{:S(2)}) collective-permute-start(f32[16,4224]{1,0:T(8,128)S(1)} %get-tuple-element.34), channel_id=1, source_target_pairs={{0,3},{1,0},{2,1},{3,2},{4,7},{5,4},{6,5},{7,6},{8,11},{9,8},{10,9... | collective-permute-start | bytes 811016 | tf_op jit(solution)/shard_map/ppermute | solution.py:504
  11.5 2.1 %collective-permute-start = (f32[16,128]{1,0:T(8,128)S(1)}, f32[16,128]{1,0:T(8,128)S(1)}, u32[]{:S(2)}, u32[]{:S(2)}) collective-permute-start(f32[16,128]{1,0:T(8,128)S(1)} %get-tuple-element.19), channel_id=1, source_target_pairs={{0,4},{4,0},{8,12},{12,8},{16,20},{20,16},{24,28},{28,24},{32,36},... | collective-permute-start | bytes 24584 | tf_op jit(solution)/shard_map/ppermute | solution.py:529
  13.6 0.8 %collective-permute-done.refs_4_ = f32[16,128]{1,0:T(8,128)S(1)} collective-permute-done((f32[16,128]{1,0:T(8,128)S(1)}, f32[16,128]{1,0:T(8,128)S(1)}, u32[]{:S(2)}, u32[]{:S(2)}) %collective-permute-start) | collective-permute-done | bytes 8224 | tf_op jit(solution)/shard_map/ppermute | solution.py:529
  14.4 4.1 %collective-permute-start.1 = (f32[16,128]{1,0:T(8,128)S(1)}, f32[16,128]{1,0:T(8,128)S(1)}, u32[]{:S(2)}, u32[]{:S(2)}) collective-permute-start(f32[16,128]{1,0:T(8,128)S(1)} %get-tuple-element.20), channel_id=1, source_target_pairs={{4,8},{12,16},{20,24},{28,32},{36,40},{44,48},{52,56},{60,64},{68,... | collective-permute-start | bytes 24584 | tf_op jit(solution)/shard_map/ppermute | solution.py:531
  18.5 1.6 %collective-permute-done.1.refs_5_ = f32[16,128]{1,0:T(8,128)S(1)} collective-permute-done((f32[16,128]{1,0:T(8,128)S(1)}, f32[16,128]{1,0:T(8,128)S(1)}, u32[]{:S(2)}, u32[]{:S(2)}) %collective-permute-start.1) | collective-permute-done | bytes 8224 | tf_op jit(solution)/shard_map/ppermute | solution.py:531
  20.1 0.1 collective-permute-start.6
  20.2 2.0 %collective-permute-start.7 = (f32[16,3584]{1,0:T(8,128)S(1)}, f32[16,3584]{1,0:T(8,128)S(1)}, u32[]{:S(2)}, u32[]{:S(2)}) collective-permute-start(f32[16,3584]{1,0:T(8,128)S(1)} %get-tuple-element.30), channel_id=1, source_target_pairs={{0,3},{1,0},{2,1},{3,2},{4,7},{5,4},{6,5},{7,6},{8,11},{9,8},{10,9... | collective-permute-start | bytes 688136 | tf_op jit(solution)/shard_map/ppermute | solution.py:504
  22.2 1.7 %shard_map.68 = (f32[16,512]{1,0:T(8,128)S(1)}, f32[16,512]{1,0:T(8,128)S(1)}, f32[16,512]{1,0:T(8,128)S(1)}, f32[16,512]{1,0:T(8,128)S(1)}) custom-call(s32[64]{0:T(128)} %first_hbm.1, s32[64]{0:T(128)} %last_hbm.1, f32[16,32768]{1,0:T(8,128)} %refs_2_.5, bf16[256,128]{1,0:T(8,128)(2,1)} %constant.20.refs_3_.taps_hbm, ...), custom_call_target="tpu_custom_call" | custom-call | flops 100663296 | bytes 524288 | tf_op jit(solution)/shard_map/pallas_call | solution.py:360
  23.9 0.1 collective-permute-start.2
  24.0 0.2 collective-permute-done.9.refs_2_
  24.2 2.1 %collective-permute-start.3 = (f32[16,512]{1,0:T(8,128)S(1)}, f32[16,512]{1,0:T(8,128)S(1)}, u32[]{:S(2)}, u32[]{:S(2)}) collective-permute-start(f32[16,512]{1,0:T(8,128)S(1)} %get-tuple-element.25), channel_id=1, source_target_pairs={{0,2},{1,3},{2,0},{3,1},{4,6},{5,7},{6,4},{7,5},{8,10},{9,11},{10,... | collective-permute-start | bytes 98312 | tf_op jit(solution)/shard_map/ppermute | solution.py:504
  26.4 0.8 %collective-permute-start.4 = (f32[16,512]{1,0:T(8,128)S(1)}, f32[16,512]{1,0:T(8,128)S(1)}, u32[]{:S(2)}, u32[]{:S(2)}) collective-permute-start(f32[16,512]{1,0:T(8,128)S(1)} %get-tuple-element.26), channel_id=1, source_target_pairs={{0,3},{1,0},{2,1},{3,2},{4,7},{5,4},{6,5},{7,6},{8,11},{9,8},{10,9... | collective-permute-start | bytes 98312 | tf_op jit(solution)/shard_map/ppermute | solution.py:504
  27.2 3.6 %shard_map.70.refs_4_ = f32[4,8,128]{2,1,0:T(8,128)S(1)} custom-call(s32[64]{0:T(128)} %first_hbm.1, s32[64]{0:T(128)} %last_hbm.1, bf16[256,128]{1,0:T(8,128)(2,1)} %constant.20.refs_3_.taps_hbm, f32[16,4224]{1,0:T(8,128)S(1)} %get-tuple-element.31.refs_0_, f32[16,4224]{1,0:T(8,128)S(1)} %collective-permute-done.8.refs_1_, ...), custom_call_target="tpu_custom_call" | custom-call | flops 805306368 | bytes 2097152 | tf_op jit(solution)/shard_map/pallas_call | solution.py:448
  30.8 1.4 %collective-permute-done.7.refs_3_ = f32[16,3584]{1,0:T(8,128)S(1)} collective-permute-done((f32[16,3584]{1,0:T(8,128)S(1)}, f32[16,3584]{1,0:T(8,128)S(1)}, u32[]{:S(2)}, u32[]{:S(2)}) %collective-permute-start.7) | collective-permute-done | bytes 229408 | tf_op jit(solution)/shard_map/ppermute | solution.py:504
  32.3 0.7 shard_map.71.refs_4_
  33.0 0.2 collective-permute-done.4.refs_3_
  33.1 1.0 %shard_map.72 = f32[16,4,8,128]{3,2,1,0:T(8,128)} custom-call(f32[16,512]{1,0:T(8,128)S(1)} %get-tuple-element.23.refs_0_, f32[16,512]{1,0:T(8,128)S(1)} %collective-permute-done.2.refs_1_, f32[16,512]{1,0:T(8,128)S(1)} %collective-permute-done.3.refs_2_, f32[16,512]{1,0:T(8,128)S(1)} %collective-permute-done.4.refs_3_, f32[4,8,128]{2,1,0:T(8,128)S(1)} %shard_map.71.refs_4_), custom_call_target="tpu_custom_call" | custom-call | flops 16777216 | bytes 131072 | tf_op jit(solution)/shard_map/pallas_call | solution.py:487
  34.1 14.3 %all-to-all-start = ((f32[128,4,128]{2,1,0:T(4,128)}), f32[128,4,128]{2,1,0:T(4,128)S(1)}, u32[]{:S(2)}, u32[]{:S(2)}) async-start(f32[128,4,128]{2,1,0:T(4,128)} %bitcast), calls=%async_computation | async-start | bytes 524288 | tf_op jit(solution)/shard_map/all_to_all | solution.py:538
  48.4 0.1 dynamic_slice.7
  48.5 0.1 dynamic_slice.6
  48.6 10.8 %all-to-all-done = f32[128,4,128]{2,1,0:T(4,128)S(1)} async-done(((f32[128,4,128]{2,1,0:T(4,128)}), f32[128,4,128]{2,1,0:T(4,128)S(1)}, u32[]{:S(2)}, u32[]{:S(2)}) %all-to-all-start) | async-done | bytes 262176 | tf_op jit(solution)/shard_map/all_to_all | solution.py:538
  59.4 0.1 reduce_sum.9
  59.6 0.0 copy-start.3
  59.6 0.8 %collective-permute-start.11 = (f32[4,128]{1,0:T(4,128)S(1)}, f32[4,128]{1,0:T(4,128)S(1)}, u32[]{:S(2)}, u32[]{:S(2)}) collective-permute-start(f32[4,128]{1,0:T(4,128)S(1)} %reduce_sum.9), channel_id=1, source_target_pairs={{0,4},{4,0},{1,5},{5,1},{2,6},{6,2},{3,7},{7,3},{8,12},{12,8},{9,1... | collective-permute-start | bytes 6152 | tf_op jit(solution)/shard_map/ppermute | solution.py:541
  60.4 5.7 %shard_map.67 = (f32[16,32768]{1,0:T(8,128)}, f32[16,32768]{1,0:T(8,128)}) custom-call(s32[64]{0:T(128)} %first_hbm.1, s32[64]{0:T(128)} %last_hbm.1, f32[16,32768]{1,0:T(8,128)} %refs_2_.5, bf16[256,256]{1,0:T(8,128)(2,1)} %constant.19.clone.refs_3_, f32[16,128]{1,0:T(8,128)S(1)} %collective-permute-done.refs_4_, f32[16,128]{1,0:T(8,128)S(1)} %collective-permute-done.1.refs_5_), custom_call_target="tpu_custom_call" | custom-call | flops 1610612736 | bytes 8388608 | tf_op jit(solution)/shard_map/pallas_call | solution.py:360
  66.2 0.1 fusion
  66.2 0.7 %maximum_divide_fusion = f32[16,64]{1,0:T(8,128)} fusion(f32[4,64]{1,0:T(4,128)S(1)} %get-tuple-element.41, f32[4,64]{1,0:T(4,128)S(1)} %get-tuple-element.38, f32[4,64]{1,0:T(4,128)S(1)} %get-tuple-element.42, f32[4,64]{1,0:T(4,128)S(1)} %get-tuple-element.37, s32[64]{0:T(128)S(1)} %copy-done.1, s32[16]{0:T(128)S(1)} %dynamic_slice.7, s32[64]{0:T(128)S(1)} %copy-done.3, ...), kind=kLoop, calls=%fused_computation | loop fusion | flops 8192 | bytes 8832 | tf_op jit(solution)/shard_map/div | solution.py:545
  (15 shorter events, 0.0 us)
Async XLA Ops:
  3.4 16.8 %collective-permute-start.5 = (f32[16,3584]{1,0:T(8,128)S(1)}, f32[16,3584]{1,0:T(8,128)S(1)}, u32[]{:S(2)}, u32[]{:S(2)}) collective-permute-start(f32[16,3584]{1,0:T(8,128)S(1)} %get-tuple-element.28), channel_id=1, source_target_pairs={{0,1},{1,2},{2,3},{3,0},{4,5},{5,6},{6,7},{7,4},{8,9},{9,10},{10,1... | collective-permute-start | bytes 688136 | tf_op jit(solution)/shard_map/ppermute | solution.py:504
  7.2 16.7 %collective-permute-start.8 = (f32[16,4224]{1,0:T(8,128)S(1)}, f32[16,4224]{1,0:T(8,128)S(1)}, u32[]{:S(2)}, u32[]{:S(2)}) collective-permute-start(f32[16,4224]{1,0:T(8,128)S(1)} %get-tuple-element.32), channel_id=1, source_target_pairs={{0,1},{1,2},{2,3},{3,0},{4,5},{5,6},{6,7},{7,4},{8,9},{9,10},{10,1... | collective-permute-start | bytes 811016 | tf_op jit(solution)/shard_map/ppermute | solution.py:504
  8.5 15.7 %collective-permute-start.9 = (f32[16,4224]{1,0:T(8,128)S(1)}, f32[16,4224]{1,0:T(8,128)S(1)}, u32[]{:S(2)}, u32[]{:S(2)}) collective-permute-start(f32[16,4224]{1,0:T(8,128)S(1)} %get-tuple-element.33), channel_id=1, source_target_pairs={{0,2},{1,3},{2,0},{3,1},{4,6},{5,7},{6,4},{7,5},{8,10},{9,11},{10,... | collective-permute-start | bytes 811016 | tf_op jit(solution)/shard_map/ppermute | solution.py:504
  9.5 16.8 %collective-permute-start.10 = (f32[16,4224]{1,0:T(8,128)S(1)}, f32[16,4224]{1,0:T(8,128)S(1)}, u32[]{:S(2)}, u32[]{:S(2)}) collective-permute-start(f32[16,4224]{1,0:T(8,128)S(1)} %get-tuple-element.34), channel_id=1, source_target_pairs={{0,3},{1,0},{2,1},{3,2},{4,7},{5,4},{6,5},{7,6},{8,11},{9,8},{10,9... | collective-permute-start | bytes 811016 | tf_op jit(solution)/shard_map/ppermute | solution.py:504
  11.5 2.9 %collective-permute-start = (f32[16,128]{1,0:T(8,128)S(1)}, f32[16,128]{1,0:T(8,128)S(1)}, u32[]{:S(2)}, u32[]{:S(2)}) collective-permute-start(f32[16,128]{1,0:T(8,128)S(1)} %get-tuple-element.19), channel_id=1, source_target_pairs={{0,4},{4,0},{8,12},{12,8},{16,20},{20,16},{24,28},{28,24},{32,36},... | collective-permute-start | bytes 24584 | tf_op jit(solution)/shard_map/ppermute | solution.py:529
  14.4 5.7 %collective-permute-start.1 = (f32[16,128]{1,0:T(8,128)S(1)}, f32[16,128]{1,0:T(8,128)S(1)}, u32[]{:S(2)}, u32[]{:S(2)}) collective-permute-start(f32[16,128]{1,0:T(8,128)S(1)} %get-tuple-element.20), channel_id=1, source_target_pairs={{4,8},{12,16},{20,24},{28,32},{36,40},{44,48},{52,56},{60,64},{68,... | collective-permute-start | bytes 24584 | tf_op jit(solution)/shard_map/ppermute | solution.py:531
  20.1 10.7 %collective-permute-start.6 = (f32[16,3584]{1,0:T(8,128)S(1)}, f32[16,3584]{1,0:T(8,128)S(1)}, u32[]{:S(2)}, u32[]{:S(2)}) collective-permute-start(f32[16,3584]{1,0:T(8,128)S(1)} %get-tuple-element.29), channel_id=1, source_target_pairs={{0,2},{1,3},{2,0},{3,1},{4,6},{5,7},{6,4},{7,5},{8,10},{9,11},{10,... | collective-permute-start | bytes 688136 | tf_op jit(solution)/shard_map/ppermute | solution.py:504
  20.2 12.1 %collective-permute-start.7 = (f32[16,3584]{1,0:T(8,128)S(1)}, f32[16,3584]{1,0:T(8,128)S(1)}, u32[]{:S(2)}, u32[]{:S(2)}) collective-permute-start(f32[16,3584]{1,0:T(8,128)S(1)} %get-tuple-element.30), channel_id=1, source_target_pairs={{0,3},{1,0},{2,1},{3,2},{4,7},{5,4},{6,5},{7,6},{8,11},{9,8},{10,9... | collective-permute-start | bytes 688136 | tf_op jit(solution)/shard_map/ppermute | solution.py:504
  23.9 9.0 %collective-permute-start.2 = (f32[16,512]{1,0:T(8,128)S(1)}, f32[16,512]{1,0:T(8,128)S(1)}, u32[]{:S(2)}, u32[]{:S(2)}) collective-permute-start(f32[16,512]{1,0:T(8,128)S(1)} %get-tuple-element.24), channel_id=1, source_target_pairs={{0,1},{1,2},{2,3},{3,0},{4,5},{5,6},{6,7},{7,4},{8,9},{9,10},{10,1... | collective-permute-start | bytes 98312 | tf_op jit(solution)/shard_map/ppermute | solution.py:504
  24.2 8.7 %collective-permute-start.3 = (f32[16,512]{1,0:T(8,128)S(1)}, f32[16,512]{1,0:T(8,128)S(1)}, u32[]{:S(2)}, u32[]{:S(2)}) collective-permute-start(f32[16,512]{1,0:T(8,128)S(1)} %get-tuple-element.25), channel_id=1, source_target_pairs={{0,2},{1,3},{2,0},{3,1},{4,6},{5,7},{6,4},{7,5},{8,10},{9,11},{10,... | collective-permute-start | bytes 98312 | tf_op jit(solution)/shard_map/ppermute | solution.py:504
  26.4 6.8 %collective-permute-start.4 = (f32[16,512]{1,0:T(8,128)S(1)}, f32[16,512]{1,0:T(8,128)S(1)}, u32[]{:S(2)}, u32[]{:S(2)}) collective-permute-start(f32[16,512]{1,0:T(8,128)S(1)} %get-tuple-element.26), channel_id=1, source_target_pairs={{0,3},{1,0},{2,1},{3,2},{4,7},{5,4},{6,5},{7,6},{8,11},{9,8},{10,9... | collective-permute-start | bytes 98312 | tf_op jit(solution)/shard_map/ppermute | solution.py:504
  27.2 21.2 %copy-start = (s32[64]{0:T(128)S(1)}, s32[64]{0:T(128)}, u32[]{:S(2)}) copy-start(s32[64]{0:T(128)} %first_hbm.1) | copy-start | bytes 772
  27.2 21.3 %copy-start.2 = (s32[64]{0:T(128)S(1)}, s32[64]{0:T(128)}, u32[]{:S(2)}) copy-start(s32[64]{0:T(128)} %last_hbm.1) | copy-start | bytes 772
  34.1 25.3 %all-to-all-start = ((f32[128,4,128]{2,1,0:T(4,128)}), f32[128,4,128]{2,1,0:T(4,128)S(1)}, u32[]{:S(2)}, u32[]{:S(2)}) async-start(f32[128,4,128]{2,1,0:T(4,128)} %bitcast), calls=%async_computation | async-start | bytes 524288 | tf_op jit(solution)/shard_map/all_to_all | solution.py:538
  59.6 6.7 %copy-start.1 = (s32[64]{0:T(128)S(1)}, s32[64]{0:T(128)}, u32[]{:S(2)}) copy-start(s32[64]{0:T(128)} %first_hbm.1) | copy-start | bytes 772
  59.6 6.7 %copy-start.3 = (s32[64]{0:T(128)S(1)}, s32[64]{0:T(128)}, u32[]{:S(2)}) copy-start(s32[64]{0:T(128)} %last_hbm.1) | copy-start | bytes 772
  59.6 6.6 %collective-permute-start.11 = (f32[4,128]{1,0:T(4,128)S(1)}, f32[4,128]{1,0:T(4,128)S(1)}, u32[]{:S(2)}, u32[]{:S(2)}) collective-permute-start(f32[4,128]{1,0:T(4,128)S(1)} %reduce_sum.9), channel_id=1, source_target_pairs={{0,4},{4,0},{1,5},{5,1},{2,6},{6,2},{3,7},{7,3},{8,12},{12,8},{9,1... | collective-permute-start | bytes 6152 | tf_op jit(solution)/shard_map/ppermute | solution.py:541

commit v16 on v15

--- a/solution.py
+++ b/solution.py
@@ -188,7 +188,7 @@
         copies.append(copy)
 
     for k in (2, 1, 3, 0):
-        start = base + (mine + k) % GROUPS * span
+        start = base + (mine ^ k) * span
         move(start - LANES, LANES, side_ref.at[2 * k])
         move(start + span, LANES, side_ref.at[2 * k + 1])
         move(start, span, pieces[k].at[:, pl.ds(0, span)])
@@ -298,7 +298,7 @@
     first, last = ends_of(mine, first_ref, last_ref)
 
     def body(n, carry):
-        k = (n // per + GROUPS - mine) % GROUPS
+        k = (n // per) ^ mine
 
         @pl.when(n + 1 < count)
         def _():
@@ -421,7 +421,7 @@
         copy.wait()
 
     def body(k, carry):
-        group = (mine + GROUPS - k) % GROUPS
+        group = mine ^ k
         first, last = ends_of(group, first_ref, last_ref)
         fit_span(
             span,
@@ -475,7 +475,7 @@
     out_ref, stack_ref = refs
     mine = lax.axis_index("series")
     for k in range(GROUPS):
-        stacked(stack_ref, (mine + GROUPS - k) % GROUPS, parts[k][...])
+        stacked(stack_ref, mine ^ k, parts[k][...])
     product(stack_ref, so_far_ref if add else None, spread, out_ref)
 
 
@@ -500,7 +500,7 @@
 def exchanged(pieces):
     parts = [pieces[0]]
     for k in (2, 1, 3):
-        pairs = [(s, (s + k) % GROUPS) for s in range(GROUPS)]
+        pairs = [(s, s ^ k) for s in range(GROUPS)]
         parts.append(lax.ppermute(pieces[k], "series", pairs))
     return [parts[0], parts[2], parts[1], parts[3]]
 
@@ -511,8 +511,8 @@
     taps = jnp.asarray(taps, jnp.bfloat16)
     mine = lax.axis_index("series")
     unit = width // 32
-    early, mid = (unit, 4 * unit, GROUPS), (17 * unit, unit * 7 // 2, GROUPS)
-    late, whole = (31 * unit, unit // 2, GROUPS), (0, 8 * unit, 4)
+    early, mid = (2 * unit, 4 * unit, GROUPS), (18 * unit, 3 * unit, GROUPS)
+    late, whole = (30 * unit, unit, GROUPS), (0, 8 * unit, 4)
 
     def fit(plan, fits, resids, halos=None):
         return fit_steps(plan, valid_start, valid_end, signal, taps, fits, resids, halos)

time: 67.2 us -> 66.4 us (0.988)
  starting transfers between devices: 33 us -> 28.5 us
  waiting for transfers between devices: 15.2 us -> 18.8 us
    all_to_all x1, starting transfers between devices: 14.3 us -> 10.3 us  [shards(): lax.all_to_all(copies, (*TIME[:2], 'series', 'core'), 0, 0, tiled=True)]
    ppermute x9, waiting for transfers between devices: 1.87 us -> 5.31 us  [exchanged(): parts.append(lax.ppermute(pieces[k], 'series', pairs))]
where the time goes in v16:
time: 66.4 us; the launch traced here: 66 us
  starting transfers between devices  28.5 us (43%)
  waiting for transfers between devices  18.8 us (28%)
  Pallas kernels  16.9 us (25%)
  other arithmetic  0.83 us (1%)
  between operations  0.78 us (1%)
    ppermute x9, starting transfers between devices, exchanged(): parts.append(lax.ppermute(pieces[k], 'series', pairs))  11.8 us
    all_to_all x1, waiting for transfers between devices, shards(): lax.all_to_all(copies, (*TIME[:2], 'series', 'core'), 0, 0, tiled=True)  10.8 us
    all_to_all x1, starting transfers between devices, shards(): lax.all_to_all(copies, (*TIME[:2], 'series', 'core'), 0, 0, tiled=True)  10.3 us
    pallas_call x3, Pallas kernels, fit_steps(): pl.pallas_call(functools.partial(fit_kernel, plan, fits, resids, ends), i...  10.2 us
    ppermute x9, waiting for transfers between devices, exchanged(): parts.append(lax.ppermute(pieces[k], 'series', pairs))  5.31 us
    pallas_call x1, Pallas kernels, raw_gram_of(): pl.pallas_call(functools.partial(raw_gram_kernel, plan, width), in_specs=...  3.61 us
    ppermute x1, starting transfers between devices, shards(): far = lax.ppermute(far, TIME, pairs + [(b, a) for a, b in pairs])  3.45 us
    ppermute x1, starting transfers between devices, shards(): near = lax.ppermute(near, TIME, [(t, t ^ 1) for t in range(devices)])  2.1 us
  transfers between devices with their start and end apart: 13, of which 6 were waited for; matrix products, arithmetic and copies ran while one was open for 0% of the time, Pallas kernels for 20%

profile of v16, /device:TPU:1, one launch (start us, length us, event | category | flops | bytes accessed | tf_op | source)
XLA Modules:
  0.0 66.0 jit_solution(11828633901715714407)
XLA Ops:
  0.6 2.6 %shard_map.69 = (f32[16,3072]{1,0:T(8,128)S(1)}, f32[16,3072]{1,0:T(8,128)S(1)}, f32[16,3072]{1,0:T(8,128)S(1)}, f32[16,3072]{1,0:T(8,128)S(1)}) custom-call(s32[64]{0:T(128)} %first_hbm.1, s32[64]{0:T(128)} %last_hbm.1, f32[16,32768]{1,0:T(8,128)} %refs_2_.5, bf16[256,128]{1,0:T(8,128)(2,1)} %constant.20.refs_3_.taps_hbm), custom_call_target="tpu_custom_call" | custom-call | flops 603979776 | bytes 3145728 | tf_op jit(solution)/shard_map/pallas_call | solution.py:360
  3.2 2.1 %collective-permute-start.5 = (f32[16,3072]{1,0:T(8,128)S(1)}, f32[16,3072]{1,0:T(8,128)S(1)}, u32[]{:S(2)}, u32[]{:S(2)}) collective-permute-start(f32[16,3072]{1,0:T(8,128)S(1)} %get-tuple-element.28), channel_id=1, source_target_pairs={{0,1},{1,0},{2,3},{3,2},{4,5},{5,4},{6,7},{7,6},{8,9},{9,8},{10,11... | collective-permute-start | bytes 589832 | tf_op jit(solution)/shard_map/ppermute | solution.py:504
  5.3 1.4 %cut_early.1 = (f32[16,4224]{1,0:T(8,128)S(1)}, f32[16,4224]{1,0:T(8,128)S(1)}, f32[16,4224]{1,0:T(8,128)S(1)}, f32[16,4224]{1,0:T(8,128)S(1)}, f32[16,128]{1,0:T(8,128)S(1)}, /*index=5*/f32[16,128]{1,0:T(8,128)S(1)}) custom-call(f32[16,32768]{1,0:T(8,128)} %refs_2_.5), custom_call_target="tpu_custom_call" | custom-call | bytes 2097152 | tf_op jit(solution)/shard_map/cut_early/pallas_call | solution.py:208
  6.7 0.1 collective-permute-start.8
  6.9 3.3 %collective-permute-start.9 = (f32[16,4224]{1,0:T(8,128)S(1)}, f32[16,4224]{1,0:T(8,128)S(1)}, u32[]{:S(2)}, u32[]{:S(2)}) collective-permute-start(f32[16,4224]{1,0:T(8,128)S(1)} %get-tuple-element.33), channel_id=1, source_target_pairs={{0,2},{1,3},{2,0},{3,1},{4,6},{5,7},{6,4},{7,5},{8,10},{9,11},{10,... | collective-permute-start | bytes 811016 | tf_op jit(solution)/shard_map/ppermute | solution.py:504
  10.1 0.6 collective-permute-start.10
  10.7 2.1 %collective-permute-start = (f32[16,128]{1,0:T(8,128)S(1)}, f32[16,128]{1,0:T(8,128)S(1)}, u32[]{:S(2)}, u32[]{:S(2)}) collective-permute-start(f32[16,128]{1,0:T(8,128)S(1)} %get-tuple-element.19), channel_id=1, source_target_pairs={{0,4},{4,0},{8,12},{12,8},{16,20},{20,16},{24,28},{28,24},{32,36},... | collective-permute-start | bytes 24584 | tf_op jit(solution)/shard_map/ppermute | solution.py:529
  12.8 0.8 %collective-permute-done.refs_4_ = f32[16,128]{1,0:T(8,128)S(1)} collective-permute-done((f32[16,128]{1,0:T(8,128)S(1)}, f32[16,128]{1,0:T(8,128)S(1)}, u32[]{:S(2)}, u32[]{:S(2)}) %collective-permute-start) | collective-permute-done | bytes 8224 | tf_op jit(solution)/shard_map/ppermute | solution.py:529
  13.6 3.5 %collective-permute-start.1 = (f32[16,128]{1,0:T(8,128)S(1)}, f32[16,128]{1,0:T(8,128)S(1)}, u32[]{:S(2)}, u32[]{:S(2)}) collective-permute-start(f32[16,128]{1,0:T(8,128)S(1)} %get-tuple-element.20), channel_id=1, source_target_pairs={{4,8},{12,16},{20,24},{28,32},{36,40},{44,48},{52,56},{60,64},{68,... | collective-permute-start | bytes 24584 | tf_op jit(solution)/shard_map/ppermute | solution.py:531
  17.1 1.8 %collective-permute-done.1.refs_5_ = f32[16,128]{1,0:T(8,128)S(1)} collective-permute-done((f32[16,128]{1,0:T(8,128)S(1)}, f32[16,128]{1,0:T(8,128)S(1)}, u32[]{:S(2)}, u32[]{:S(2)}) %collective-permute-start.1) | collective-permute-done | bytes 8224 | tf_op jit(solution)/shard_map/ppermute | solution.py:531
  18.9 1.4 %collective-permute-start.6 = (f32[16,3072]{1,0:T(8,128)S(1)}, f32[16,3072]{1,0:T(8,128)S(1)}, u32[]{:S(2)}, u32[]{:S(2)}) collective-permute-start(f32[16,3072]{1,0:T(8,128)S(1)} %get-tuple-element.29), channel_id=1, source_target_pairs={{0,2},{1,3},{2,0},{3,1},{4,6},{5,7},{6,4},{7,5},{8,10},{9,11},{10,... | collective-permute-start | bytes 589832 | tf_op jit(solution)/shard_map/ppermute | solution.py:504
  20.2 0.6 collective-permute-start.7
  20.8 2.0 %shard_map.68 = (f32[16,1024]{1,0:T(8,128)S(1)}, f32[16,1024]{1,0:T(8,128)S(1)}, f32[16,1024]{1,0:T(8,128)S(1)}, f32[16,1024]{1,0:T(8,128)S(1)}) custom-call(s32[64]{0:T(128)} %first_hbm.1, s32[64]{0:T(128)} %last_hbm.1, f32[16,32768]{1,0:T(8,128)} %refs_2_.5, bf16[256,128]{1,0:T(8,128)(2,1)} %constant.20.refs_3_.taps_hbm, ...), custom_call_target="tpu_custom_call" | custom-call | flops 201326592 | bytes 1048576 | tf_op jit(solution)/shard_map/pallas_call | solution.py:360
  22.8 0.8 %collective-permute-start.2 = (f32[16,1024]{1,0:T(8,128)S(1)}, f32[16,1024]{1,0:T(8,128)S(1)}, u32[]{:S(2)}, u32[]{:S(2)}) collective-permute-start(f32[16,1024]{1,0:T(8,128)S(1)} %get-tuple-element.24), channel_id=1, source_target_pairs={{0,1},{1,0},{2,3},{3,2},{4,5},{5,4},{6,7},{7,6},{8,9},{9,8},{10,11... | collective-permute-start | bytes 196616 | tf_op jit(solution)/shard_map/ppermute | solution.py:504
  23.6 0.1 collective-permute-done.9.refs_2_
  23.7 2.4 %collective-permute-start.3 = (f32[16,1024]{1,0:T(8,128)S(1)}, f32[16,1024]{1,0:T(8,128)S(1)}, u32[]{:S(2)}, u32[]{:S(2)}) collective-permute-start(f32[16,1024]{1,0:T(8,128)S(1)} %get-tuple-element.25), channel_id=1, source_target_pairs={{0,2},{1,3},{2,0},{3,1},{4,6},{5,7},{6,4},{7,5},{8,10},{9,11},{10,... | collective-permute-start | bytes 196616 | tf_op jit(solution)/shard_map/ppermute | solution.py:504
  26.2 0.6 collective-permute-start.4
  26.7 3.6 %shard_map.70.refs_4_ = f32[4,8,128]{2,1,0:T(8,128)S(1)} custom-call(s32[64]{0:T(128)} %first_hbm.1, s32[64]{0:T(128)} %last_hbm.1, bf16[256,128]{1,0:T(8,128)(2,1)} %constant.20.refs_3_.taps_hbm, f32[16,4224]{1,0:T(8,128)S(1)} %get-tuple-element.31.refs_0_, f32[16,4224]{1,0:T(8,128)S(1)} %collective-permute-done.8.refs_1_, ...), custom_call_target="tpu_custom_call" | custom-call | flops 805306368 | bytes 2097152 | tf_op jit(solution)/shard_map/pallas_call | solution.py:448
  30.4 4.4 %collective-permute-done.7.refs_3_ = f32[16,3072]{1,0:T(8,128)S(1)} collective-permute-done((f32[16,3072]{1,0:T(8,128)S(1)}, f32[16,3072]{1,0:T(8,128)S(1)}, u32[]{:S(2)}, u32[]{:S(2)}) %collective-permute-start.7) | collective-permute-done | bytes 196640 | tf_op jit(solution)/shard_map/ppermute | solution.py:504
  34.7 0.6 shard_map.71.refs_4_
  35.3 0.8 %collective-permute-done.4.refs_3_ = f32[16,1024]{1,0:T(8,128)S(1)} collective-permute-done((f32[16,1024]{1,0:T(8,128)S(1)}, f32[16,1024]{1,0:T(8,128)S(1)}, u32[]{:S(2)}, u32[]{:S(2)}) %collective-permute-start.4) | collective-permute-done | bytes 65568 | tf_op jit(solution)/shard_map/ppermute | solution.py:504
  36.1 1.1 %shard_map.72 = f32[16,4,8,128]{3,2,1,0:T(8,128)} custom-call(f32[16,1024]{1,0:T(8,128)S(1)} %get-tuple-element.23.refs_0_, f32[16,1024]{1,0:T(8,128)S(1)} %collective-permute-done.2.refs_1_, f32[16,1024]{1,0:T(8,128)S(1)} %collective-permute-done.3.refs_2_, f32[16,1024]{1,0:T(8,128)S(1)} %collective-permute-done.4.refs_3_, f32[4,8,128]{2,1,0:T(8,128)S(1)} %shard_map.71.refs_4_), custom_call_target="tpu_custom_call" | custom-call | flops 33554432 | bytes 262144 | tf_op jit(solution)/shard_map/pallas_call | solution.py:487
  37.2 10.3 %all-to-all-start = ((f32[128,4,128]{2,1,0:T(4,128)}), f32[128,4,128]{2,1,0:T(4,128)S(1)}, u32[]{:S(2)}, u32[]{:S(2)}) async-start(f32[128,4,128]{2,1,0:T(4,128)} %bitcast), calls=%async_computation | async-start | bytes 524288 | tf_op jit(solution)/shard_map/all_to_all | solution.py:538
  47.5 0.1 dynamic_slice.7
  47.6 0.1 dynamic_slice.6
  47.7 10.8 %all-to-all-done = f32[128,4,128]{2,1,0:T(4,128)S(1)} async-done(((f32[128,4,128]{2,1,0:T(4,128)}), f32[128,4,128]{2,1,0:T(4,128)S(1)}, u32[]{:S(2)}, u32[]{:S(2)}) %all-to-all-start) | async-done | bytes 262176 | tf_op jit(solution)/shard_map/all_to_all | solution.py:538
  58.5 0.1 reduce_sum.9
  58.7 0.0 copy-start.3
  58.7 0.8 %collective-permute-start.11 = (f32[4,128]{1,0:T(4,128)S(1)}, f32[4,128]{1,0:T(4,128)S(1)}, u32[]{:S(2)}, u32[]{:S(2)}) collective-permute-start(f32[4,128]{1,0:T(4,128)S(1)} %reduce_sum.9), channel_id=1, source_target_pairs={{0,4},{4,0},{1,5},{5,1},{2,6},{6,2},{3,7},{7,3},{8,12},{12,8},{9,1... | collective-permute-start | bytes 6152 | tf_op jit(solution)/shard_map/ppermute | solution.py:541
  59.5 5.7 %shard_map.67 = (f32[16,32768]{1,0:T(8,128)}, f32[16,32768]{1,0:T(8,128)}) custom-call(s32[64]{0:T(128)} %first_hbm.1, s32[64]{0:T(128)} %last_hbm.1, f32[16,32768]{1,0:T(8,128)} %refs_2_.5, bf16[256,256]{1,0:T(8,128)(2,1)} %constant.19.clone.refs_3_, f32[16,128]{1,0:T(8,128)S(1)} %collective-permute-done.refs_4_, f32[16,128]{1,0:T(8,128)S(1)} %collective-permute-done.1.refs_5_), custom_call_target="tpu_custom_call" | custom-call | flops 1610612736 | bytes 8388608 | tf_op jit(solution)/shard_map/pallas_call | solution.py:360
  65.3 0.1 fusion
  65.3 0.7 %maximum_divide_fusion = f32[16,64]{1,0:T(8,128)} fusion(f32[4,64]{1,0:T(4,128)S(1)} %get-tuple-element.41, f32[4,64]{1,0:T(4,128)S(1)} %get-tuple-element.38, f32[4,64]{1,0:T(4,128)S(1)} %get-tuple-element.42, f32[4,64]{1,0:T(4,128)S(1)} %get-tuple-element.37, s32[64]{0:T(128)S(1)} %copy-done.1, s32[16]{0:T(128)S(1)} %dynamic_slice.7, s32[64]{0:T(128)S(1)} %copy-done.3, ...), kind=kLoop, calls=%fused_computation | loop fusion | flops 8192 | bytes 8832 | tf_op jit(solution)/shard_map/div | solution.py:545
  (15 shorter events, 0.0 us)
Async XLA Ops:
  3.2 17.0 %collective-permute-start.5 = (f32[16,3072]{1,0:T(8,128)S(1)}, f32[16,3072]{1,0:T(8,128)S(1)}, u32[]{:S(2)}, u32[]{:S(2)}) collective-permute-start(f32[16,3072]{1,0:T(8,128)S(1)} %get-tuple-element.28), channel_id=1, source_target_pairs={{0,1},{1,0},{2,3},{3,2},{4,5},{5,4},{6,7},{7,6},{8,9},{9,8},{10,11... | collective-permute-start | bytes 589832 | tf_op jit(solution)/shard_map/ppermute | solution.py:504
  6.7 16.0 %collective-permute-start.8 = (f32[16,4224]{1,0:T(8,128)S(1)}, f32[16,4224]{1,0:T(8,128)S(1)}, u32[]{:S(2)}, u32[]{:S(2)}) collective-permute-start(f32[16,4224]{1,0:T(8,128)S(1)} %get-tuple-element.32), channel_id=1, source_target_pairs={{0,1},{1,0},{2,3},{3,2},{4,5},{5,4},{6,7},{7,6},{8,9},{9,8},{10,11... | collective-permute-start | bytes 811016 | tf_op jit(solution)/shard_map/ppermute | solution.py:504
  6.9 16.9 %collective-permute-start.9 = (f32[16,4224]{1,0:T(8,128)S(1)}, f32[16,4224]{1,0:T(8,128)S(1)}, u32[]{:S(2)}, u32[]{:S(2)}) collective-permute-start(f32[16,4224]{1,0:T(8,128)S(1)} %get-tuple-element.33), channel_id=1, source_target_pairs={{0,2},{1,3},{2,0},{3,1},{4,6},{5,7},{6,4},{7,5},{8,10},{9,11},{10,... | collective-permute-start | bytes 811016 | tf_op jit(solution)/shard_map/ppermute | solution.py:504
  10.1 16.0 %collective-permute-start.10 = (f32[16,4224]{1,0:T(8,128)S(1)}, f32[16,4224]{1,0:T(8,128)S(1)}, u32[]{:S(2)}, u32[]{:S(2)}) collective-permute-start(f32[16,4224]{1,0:T(8,128)S(1)} %get-tuple-element.34), channel_id=1, source_target_pairs={{0,3},{1,2},{2,1},{3,0},{4,7},{5,6},{6,5},{7,4},{8,11},{9,10},{10,... | collective-permute-start | bytes 811016 | tf_op jit(solution)/shard_map/ppermute | solution.py:504
  10.7 2.9 %collective-permute-start = (f32[16,128]{1,0:T(8,128)S(1)}, f32[16,128]{1,0:T(8,128)S(1)}, u32[]{:S(2)}, u32[]{:S(2)}) collective-permute-start(f32[16,128]{1,0:T(8,128)S(1)} %get-tuple-element.19), channel_id=1, source_target_pairs={{0,4},{4,0},{8,12},{12,8},{16,20},{20,16},{24,28},{28,24},{32,36},... | collective-permute-start | bytes 24584 | tf_op jit(solution)/shard_map/ppermute | solution.py:529
  13.6 5.3 %collective-permute-start.1 = (f32[16,128]{1,0:T(8,128)S(1)}, f32[16,128]{1,0:T(8,128)S(1)}, u32[]{:S(2)}, u32[]{:S(2)}) collective-permute-start(f32[16,128]{1,0:T(8,128)S(1)} %get-tuple-element.20), channel_id=1, source_target_pairs={{4,8},{12,16},{20,24},{28,32},{36,40},{44,48},{52,56},{60,64},{68,... | collective-permute-start | bytes 24584 | tf_op jit(solution)/shard_map/ppermute | solution.py:531
  18.9 11.5 %collective-permute-start.6 = (f32[16,3072]{1,0:T(8,128)S(1)}, f32[16,3072]{1,0:T(8,128)S(1)}, u32[]{:S(2)}, u32[]{:S(2)}) collective-permute-start(f32[16,3072]{1,0:T(8,128)S(1)} %get-tuple-element.29), channel_id=1, source_target_pairs={{0,2},{1,3},{2,0},{3,1},{4,6},{5,7},{6,4},{7,5},{8,10},{9,11},{10,... | collective-permute-start | bytes 589832 | tf_op jit(solution)/shard_map/ppermute | solution.py:504
  20.2 14.5 %collective-permute-start.7 = (f32[16,3072]{1,0:T(8,128)S(1)}, f32[16,3072]{1,0:T(8,128)S(1)}, u32[]{:S(2)}, u32[]{:S(2)}) collective-permute-start(f32[16,3072]{1,0:T(8,128)S(1)} %get-tuple-element.30), channel_id=1, source_target_pairs={{0,3},{1,2},{2,1},{3,0},{4,7},{5,6},{6,5},{7,4},{8,11},{9,10},{10,... | collective-permute-start | bytes 589832 | tf_op jit(solution)/shard_map/ppermute | solution.py:504
  22.8 12.5 %collective-permute-start.2 = (f32[16,1024]{1,0:T(8,128)S(1)}, f32[16,1024]{1,0:T(8,128)S(1)}, u32[]{:S(2)}, u32[]{:S(2)}) collective-permute-start(f32[16,1024]{1,0:T(8,128)S(1)} %get-tuple-element.24), channel_id=1, source_target_pairs={{0,1},{1,0},{2,3},{3,2},{4,5},{5,4},{6,7},{7,6},{8,9},{9,8},{10,11... | collective-permute-start | bytes 196616 | tf_op jit(solution)/shard_map/ppermute | solution.py:504
  23.7 11.6 %collective-permute-start.3 = (f32[16,1024]{1,0:T(8,128)S(1)}, f32[16,1024]{1,0:T(8,128)S(1)}, u32[]{:S(2)}, u32[]{:S(2)}) collective-permute-start(f32[16,1024]{1,0:T(8,128)S(1)} %get-tuple-element.25), channel_id=1, source_target_pairs={{0,2},{1,3},{2,0},{3,1},{4,6},{5,7},{6,4},{7,5},{8,10},{9,11},{10,... | collective-permute-start | bytes 196616 | tf_op jit(solution)/shard_map/ppermute | solution.py:504
  26.2 10.0 %collective-permute-start.4 = (f32[16,1024]{1,0:T(8,128)S(1)}, f32[16,1024]{1,0:T(8,128)S(1)}, u32[]{:S(2)}, u32[]{:S(2)}) collective-permute-start(f32[16,1024]{1,0:T(8,128)S(1)} %get-tuple-element.26), channel_id=1, source_target_pairs={{0,3},{1,2},{2,1},{3,0},{4,7},{5,6},{6,5},{7,4},{8,11},{9,10},{10,... | collective-permute-start | bytes 196616 | tf_op jit(solution)/shard_map/ppermute | solution.py:504
  26.7 20.8 %copy-start = (s32[64]{0:T(128)S(1)}, s32[64]{0:T(128)}, u32[]{:S(2)}) copy-start(s32[64]{0:T(128)} %first_hbm.1) | copy-start | bytes 772
  26.7 20.9 %copy-start.2 = (s32[64]{0:T(128)S(1)}, s32[64]{0:T(128)}, u32[]{:S(2)}) copy-start(s32[64]{0:T(128)} %last_hbm.1) | copy-start | bytes 772
  37.2 21.3 %all-to-all-start = ((f32[128,4,128]{2,1,0:T(4,128)}), f32[128,4,128]{2,1,0:T(4,128)S(1)}, u32[]{:S(2)}, u32[]{:S(2)}) async-start(f32[128,4,128]{2,1,0:T(4,128)} %bitcast), calls=%async_computation | async-start | bytes 524288 | tf_op jit(solution)/shard_map/all_to_all | solution.py:538
  58.7 6.7 %copy-start.1 = (s32[64]{0:T(128)S(1)}, s32[64]{0:T(128)}, u32[]{:S(2)}) copy-start(s32[64]{0:T(128)} %first_hbm.1) | copy-start | bytes 772
  58.7 6.7 %copy-start.3 = (s32[64]{0:T(128)S(1)}, s32[64]{0:T(128)}, u32[]{:S(2)}) copy-start(s32[64]{0:T(128)} %last_hbm.1) | copy-start | bytes 772
  58.7 6.6 %collective-permute-start.11 = (f32[4,128]{1,0:T(4,128)S(1)}, f32[4,128]{1,0:T(4,128)S(1)}, u32[]{:S(2)}, u32[]{:S(2)}) collective-permute-start(f32[4,128]{1,0:T(4,128)S(1)} %reduce_sum.9), channel_id=1, source_target_pairs={{0,4},{4,0},{1,5},{5,1},{2,6},{6,2},{3,7},{7,3},{8,12},{12,8},{9,1... | collective-permute-start | bytes 6152 | tf_op jit(solution)/shard_map/ppermute | solution.py:541
